TPU v7x, 32 devices: a whole 2x2x4 slice. The times are simulated.
32 devices in a mesh: dom: 16 (over z, x, core), head: 2 (over y).
Axes of the slice: x: 2, y: 2, z: 4, core: 2. Of those that a mesh axis runs over, the one named last changes fastest.
Arguments:
- node_features: float32 [16384, 256], P('dom'), may hold values from -16 to 16, as said below
- w_query: float32 [256, 256], P(None, 'head'), may hold values from -0.375 to 0.375
- w_key: float32 [256, 256], P(None, 'head'), may hold values from -0.375 to 0.375
- w_value: float32 [256, 256], P(None, 'head'), may hold values from -0.375 to 0.375
- w_out: float32 [256, 256], P('head'), may hold values from -0.375 to 0.375
- nbr_part: int32 [128, 7], P('dom'), may hold values from 0 to 15, all different within a row; in each aligned block of 8 rows (0 to 7, 8 to 15, ...) at most 4 rows name the same one
- nbr_slot: int32 [128, 7], P('dom'), may hold values from 0 to 7
- key_mask: int32 [128, 7, 128], P('dom'), may hold values 0 or 1
- out_cotangent: float32 [16384, 256], P('dom'), may hold values from -6 to 6
Outputs:
- layer_out: float32 [16384, 256], P('dom', 'head')
- grad_features: float32 [16384, 256], P('dom', 'head')
- grad_query: float32 [256, 256], P(None, 'head')
- grad_key: float32 [256, 256], P(None, 'head')
- grad_value: float32 [256, 256], P(None, 'head')
- grad_out: float32 [256, 256], P('head')
Inputs may be any that keep to these rules, and one draw needn't show every extreme that they name: `nbr_part`: each block's 7 entries name different partitions; among the blocks of one partition, no partition is named by more than 4 entries, and 4 is reached. `node_features`: real node features.
All inputs are finite; a program needn't handle non-finite values. No bound on the sum of `key_mask` on one device may be relied on, other than what follows from the above.
Results may differ from a plain program's by a relative error of at most 0.0003.
Values sent between devices are 32-bit elements; how exact they have to be, the bound alone decides.
No kernel may reach another device: no remote copies, remote signals or barrier semaphores. Data moves between devices by JAX's collectives and lax.ppermute only.
A program may use at most 192 MiB of HBM per device.

v0:
```python
import jax
import jax.numpy as jnp
from jax import lax
from jax.sharding import PartitionSpec as P

D = 256
H = 8


def dot_high(left, right):
    return jnp.dot(left, right, precision=lax.Precision.HIGHEST)


def per_device(
    node_features, w_query, w_key, w_value, w_out, nbr_part, nbr_slot, key_mask, out_cotangent
):
    highest = lax.Precision.HIGHEST
    dom_count = lax.axis_size("dom")
    block_count, list_len = nbr_part.shape
    node_rows, model_width = node_features.shape
    block_rows = node_rows // block_count
    head_cols = w_query.shape[1]
    head_size = D // H
    local_heads = head_cols // head_size
    scale = head_size ** (-0.5)
    slot_cap = min(block_count, max(2, (block_count * list_len + dom_count - 1) // dom_count))
    request_count = block_count * list_len
    queries = dot_high(node_features, w_query)
    key_self = dot_high(node_features, w_key)
    value_self = dot_high(node_features, w_value)
    flat_part = nbr_part.reshape(-1)
    flat_slot = nbr_slot.reshape(-1)
    onehot = (flat_part[:, None] == jnp.arange(dom_count, dtype=jnp.int32)[None, :]).astype(
        jnp.int32
    )
    ranks = jnp.sum((jnp.cumsum(onehot, axis=0) - onehot) * onehot, axis=1)
    wanted = jnp.zeros((dom_count, slot_cap), jnp.int32).at[flat_part, ranks].set(flat_slot)
    asked = lax.all_to_all(wanted, "dom", split_axis=0, concat_axis=0, tiled=True)
    own_feats = node_features.reshape(block_count, block_rows, model_width)
    fetched = lax.all_to_all(own_feats[asked], "dom", split_axis=0, concat_axis=0, tiled=True)
    remote_inputs = fetched[flat_part, ranks].reshape(request_count * block_rows, model_width)
    remote_keys = dot_high(remote_inputs, w_key)
    remote_values = dot_high(remote_inputs, w_value)
    remote_pairs = jnp.concatenate([remote_keys, remote_values], axis=1).reshape(
        block_count, list_len, block_rows, 2 * head_cols
    )
    self_pairs = jnp.concatenate([key_self, value_self], axis=1).reshape(
        block_count, 1, block_rows, 2 * head_cols
    )
    all_pairs = jnp.concatenate([self_pairs, remote_pairs], axis=1).reshape(
        block_count, (list_len + 1) * block_rows, 2 * head_cols
    )
    mask_all = jnp.concatenate(
        [jnp.ones((block_count, 1, block_rows), jnp.int32), key_mask], axis=1
    )
    mask_all = mask_all.reshape(block_count, (list_len + 1) * block_rows) > 0

    def attend(query_blocks, pair_blocks):
        query_heads = query_blocks.reshape(block_count, block_rows, local_heads, head_size)
        key_heads = pair_blocks[..., :head_cols].reshape(block_count, -1, local_heads, head_size)
        value_heads = pair_blocks[..., head_cols:].reshape(block_count, -1, local_heads, head_size)
        scores = jnp.einsum("bqhd,bkhd->bhqk", query_heads, key_heads, precision=highest) * scale
        scores = jnp.where(mask_all[:, None, None, :], scores, -1e30)
        scores = scores - jnp.max(scores, axis=-1, keepdims=True)
        probs = jnp.exp(scores)
        probs = probs / jnp.sum(probs, axis=-1, keepdims=True)
        mixed = jnp.einsum("bhqk,bkhd->bqhd", probs, value_heads, precision=highest)
        return mixed.reshape(block_count, block_rows, head_cols)

    attended, pullback = jax.vjp(
        attend, queries.reshape(block_count, block_rows, head_cols), all_pairs
    )
    attended = attended.reshape(node_rows, head_cols)
    out_part = dot_high(attended, w_out)
    grad_attended = dot_high(out_cotangent, w_out.T)
    grad_out = dot_high(attended.T, out_cotangent)
    grad_queries, grad_pairs = pullback(grad_attended.reshape(block_count, block_rows, head_cols))
    grad_queries = grad_queries.reshape(node_rows, head_cols)
    grad_pairs = grad_pairs.reshape(block_count, list_len + 1, block_rows, 2 * head_cols)
    grad_self = grad_pairs[:, 0].reshape(node_rows, 2 * head_cols)
    grad_remote = grad_pairs[:, 1:].reshape(request_count, block_rows, 2 * head_cols)
    matches = (
        asked.reshape(-1)[None, :] == jnp.arange(block_count, dtype=jnp.int32)[:, None]
    ).astype(jnp.float32)
    remote_grad_keys = grad_remote[..., :head_cols].reshape(request_count * block_rows, head_cols)
    remote_grad_values = grad_remote[..., head_cols:].reshape(request_count * block_rows, head_cols)
    remote_grad_inputs = dot_high(remote_grad_keys, w_key.T) + dot_high(
        remote_grad_values, w_value.T
    )
    outgoing = (
        jnp.zeros((dom_count, slot_cap, block_rows, model_width), jnp.float32)
        .at[flat_part, ranks]
        .set(remote_grad_inputs.reshape(request_count, block_rows, model_width))
    )
    returned = lax.all_to_all(outgoing, "dom", split_axis=0, concat_axis=0, tiled=True)
    added = dot_high(matches, returned.reshape(dom_count * slot_cap, block_rows * model_width))
    grad_keys = grad_self[:, :head_cols]
    grad_values = grad_self[:, head_cols:]
    features_part = (
        dot_high(grad_queries, w_query.T)
        + dot_high(grad_keys, w_key.T)
        + dot_high(grad_values, w_value.T)
    )
    features_part = features_part + added.reshape(node_rows, model_width)
    grad_key = dot_high(node_features.T, grad_keys) + dot_high(remote_inputs.T, remote_grad_keys)
    grad_value = dot_high(node_features.T, grad_values) + dot_high(
        remote_inputs.T, remote_grad_values
    )
    grad_query = dot_high(node_features.T, grad_queries)
    layer_out, grad_features = (
        lax.psum_scatter(out_part, "head", scatter_dimension=1, tiled=True),
        lax.psum_scatter(features_part, "head", scatter_dimension=1, tiled=True),
    )
    grad_query, grad_key, grad_value, grad_out = lax.psum(
        (grad_query, grad_key, grad_value, grad_out), "dom"
    )
    return (layer_out, grad_features, grad_query, grad_key, grad_value, grad_out)


def solution(mesh):
    placed = (
        P("dom", None),
        P(None, "head"),
        P(None, "head"),
        P(None, "head"),
        P("head", None),
        P("dom", None),
        P("dom", None),
        P("dom", None, None),
        P("dom", None),
    )
    return jax.shard_map(
        per_device,
        mesh=mesh,
        in_specs=placed,
        out_specs=(
            P("dom", "head"),
            P("dom", "head"),
            P(None, "head"),
            P(None, "head"),
            P(None, "head"),
            P("head", None),
        ),
        check_vma=False,
    )
```

profile of v0, /device:TPU:0, one launch (start us, length us, event | category | flops | bytes accessed | tf_op | source)
XLA Modules:
  0.0 680.0 jit_solution(7281873127455355697)
XLA Ops:
  8.0 0.9 eq.36
  8.9 0.8 reshape.172
  10.0 0.8 reshape.206
  10.8 3.5 scatter_fusion
  14.4 13.6 %all_to_all.22 = s32[16,1,4]{2,1,0:T(1,128)S(1)} all-to-all(s32[16,1,4]{2,1,0:T(1,128)S(1)} %copy.74), channel_id=1, replica_groups=mesh['dom'=16,'head'=2] {'dom'}, dimensions={0} | all-to-all | bytes 512 | tf_op jit(solution)/shard_map/all_to_all | solution.py:38
  28.2 4.3 gather_fusion
  32.6 4.9 all-to-all-start.1
  37.5 1.2 fusion.62
  38.7 1.2 fusion.63
  40.0 1.1 pad_maximum_fusion.2
  41.0 1.6 copy.104
  42.6 1.2 convolution_bitcast_fusion.1
  44.0 2.6 convolution_bitcast_fusion
  46.6 0.9 copy.111
  47.5 140.6 %all-to-all-done.1 = f32[16,4,128,256]{3,2,1,0:T(8,128)} async-done(((f32[16,4,128,256]{3,2,1,0:T(8,128)}), f32[16,4,128,256]{3,2,1,0:T(8,128)}, u32[]{:S(2)}, u32[]{:S(2)}) %all-to-all-start.1) | async-done | bytes 8388640 | tf_op jit(solution)/shard_map/all_to_all | solution.py:40
  188.1 7.4 %gather_fusion.1 = f32[56,128,256]{2,1,0:T(8,128)} fusion(f32[16,4,128,256]{3,2,1,0:T(8,128)} %all-to-all-done.1, s32[56]{0:T(128)S(1)} %bitcast.161), kind=kCustom, calls=%fused_computation.1 | custom fusion | bytes 14680512 | tf_op jit(solution)/shard_map/gather | solution.py:41
  195.5 10.9 %fusion.64 = f32[7168,128]{0,1:T(8,128)S(1)} fusion(f32[7168,256]{1,0:T(8,128)} %bitcast.125, f32[256,128]{1,0:T(8,128)S(1)} %copy-done.7), kind=kOutput, calls=%fused_computation.100 | convolution fusion | flops 2818572288 | bytes 11141120 | tf_op jit(solution)/shard_map/dot_general | solution.py:11
  206.4 8.0 %fusion.65 = f32[7168,128]{0,1:T(8,128)S(1)} fusion(f32[7168,256]{1,0:T(8,128)S(1)} %bitcast.126, f32[256,128]{1,0:T(8,128)S(1)} %copy-done.8), kind=kOutput, calls=%fused_computation.101 | convolution fusion | flops 2818572288 | bytes 11141120 | tf_op jit(solution)/shard_map/dot_general | solution.py:11
  214.5 3.4 pad_maximum_fusion.1
  217.9 8.4 %copy.77 = f32[7168,256]{1,0:T(8,128)} copy(f32[7168,256]{0,1:T(8,128)} %pad_maximum_fusion.1) | data formatting | bytes 14680064 | tf_op jit(solution)/shard_map/concatenate | solution.py:44
  226.3 4.1 pad_maximum_fusion
  230.3 4.1 fusion.60
  234.4 5.3 copy.108
  239.8 17.4 %fusion.1 = (f32[8,4,128]{2,1,0:T(4,128)S(1)}, f32[8,4,128,1024]{3,2,1,0:T(8,128)S(1)}) fusion(pred[8,1024]{1,0:T(8,128)(4,1)S(1)} %fusion.41, f32[8,1024,4,32]{1,3,2,0:T(8,128)} %bitcast.143, f32[8,128,4,32]{1,0,3,2:T(8,128)S(1)} %bitcast.159), kind=kOutput, calls=%fused_computation.11 | convolution fusion | flops 1623191552 | bytes 21520384 | tf_op jit(solution)/shard_map/jvp(bqhd,bkhd->bhqk)/dot_general | solution.py:62
  257.3 4.2 fusion.19
  261.5 1.5 copy-done.2
  263.0 14.1 %fusion.12 = f32[8,4,32,1024]{3,2,1,0:T(8,128)} fusion(f32[8,4,128]{2,1,0:T(4,128)S(1)} %fusion.19, f32[8,4,128,1024]{3,2,1,0:T(8,128)S(1)} %get-tuple-element.46, f32[8,4,128]{2,1,0:T(4,128)S(1)} %get-tuple-element.45, pred[8,1024]{1,0:T(8,128)(4,1)S(1)} %fusion.41, f32[8,4,32,128]{3,0,2,1:T(8,128)S(1)} %bitcast.162), kind=kOutput, calls=%fused_computation.27 | convolution fusion | flops 1627389952 | bytes 21536768 | tf_op jit(solution)/shard_map/transpose(jvp(bhqk,bkhd->bqhd))/dot_general | solution.py:67
  277.1 5.3 copy.88
  282.4 5.3 copy.107
  287.7 28.2 %convert_reduce_fusion = (f32[8,4,128]{2,1,0:T(4,128)S(1)}, pred[8,4,128,1024]{3,2,1,0:T(32,128)(4,1)}, f32[8,4,128]{2,1,0:T(4,128)S(1)}, f32[8,4,128,1024]{3,2,1,0:T(8,128)}) fusion(f32[8,4,128]{2,1,0:T(4,128)S(1)} %get-tuple-element.45, f32[8,4,128,1024]{3,2,1,0:T(8,128)} %copy-done.2, pred[8,1024]{1,0:T(8,128)(4,1)S(1)} %fusion.41, ...), kind=kOutput, calls=%fused_computation.5 | convolution fusion | flops 1648353280 | bytes 42541056 | tf_op jit(solution)/shard_map/transpose(jvp(bhqk,bkhd->bqhd))/dot_general | solution.py:67
  316.0 12.9 %fusion.57 = (f32[8,4,128]{2,1,0:T(4,128)S(1)}, f32[8,4,128,1024]{3,2,1,0:T(8,128)S(1)}) fusion(f32[8,4,128]{2,1,0:T(4,128)S(1)} %get-tuple-element.45, f32[8,4,128,1024]{3,2,1,0:T(8,128)} %copy-done.2, pred[8,1024]{1,0:T(8,128)(4,1)S(1)} %fusion.41, f32[8,4,128]{2,1,0:T(4,128)S(1)} %neg.9, f32[8,4,128,1024]{3,2,1,0:T(8,128)} %get-tuple-element.47, ...), kind=kLoop, calls=%fused_computation.95 | loop fusion | flops 29356032 | bytes 50405376 | tf_op jit(solution)/shard_map/transpose(jvp())/reduce_sum | solution.py:64
  329.0 16.7 %fusion.2 = f32[8,4,1024,32]{2,3,1,0:T(8,128)} fusion(f32[8,4,128,1024]{3,2,1,0:T(8,128)S(1)} %get-tuple-element.35, pred[8,4,128,1024]{3,2,1,0:T(32,128)(4,1)} %get-tuple-element.37, f32[8,4,128]{2,1,0:T(4,128)S(1)} %bitcast.165, pred[8,1024]{1,0:T(8,128)(4,1)S(1)} %fusion.41, f32[8,128,4,32]{1,0,3,2:T(8,128)S(1)} %bitcast.160), kind=kOutput, calls=%fused_computation.12 | convolution fusion | flops 1627389952 | bytes 25714688 | tf_op jit(solution)/shard_map/transpose(jvp(bqhd,bkhd->bhqk))/dot_general | solution.py:62
  345.6 5.8 copy.90
  351.4 4.0 pad_add_fusion
  355.4 0.8 slice.45
  356.3 1.0 fusion.61
  357.3 1.9 copy-done.4
  359.2 6.0 fusion.66
  365.2 8.0 %convolution_add_fusion = f32[7168,256]{1,0:T(8,128)} fusion(f32[7168,256]{1,0:T(8,128)S(1)} %fusion.66, f32[7168,128]{1,0:T(8,128)S(1)} %bitcast.145, f32[256,128]{1,0:T(8,128)S(1)} %copy-done.8), kind=kOutput, calls=%fused_computation.14 | convolution fusion | flops 2820407296 | bytes 18481152 | tf_op jit(solution)/shard_map/dot_general | solution.py:11
  373.2 4.2 broadcast_in_dim.44
  377.4 16.5 %scatter_fusion.1 = f32[16,4,128,256]{3,2,1,0:T(8,128)} fusion(f32[16,4,128,256]{3,2,1,0:T(8,128)} %broadcast_in_dim.44, s32[56]{0:T(128)S(1)} %get-tuple-element.38, f32[56,128,256]{2,1,0:T(8,128)} %bitcast.140), kind=kCustom, calls=%fused_computation.3 | custom fusion | bytes 22020544 | tf_op jit(solution)/shard_map/scatter | solution.py:93
  393.9 36.5 %all-to-all-start.2 = ((f32[16,4,128,256]{3,2,1,0:T(8,128)}), f32[16,4,128,256]{3,2,1,0:T(8,128)}, u32[]{:S(2)}, u32[]{:S(2)}) async-start(f32[16,4,128,256]{3,2,1,0:T(8,128)} %scatter_fusion.1), calls=%async_computation.3 | async-start | bytes 16777216 | tf_op jit(solution)/shard_map/all_to_all | solution.py:95
  430.5 1.3 slice.42
  431.9 24.8 %fusion.16 = f32[8,128,4,32]{1,3,2,0:T(8,128)S(1)} fusion(f32[8,1024,4,32]{1,3,2,0:T(8,128)} %bitcast.144, f32[8,4,128,1024]{3,2,1,0:T(8,128)} %copy-done.5, pred[8,4,128,1024]{3,2,1,0:T(32,128)(4,1)} %get-tuple-element.37, f32[8,4,128]{2,1,0:T(4,128)S(1)} %bitcast.166, pred[8,1024]{1,0:T(8,128)(4,1)S(1)} %fusion.41), kind=kOutput, calls=%fused_computation.35 | convolution fusion | flops 1627389952 | bytes 25714688 | tf_op jit(solution)/shard_map/transpose(jvp(bqhd,bkhd->bhqk))/dot_general | solution.py:62
  457.0 22.5 %fusion.15 = f32[8,128,4,32]{1,3,2,0:T(8,128)S(1)} fusion(f32[8,1024,4,32]{1,3,2,0:T(8,128)} %bitcast.156, f32[8,4,128]{2,1,0:T(4,128)S(1)} %fusion.19, f32[8,4,128,1024]{3,2,1,0:T(8,128)} %copy-done.2, f32[8,4,128]{2,1,0:T(4,128)S(1)} %get-tuple-element.45, pred[8,1024]{1,0:T(8,128)(4,1)S(1)} %fusion.41), kind=kOutput, calls=%fused_computation.34 | convolution fusion | flops 1627389952 | bytes 21536768 | tf_op jit(solution)/shard_map/jvp(bhqk,bkhd->bqhd)/dot_general | solution.py:67
  479.8 1.3 convolution_bitcast_fusion.6
  481.1 1.3 fusion.23
  482.5 6.8 convolution_bitcast_fusion.2
  489.3 1.7 fusion.17
  491.0 6.8 convolution_bitcast_fusion.3
  497.8 1.7 fusion.18
  499.6 2.0 fusion.25
  502.9 1.9 fusion.21
  504.9 2.0 convolution_add_fusion.2
  506.9 78.2 %all-to-all-done.2 = f32[16,4,128,256]{3,2,1,0:T(8,128)} async-done(((f32[16,4,128,256]{3,2,1,0:T(8,128)}), f32[16,4,128,256]{3,2,1,0:T(8,128)}, u32[]{:S(2)}, u32[]{:S(2)}) %all-to-all-start.2) | async-done | bytes 8388640 | tf_op jit(solution)/shard_map/all_to_all | solution.py:95
  585.1 8.1 %copy.113 = f32[8,8,128,256]{3,1,2,0:T(8,128)S(1)} copy(f32[8,8,128,256]{3,2,1,0:T(8,128)} %bitcast.56) | data formatting | bytes 16777216
  593.2 2.8 fusion.43
  596.1 1.1 reshape.189
  597.2 3.5 fusion.14
  600.7 65.1 %all-reduce.6.cloned.1.call-done = (f32[256,128]{0,1:T(8,128)}, f32[256,128]{0,1:T(8,128)}, f32[256,128]{0,1:T(8,128)}, f32[128,256]{1,0:T(8,128)}) async-done(((f32[256,128]{0,1:T(8,128)}, f32[256,128]{0,1:T(8,128)}, f32[256,128]{0,1:T(8,128)}, f32[128,256]{1,0:T(8,128)}), (f32[256,128]{0,1:T(8,128)}, f32[256,128]{0,1:T(8,128)}, f32[256,128]{0,1:T(8,128)}, ...) | async-done | bytes 524304 | tf_op jit(solution)/shard_map/psum | solution.py:114
  665.8 1.7 copy.95
  667.5 1.7 copy.96
  669.1 1.7 copy.97
  670.8 1.6 copy.151
  (73 shorter events, 3.0 us)
Async XLA Ops:
  8.0 20.2 %copy-start = (f32[1024,256]{1,0:T(8,128)S(1)}, f32[1024,256]{1,0:T(8,128)}, u32[]{:S(2)}) copy-start(f32[1024,256]{1,0:T(8,128)} %param.9) | copy-start | bytes 3145732
  27.9 4.6 copy-start.15
  32.5 4.9 copy-start.7
  32.5 6.2 copy-start.8
  32.5 10.0 %copy-start.14 = (f32[256,128]{1,0:T(8,128)S(1)}, f32[256,128]{1,0:T(8,128)}, u32[]{:S(2)}) copy-start(f32[256,128]{1,0:T(8,128)} %param.10) | copy-start | bytes 393220
  32.6 155.5 %all-to-all-start.1 = ((f32[16,4,128,256]{3,2,1,0:T(8,128)}), f32[16,4,128,256]{3,2,1,0:T(8,128)}, u32[]{:S(2)}, u32[]{:S(2)}) async-start(f32[16,4,128,256]{3,2,1,0:T(8,128)} %bitcast.137), calls=%async_computation.1 | async-start | bytes 16777216 | tf_op jit(solution)/shard_map/all_to_all | solution.py:40
  37.5 6.5 copy-start.12
  37.5 10.0 %copy-start.17 = (s32[8,7,128]{2,0,1:T(8,128)S(1)}, s32[8,7,128]{2,0,1:T(8,128)}, u32[]{:S(2)}) copy-start(s32[8,7,128]{2,0,1:T(8,128)} %param.16) | copy-start | bytes 86020
  44.0 195.8 %copy-start.9 = (f32[16,8,8,128]{3,2,1,0:T(8,128)}, f32[16,8,8,128]{3,2,1,0:T(8,128)S(1)}, u32[]{:S(2)}) copy-start(f32[16,8,8,128]{3,2,1,0:T(8,128)S(1)} %copy.109) | copy-start | bytes 1572868
  195.5 10.9 %copy-start.1 = (f32[56,128,256]{2,1,0:T(8,128)S(1)}, f32[56,128,256]{2,1,0:T(8,128)}, u32[]{:S(2)}) copy-start(f32[56,128,256]{2,1,0:T(8,128)} %gather_fusion.1) | copy-start | bytes 22020100
  257.2 5.7 copy-start.2
  257.3 5.7 copy-start.11
  316.0 13.0 %copy-start.10 = (f32[16,8,8,128]{3,2,1,0:T(8,128)S(1)}, f32[16,8,8,128]{3,2,1,0:T(8,128)}, u32[]{:S(2)}) copy-start(f32[16,8,8,128]{3,2,1,0:T(8,128)} %copy-done.9) | copy-start | bytes 1572868
  328.9 16.7 %copy-start.5 = (f32[8,4,128,1024]{3,2,1,0:T(8,128)}, f32[8,4,128,1024]{3,2,1,0:T(8,128)S(1)}, u32[]{:S(2)}) copy-start(f32[8,4,128,1024]{3,2,1,0:T(8,128)S(1)} %get-tuple-element.35) | copy-start | bytes 50331652
  355.4 3.8 copy-start.4
  356.3 8.9 %copy-start.3 = (f32[8,7,128,256]{3,2,1,0:T(8,128)}, f32[8,7,128,256]{3,2,1,0:T(8,128)S(1)}, u32[]{:S(2)}) copy-start(f32[8,7,128,256]{3,2,1,0:T(8,128)S(1)} %slice.45) | copy-start | bytes 22020100
  393.9 191.2 %all-to-all-start.2 = ((f32[16,4,128,256]{3,2,1,0:T(8,128)}), f32[16,4,128,256]{3,2,1,0:T(8,128)}, u32[]{:S(2)}, u32[]{:S(2)}) async-start(f32[16,4,128,256]{3,2,1,0:T(8,128)} %scatter_fusion.1), calls=%async_computation.3 | async-start | bytes 16777216 | tf_op jit(solution)/shard_map/all_to_all | solution.py:95
  430.5 235.4 %all-reduce.6.cloned.1.call-start = ((), (), s32[]{:S(2)}) async-start(), calls=%async_computation.7 | async-start | bytes 1048576 | tf_op jit(solution)/shard_map/psum | solution.py:114
  431.9 50.6 %slice-start.2 = ((s8[7340032]{0:T(1024)(128)(4,1)}), s8[4194304]{0:T(1024)(128)(4,1)S(1)}, s32[]{:S(2)}) async-start(s8[7340032]{0:T(1024)(128)(4,1)} %bitcast.131), calls=%async_computation.10 | async-start | bytes 8388608
  456.7 25.8 %slice-start = ((s8[7340032]{0:T(1024)(128)(4,1)}), s8[4194304]{0:T(1024)(128)(4,1)S(1)}, s32[]{:S(2)}) async-start(s8[7340032]{0:T(1024)(128)(4,1)} %bitcast.127), calls=%async_computation.8 | async-start | bytes 8388608
  457.0 24.2 %copy-start.6 = (f32[1024,256]{1,0:T(8,128)S(1)}, f32[1024,256]{1,0:T(8,128)}, u32[]{:S(2)}) copy-start(f32[1024,256]{1,0:T(8,128)} %param.17) | copy-start | bytes 3145732
  457.0 25.5 %slice-start.1 = ((s8[7340032]{0:T(1024)(128)(4,1)}), s8[3145728]{0:T(1024)(128)(4,1)S(1)}, s32[]{:S(2)}) async-start(s8[7340032]{0:T(1024)(128)(4,1)} %bitcast.127), calls=%async_computation.9 | async-start | bytes 6291456
  457.0 25.5 %slice-start.3 = ((s8[7340032]{0:T(1024)(128)(4,1)}), s8[3145728]{0:T(1024)(128)(4,1)S(1)}, s32[]{:S(2)}) async-start(s8[7340032]{0:T(1024)(128)(4,1)} %bitcast.131), calls=%async_computation.11 | async-start | bytes 6291456
  489.3 10.3 %copy-start.13 = (f32[128,256]{1,0:T(8,128)S(1)}, f32[128,256]{1,0:T(8,128)}, u32[]{:S(2)}) copy-start(f32[128,256]{1,0:T(8,128)} %param.13) | copy-start | bytes 393220
  491.0 11.2 %copy-start.16 = (s32[16,1,4]{2,1,0:T(1,128)S(1)}, s32[16,1,4]{2,1,0:T(1,128)}, u32[]{:S(2)}) copy-start(s32[16,1,4]{2,1,0:T(1,128)} %copy-done.15) | copy-start | bytes 772
  499.5 171.3 %reduce-scatter.3.cloned.1.call-start = ((), (), s32[]{:S(2)}) async-start(), calls=%async_computation.5 | async-start | bytes 1572864 | tf_op jit(solution)/shard_map/reduce_scatter | solution.py:111
  501.6 169.2 %reduce-scatter.5.cloned.1.call-start = ((), (), s32[]{:S(2)}) async-start(), calls=%async_computation.6 | async-start | bytes 1572864 | tf_op jit(solution)/shard_map/reduce_scatter | solution.py:112
Sparse Core Ops, SparseCore 0:
  499.6 166.1 all-reduce.5
Sparse Core Ops, SparseCore 1:
  502.8 21.5 reduce-scatter.2
  600.8 52.7 reduce-scatter.4
where the time goes:
time: 689 us; the launch traced here: 680 us
  waiting for transfers between devices  284 us (41%)
  matrix products  195 us (28%)
  local copies, waits for them, and re-layouts  99.1 us (14%)
  starting transfers between devices  41.5 us (6%)
  other arithmetic  30.8 us (4%)
  between operations  16.2 us (2%)
  blocking collectives  13.6 us (2%)
    all_to_all x1, waiting for transfers between devices, per_device(): lax.all_to_all(own_feats[asked], 'dom', split_axis=0, concat_axis=0, tile...  141 us
    all_to_all x1, waiting for transfers between devices, per_device(): lax.all_to_all(outgoing, 'dom', split_axis=0, concat_axis=0, tiled=True)  78.2 us
    dot_general x19, matrix products, dot_high(): return jnp.dot(left, right, precision=lax.Precision.HIGHEST)  71.1 us
    psum x1, waiting for transfers between devices, per_device(): lax.psum((grad_query, grad_key, grad_value, grad_out), 'dom')  65.1 us
    dot_general x3, matrix products, attend(): mixed = jnp.einsum('bhqk,bkhd->bqhd', probs, value_heads, precision=highest)  64.8 us
    dot_general x3, matrix products, attend(): jnp.einsum('bqhd,bkhd->bhqk', query_heads, key_heads, precision=highest)  58.9 us
    all_to_all x1, starting transfers between devices, per_device(): lax.all_to_all(outgoing, 'dom', split_axis=0, concat_axis=0, tiled=True)  36.5 us
    unnamed x53, local copies, waits for them, and re-layouts  29.8 us
  transfers between devices with their start and end apart: 5, of which 3 were waited for; matrix products, arithmetic and copies ran while one was open for 16% of the time, Pallas kernels for 0%

commit v1 on v0

v1 whole, which is shorter than its diff:
```python
import functools

import jax
import jax.numpy as jnp
from jax import lax
from jax.experimental import pallas as pl
from jax.experimental.pallas import tpu as pltpu
from jax.sharding import PartitionSpec as P

HEAD_SIZE = 32
GROUP = 4
SCALE = HEAD_SIZE ** (-0.5)
MASKED = -1e30
F32 = jnp.float32
BF16 = jnp.bfloat16


def split(value):
    high = value.astype(BF16)
    return high, (value - high.astype(F32)).astype(BF16)


def mul(left, right, left_dim=1, right_dim=0):
    return lax.dot_general(
        left, right, (((left_dim,), (right_dim,)), ((), ())), preferred_element_type=F32
    )


def mul3(left, right, left_dim=1, right_dim=0):
    left_high, left_low = left
    right_high, right_low = right
    return (
        mul(left_high, right_high, left_dim, right_dim)
        + mul(left_high, right_low, left_dim, right_dim)
        + mul(left_low, right_high, left_dim, right_dim)
    )


def wide(first, second):
    return jnp.concatenate([first, second], axis=1)


def fold(value):
    half = value.shape[1] // 2
    return value[:, :half] + value[:, half:]


def forward_kernel(entries, ids, *refs):
    feats = refs[:entries]
    (cot_ref, bias_ref, wq_ref, wk_ref, wv_ref, wo_ref,
     out_ref, feat_ref, stat_ref, gq_ref, go_ref) = refs[entries:]
    rows = cot_ref.shape[0]
    cols = wq_ref.shape[1]
    heads = cols // HEAD_SIZE
    inputs = split(jnp.concatenate([ref[...] for ref in feats], axis=0))
    w_query = split(wq_ref[...])
    w_out = split(wo_ref[...])
    pairs = mul3(inputs, split(wide(wk_ref[...], wv_ref[...])))
    key_high, key_low = split(pairs[:, :cols])
    value_high, value_low = split(pairs[:, cols:])
    key_twice, key_both = wide(key_high, key_high), wide(key_high, key_low)
    value_twice, value_both = wide(value_high, value_high), wide(value_high, value_low)
    own = (inputs[0][:rows], inputs[1][:rows])
    query = mul3(own, w_query) * SCALE
    cot = split(cot_ref[...])
    grad_mixed = mul3(cot, w_out, 1, 1)
    bias = bias_ref[0]
    lane = lax.broadcasted_iota(jnp.int32, (rows, cols), 1) // HEAD_SIZE
    stat_lane = lax.broadcasted_iota(jnp.int32, (rows, rows), 1)
    mixed = jnp.zeros((rows, cols), F32)
    grad_query = jnp.zeros((rows, cols), F32)
    stats = jnp.zeros((rows, rows), F32)
    for head in range(heads):
        here = lane == head
        q_high, q_low = split(jnp.where(here, query, 0.0))
        scores = mul(wide(q_high, q_low), key_twice, 1, 1) + mul(q_high, key_low, 1, 1) + bias
        top = jnp.max(scores, axis=1, keepdims=True)
        probs = jnp.exp(scores - top)
        total = jnp.sum(probs, axis=1, keepdims=True)
        p_high, p_low = split(probs)
        weighted = fold(mul(p_high, value_both)) + mul(p_low, value_high)
        inverse = 1.0 / total
        part = jnp.where(here, weighted * inverse, 0.0)
        mixed = mixed + part
        grad_part = jnp.where(here, grad_mixed, 0.0)
        delta = jnp.sum(grad_part * part, axis=1, keepdims=True)
        g_high, g_low = split(grad_part)
        grad_probs = mul(wide(g_high, g_low), value_twice, 1, 1) + mul(g_high, value_low, 1, 1)
        s_high, s_low = split(probs * (grad_probs - delta))
        back = fold(mul(s_high, key_both)) + mul(s_low, key_high)
        grad_query = grad_query + jnp.where(here, back * (inverse * SCALE), 0.0)
        stats = jnp.where(stat_lane == head, top + jnp.log(total), stats)
        stats = jnp.where(stat_lane == heads + head, delta, stats)
    mixed = split(mixed)
    grad_query = split(grad_query)
    out_ref[...] = mul3(mixed, w_out)
    feat_ref[...] = mul3(grad_query, w_query, 1, 1)
    stat_ref[0] = jnp.transpose(stats)[: 2 * heads]

    @pl.when(pl.program_id(0) == 0)
    def _():
        gq_ref[...] = jnp.zeros_like(gq_ref)
        go_ref[...] = jnp.zeros_like(go_ref)

    gq_ref[...] += mul3(own, grad_query, 0, 0)
    go_ref[...] += mul3(mixed, cot, 0, 0)


def attend_forward(ids, all_feats, out_cotangent, bias, w_query, w_key, w_value, w_out):
    block_count, entries = ids.shape
    node_rows, width = out_cotangent.shape
    rows = node_rows // block_count
    cols = w_query.shape[1]
    heads = cols // HEAD_SIZE

    def picked(entry):
        return pl.BlockSpec((rows, width), lambda b, ids: (ids[b, entry], 0))

    def whole(array):
        return pl.BlockSpec(array.shape, lambda b, ids: (0,) * array.ndim)

    own = pl.BlockSpec((rows, width), lambda b, ids: (b, 0))
    grad_shape = jax.ShapeDtypeStruct((width, cols), F32)
    out_shape = jax.ShapeDtypeStruct((cols, width), F32)
    node_shape = jax.ShapeDtypeStruct((node_rows, width), F32)
    return pl.pallas_call(
        functools.partial(forward_kernel, entries),
        out_shape=(
            node_shape,
            node_shape,
            jax.ShapeDtypeStruct((block_count, 2 * heads, rows), F32),
            grad_shape,
            out_shape,
        ),
        grid_spec=pltpu.PrefetchScalarGridSpec(
            num_scalar_prefetch=1,
            grid=(block_count,),
            in_specs=[picked(entry) for entry in range(entries)]
            + [own, pl.BlockSpec((1, 1, entries * rows), lambda b, ids: (b, 0, 0))]
            + [whole(w) for w in (w_query, w_key, w_value, w_out)],
            out_specs=(
                own,
                own,
                pl.BlockSpec((1, 2 * heads, rows), lambda b, ids: (b, 0, 0)),
                whole(grad_shape),
                whole(out_shape),
            ),
        ),
        compiler_params=pltpu.CompilerParams(
            dimension_semantics=("arbitrary",), vmem_limit_bytes=50 * 1024 * 1024
        ),
        name="attend_forward",
    )(ids, *([all_feats] * entries), out_cotangent, bias, w_query, w_key, w_value, w_out)


def backward_kernel(steps_ref, readers_ref, *refs):
    feats, cots, stats = refs[:GROUP], refs[GROUP:2 * GROUP], refs[2 * GROUP:3 * GROUP]
    (own_ref, bias_ref, part_ref, wq_ref, wk_ref, wv_ref, wo_ref,
     feat_ref, gk_ref, gv_ref, key_mem, value_mem, dk_mem, dv_mem) = refs[3 * GROUP:]
    step = pl.program_id(0)
    rows = own_ref.shape[0]
    cols = wq_ref.shape[1]
    heads = cols // HEAD_SIZE
    lane = lax.broadcasted_iota(jnp.int32, (rows, cols), 1) // HEAD_SIZE
    kind = steps_ref[1, step]

    @pl.when(step == 0)
    def _():
        gk_ref[...] = jnp.zeros_like(gk_ref)
        gv_ref[...] = jnp.zeros_like(gv_ref)

    @pl.when(kind % 2 == 1)
    def _():
        pairs = mul3(split(own_ref[...]), split(wide(wk_ref[...], wv_ref[...])))
        for head in range(heads):
            here = lane == head
            at = pl.ds(head * rows, rows)
            key_mem[at, :] = wide(*split(jnp.where(here, pairs[:, :cols], 0.0)))
            value_mem[at, :] = wide(*split(jnp.where(here, pairs[:, cols:], 0.0)))
        dk_mem[...] = jnp.zeros_like(dk_mem)
        dv_mem[...] = jnp.zeros_like(dv_mem)

    @pl.when(kind >= 4)
    def _():
        inputs = split(jnp.concatenate([ref[...] for ref in feats], axis=0))
        q_high, q_low = split(mul3(inputs, split(wq_ref[...])) * SCALE)
        cot = split(jnp.concatenate([ref[...] for ref in cots], axis=0))
        g_high, g_low = split(mul3(cot, split(wo_ref[...]), 1, 1))
        q_twice, q_both = wide(q_high, q_high), wide(q_high, q_low)
        g_twice, g_both = wide(g_high, g_high), wide(g_high, g_low)
        mark_row = lax.broadcasted_iota(jnp.int32, (8, GROUP * rows), 0)
        mark_col = lax.broadcasted_iota(jnp.int32, (8, GROUP * rows), 1)
        marks = (mark_row == mark_col // rows).astype(BF16)
        bias = mul(bias_ref[0].astype(BF16), marks, 0, 0)
        stat = jnp.concatenate([ref[0] for ref in stats], axis=1)
        grad_key = dk_mem[...]
        grad_value = dv_mem[...]
        for head in range(heads):
            here = lane == head
            keys = key_mem[pl.ds(head * rows, rows), :]
            values = value_mem[pl.ds(head * rows, rows), :]
            scores = mul(keys, q_twice, 1, 1) + mul(keys[:, :cols], q_low, 1, 1)
            probs = jnp.exp(scores + (bias - stat[head:head + 1]))
            grad_probs = mul(values, g_twice, 1, 1) + mul(values[:, :cols], g_low, 1, 1)
            grad_scores = probs * (grad_probs - stat[heads + head:heads + head + 1])
            p_high, p_low = split(probs)
            term = fold(mul(p_high, g_both)) + mul(p_low, g_high)
            grad_value = grad_value + jnp.where(here, term, 0.0)
            s_high, s_low = split(grad_scores)
            term = fold(mul(s_high, q_both)) + mul(s_low, q_high)
            grad_key = grad_key + jnp.where(here, term, 0.0)
        dk_mem[...] = grad_key
        dv_mem[...] = grad_value

    @pl.when((kind // 2) % 2 == 1)
    def _():
        grad_key, grad_value = split(dk_mem[...]), split(dv_mem[...])
        own = split(own_ref[...])
        feat_ref[...] = (
            part_ref[...]
            + mul3(grad_key, split(wk_ref[...]), 1, 1)
            + mul3(grad_value, split(wv_ref[...]), 1, 1)
        )
        gk_ref[...] += mul3(own, grad_key, 0, 0)
        gv_ref[...] += mul3(own, grad_value, 0, 0)


def attend_backward(
    steps, readers, all_feats, all_cots, all_stats, own_feats, bias, part,
    w_query, w_key, w_value, w_out, rows,
):
    count = steps.shape[1]
    node_rows, width = own_feats.shape
    cols = w_query.shape[1]
    heads = cols // HEAD_SIZE

    def picked(at):
        return pl.BlockSpec((rows, width), lambda s, steps, readers: (readers[s * GROUP + at], 0))

    def picked_stat(at):
        return pl.BlockSpec(
            (1, 2 * heads, rows), lambda s, steps, readers: (readers[s * GROUP + at], 0, 0)
        )

    def whole(array):
        return pl.BlockSpec(array.shape, lambda s, steps, readers: (0,) * array.ndim)

    own = pl.BlockSpec((rows, width), lambda s, steps, readers: (steps[0, s], 0))
    grad_shape = jax.ShapeDtypeStruct((width, cols), F32)
    return pl.pallas_call(
        backward_kernel,
        out_shape=(jax.ShapeDtypeStruct((node_rows, width), F32), grad_shape, grad_shape),
        grid_spec=pltpu.PrefetchScalarGridSpec(
            num_scalar_prefetch=2,
            grid=(count,),
            in_specs=[picked(at) for at in range(GROUP)]
            + [picked(at) for at in range(GROUP)]
            + [picked_stat(at) for at in range(GROUP)]
            + [own, pl.BlockSpec((1, 8, rows), lambda s, steps, readers: (s, 0, 0)), own]
            + [whole(w) for w in (w_query, w_key, w_value, w_out)],
            out_specs=(own, whole(grad_shape), whole(grad_shape)),
            scratch_shapes=[
                pltpu.VMEM((heads * rows, 2 * cols), BF16),
                pltpu.VMEM((heads * rows, 2 * cols), BF16),
                pltpu.VMEM((rows, cols), F32),
                pltpu.VMEM((rows, cols), F32),
            ],
        ),
        compiler_params=pltpu.CompilerParams(
            dimension_semantics=("arbitrary",), vmem_limit_bytes=50 * 1024 * 1024
        ),
        name="attend_backward",
    )(
        steps, readers, *([all_feats] * GROUP), *([all_cots] * GROUP), *([all_stats] * GROUP),
        own_feats, bias, part, w_query, w_key, w_value, w_out,
    )


def plan_backward(all_ids, all_mask, me, block_count, pair_limit):
    blocks, entries = all_ids.shape
    candidates = blocks * entries
    flat = all_ids.reshape(-1)
    slot = jnp.where(flat // block_count == me, flat % block_count, block_count)
    order = jnp.arange(candidates, dtype=jnp.int32)
    same = (slot[:, None] == slot[None, :]) & (order[None, :] < order[:, None])
    rank = jnp.sum(same.astype(jnp.int32), axis=1)
    block_range = jnp.arange(block_count, dtype=jnp.int32)
    tally = jnp.sum((slot[None, :] == block_range[:, None]).astype(jnp.int32), axis=1)
    chunks = (tally + GROUP - 1) // GROUP
    ends = jnp.sum(
        jnp.where(block_range[None, :] <= block_range[:, None], chunks[None, :], 0), axis=1
    )
    starts = ends - chunks
    count = (pair_limit + block_count * GROUP) // GROUP
    places = count * GROUP
    start_of = jnp.sum(
        jnp.where(slot[:, None] == block_range[None, :], starts[None, :], 0), axis=1
    )
    place = jnp.where(slot < block_count, start_of * GROUP + rank, places)
    spot = jnp.arange(places, dtype=jnp.int32)
    hit = place[None, :] == spot[:, None]
    source = jnp.sum(jnp.where(hit, order[None, :], 0), axis=1)
    filled = jnp.sum(hit.astype(jnp.int32), axis=1) > 0
    readers = source // entries
    mask = all_mask.reshape(candidates, -1)[source]
    bias = jnp.where((mask > 0) & filled[:, None], 0.0, MASKED)
    bias = bias.reshape(count, GROUP, -1)
    bias = jnp.concatenate([bias, jnp.zeros((count, 8 - GROUP, bias.shape[2]), F32)], axis=1)
    step = jnp.arange(count, dtype=jnp.int32)
    block = jnp.sum((step[:, None] >= ends[None, :]).astype(jnp.int32), axis=1)
    live = block < block_count
    block = jnp.minimum(block, block_count - 1)
    first = jnp.sum((step[:, None] == starts[None, :]).astype(jnp.int32), axis=1) > 0
    last = jnp.sum((step[:, None] == ends[None, :] - 1).astype(jnp.int32), axis=1) > 0
    kind = jnp.where(
        live, first.astype(jnp.int32) + 2 * last.astype(jnp.int32) + 4, 0
    )
    return jnp.stack([block, kind]), readers, bias


def head_scatter(part):
    size = lax.axis_size("head")
    if size != 2:
        return lax.psum_scatter(part, "head", scatter_dimension=1, tiled=True)
    me = lax.axis_index("head")
    half = part.shape[1] // 2
    sent = lax.dynamic_slice_in_dim(part, (1 - me) * half, half, axis=1)
    kept = lax.dynamic_slice_in_dim(part, me * half, half, axis=1)
    return kept + lax.ppermute(sent, "head", [(0, 1), (1, 0)])


def per_device(
    node_features, w_query, w_key, w_value, w_out, nbr_part, nbr_slot, key_mask, out_cotangent
):
    dom_count = lax.axis_size("dom")
    block_count, list_len = nbr_part.shape
    node_rows, width = node_features.shape
    rows = node_rows // block_count
    me = lax.axis_index("dom")
    slot_cap = min(block_count, max(2, (block_count * list_len + dom_count - 1) // dom_count))
    self_ids = me * block_count + jnp.arange(block_count, dtype=jnp.int32)[:, None]
    ids = jnp.concatenate([self_ids, nbr_part * block_count + nbr_slot], axis=1)
    mask = jnp.concatenate([jnp.ones((block_count, 1, rows), jnp.int32), key_mask], axis=1)
    bias = jnp.where(mask > 0, 0.0, MASKED).reshape(block_count, 1, (list_len + 1) * rows)
    all_feats = lax.all_gather(node_features, "dom", axis=0, tiled=True)
    all_cots = lax.all_gather(out_cotangent, "dom", axis=0, tiled=True)
    all_ids = lax.all_gather(ids, "dom", axis=0, tiled=True)
    all_mask = lax.all_gather(mask, "dom", axis=0, tiled=True)
    steps, readers, back_bias = plan_backward(
        all_ids, all_mask, me, block_count, dom_count * slot_cap
    )
    out_part, feat_part, stats, grad_query, grad_out = attend_forward(
        ids, all_feats, out_cotangent, bias, w_query, w_key, w_value, w_out
    )
    layer_out = head_scatter(out_part)
    all_stats = lax.all_gather(stats, "dom", axis=0, tiled=True)
    feats_part, grad_key, grad_value = attend_backward(
        steps, readers, all_feats, all_cots, all_stats, node_features, back_bias, feat_part,
        w_query, w_key, w_value, w_out, rows,
    )
    grad_features = head_scatter(feats_part)
    grad_query, grad_key, grad_value, grad_out = lax.psum(
        (grad_query, grad_key, grad_value, grad_out), "dom"
    )
    return (layer_out, grad_features, grad_query, grad_key, grad_value, grad_out)


def solution(mesh):
    placed = (
        P("dom", None),
        P(None, "head"),
        P(None, "head"),
        P(None, "head"),
        P("head", None),
        P("dom", None),
        P("dom", None),
        P("dom", None, None),
        P("dom", None),
    )
    return jax.shard_map(
        per_device,
        mesh=mesh,
        in_specs=placed,
        out_specs=(
            P("dom", "head"),
            P("dom", "head"),
            P(None, "head"),
            P(None, "head"),
            P(None, "head"),
            P("head", None),
        ),
        check_vma=False,
    )
```

time: 689 us -> 441 us (0.64); the launches traced: 680 us -> 440 us
  matrix products: 195 us -> 0 us
  Pallas kernels: 0 us -> 102 us
  local copies, waits for them, and re-layouts: 99.1 us -> 10.1 us
  blocking collectives: 13.6 us -> 68.3 us
  waiting for transfers between devices: 284 us -> 236 us
  starting transfers between devices: 41.5 us -> 2.87 us
  other arithmetic: 30.8 us -> 6.7 us
    all_to_all x2 -> x0, waiting for transfers between devices: 219 us -> none  [the longest x1 141 us: per_device(): lax.all_to_all(own_feats[asked], 'dom', split_axis=0, concat_axis=0, tile...]
    dot_general x25 -> x0, matrix products: 195 us -> none  [the longest x19 71.1 us: dot_high(): return jnp.dot(left, right, precision=lax.Precision.HIGHEST)]
    all_gather x0 -> x2, waiting for transfers between devices: none -> 142 us  [the longest x1 83.7 us: per_device(): all_feats = lax.all_gather(node_features, 'dom', axis=0, tiled=True)]
    pallas_call x0 -> x2, Pallas kernels: none -> 102 us  [the longest x1 53 us: attend_backward(): pl.pallas_call(backward_kernel, out_shape=(jax.ShapeDtypeStruct((node_row...]
    all_gather x0 -> x3, blocking collectives: none -> 68.3 us  [the longest x1 23.7 us: per_device(): all_ids = lax.all_gather(ids, 'dom', axis=0, tiled=True)]
    all_to_all x2 -> x0, starting transfers between devices: 41.4 us -> none  [the longest x1 36.5 us: per_device(): lax.all_to_all(outgoing, 'dom', split_axis=0, concat_axis=0, tiled=True)]
    unnamed x53 -> x24, local copies, waits for them, and re-layouts: 29.8 us -> 7.29 us
    scatter x2 -> x0, local copies, waits for them, and re-layouts: 20 us -> none  [the longest x1 16.5 us: per_device(): outgoing = jnp.zeros((dom_count, slot_cap, block_rows, model_width), jnp....]
  transfers between devices with their start and end apart: 5 -> 5, of which waited for: 3 -> 4; matrix products, arithmetic and copies ran while one was open for 16% -> 2% of each run, Pallas kernels for 0% -> 23%
where the time goes in v1:
time: 441 us; the launch traced here: 440 us
  waiting for transfers between devices  236 us (54%)
  Pallas kernels  102 us (23%)
  blocking collectives  68.3 us (15%)
  between operations  13.9 us (3%)
  local copies, waits for them, and re-layouts  10.1 us (2%)
  other arithmetic  6.7 us (2%)
    all_gather x1, waiting for transfers between devices, per_device(): all_feats = lax.all_gather(node_features, 'dom', axis=0, tiled=True)  83.7 us
    psum x1, waiting for transfers between devices, per_device(): lax.psum((grad_query, grad_key, grad_value, grad_out), 'dom')  82.2 us
    all_gather x1, waiting for transfers between devices, per_device(): all_cots = lax.all_gather(out_cotangent, 'dom', axis=0, tiled=True)  58.3 us
    pallas_call x1, Pallas kernels, attend_backward(): pl.pallas_call(backward_kernel, out_shape=(jax.ShapeDtypeStruct((node_row...  53 us
    pallas_call x1, Pallas kernels, attend_forward(): pl.pallas_call(functools.partial(forward_kernel, entries), out_shape=(nod...  49.1 us
    all_gather x1, blocking collectives, per_device(): all_ids = lax.all_gather(ids, 'dom', axis=0, tiled=True)  23.7 us
    all_gather x1, blocking collectives, per_device(): all_stats = lax.all_gather(stats, 'dom', axis=0, tiled=True)  22.7 us
    all_gather x1, blocking collectives, per_device(): all_mask = lax.all_gather(mask, 'dom', axis=0, tiled=True)  21.8 us
  transfers between devices with their start and end apart: 5, of which 4 were waited for; matrix products, arithmetic and copies ran while one was open for 2% of the time, Pallas kernels for 23%

profile of v1, /device:TPU:0, one launch (start us, length us, event | category | flops | bytes accessed | tf_op | source)
XLA Modules:
  0.0 440.4 jit_solution(14340846539605891834)
XLA Ops:
  7.2 0.0 copy-start
  7.2 0.0 copy-start.6
  7.2 0.0 copy-start.7
  7.2 0.0 copy-start.8
  7.2 0.0 copy-start.9
  7.2 0.0 all-gather.3.cloned.1.call-start
  7.3 0.7 all-gather.3.cloned.1.call-update
  8.0 0.0 all-gather.5.cloned.1.call-start
  8.0 0.7 all-gather.5.cloned.1.call-update
  8.7 0.0 all-reduce.5.cloned.1.call-start
  8.8 0.8 compare_select_fusion
  9.5 0.8 concatenate.10
  10.3 0.7 multiply_add_fusion
  11.0 0.1 pad_add_fusion.ids
  11.1 23.7 %all_gather.16 = s32[128,8]{1,0:T(8,128)S(1)} all-gather(s32[8,8]{1,0:T(8,128)S(1)} %pad_add_fusion.ids), channel_id=1, replica_groups=mesh['dom'=16,'head'=2] {'dom'}, dimensions={0}, use_global_device_ids=true | all-gather | bytes 4352 | tf_op jit(solution)/shard_map/all_gather | solution.py:347
  34.8 0.1 reshape.267
  34.9 21.8 %all_gather.19 = s32[128,8,128]{2,0,1:T(8,128)S(1)} all-gather(s32[8,8,128]{2,0,1:T(8,128)S(1)} %concatenate.10), channel_id=1, replica_groups=mesh['dom'=16,'head'=2] {'dom'}, dimensions={0}, use_global_device_ids=true | all-gather | bytes 557056 | tf_op jit(solution)/shard_map/all_gather | solution.py:348
  56.7 0.3 copy.24
  57.0 0.1 convert_reduce_fusion.2
  57.2 0.1 select_reduce_fusion.2
  57.3 0.1 select_reduce_fusion.1
  57.4 0.5 convert_reduce_fusion
  57.9 0.2 convert_reduce_fusion.1
  58.1 0.1 gt.56
  58.2 0.6 gather_fusion
  58.9 0.1 and_select_fusion
  59.0 0.1 convert_reduce_fusion.5
  59.1 0.1 convert_reduce_fusion.3
  59.2 83.7 %all-gather.3.cloned.1.call-done.refs_0_.refs_1_.refs_2_.refs_3_.refs_4_.refs_5_.refs_6_.refs_7_ = f32[16384,256]{1,0:T(8,128)} async-done(((f32[1024,256]{1,0:T(8,128)}), f32[16384,256]{1,0:T(8,128)}) %all-gather.3.cloned.1.call-update) | async-done | bytes 16777232 | tf_op jit(solution)/shard_map/all_gather | solution.py:345
  142.9 0.0 copy-done
  142.9 0.0 copy-done.6
  142.9 0.0 copy-done.7
  142.9 0.0 copy-done.8
  142.9 0.0 copy-done.9
  142.9 0.0 copy-start.1
  142.9 49.1 %attend_forward.1 = (f32[1024,256]{1,0:T(8,128)S(1)}, f32[1024,256]{1,0:T(8,128)S(1)}, f32[8,8,128]{2,1,0:T(8,128)S(1)}, f32[256,128]{1,0:T(8,128)}, f32[128,256]{1,0:T(8,128)}) custom-call(s32[8,8]{1,0:T(8,128)S(1)} %pad_add_fusion.ids, f32[16384,256]{1,0:T(8,128)} %all-gather.3.cloned.1.call-done.refs_0_.refs_1_.refs_2_.refs_3_.refs_4_.refs_5_.refs_6_.refs_7_, ...), custom_call_target="tpu_custom_call" | custom-call | tf_op jit(solution)/shard_map/attend_forward/pallas_call | solution.py:126
  192.1 0.0 copy-start.2
  192.1 0.0 copy-start.3
  192.1 0.9 constant_dynamic-slice_fusion.1
  193.0 1.5 collective-permute-start
  194.5 0.0 copy-done.2
  194.5 0.0 copy-done.3
  194.5 22.7 %all_gather.18.refs_8_.refs_9_.refs_10_.refs_11_ = f32[128,8,128]{2,1,0:T(8,128)S(1)} all-gather(f32[8,8,128]{2,1,0:T(8,128)S(1)} %get-tuple-element.15), channel_id=1, replica_groups=mesh['dom'=16,'head'=2] {'dom'}, dimensions={0}, use_global_device_ids=true | all-gather | bytes 557056 | tf_op jit(solution)/shard_map/all_gather | solution.py:356
  217.2 58.3 %all-gather.5.cloned.1.call-done.refs_4_.refs_5_.refs_6_.refs_7_ = f32[16384,256]{1,0:T(8,128)} async-done(((f32[1024,256]{1,0:T(8,128)}), f32[16384,256]{1,0:T(8,128)}) %all-gather.5.cloned.1.call-update) | async-done | bytes 16777232 | tf_op jit(solution)/shard_map/all_gather | solution.py:346
  275.5 0.0 copy-done.1
  275.5 0.0 copy-start.4
  275.5 53.0 %attend_backward.1 = (f32[1024,256]{1,0:T(8,128)S(1)}, f32[256,128]{1,0:T(8,128)}, f32[256,128]{1,0:T(8,128)}) custom-call(s32[2,24]{1,0:T(2,128)S(1)} %pad_add_fusion.1.steps_ref, s32[96]{0:T(128)S(1)} %and_select_fusion.1.readers_ref, f32[16384,256]{1,0:T(8,128)} %all-gather.3.cloned.1.call-done.refs_0_.refs_1_.refs_2_.refs_3_.refs_4_.refs_5_.refs_6_.refs_7_, ...), custom_call_target="tpu_custom_call" | custom-call | tf_op jit(solution)/shard_map/attend_backward/pallas_call | solution.py:250
  328.4 0.0 copy-start.5
  328.4 1.0 copy-done.5
  329.5 1.3 collective-permute-start.1
  330.7 0.0 all-reduce.5.cloned.1.call-update
  330.8 0.0 collective-permute-done
  330.8 0.0 copy-done.4
  330.8 1.9 dynamic-slice_add_fusion.1
  332.7 10.9 %collective-permute-done.1 = f32[1024,128]{1,0:T(8,128)S(1)} collective-permute-done((f32[1024,128]{1,0:T(8,128)S(1)}, f32[1024,128]{1,0:T(8,128)S(1)}, u32[]{:S(2)}, u32[]{:S(2)}) %collective-permute-start.1) | collective-permute-done | bytes 524320 | tf_op jit(solution)/shard_map/ppermute | solution.py:329
  343.6 1.9 dynamic-slice_add_fusion
  345.4 82.2 %all-reduce.5.cloned.1.call-done = (f32[256,128]{1,0:T(8,128)}, f32[256,128]{1,0:T(8,128)}, f32[256,128]{1,0:T(8,128)}, f32[128,256]{1,0:T(8,128)}) async-done(((f32[256,128]{1,0:T(8,128)}, f32[256,128]{1,0:T(8,128)}, f32[256,128]{1,0:T(8,128)}, f32[128,256]{1,0:T(8,128)}), (f32[256,128]{1,0:T(8,128)}, f32[256,128]{1,0:T(8,128)}, f32[256,128]{1,0:T(8,128)}, ...) | async-done | bytes 524304 | tf_op jit(solution)/shard_map/psum | solution.py:362
  427.6 1.6 copy.29
  429.2 1.6 copy.30
  430.8 1.6 copy.31
  432.3 1.6 copy.32
  (15 shorter events, 0.2 us)
Async XLA Ops:
  7.2 135.7 %copy-start = (f32[1024,256]{1,0:T(8,128)S(1)}, f32[1024,256]{1,0:T(8,128)}, u32[]{:S(2)}) copy-start(f32[1024,256]{1,0:T(8,128)} %refs_8_.1) | copy-start | bytes 3145732
  7.2 135.7 %copy-start.6 = (f32[256,128]{1,0:T(8,128)S(1)}, f32[256,128]{1,0:T(8,128)}, u32[]{:S(2)}) copy-start(f32[256,128]{1,0:T(8,128)} %refs_15_.1) | copy-start | bytes 393220
  7.2 135.7 %copy-start.7 = (f32[256,128]{1,0:T(8,128)S(1)}, f32[256,128]{1,0:T(8,128)}, u32[]{:S(2)}) copy-start(f32[256,128]{1,0:T(8,128)} %refs_16_.1) | copy-start | bytes 393220
  7.2 135.7 %copy-start.8 = (f32[256,128]{1,0:T(8,128)S(1)}, f32[256,128]{1,0:T(8,128)}, u32[]{:S(2)}) copy-start(f32[256,128]{1,0:T(8,128)} %refs_17_.1) | copy-start | bytes 393220
  7.2 135.7 %copy-start.9 = (f32[128,256]{1,0:T(8,128)S(1)}, f32[128,256]{1,0:T(8,128)}, u32[]{:S(2)}) copy-start(f32[128,256]{1,0:T(8,128)} %refs_18_.1) | copy-start | bytes 393220
  7.2 135.7 %all-gather.3.cloned.1.call-start = ((), (), s32[]{:S(2)}) async-start(), calls=%async_computation | async-start | bytes 17825792 | tf_op jit(solution)/shard_map/all_gather | solution.py:345
  8.0 267.5 %all-gather.5.cloned.1.call-start = ((), (), s32[]{:S(2)}) async-start(), calls=%async_computation.1 | async-start | bytes 17825792 | tf_op jit(solution)/shard_map/all_gather | solution.py:346
  8.7 418.9 %all-reduce.5.cloned.1.call-start = ((), (), s32[]{:S(2)}) async-start(), calls=%async_computation.2 | async-start | bytes 1048576 | tf_op jit(solution)/shard_map/psum | solution.py:362
  142.9 132.5 %copy-start.1 = (f32[1024,256]{1,0:T(8,128)S(1)}, f32[1024,256]{1,0:T(8,128)}, u32[]{:S(2)}) copy-start(f32[1024,256]{1,0:T(8,128)} %refs_12_.3) | copy-start | bytes 3145732
  192.1 2.4 copy-start.2
  192.1 2.4 copy-start.3
  193.0 137.8 %collective-permute-start = (f32[1024,128]{1,0:T(8,128)}, f32[1024,128]{1,0:T(8,128)}, u32[]{:S(2)}, u32[]{:S(2)}) collective-permute-start(f32[1024,128]{1,0:T(8,128)} %constant_dynamic-slice_fusion.1), channel_id=1, source_target_pairs={{0,1},{1,0},{2,3},{3,2},{4,5},{5,4},{6,7},{7,6},{8,9},{9,8},{10,11... | collective-permute-start | bytes 1572872 | tf_op jit(solution)/shard_map/ppermute | solution.py:329
  275.5 55.3 %copy-start.4 = (f32[1024,256]{1,0:T(8,128)S(1)}, f32[1024,256]{1,0:T(8,128)}, u32[]{:S(2)}) copy-start(f32[1024,256]{1,0:T(8,128)} %copy-done.3) | copy-start | bytes 3145732
  328.4 1.0 copy-start.5
  329.5 14.1 %collective-permute-start.1 = (f32[1024,128]{1,0:T(8,128)S(1)}, f32[1024,128]{1,0:T(8,128)S(1)}, u32[]{:S(2)}, u32[]{:S(2)}) collective-permute-start(f32[1024,128]{1,0:T(8,128)S(1)} %constant_dynamic-slice_fusion), channel_id=1, source_target_pairs={{0,1},{1,0},{2,3},{3,2},{4,5},{5,4},{6,7},{7,6},{8,9},{9,8},{10,11... | collective-permute-start | bytes 1572872 | tf_op jit(solution)/shard_map/ppermute | solution.py:329
Sparse Core Ops, SparseCore 0:
  10.2 132.6 all-gather.2
  145.1 130.3 all-gather.4
  330.9 96.7 all-reduce.4

commit v2 on v1

--- a/solution.py
+++ b/solution.py
@@ -47,7 +47,7 @@
 
 def forward_kernel(entries, ids, *refs):
     feats = refs[:entries]
-    (cot_ref, bias_ref, wq_ref, wk_ref, wv_ref, wo_ref,
+    (cot_ref, grad_ref, bias_ref, wq_ref, wk_ref, wv_ref, wo_ref,
      out_ref, feat_ref, stat_ref, gq_ref, go_ref) = refs[entries:]
     rows = cot_ref.shape[0]
     cols = wq_ref.shape[1]
@@ -63,7 +63,7 @@
     own = (inputs[0][:rows], inputs[1][:rows])
     query = mul3(own, w_query) * SCALE
     cot = split(cot_ref[...])
-    grad_mixed = mul3(cot, w_out, 1, 1)
+    grad_mixed = grad_ref[...]
     bias = bias_ref[0]
     lane = lax.broadcasted_iota(jnp.int32, (rows, cols), 1) // HEAD_SIZE
     stat_lane = lax.broadcasted_iota(jnp.int32, (rows, rows), 1)
@@ -106,7 +106,7 @@
     go_ref[...] += mul3(mixed, cot, 0, 0)
 
 
-def attend_forward(ids, all_feats, out_cotangent, bias, w_query, w_key, w_value, w_out):
+def attend_forward(ids, all_feats, out_cotangent, grad_mixed, bias, w_query, w_key, w_value, w_out):
     block_count, entries = ids.shape
     node_rows, width = out_cotangent.shape
     rows = node_rows // block_count
@@ -136,7 +136,8 @@
             num_scalar_prefetch=1,
             grid=(block_count,),
             in_specs=[picked(entry) for entry in range(entries)]
-            + [own, pl.BlockSpec((1, 1, entries * rows), lambda b, ids: (b, 0, 0))]
+            + [own, pl.BlockSpec((rows, cols), lambda b, ids: (b, 0))]
+            + [pl.BlockSpec((1, 1, entries * rows), lambda b, ids: (b, 0, 0))]
             + [whole(w) for w in (w_query, w_key, w_value, w_out)],
             out_specs=(
                 own,
@@ -150,12 +151,12 @@
             dimension_semantics=("arbitrary",), vmem_limit_bytes=50 * 1024 * 1024
         ),
         name="attend_forward",
-    )(ids, *([all_feats] * entries), out_cotangent, bias, w_query, w_key, w_value, w_out)
+    )(ids, *([all_feats] * entries), out_cotangent, grad_mixed, bias, w_query, w_key, w_value, w_out)
 
 
 def backward_kernel(steps_ref, readers_ref, *refs):
     feats, cots, stats = refs[:GROUP], refs[GROUP:2 * GROUP], refs[2 * GROUP:3 * GROUP]
-    (own_ref, bias_ref, part_ref, wq_ref, wk_ref, wv_ref, wo_ref,
+    (own_ref, bias_ref, part_ref, wq_ref, wk_ref, wv_ref,
      feat_ref, gk_ref, gv_ref, key_mem, value_mem, dk_mem, dv_mem) = refs[3 * GROUP:]
     step = pl.program_id(0)
     rows = own_ref.shape[0]
@@ -184,8 +185,7 @@
     def _():
         inputs = split(jnp.concatenate([ref[...] for ref in feats], axis=0))
         q_high, q_low = split(mul3(inputs, split(wq_ref[...])) * SCALE)
-        cot = split(jnp.concatenate([ref[...] for ref in cots], axis=0))
-        g_high, g_low = split(mul3(cot, split(wo_ref[...]), 1, 1))
+        g_high, g_low = split(jnp.concatenate([ref[...] for ref in cots], axis=0))
         q_twice, q_both = wide(q_high, q_high), wide(q_high, q_low)
         g_twice, g_both = wide(g_high, g_high), wide(g_high, g_low)
         mark_row = lax.broadcasted_iota(jnp.int32, (8, GROUP * rows), 0)
@@ -227,15 +227,15 @@
 
 def attend_backward(
     steps, readers, all_feats, all_cots, all_stats, own_feats, bias, part,
-    w_query, w_key, w_value, w_out, rows,
+    w_query, w_key, w_value, rows,
 ):
     count = steps.shape[1]
     node_rows, width = own_feats.shape
     cols = w_query.shape[1]
     heads = cols // HEAD_SIZE
 
-    def picked(at):
-        return pl.BlockSpec((rows, width), lambda s, steps, readers: (readers[s * GROUP + at], 0))
+    def picked(at, lanes):
+        return pl.BlockSpec((rows, lanes), lambda s, steps, readers: (readers[s * GROUP + at], 0))
 
     def picked_stat(at):
         return pl.BlockSpec(
@@ -253,11 +253,11 @@
         grid_spec=pltpu.PrefetchScalarGridSpec(
             num_scalar_prefetch=2,
             grid=(count,),
-            in_specs=[picked(at) for at in range(GROUP)]
-            + [picked(at) for at in range(GROUP)]
+            in_specs=[picked(at, width) for at in range(GROUP)]
+            + [picked(at, cols) for at in range(GROUP)]
             + [picked_stat(at) for at in range(GROUP)]
             + [own, pl.BlockSpec((1, 8, rows), lambda s, steps, readers: (s, 0, 0)), own]
-            + [whole(w) for w in (w_query, w_key, w_value, w_out)],
+            + [whole(w) for w in (w_query, w_key, w_value)],
             out_specs=(own, whole(grad_shape), whole(grad_shape)),
             scratch_shapes=[
                 pltpu.VMEM((heads * rows, 2 * cols), BF16),
@@ -272,7 +272,7 @@
         name="attend_backward",
     )(
         steps, readers, *([all_feats] * GROUP), *([all_cots] * GROUP), *([all_stats] * GROUP),
-        own_feats, bias, part, w_query, w_key, w_value, w_out,
+        own_feats, bias, part, w_query, w_key, w_value,
     )
 
 
@@ -329,6 +329,22 @@
     return kept + lax.ppermute(sent, "head", [(0, 1), (1, 0)])
 
 
+def dom_sum(first, second):
+    size = lax.axis_size("dom")
+    odd = lax.axis_index("dom") % 2 == 1
+
+    def from_across(value, bit):
+        return lax.ppermute(value, "dom", [(at, at ^ bit) for at in range(size)])
+
+    mine = jnp.where(odd, second, first) + from_across(jnp.where(odd, first, second), 1)
+    bit = 2
+    while bit < size:
+        mine = mine + from_across(mine, bit)
+        bit *= 2
+    other = from_across(mine, 1)
+    return jnp.where(odd, other, mine), jnp.where(odd, mine, other)
+
+
 def per_device(
     node_features, w_query, w_key, w_value, w_out, nbr_part, nbr_slot, key_mask, out_cotangent
 ):
@@ -343,25 +359,31 @@
     mask = jnp.concatenate([jnp.ones((block_count, 1, rows), jnp.int32), key_mask], axis=1)
     bias = jnp.where(mask > 0, 0.0, MASKED).reshape(block_count, 1, (list_len + 1) * rows)
     all_feats = lax.all_gather(node_features, "dom", axis=0, tiled=True)
-    all_cots = lax.all_gather(out_cotangent, "dom", axis=0, tiled=True)
+    grad_mixed = lax.dot_general(
+        out_cotangent, w_out, (((1,), (1,)), ((), ())), precision=lax.Precision.HIGHEST
+    )
+    all_grads = lax.all_gather(grad_mixed, "dom", axis=0, tiled=True)
     all_ids = lax.all_gather(ids, "dom", axis=0, tiled=True)
     all_mask = lax.all_gather(mask, "dom", axis=0, tiled=True)
     steps, readers, back_bias = plan_backward(
         all_ids, all_mask, me, block_count, dom_count * slot_cap
     )
     out_part, feat_part, stats, grad_query, grad_out = attend_forward(
-        ids, all_feats, out_cotangent, bias, w_query, w_key, w_value, w_out
+        ids, all_feats, out_cotangent, grad_mixed, bias, w_query, w_key, w_value, w_out
     )
     layer_out = head_scatter(out_part)
+    cols = w_query.shape[1]
+    pieces = [grad_out[:, at:at + cols] for at in range(0, width, cols)]
+    grad_query, grad_out = dom_sum(grad_query, jnp.concatenate(pieces, axis=0))
+    pieces = [grad_out[at:at + cols] for at in range(0, width, cols)]
+    grad_out = jnp.concatenate(pieces, axis=1)
     all_stats = lax.all_gather(stats, "dom", axis=0, tiled=True)
     feats_part, grad_key, grad_value = attend_backward(
-        steps, readers, all_feats, all_cots, all_stats, node_features, back_bias, feat_part,
-        w_query, w_key, w_value, w_out, rows,
+        steps, readers, all_feats, all_grads, all_stats, node_features, back_bias, feat_part,
+        w_query, w_key, w_value, rows,
     )
     grad_features = head_scatter(feats_part)
-    grad_query, grad_key, grad_value, grad_out = lax.psum(
-        (grad_query, grad_key, grad_value, grad_out), "dom"
-    )
+    grad_key, grad_value = dom_sum(grad_key, grad_value)
     return (layer_out, grad_features, grad_query, grad_key, grad_value, grad_out)
 
 

time: 441 us -> 324 us (0.73)
  waiting for transfers between devices: 236 us -> 99.5 us
  Pallas kernels: 102 us -> 113 us
  starting transfers between devices: 2.87 us -> 12.7 us
  local copies, waits for them, and re-layouts: 10.1 us -> 4.72 us
    psum x1 -> x0, waiting for transfers between devices: 82.2 us -> none  [per_device(): lax.psum((grad_query, grad_key, grad_value, grad_out), 'dom')]
    all_gather x1, waiting for transfers between devices: 58.3 us -> 1.93 us  [per_device(): all_grads = lax.all_gather(grad_mixed, 'dom', axis=0, tiled=True)]
    ppermute x0 -> x10, waiting for transfers between devices: none -> 15.6 us  [from_across(): return lax.ppermute(value, 'dom', [(at, at ^ bit) for at in range(size)])]
    ppermute x2, waiting for transfers between devices: 10.9 us -> 0.01 us  [head_scatter(): return kept + lax.ppermute(sent, 'head', [(0, 1), (1, 0)])]
    pallas_call x1, Pallas kernels: 53 us -> 63.2 us  [attend_backward(): pl.pallas_call(backward_kernel, out_shape=(jax.ShapeDtypeStruct((node_row...]
    ppermute x0 -> x10, starting transfers between devices: none -> 9.81 us  [from_across(): return lax.ppermute(value, 'dom', [(at, at ^ bit) for at in range(size)])]
    unnamed x24 -> x18, local copies, waits for them, and re-layouts: 7.29 us -> 1.07 us
  transfers between devices with their start and end apart: 5 -> 14, of which waited for: 4 -> 8; matrix products, arithmetic and copies ran while one was open for 2% -> 4% of each run, Pallas kernels for 23% -> 35%
where the time goes in v2:
time: 324 us; the launch traced here: 323 us
  Pallas kernels  113 us (35%)
  waiting for transfers between devices  99.5 us (31%)
  blocking collectives  67.4 us (21%)
  between operations  14.3 us (4%)
  starting transfers between devices  12.7 us (4%)
  other arithmetic  8.57 us (3%)
  local copies, waits for them, and re-layouts  4.72 us (1%)
    all_gather x1, waiting for transfers between devices, per_device(): all_feats = lax.all_gather(node_features, 'dom', axis=0, tiled=True)  81.3 us
    pallas_call x1, Pallas kernels, attend_backward(): pl.pallas_call(backward_kernel, out_shape=(jax.ShapeDtypeStruct((node_row...  63.2 us
    pallas_call x1, Pallas kernels, attend_forward(): pl.pallas_call(functools.partial(forward_kernel, entries), out_shape=(nod...  50 us
    all_gather x1, blocking collectives, per_device(): all_ids = lax.all_gather(ids, 'dom', axis=0, tiled=True)  23.7 us
    all_gather x1, blocking collectives, per_device(): all_stats = lax.all_gather(stats, 'dom', axis=0, tiled=True)  21.9 us
    all_gather x1, blocking collectives, per_device(): all_mask = lax.all_gather(mask, 'dom', axis=0, tiled=True)  21.8 us
    ppermute x10, waiting for transfers between devices, from_across(): return lax.ppermute(value, 'dom', [(at, at ^ bit) for at in range(size)])  15.6 us
    ppermute x10, starting transfers between devices, from_across(): return lax.ppermute(value, 'dom', [(at, at ^ bit) for at in range(size)])  9.81 us
  transfers between devices with their start and end apart: 14, of which 8 were waited for; matrix products, arithmetic and copies ran while one was open for 4% of the time, Pallas kernels for 35%

profile of v2, /device:TPU:0, one launch (start us, length us, event | category | flops | bytes accessed | tf_op | source)
XLA Modules:
  0.0 323.4 jit_solution(13791881125751262966)
XLA Ops:
  7.2 0.0 all-gather.3.cloned.1.call-start
  7.3 0.7 all-gather.3.cloned.1.call-update
  7.9 0.0 all-gather.5.cloned.1.call-start
  8.0 3.0 fusion.12.refs_9_
  11.0 0.0 all-gather.5.cloned.1.call-update
  11.0 0.8 concatenate.16
  11.8 0.8 compare_select_fusion
  12.6 0.7 multiply_add_fusion
  13.3 0.1 pad_add_fusion.ids
  13.4 23.7 %all_gather.16 = s32[128,8]{1,0:T(8,128)S(1)} all-gather(s32[8,8]{1,0:T(8,128)S(1)} %pad_add_fusion.ids), channel_id=1, replica_groups=mesh['dom'=16,'head'=2] {'dom'}, dimensions={0}, use_global_device_ids=true | all-gather | bytes 4352 | tf_op jit(solution)/shard_map/all_gather | solution.py:366
  37.0 0.1 reshape.267
  37.1 21.8 %all_gather.19 = s32[128,8,128]{2,0,1:T(8,128)S(1)} all-gather(s32[8,8,128]{2,0,1:T(8,128)S(1)} %concatenate.16), channel_id=1, replica_groups=mesh['dom'=16,'head'=2] {'dom'}, dimensions={0}, use_global_device_ids=true | all-gather | bytes 557056 | tf_op jit(solution)/shard_map/all_gather | solution.py:367
  59.0 0.3 copy.24
  59.3 0.1 convert_reduce_fusion.2
  59.4 0.1 select_reduce_fusion.2
  59.6 0.1 select_reduce_fusion.1
  59.6 0.5 convert_reduce_fusion
  60.2 0.2 convert_reduce_fusion.1
  60.4 0.1 gt.56
  60.5 0.6 gather_fusion
  61.1 0.1 and_select_fusion
  61.3 0.1 convert_reduce_fusion.5
  61.3 0.1 convert_reduce_fusion.3
  61.5 81.3 %all-gather.3.cloned.1.call-done.refs_0_.refs_1_.refs_2_.refs_3_.refs_4_.refs_5_.refs_6_.refs_7_ = f32[16384,256]{1,0:T(8,128)} async-done(((f32[1024,256]{1,0:T(8,128)}), f32[16384,256]{1,0:T(8,128)}) %all-gather.3.cloned.1.call-update) | async-done | bytes 16777232 | tf_op jit(solution)/shard_map/all_gather | solution.py:361
  142.8 0.0 copy-done.6
  142.8 0.0 copy-start
  142.8 1.0 copy-done
  143.8 50.0 %attend_forward.1 = (f32[1024,256]{1,0:T(8,128)S(1)}, f32[1024,256]{1,0:T(8,128)S(1)}, f32[8,8,128]{2,1,0:T(8,128)S(1)}, f32[256,128]{1,0:T(8,128)S(1)}, f32[128,256]{1,0:T(8,128)S(1)}) custom-call(s32[8,8]{1,0:T(8,128)S(1)} %pad_add_fusion.ids, f32[16384,256]{1,0:T(8,128)} %all-gather.3.cloned.1.call-done.refs_0_.refs_1_.refs_2_.refs_3_.refs_4_.refs_5_.refs_6_.refs_7_, ...), custom_call_target="tpu_custom_call" | custom-call | tf_op jit(solution)/shard_map/attend_forward/pallas_call | solution.py:126
  193.8 0.9 constant_dynamic-slice_fusion.1
  194.7 1.5 collective-permute-start
  196.2 0.7 fusion.1
  196.9 0.0 collective-permute-start.2
  196.9 0.0 copy-done.4
  196.9 21.9 %all_gather.18.refs_8_.refs_9_.refs_10_.refs_11_ = f32[128,8,128]{2,1,0:T(8,128)S(1)} all-gather(f32[8,8,128]{2,1,0:T(8,128)S(1)} %get-tuple-element.15), channel_id=1, replica_groups=mesh['dom'=16,'head'=2] {'dom'}, dimensions={0}, use_global_device_ids=true | all-gather | bytes 557056 | tf_op jit(solution)/shard_map/all_gather | solution.py:380
  218.8 1.9 all-gather.5.cloned.1.call-done.refs_4_.refs_5_.refs_6_.refs_7_
  220.7 63.2 %attend_backward.1 = (f32[1024,256]{1,0:T(8,128)S(1)}, f32[256,128]{1,0:T(8,128)S(1)}, f32[256,128]{1,0:T(8,128)S(1)}) custom-call(s32[2,24]{1,0:T(2,128)S(1)} %pad_add_fusion.1.steps_ref, s32[96]{0:T(128)S(1)} %and_select_fusion.1.readers_ref, f32[16384,256]{1,0:T(8,128)} %all-gather.3.cloned.1.call-done.refs_0_.refs_1_.refs_2_.refs_3_.refs_4_.refs_5_.refs_6_.refs_7_, ...), custom_call_target="tpu_custom_call" | custom-call | tf_op jit(solution)/shard_map/attend_backward/pallas_call | solution.py:250
  283.9 0.1 collective-permute-start.7
  284.0 0.0 collective-permute-done.2
  284.1 4.4 %collective-permute-start.3 = (f32[256,128]{1,0:T(8,128)S(1)}, f32[256,128]{1,0:T(8,128)S(1)}, u32[]{:S(2)}, u32[]{:S(2)}) collective-permute-start(f32[256,128]{1,0:T(8,128)S(1)} %select_add_fusion.1), channel_id=1, source_target_pairs={{0,4},{2,6},{4,0},{6,2},{8,12},{10,14},{12,8},{14,10},{16,20},{18,... | collective-permute-start | bytes 393224 | tf_op jit(solution)/shard_map/ppermute | solution.py:337
  288.4 0.0 collective-permute-done.7
  288.5 1.3 collective-permute-start.8
  289.8 0.8 constant_dynamic-slice_fusion
  290.6 1.3 collective-permute-start.1
  291.9 0.9 collective-permute-done.3
  292.8 0.1 collective-permute-start.4
  292.9 2.5 collective-permute-done.8
  295.4 0.1 collective-permute-start.9
  295.5 2.5 collective-permute-done.4
  298.0 1.9 collective-permute-start.5
  299.9 1.7 collective-permute-done.9
  301.7 1.9 collective-permute-start.10
  303.5 6.5 %collective-permute-done.5 = f32[256,128]{1,0:T(8,128)S(1)} collective-permute-done((f32[256,128]{1,0:T(8,128)S(1)}, f32[256,128]{1,0:T(8,128)S(1)}, u32[]{:S(2)}, u32[]{:S(2)}) %collective-permute-start.5) | collective-permute-done | bytes 131104 | tf_op jit(solution)/shard_map/ppermute | solution.py:337
  310.0 0.1 collective-permute-start.6
  310.1 1.5 collective-permute-done.10
  311.6 0.1 collective-permute-start.11
  311.7 0.0 collective-permute-done
  311.7 1.9 dynamic-slice_add_fusion.1
  313.6 0.0 collective-permute-done.1
  313.6 0.8 dynamic-slice_add_fusion
  314.5 0.0 collective-permute-done.6
  314.5 0.7 broadcast_select_fusion
  315.2 0.7 pad_maximum_fusion.1
  315.8 0.0 collective-permute-done.11
  315.8 0.7 broadcast_select_fusion.1
  (39 shorter events, 0.4 us)
Async XLA Ops:
  7.2 135.6 %copy-start.8 = (f32[128,256]{1,0:T(8,128)S(1)}, f32[128,256]{1,0:T(8,128)}, u32[]{:S(2)}) copy-start(f32[128,256]{1,0:T(8,128)} %refs_14_.1) | copy-start | bytes 393220
  7.2 135.6 %copy-start.5 = (f32[256,128]{1,0:T(8,128)S(1)}, f32[256,128]{1,0:T(8,128)}, u32[]{:S(2)}) copy-start(f32[256,128]{1,0:T(8,128)} %refs_15_.1) | copy-start | bytes 393220
  7.2 135.6 %copy-start.6 = (f32[256,128]{1,0:T(8,128)S(1)}, f32[256,128]{1,0:T(8,128)}, u32[]{:S(2)}) copy-start(f32[256,128]{1,0:T(8,128)} %refs_16_.1) | copy-start | bytes 393220
  7.2 135.6 %copy-start.7 = (f32[256,128]{1,0:T(8,128)S(1)}, f32[256,128]{1,0:T(8,128)}, u32[]{:S(2)}) copy-start(f32[256,128]{1,0:T(8,128)} %refs_17_.1) | copy-start | bytes 393220
  7.2 135.6 %all-gather.3.cloned.1.call-start = ((), (), s32[]{:S(2)}) async-start(), calls=%async_computation | async-start | bytes 17825792 | tf_op jit(solution)/shard_map/all_gather | solution.py:361
  7.9 212.8 %all-gather.5.cloned.1.call-start = ((), (), s32[]{:S(2)}) async-start(), calls=%async_computation.1 | async-start | bytes 8912896 | tf_op jit(solution)/shard_map/all_gather | solution.py:365
  142.8 1.0 copy-start
  143.8 76.9 %copy-start.1 = (f32[1024,256]{1,0:T(8,128)S(1)}, f32[1024,256]{1,0:T(8,128)}, u32[]{:S(2)}) copy-start(f32[1024,256]{1,0:T(8,128)} %refs_12_.3) | copy-start | bytes 3145732
  193.8 3.1 copy-start.4
  194.7 117.0 %collective-permute-start = (f32[1024,128]{1,0:T(8,128)}, f32[1024,128]{1,0:T(8,128)}, u32[]{:S(2)}, u32[]{:S(2)}) collective-permute-start(f32[1024,128]{1,0:T(8,128)} %constant_dynamic-slice_fusion.1), channel_id=1, source_target_pairs={{0,1},{1,0},{2,3},{3,2},{4,5},{5,4},{6,7},{7,6},{8,9},{9,8},{10,11... | collective-permute-start | bytes 1572872 | tf_op jit(solution)/shard_map/ppermute | solution.py:329
  196.9 87.1 %collective-permute-start.2 = (f32[256,128]{1,0:T(8,128)}, f32[256,128]{1,0:T(8,128)S(1)}, u32[]{:S(2)}, u32[]{:S(2)}) collective-permute-start(f32[256,128]{1,0:T(8,128)} %fusion.1), channel_id=1, source_target_pairs={{0,2},{2,0},{4,6},{6,4},{8,10},{10,8},{12,14},{14,12},{16,18},{18,... | collective-permute-start | bytes 393224 | tf_op jit(solution)/shard_map/ppermute | solution.py:337
  283.9 5.9 %copy-start.2 = (f32[1024,256]{1,0:T(8,128)}, f32[1024,256]{1,0:T(8,128)S(1)}, u32[]{:S(2)}) copy-start(f32[1024,256]{1,0:T(8,128)S(1)} %get-tuple-element.17) | copy-start | bytes 3145732
  283.9 4.5 %collective-permute-start.7 = (f32[256,128]{1,0:T(8,128)S(1)}, f32[256,128]{1,0:T(8,128)S(1)}, u32[]{:S(2)}, u32[]{:S(2)}) collective-permute-start(f32[256,128]{1,0:T(8,128)S(1)} %broadcast_select_fusion.3), channel_id=1, source_target_pairs={{0,2},{2,0},{4,6},{6,4},{8,10},{10,8},{12,14},{14,12},{16,18},{18,... | collective-permute-start | bytes 393224 | tf_op jit(solution)/shard_map/ppermute | solution.py:337
  284.1 8.7 %collective-permute-start.3 = (f32[256,128]{1,0:T(8,128)S(1)}, f32[256,128]{1,0:T(8,128)S(1)}, u32[]{:S(2)}, u32[]{:S(2)}) collective-permute-start(f32[256,128]{1,0:T(8,128)S(1)} %select_add_fusion.1), channel_id=1, source_target_pairs={{0,4},{2,6},{4,0},{6,2},{8,12},{10,14},{12,8},{14,10},{16,20},{18,... | collective-permute-start | bytes 393224 | tf_op jit(solution)/shard_map/ppermute | solution.py:337
  288.5 6.9 %collective-permute-start.8 = (f32[256,128]{1,0:T(8,128)S(1)}, f32[256,128]{1,0:T(8,128)S(1)}, u32[]{:S(2)}, u32[]{:S(2)}) collective-permute-start(f32[256,128]{1,0:T(8,128)S(1)} %select_add_fusion), channel_id=1, source_target_pairs={{0,4},{2,6},{4,0},{6,2},{8,12},{10,14},{12,8},{14,10},{16,20},{18,... | collective-permute-start | bytes 393224 | tf_op jit(solution)/shard_map/ppermute | solution.py:337
  290.6 23.0 %copy-start.3 = (f32[1024,256]{1,0:T(8,128)S(1)}, f32[1024,256]{1,0:T(8,128)}, u32[]{:S(2)}) copy-start(f32[1024,256]{1,0:T(8,128)} %copy-done.2) | copy-start | bytes 3145732
  290.6 23.0 %collective-permute-start.1 = (f32[1024,128]{1,0:T(8,128)}, f32[1024,128]{1,0:T(8,128)S(1)}, u32[]{:S(2)}, u32[]{:S(2)}) collective-permute-start(f32[1024,128]{1,0:T(8,128)} %constant_dynamic-slice_fusion), channel_id=1, source_target_pairs={{0,1},{1,0},{2,3},{3,2},{4,5},{5,4},{6,7},{7,6},{8,9},{9,8},{10,11... | collective-permute-start | bytes 1572872 | tf_op jit(solution)/shard_map/ppermute | solution.py:329
  292.8 5.2 %collective-permute-start.4 = (f32[256,128]{1,0:T(8,128)S(1)}, f32[256,128]{1,0:T(8,128)S(1)}, u32[]{:S(2)}, u32[]{:S(2)}) collective-permute-start(f32[256,128]{1,0:T(8,128)S(1)} %add.181), channel_id=1, source_target_pairs={{0,8},{2,10},{4,12},{6,14},{8,0},{10,2},{12,4},{14,6},{16,24},{18,... | collective-permute-start | bytes 393224 | tf_op jit(solution)/shard_map/ppermute | solution.py:337
  295.4 6.2 %collective-permute-start.9 = (f32[256,128]{1,0:T(8,128)S(1)}, f32[256,128]{1,0:T(8,128)S(1)}, u32[]{:S(2)}, u32[]{:S(2)}) collective-permute-start(f32[256,128]{1,0:T(8,128)S(1)} %add.185), channel_id=1, source_target_pairs={{0,8},{2,10},{4,12},{6,14},{8,0},{10,2},{12,4},{14,6},{16,24},{18,... | collective-permute-start | bytes 393224 | tf_op jit(solution)/shard_map/ppermute | solution.py:337
  298.0 12.0 %collective-permute-start.5 = (f32[256,128]{1,0:T(8,128)S(1)}, f32[256,128]{1,0:T(8,128)S(1)}, u32[]{:S(2)}, u32[]{:S(2)}) collective-permute-start(f32[256,128]{1,0:T(8,128)S(1)} %add.182), channel_id=1, source_target_pairs={{0,16},{2,18},{4,20},{6,22},{8,24},{10,26},{12,28},{14,30},{16,0},... | collective-permute-start | bytes 393224 | tf_op jit(solution)/shard_map/ppermute | solution.py:337
  301.7 9.9 %collective-permute-start.10 = (f32[256,128]{1,0:T(8,128)S(1)}, f32[256,128]{1,0:T(8,128)S(1)}, u32[]{:S(2)}, u32[]{:S(2)}) collective-permute-start(f32[256,128]{1,0:T(8,128)S(1)} %add.186), channel_id=1, source_target_pairs={{0,16},{2,18},{4,20},{6,22},{8,24},{10,26},{12,28},{14,30},{16,0},... | collective-permute-start | bytes 393224 | tf_op jit(solution)/shard_map/ppermute | solution.py:337
  310.0 4.4 %collective-permute-start.6 = (f32[256,128]{1,0:T(8,128)S(1)}, f32[256,128]{1,0:T(8,128)S(1)}, u32[]{:S(2)}, u32[]{:S(2)}) collective-permute-start(f32[256,128]{1,0:T(8,128)S(1)} %add.183), channel_id=1, source_target_pairs={{0,2},{2,0},{4,6},{6,4},{8,10},{10,8},{12,14},{14,12},{16,18},{18,... | collective-permute-start | bytes 393224 | tf_op jit(solution)/shard_map/ppermute | solution.py:337
  311.6 4.2 %collective-permute-start.11 = (f32[256,128]{1,0:T(8,128)S(1)}, f32[256,128]{1,0:T(8,128)S(1)}, u32[]{:S(2)}, u32[]{:S(2)}) collective-permute-start(f32[256,128]{1,0:T(8,128)S(1)} %add.187), channel_id=1, source_target_pairs={{0,2},{2,0},{4,6},{6,4},{8,10},{10,8},{12,14},{14,12},{16,18},{18,... | collective-permute-start | bytes 393224 | tf_op jit(solution)/shard_map/ppermute | solution.py:337
Sparse Core Ops, SparseCore 0:
  10.2 132.5 all-gather.2
  145.5 75.1 all-gather.4

commit v3 on v2

--- a/solution.py
+++ b/solution.py
@@ -234,12 +234,14 @@
     cols = w_query.shape[1]
     heads = cols // HEAD_SIZE
 
-    def picked(at, lanes):
-        return pl.BlockSpec((rows, lanes), lambda s, steps, readers: (readers[s * GROUP + at], 0))
+    def picked(at, lanes, kind):
+        return pl.BlockSpec(
+            (rows, lanes), lambda s, steps, readers: (readers[kind, s * GROUP + at], 0)
+        )
 
     def picked_stat(at):
         return pl.BlockSpec(
-            (1, 2 * heads, rows), lambda s, steps, readers: (readers[s * GROUP + at], 0, 0)
+            (1, 2 * heads, rows), lambda s, steps, readers: (readers[0, s * GROUP + at], 0, 0)
         )
 
     def whole(array):
@@ -253,8 +255,8 @@
         grid_spec=pltpu.PrefetchScalarGridSpec(
             num_scalar_prefetch=2,
             grid=(count,),
-            in_specs=[picked(at, width) for at in range(GROUP)]
-            + [picked(at, cols) for at in range(GROUP)]
+            in_specs=[picked(at, width, 1) for at in range(GROUP)]
+            + [picked(at, cols, 2) for at in range(GROUP)]
             + [picked_stat(at) for at in range(GROUP)]
             + [own, pl.BlockSpec((1, 8, rows), lambda s, steps, readers: (s, 0, 0)), own]
             + [whole(w) for w in (w_query, w_key, w_value)],
@@ -345,6 +347,96 @@
     return jnp.where(odd, other, mine), jnp.where(odd, mine, other)
 
 
+def gather_feats(part, block_count):
+    size, me = lax.axis_size("dom"), lax.axis_index("dom")
+    if size != 16 or lax.axis_size("head") != 2 or block_count != 8:
+        return lax.all_gather(part, "dom", axis=0, tiled=True), lambda ids: ids, part
+    side = lax.axis_index("head")
+    rows = part.shape[0] // block_count
+    total = size * block_count
+
+    ring = [0, 2, 4, 6, 7, 5, 3, 1]
+    onward, back = [], []
+    for at in range(8):
+        for core in range(2):
+            here, there = 2 * ring[at] + core, 2 * ring[(at + 1) % 8] + core
+            onward.append((here, there))
+            back.append((there, here))
+    across = [(at, at ^ 1) for at in range(size)]
+    other_head = [(0, 1), (1, 0)]
+
+    def blocks(value, start, count):
+        return lax.slice_in_dim(value, start * rows, (start + count) * rows, axis=0)
+
+    def lacking(value):
+        return lax.dynamic_slice_in_dim(value, 2 * side * rows, 3 * rows, axis=0)
+
+    result = jnp.zeros((total * rows, part.shape[1]), F32)
+
+    def put(value, start):
+        nonlocal result
+        result = lax.dynamic_update_slice_in_dim(result, value, start * rows, axis=0)
+
+    half = total // 2
+    put(part, 0)
+
+    def swap(value):
+        return lax.ppermute(value, "dom", across)
+
+    start = lax.dynamic_slice_in_dim(part, 3 * side * rows, 5 * rows, axis=0)
+    held = (lax.ppermute(start, "dom", onward), lax.ppermute(start, "dom", back))
+    twin = swap(part)
+    held, twin = lax.optimization_barrier((held, twin))
+    put(twin, half)
+    slots, lack, lack_slots = (1, 2), (), ()
+    for step in range(1, 5):
+        if step < 3:
+            coming = (
+                lax.ppermute(held[0], "dom", onward), lax.ppermute(held[1], "dom", back)
+            )
+        elif step == 3:
+            coming = (
+                lax.ppermute(blocks(held[0], 0, 3), "dom", onward),
+                lax.ppermute(blocks(held[1], 3, 2), "dom", back),
+            )
+        else:
+            coming = ()
+        more = tuple(lax.ppermute(lacking(value), "head", other_head) for value in held)
+        swapped = tuple(swap(value) for value in held)
+        swapped_lack = tuple(swap(value) for value in lack)
+        coming, held, more, swapped, lack, swapped_lack = lax.optimization_barrier(
+            (coming, held, more, swapped, lack, swapped_lack)
+        )
+        for at, slot in enumerate(slots):
+            put(held[at], slot * block_count)
+            put(swapped[at], half + slot * block_count)
+        for at, slot in enumerate(lack_slots):
+            put(lack[at], slot * block_count + 5)
+            put(swapped_lack[at], half + slot * block_count + 5)
+        lack, lack_slots = more, slots
+        if step == 3:
+            held, slots = (jnp.concatenate(coming, axis=0),), (7,)
+            late = held[0]
+        else:
+            held, slots = coming, (2 * step + 1, 2 * step + 2)
+    put(lack[0], 7 * block_count + 5)
+    put(swap(lack[0]), half + 7 * block_count + 5)
+
+    def chip_place(chip):
+        level, column = chip // 2, chip % 2
+        return jnp.where(column == 0, level, 7 - level)
+
+    def place(ids):
+        owner, block = ids // block_count, ids % block_count
+        gap = (chip_place(owner // 2) - chip_place(me // 2)) % 8
+        slot = jnp.where(gap < 4, 2 * gap, 2 * (8 - gap) - 1)
+        moved = jnp.where(gap == 0, block, (block + 5 * side) % block_count)
+        spot = slot * block_count + moved
+        return spot + jnp.where(owner % 2 == me % 2, 0, half)
+
+    return result, place, late
+
+
 def per_device(
     node_features, w_query, w_key, w_value, w_out, nbr_part, nbr_slot, key_mask, out_cotangent
 ):
@@ -358,28 +450,39 @@
     ids = jnp.concatenate([self_ids, nbr_part * block_count + nbr_slot], axis=1)
     mask = jnp.concatenate([jnp.ones((block_count, 1, rows), jnp.int32), key_mask], axis=1)
     bias = jnp.where(mask > 0, 0.0, MASKED).reshape(block_count, 1, (list_len + 1) * rows)
-    all_feats = lax.all_gather(node_features, "dom", axis=0, tiled=True)
+    all_feats, place, late = gather_feats(node_features, block_count)
     grad_mixed = lax.dot_general(
         out_cotangent, w_out, (((1,), (1,)), ((), ())), precision=lax.Precision.HIGHEST
     )
-    all_grads = lax.all_gather(grad_mixed, "dom", axis=0, tiled=True)
-    all_ids = lax.all_gather(ids, "dom", axis=0, tiled=True)
-    all_mask = lax.all_gather(mask, "dom", axis=0, tiled=True)
+    cols = w_query.shape[1]
+    names = jnp.pad(ids, ((0, 0), (0, rows - list_len - 1))).astype(F32)
+    extra = jnp.concatenate([names, key_mask.reshape(-1, rows).astype(F32)], axis=0)
+    extra = extra.reshape(-1, cols)
+    extra_blocks = -(-extra.shape[0] // rows)
+    extra = jnp.pad(extra, ((0, extra_blocks * rows - extra.shape[0]), (0, 0)))
+    sent = jnp.concatenate([grad_mixed, extra], axis=0)
+    sent, late = lax.optimization_barrier((sent, late))
+    all_grads = lax.all_gather(sent, "dom", axis=0, tiled=True)
+    extra = all_grads.reshape(dom_count, -1, cols)[:, node_rows:].reshape(dom_count, -1, rows)
+    all_ids = extra[:, :block_count, : list_len + 1].astype(jnp.int32)
+    all_ids = all_ids.reshape(-1, list_len + 1)
+    all_mask = extra[:, block_count:(list_len + 1) * block_count].reshape(-1, list_len, rows)
+    all_mask = jnp.concatenate([jnp.ones_like(all_mask[:, :1]), all_mask], axis=1)
     steps, readers, back_bias = plan_backward(
         all_ids, all_mask, me, block_count, dom_count * slot_cap
     )
+    grad_spots = readers + readers // block_count * extra_blocks
     out_part, feat_part, stats, grad_query, grad_out = attend_forward(
-        ids, all_feats, out_cotangent, grad_mixed, bias, w_query, w_key, w_value, w_out
+        place(ids), all_feats, out_cotangent, grad_mixed, bias, w_query, w_key, w_value, w_out
     )
     layer_out = head_scatter(out_part)
-    cols = w_query.shape[1]
     pieces = [grad_out[:, at:at + cols] for at in range(0, width, cols)]
     grad_query, grad_out = dom_sum(grad_query, jnp.concatenate(pieces, axis=0))
     pieces = [grad_out[at:at + cols] for at in range(0, width, cols)]
     grad_out = jnp.concatenate(pieces, axis=1)
     all_stats = lax.all_gather(stats, "dom", axis=0, tiled=True)
     feats_part, grad_key, grad_value = attend_backward(
-        steps, readers, all_feats, all_grads, all_stats, node_features, back_bias, feat_part,
+        steps, jnp.stack([readers, place(readers), grad_spots]), all_feats, all_grads, all_stats, node_features, back_bias, feat_part,
         w_query, w_key, w_value, rows,
     )
     grad_features = head_scatter(feats_part)

time: 324 us -> 309 us (0.954)
  blocking collectives: 67.4 us -> 20.8 us
  local copies, waits for them, and re-layouts: 4.72 us -> 33.4 us
  starting transfers between devices: 12.7 us -> 39.8 us
  waiting for transfers between devices: 99.5 us -> 76.3 us
  Pallas kernels: 113 us -> 104 us
  other arithmetic: 8.57 us -> 16.4 us
    all_gather x2 -> x1, waiting for transfers between devices: 83.2 us -> 0.01 us  [per_device(): all_grads = lax.all_gather(sent, 'dom', axis=0, tiled=True)]
    ppermute x0 -> x30, waiting for transfers between devices: none -> 62.8 us  [the longest x7 39.4 us: gather_feats(): lax.ppermute(lacking(value), 'head', other_head)]
    all_gather x2 -> x0, blocking collectives: 45.5 us -> none  [the longest x1 23.7 us: per_device(): all_ids = lax.all_gather(ids, 'dom', axis=0, tiled=True)]
    ppermute x0 -> x30, starting transfers between devices: none -> 19.7 us  [the longest x7 7.86 us: gather_feats(): lax.ppermute(lacking(value), 'head', other_head)]
    dynamic_update_slice x0 -> x30, local copies, waits for them, and re-layouts: none -> 11.8 us  [put(): lax.dynamic_update_slice_in_dim(result, value, start * rows, axis=0)]
    ppermute x10, starting transfers between devices: 9.81 us -> 19 us  [from_across(): return lax.ppermute(value, 'dom', [(at, at ^ bit) for at in range(size)])]
    pallas_call x1, Pallas kernels: 63.2 us -> 54.1 us  [attend_backward(): pl.pallas_call(backward_kernel, out_shape=(jax.ShapeDtypeStruct((node_row...]
    unnamed x18 -> x75, local copies, waits for them, and re-layouts: 1.07 us -> 10.1 us
  transfers between devices with their start and end apart: 14 -> 43, of which waited for: 8 -> 16; matrix products, arithmetic and copies ran while one was open for 4% -> 13% of each run, Pallas kernels for 35% -> 34%
where the time goes in v3:
time: 309 us; the launch traced here: 308 us
  Pallas kernels  104 us (34%)
  waiting for transfers between devices  76.3 us (25%)
  starting transfers between devices  39.8 us (13%)
  local copies, waits for them, and re-layouts  33.4 us (11%)
  blocking collectives  20.8 us (7%)
  other arithmetic  16.4 us (5%)
  between operations  15 us (5%)
    pallas_call x1, Pallas kernels, attend_backward(): pl.pallas_call(backward_kernel, out_shape=(jax.ShapeDtypeStruct((node_row...  54.1 us
    pallas_call x1, Pallas kernels, attend_forward(): pl.pallas_call(functools.partial(forward_kernel, entries), out_shape=(nod...  49.9 us
    ppermute x7, waiting for transfers between devices, gather_feats(): lax.ppermute(lacking(value), 'head', other_head)  39.4 us
    all_gather x1, blocking collectives, per_device(): all_stats = lax.all_gather(stats, 'dom', axis=0, tiled=True)  20.8 us
    ppermute x10, starting transfers between devices, from_across(): return lax.ppermute(value, 'dom', [(at, at ^ bit) for at in range(size)])  19 us
    ppermute x1, waiting for transfers between devices, gather_feats(): lax.ppermute(start, 'dom', onward)  15.3 us
    ppermute x10, waiting for transfers between devices, from_across(): return lax.ppermute(value, 'dom', [(at, at ^ bit) for at in range(size)])  13.5 us
    dynamic_update_slice x30, local copies, waits for them, and re-layouts, put(): lax.dynamic_update_slice_in_dim(result, value, start * rows, axis=0)  11.8 us
  transfers between devices with their start and end apart: 43, of which 16 were waited for; matrix products, arithmetic and copies ran while one was open for 13% of the time, Pallas kernels for 34%

profile of v3, /device:TPU:0, one launch (start us, length us, event | category | flops | bytes accessed | tf_op | source)
XLA Modules:
  0.0 307.9 jit_solution(12007373393792887998)
XLA Ops:
  7.7 1.1 constant_dynamic-slice_fusion.9
  8.9 2.6 collective-permute-start
  11.5 15.3 %collective-permute-done = f32[640,256]{1,0:T(8,128)S(1)} collective-permute-done((f32[640,256]{1,0:T(8,128)S(1)}, f32[640,256]{1,0:T(8,128)S(1)}, u32[]{:S(2)}, u32[]{:S(2)}) %collective-permute-start) | collective-permute-done | bytes 655392 | tf_op jit(solution)/shard_map/ppermute | solution.py:387
  26.8 1.5 collective-permute-done.1
  28.4 1.6 collective-permute-start.5
  30.0 1.6 collective-permute-start.3
  32.6 6.3 %collective-permute-done.5 = f32[384,256]{1,0:T(8,128)S(1)} collective-permute-done((f32[384,256]{1,0:T(8,128)S(1)}, f32[384,256]{1,0:T(8,128)S(1)}, u32[]{:S(2)}, u32[]{:S(2)}) %collective-permute-start.5) | collective-permute-done | bytes 393248 | tf_op jit(solution)/shard_map/ppermute | solution.py:404
  38.9 1.5 collective-permute-start.6
  40.4 8.0 %collective-permute-done.6 = f32[384,256]{1,0:T(8,128)S(1)} collective-permute-done((f32[384,256]{1,0:T(8,128)S(1)}, f32[384,256]{1,0:T(8,128)S(1)}, u32[]{:S(2)}, u32[]{:S(2)}) %collective-permute-start.6) | collective-permute-done | bytes 393248 | tf_op jit(solution)/shard_map/ppermute | solution.py:404
  48.5 1.6 collective-permute-start.11
  50.6 1.6 collective-permute-start.9
  52.7 8.0 %collective-permute-done.11 = f32[384,256]{1,0:T(8,128)} collective-permute-done((f32[384,256]{1,0:T(8,128)S(1)}, f32[384,256]{1,0:T(8,128)}, u32[]{:S(2)}, u32[]{:S(2)}) %collective-permute-start.11) | collective-permute-done | bytes 393248 | tf_op jit(solution)/shard_map/ppermute | solution.py:404
  60.7 4.8 %collective-permute-done.12 = f32[384,256]{1,0:T(8,128)S(1)} collective-permute-done((f32[384,256]{1,0:T(8,128)S(1)}, f32[384,256]{1,0:T(8,128)S(1)}, u32[]{:S(2)}, u32[]{:S(2)}) %collective-permute-start.12) | collective-permute-done | bytes 393248 | tf_op jit(solution)/shard_map/ppermute | solution.py:404
  65.6 0.8 copy-done.32
  66.8 2.2 fusion.32.refs_9_
  69.1 1.1 constant_dynamic-slice_fusion.4
  70.5 1.6 collective-permute-start.17
  72.1 1.5 collective-permute-start.19
  73.6 0.7 multiply_add_fusion
  74.3 0.7 slice.28
  76.1 0.8 constant_dynamic-slice_fusion.3
  76.9 6.0 %collective-permute-done.18 = f32[256,256]{1,0:T(8,128)S(1)} collective-permute-done((f32[256,256]{1,0:T(8,128)}, f32[256,256]{1,0:T(8,128)S(1)}, u32[]{:S(2)}, u32[]{:S(2)}) %collective-permute-start.18) | collective-permute-done | bytes 262176 | tf_op jit(solution)/shard_map/ppermute | solution.py:400
  84.0 0.8 convert_element_type.45
  84.8 0.9 pad_maximum_fusion
  85.7 7.3 %collective-permute-done.20 = f32[384,256]{1,0:T(8,128)} collective-permute-done((f32[384,256]{1,0:T(8,128)}, f32[384,256]{1,0:T(8,128)}, u32[]{:S(2)}, u32[]{:S(2)}) %collective-permute-start.20) | collective-permute-done | bytes 393248 | tf_op jit(solution)/shard_map/ppermute | solution.py:404
  93.0 1.0 constant_dynamic-update-slice_fusion.30
  94.2 2.5 dynamic_update_slice.90
  97.3 1.1 constant_dynamic-update-slice_fusion.20
  98.5 1.0 constant_dynamic-update-slice_fusion.17
  100.9 1.2 constant_dynamic-update-slice_fusion.14
  102.1 1.1 constant_dynamic-update-slice_fusion.12
  103.2 1.0 constant_dynamic-update-slice_fusion.11
  104.2 1.0 constant_dynamic-update-slice_fusion.10
  105.3 1.0 constant_dynamic-update-slice_fusion.8
  106.3 5.0 %collective-permute-done.25 = f32[384,256]{1,0:T(8,128)S(1)} collective-permute-done((f32[384,256]{1,0:T(8,128)S(1)}, f32[384,256]{1,0:T(8,128)S(1)}, u32[]{:S(2)}, u32[]{:S(2)}) %collective-permute-start.25) | collective-permute-done | bytes 393248 | tf_op jit(solution)/shard_map/ppermute | solution.py:404
  111.6 1.0 constant_dynamic-update-slice_fusion.3
  113.1 5.8 %copy-done.7 = f32[16384,256]{1,0:T(8,128)} copy-done((f32[16384,256]{1,0:T(8,128)}, f32[16384,256]{1,0:T(8,128)S(1)}, u32[]{:S(2)}) %copy-start.7) | copy-done | bytes 16777240
  118.9 49.9 %attend_forward.1 = (f32[1024,256]{1,0:T(8,128)S(1)}, f32[1024,256]{1,0:T(8,128)S(1)}, f32[8,8,128]{2,1,0:T(8,128)S(1)}, f32[256,128]{1,0:T(8,128)S(1)}, f32[128,256]{1,0:T(8,128)S(1)}) custom-call(s32[8,8]{1,0:T(8,128)S(1)} %get-tuple-element.110.ids, f32[16384,256]{1,0:T(8,128)} %copy-done.7, f32[16384,256]{1,0:T(8,128)} %copy-done.7, ...), custom_call_target="tpu_custom_call" | custom-call | tf_op jit(solution)/shard_map/attend_forward/pallas_call | solution.py:126
  168.9 1.0 copy-done.1
  170.1 1.2 collective-permute-done.32
  171.9 0.8 constant_dynamic-slice_fusion.1
  173.2 3.8 %collective-permute-done.33 = f32[256,128]{1,0:T(8,128)S(1)} collective-permute-done((f32[256,128]{1,0:T(8,128)S(1)}, f32[256,128]{1,0:T(8,128)S(1)}, u32[]{:S(2)}, u32[]{:S(2)}) %collective-permute-start.33) | collective-permute-done | bytes 131104 | tf_op jit(solution)/shard_map/ppermute | solution.py:339
  177.0 1.8 collective-permute-start.34
  178.8 20.8 %all_gather.7.refs_8_.refs_9_.refs_10_.refs_11_ = f32[128,8,128]{2,1,0:T(8,128)S(1)} all-gather(f32[8,8,128]{2,1,0:T(8,128)S(1)} %get-tuple-element.101), channel_id=1, replica_groups=mesh['dom'=16,'head'=2] {'dom'}, dimensions={0}, use_global_device_ids=true | all-gather | bytes 557056 | tf_op jit(solution)/shard_map/all_gather | solution.py:483
  200.3 0.8 slice_convert_fusion
  202.6 1.8 slice.38
  204.6 0.7 convert_reduce_fusion.1
  206.4 1.1 reshape.645
  207.5 0.9 pad_bitcast_fusion
  209.0 1.7 gather_fusion
  211.5 0.7 minimum_bitcast_fusion
  212.2 54.1 %attend_backward.1 = (f32[1024,256]{1,0:T(8,128)S(1)}, f32[256,128]{1,0:T(8,128)S(1)}, f32[256,128]{1,0:T(8,128)S(1)}) custom-call(s32[2,24]{1,0:T(2,128)S(1)} %pad_add_fusion.2.steps_ref, s32[3,96]{1,0:T(4,128)S(1)} %pad_add_fusion.1.readers_ref, f32[16384,256]{1,0:T(8,128)} %copy-done.7, f32[16384,256]{1,0:T(8,128)} %copy-done.7, f32[16384,256]{1,0:T(8,128)} %copy-done.7, ...), custom_call_target="tpu_custom_call" | custom-call | tf_op jit(solution)/shard_map/attend_backward/pallas_call | solution.py:252
  266.4 1.0 copy-done.2
  267.4 7.8 %collective-permute-start.37 = (f32[256,128]{1,0:T(8,128)S(1)}, f32[256,128]{1,0:T(8,128)S(1)}, u32[]{:S(2)}, u32[]{:S(2)}) collective-permute-start(f32[256,128]{1,0:T(8,128)S(1)} %broadcast_select_fusion.3), channel_id=1, source_target_pairs={{0,2},{2,0},{4,6},{6,4},{8,10},{10,8},{12,14},{14,12},{16,18},{18,... | collective-permute-start | bytes 393224 | tf_op jit(solution)/shard_map/ppermute | solution.py:339
  275.2 1.0 add.422
  276.3 2.4 collective-permute-start.38
  278.6 1.9 dynamic-slice_add_fusion.1
  280.5 1.1 constant_dynamic-slice_fusion
  282.8 3.4 %collective-permute-start.39 = (f32[256,128]{1,0:T(8,128)S(1)}, f32[256,128]{1,0:T(8,128)S(1)}, u32[]{:S(2)}, u32[]{:S(2)}) collective-permute-start(f32[256,128]{1,0:T(8,128)S(1)} %add.424), channel_id=1, source_target_pairs={{0,8},{2,10},{4,12},{6,14},{8,0},{10,2},{12,4},{14,6},{16,24},{18,... | collective-permute-start | bytes 393224 | tf_op jit(solution)/shard_map/ppermute | solution.py:339
  286.9 2.9 collective-permute-done.39
  289.8 2.8 collective-permute-start.40
  293.3 5.1 %collective-permute-done.40 = f32[256,128]{1,0:T(8,128)S(1)} collective-permute-done((f32[256,128]{1,0:T(8,128)S(1)}, f32[256,128]{1,0:T(8,128)S(1)}, u32[]{:S(2)}, u32[]{:S(2)}) %collective-permute-start.40) | collective-permute-done | bytes 131104 | tf_op jit(solution)/shard_map/ppermute | solution.py:339
  298.4 1.9 dynamic-slice_add_fusion
  300.3 0.7 broadcast_select_fusion.1
  (200 shorter events, 17.3 us)
Async XLA Ops:
  7.2 193.1 %all-gather.2.cloned.1.call-start = ((), (), s32[]{:S(2)}) async-start(), calls=%async_computation | async-start | bytes 10027008 | tf_op jit(solution)/shard_map/all_gather | solution.py:465
  7.2 21.1 %collective-permute-start.2 = (f32[1024,256]{1,0:T(8,128)}, f32[1024,256]{1,0:T(8,128)S(1)}, u32[]{:S(2)}, u32[]{:S(2)}) collective-permute-start(f32[1024,256]{1,0:T(8,128)} %refs_12_.3), channel_id=1, source_target_pairs={{0,2},{2,0},{4,6},{6,4},{8,10},{10,8},{12,14},{14,12},{16,18},{18,... | collective-permute-start | bytes 3145736 | tf_op jit(solution)/shard_map/ppermute | solution.py:384
  8.9 17.9 %collective-permute-start = (f32[640,256]{1,0:T(8,128)S(1)}, f32[640,256]{1,0:T(8,128)S(1)}, u32[]{:S(2)}, u32[]{:S(2)}) collective-permute-start(f32[640,256]{1,0:T(8,128)S(1)} %constant_dynamic-slice_fusion.9), channel_id=1, source_target_pairs={{0,8},{2,10},{8,16},{10,18},{16,24},{18,26},{24,28},{26,30},{28,20... | collective-permute-start | bytes 1966088 | tf_op jit(solution)/shard_map/ppermute | solution.py:387
  11.5 16.8 %collective-permute-start.1 = (f32[640,256]{1,0:T(8,128)S(1)}, f32[640,256]{1,0:T(8,128)S(1)}, u32[]{:S(2)}, u32[]{:S(2)}) collective-permute-start(f32[640,256]{1,0:T(8,128)S(1)} %constant_dynamic-slice_fusion.9), channel_id=1, source_target_pairs={{8,0},{10,2},{16,8},{18,10},{24,16},{26,18},{28,24},{30,26},{20,28... | collective-permute-start | bytes 1966088 | tf_op jit(solution)/shard_map/ppermute | solution.py:387
  26.8 23.8 %copy-start.10 = (f32[640,256]{1,0:T(8,128)}, f32[640,256]{1,0:T(8,128)S(1)}, u32[]{:S(2)}) copy-start(f32[640,256]{1,0:T(8,128)S(1)} %collective-permute-done) | copy-start | bytes 1966084
  28.4 37.2 %copy-start.8 = (f32[640,256]{1,0:T(8,128)}, f32[640,256]{1,0:T(8,128)S(1)}, u32[]{:S(2)}) copy-start(f32[640,256]{1,0:T(8,128)S(1)} %collective-permute-done.1) | copy-start | bytes 1966084
  28.4 10.5 %collective-permute-start.5 = (f32[384,256]{1,0:T(8,128)S(1)}, f32[384,256]{1,0:T(8,128)S(1)}, u32[]{:S(2)}, u32[]{:S(2)}) collective-permute-start(f32[384,256]{1,0:T(8,128)S(1)} %constant_dynamic-slice_fusion.8), channel_id=1, source_target_pairs={{0,1},{1,0},{2,3},{3,2},{4,5},{5,4},{6,7},{7,6},{8,9},{9,8},{10,11... | collective-permute-start | bytes 1179656 | tf_op jit(solution)/shard_map/ppermute | solution.py:404
  30.0 18.4 %collective-permute-start.3 = (f32[640,256]{1,0:T(8,128)S(1)}, f32[640,256]{1,0:T(8,128)S(1)}, u32[]{:S(2)}, u32[]{:S(2)}) collective-permute-start(f32[640,256]{1,0:T(8,128)S(1)} %collective-permute-done), channel_id=1, source_target_pairs={{0,8},{2,10},{8,16},{10,18},{16,24},{18,26},{24,28},{26,30},{28,20... | collective-permute-start | bytes 1966088 | tf_op jit(solution)/shard_map/ppermute | solution.py:395
  31.6 16.8 %collective-permute-start.4 = (f32[640,256]{1,0:T(8,128)S(1)}, f32[640,256]{1,0:T(8,128)S(1)}, u32[]{:S(2)}, u32[]{:S(2)}) collective-permute-start(f32[640,256]{1,0:T(8,128)S(1)} %collective-permute-done.1), channel_id=1, source_target_pairs={{8,0},{10,2},{16,8},{18,10},{24,16},{26,18},{28,24},{30,26},{20,28... | collective-permute-start | bytes 1966088 | tf_op jit(solution)/shard_map/ppermute | solution.py:395
  32.0 16.4 %collective-permute-start.7 = (f32[640,256]{1,0:T(8,128)S(1)}, f32[640,256]{1,0:T(8,128)S(1)}, u32[]{:S(2)}, u32[]{:S(2)}) collective-permute-start(f32[640,256]{1,0:T(8,128)S(1)} %collective-permute-done), channel_id=1, source_target_pairs={{0,2},{2,0},{4,6},{6,4},{8,10},{10,8},{12,14},{14,12},{16,18},{18,... | collective-permute-start | bytes 1966088 | tf_op jit(solution)/shard_map/ppermute | solution.py:384
  32.0 16.4 %collective-permute-start.8 = (f32[640,256]{1,0:T(8,128)S(1)}, f32[640,256]{1,0:T(8,128)S(1)}, u32[]{:S(2)}, u32[]{:S(2)}) collective-permute-start(f32[640,256]{1,0:T(8,128)S(1)} %collective-permute-done.1), channel_id=1, source_target_pairs={{0,2},{2,0},{4,6},{6,4},{8,10},{10,8},{12,14},{14,12},{16,18},{18,... | collective-permute-start | bytes 1966088 | tf_op jit(solution)/shard_map/ppermute | solution.py:384
  38.9 33.2 %copy-start.25 = (f32[384,256]{1,0:T(8,128)}, f32[384,256]{1,0:T(8,128)S(1)}, u32[]{:S(2)}) copy-start(f32[384,256]{1,0:T(8,128)S(1)} %collective-permute-done.5) | copy-start | bytes 1179652
  38.9 9.5 %collective-permute-start.6 = (f32[384,256]{1,0:T(8,128)S(1)}, f32[384,256]{1,0:T(8,128)S(1)}, u32[]{:S(2)}, u32[]{:S(2)}) collective-permute-start(f32[384,256]{1,0:T(8,128)S(1)} %constant_dynamic-slice_fusion.7), channel_id=1, source_target_pairs={{0,1},{1,0},{2,3},{3,2},{4,5},{5,4},{6,7},{7,6},{8,9},{9,8},{10,11... | collective-permute-start | bytes 1179656 | tf_op jit(solution)/shard_map/ppermute | solution.py:404
  48.3 23.8 %copy-start.29 = (f32[384,256]{1,0:T(8,128)}, f32[384,256]{1,0:T(8,128)S(1)}, u32[]{:S(2)}) copy-start(f32[384,256]{1,0:T(8,128)S(1)} %collective-permute-done.6) | copy-start | bytes 1179652
  48.4 20.8 %copy-start.14 = (f32[640,256]{1,0:T(8,128)}, f32[640,256]{1,0:T(8,128)S(1)}, u32[]{:S(2)}) copy-start(f32[640,256]{1,0:T(8,128)S(1)} %collective-permute-done.3) | copy-start | bytes 1966084
  48.4 27.2 %copy-start.12 = (f32[640,256]{1,0:T(8,128)}, f32[640,256]{1,0:T(8,128)S(1)}, u32[]{:S(2)}) copy-start(f32[640,256]{1,0:T(8,128)S(1)} %collective-permute-done.4) | copy-start | bytes 1966084
  48.4 17.1 %copy-start.20 = (f32[640,256]{1,0:T(8,128)}, f32[640,256]{1,0:T(8,128)S(1)}, u32[]{:S(2)}) copy-start(f32[640,256]{1,0:T(8,128)S(1)} %collective-permute-done.7) | copy-start | bytes 1966084
  48.4 17.1 %copy-start.18 = (f32[640,256]{1,0:T(8,128)}, f32[640,256]{1,0:T(8,128)S(1)}, u32[]{:S(2)}) copy-start(f32[640,256]{1,0:T(8,128)S(1)} %collective-permute-done.8) | copy-start | bytes 1966084
  48.5 12.2 %collective-permute-start.11 = (f32[384,256]{1,0:T(8,128)S(1)}, f32[384,256]{1,0:T(8,128)}, u32[]{:S(2)}, u32[]{:S(2)}) collective-permute-start(f32[384,256]{1,0:T(8,128)S(1)} %constant_dynamic-slice_fusion.6), channel_id=1, source_target_pairs={{0,1},{1,0},{2,3},{3,2},{4,5},{5,4},{6,7},{7,6},{8,9},{9,8},{10,11... | collective-permute-start | bytes 1179656 | tf_op jit(solution)/shard_map/ppermute | solution.py:404
  50.1 15.4 %collective-permute-start.12 = (f32[384,256]{1,0:T(8,128)S(1)}, f32[384,256]{1,0:T(8,128)S(1)}, u32[]{:S(2)}, u32[]{:S(2)}) collective-permute-start(f32[384,256]{1,0:T(8,128)S(1)} %constant_dynamic-slice_fusion.5), channel_id=1, source_target_pairs={{0,1},{1,0},{2,3},{3,2},{4,5},{5,4},{6,7},{7,6},{8,9},{9,8},{10,11... | collective-permute-start | bytes 1179656 | tf_op jit(solution)/shard_map/ppermute | solution.py:404
  50.6 14.9 %collective-permute-start.15 = (f32[384,256]{1,0:T(8,128)S(1)}, f32[384,256]{1,0:T(8,128)S(1)}, u32[]{:S(2)}, u32[]{:S(2)}) collective-permute-start(f32[384,256]{1,0:T(8,128)S(1)} %collective-permute-done.5), channel_id=1, source_target_pairs={{0,2},{2,0},{4,6},{6,4},{8,10},{10,8},{12,14},{14,12},{16,18},{18,... | collective-permute-start | bytes 1179656 | tf_op jit(solution)/shard_map/ppermute | solution.py:384
  50.6 18.4 %collective-permute-start.9 = (f32[640,256]{1,0:T(8,128)S(1)}, f32[640,256]{1,0:T(8,128)S(1)}, u32[]{:S(2)}, u32[]{:S(2)}) collective-permute-start(f32[640,256]{1,0:T(8,128)S(1)} %collective-permute-done.3), channel_id=1, source_target_pairs={{0,8},{2,10},{8,16},{10,18},{16,24},{18,26},{24,28},{26,30},{28,20... | collective-permute-start | bytes 1966088 | tf_op jit(solution)/shard_map/ppermute | solution.py:395
  52.2 16.9 %collective-permute-start.10 = (f32[640,256]{1,0:T(8,128)S(1)}, f32[640,256]{1,0:T(8,128)S(1)}, u32[]{:S(2)}, u32[]{:S(2)}) collective-permute-start(f32[640,256]{1,0:T(8,128)S(1)} %collective-permute-done.4), channel_id=1, source_target_pairs={{8,0},{10,2},{16,8},{18,10},{24,16},{26,18},{28,24},{30,26},{20,28... | collective-permute-start | bytes 1966088 | tf_op jit(solution)/shard_map/ppermute | solution.py:395
  60.7 8.4 %collective-permute-start.13 = (f32[640,256]{1,0:T(8,128)S(1)}, f32[640,256]{1,0:T(8,128)S(1)}, u32[]{:S(2)}, u32[]{:S(2)}) collective-permute-start(f32[640,256]{1,0:T(8,128)S(1)} %collective-permute-done.3), channel_id=1, source_target_pairs={{0,2},{2,0},{4,6},{6,4},{8,10},{10,8},{12,14},{14,12},{16,18},{18,... | collective-permute-start | bytes 1966088 | tf_op jit(solution)/shard_map/ppermute | solution.py:384
  65.5 27.5 %copy-start.27 = (f32[384,256]{1,0:T(8,128)}, f32[384,256]{1,0:T(8,128)S(1)}, u32[]{:S(2)}) copy-start(f32[384,256]{1,0:T(8,128)S(1)} %collective-permute-done.12) | copy-start | bytes 1179652
  65.5 3.6 %collective-permute-start.14 = (f32[640,256]{1,0:T(8,128)S(1)}, f32[640,256]{1,0:T(8,128)S(1)}, u32[]{:S(2)}, u32[]{:S(2)}) collective-permute-start(f32[640,256]{1,0:T(8,128)S(1)} %collective-permute-done.4), channel_id=1, source_target_pairs={{0,2},{2,0},{4,6},{6,4},{8,10},{10,8},{12,14},{14,12},{16,18},{18,... | collective-permute-start | bytes 1966088 | tf_op jit(solution)/shard_map/ppermute | solution.py:384
  66.4 2.6 collective-permute-start.16
  69.0 4.6 %copy-start.34 = (f32[384,256]{1,0:T(8,128)}, f32[384,256]{1,0:T(8,128)S(1)}, u32[]{:S(2)}) copy-start(f32[384,256]{1,0:T(8,128)S(1)} %collective-permute-done.16) | copy-start | bytes 1179652
  70.5 12.9 %collective-permute-start.17 = (f32[384,256]{1,0:T(8,128)}, f32[384,256]{1,0:T(8,128)}, u32[]{:S(2)}, u32[]{:S(2)}) collective-permute-start(f32[384,256]{1,0:T(8,128)} %get-tuple-element.113), channel_id=1, source_target_pairs={{0,8},{2,10},{8,16},{10,18},{16,24},{18,26},{24,28},{26,30},{28,20... | collective-permute-start | bytes 1179656 | tf_op jit(solution)/shard_map/ppermute | solution.py:399
  72.1 11.4 %collective-permute-start.19 = (f32[384,256]{1,0:T(8,128)}, f32[384,256]{1,0:T(8,128)S(1)}, u32[]{:S(2)}, u32[]{:S(2)}) collective-permute-start(f32[384,256]{1,0:T(8,128)} %get-tuple-element.112), channel_id=1, source_target_pairs={{0,1},{1,0},{2,3},{3,2},{4,5},{5,4},{6,7},{7,6},{8,9},{9,8},{10,11... | collective-permute-start | bytes 1179656 | tf_op jit(solution)/shard_map/ppermute | solution.py:404
  75.1 7.9 %collective-permute-start.18 = (f32[256,256]{1,0:T(8,128)}, f32[256,256]{1,0:T(8,128)S(1)}, u32[]{:S(2)}, u32[]{:S(2)}) collective-permute-start(f32[256,256]{1,0:T(8,128)} %slice.28), channel_id=1, source_target_pairs={{8,0},{10,2},{16,8},{18,10},{24,16},{26,18},{28,24},{30,26},{20,28... | collective-permute-start | bytes 786440 | tf_op jit(solution)/shard_map/ppermute | solution.py:400
  75.5 17.5 %collective-permute-start.21 = (f32[640,256]{1,0:T(8,128)S(1)}, f32[640,256]{1,0:T(8,128)}, u32[]{:S(2)}, u32[]{:S(2)}) collective-permute-start(f32[640,256]{1,0:T(8,128)S(1)} %collective-permute-done.9), channel_id=1, source_target_pairs={{0,2},{2,0},{4,6},{6,4},{8,10},{10,8},{12,14},{14,12},{16,18},{18,... | collective-permute-start | bytes 1966088 | tf_op jit(solution)/shard_map/ppermute | solution.py:384
  75.5 17.5 %collective-permute-start.22 = (f32[640,256]{1,0:T(8,128)S(1)}, f32[640,256]{1,0:T(8,128)}, u32[]{:S(2)}, u32[]{:S(2)}) collective-permute-start(f32[640,256]{1,0:T(8,128)S(1)} %collective-permute-done.10), channel_id=1, source_target_pairs={{0,2},{2,0},{4,6},{6,4},{8,10},{10,8},{12,14},{14,12},{16,18},{18,... | collective-permute-start | bytes 1966088 | tf_op jit(solution)/shard_map/ppermute | solution.py:384
  83.0 10.0 %collective-permute-start.20 = (f32[384,256]{1,0:T(8,128)}, f32[384,256]{1,0:T(8,128)}, u32[]{:S(2)}, u32[]{:S(2)}) collective-permute-start(f32[384,256]{1,0:T(8,128)} %constant_dynamic-slice_fusion.3), channel_id=1, source_target_pairs={{0,1},{1,0},{2,3},{3,2},{4,5},{5,4},{6,7},{7,6},{8,9},{9,8},{10,11... | collective-permute-start | bytes 1179656 | tf_op jit(solution)/shard_map/ppermute | solution.py:404
  83.5 9.5 %collective-permute-start.23 = (f32[384,256]{1,0:T(8,128)}, f32[384,256]{1,0:T(8,128)}, u32[]{:S(2)}, u32[]{:S(2)}) collective-permute-start(f32[384,256]{1,0:T(8,128)} %collective-permute-done.11), channel_id=1, source_target_pairs={{0,2},{2,0},{4,6},{6,4},{8,10},{10,8},{12,14},{14,12},{16,18},{18,... | collective-permute-start | bytes 1179656 | tf_op jit(solution)/shard_map/ppermute | solution.py:384
  83.5 10.6 %copy-start.30 = (f32[384,256]{1,0:T(8,128)}, f32[384,256]{1,0:T(8,128)S(1)}, u32[]{:S(2)}) copy-start(f32[384,256]{1,0:T(8,128)S(1)} %collective-permute-done.19) | copy-start | bytes 1179652
  83.5 9.5 %collective-permute-start.24 = (f32[384,256]{1,0:T(8,128)S(1)}, f32[384,256]{1,0:T(8,128)}, u32[]{:S(2)}, u32[]{:S(2)}) collective-permute-start(f32[384,256]{1,0:T(8,128)S(1)} %collective-permute-done.12), channel_id=1, source_target_pairs={{0,2},{2,0},{4,6},{6,4},{8,10},{10,8},{12,14},{14,12},{16,18},{18,... | collective-permute-start | bytes 1179656 | tf_op jit(solution)/shard_map/ppermute | solution.py:384
  84.8 13.7 %copy-start.26 = (f32[384,256]{1,0:T(8,128)S(1)}, f32[384,256]{1,0:T(8,128)}, u32[]{:S(2)}) copy-start(f32[384,256]{1,0:T(8,128)} %copy-done.25) | copy-start | bytes 1179652
  94.2 5.4 %copy-start.35 = (f32[384,256]{1,0:T(8,128)S(1)}, f32[384,256]{1,0:T(8,128)}, u32[]{:S(2)}) copy-start(f32[384,256]{1,0:T(8,128)} %copy-done.34) | copy-start | bytes 1179652
  94.2 11.1 %copy-start.28 = (f32[384,256]{1,0:T(8,128)S(1)}, f32[384,256]{1,0:T(8,128)}, u32[]{:S(2)}) copy-start(f32[384,256]{1,0:T(8,128)} %copy-done.27) | copy-start | bytes 1179652
  96.7 14.8 %copy-start.31 = (f32[384,256]{1,0:T(8,128)S(1)}, f32[384,256]{1,0:T(8,128)}, u32[]{:S(2)}) copy-start(f32[384,256]{1,0:T(8,128)} %copy-done.30) | copy-start | bytes 1179652
  96.7 22.2 %copy-start.3 = (f32[256,128]{1,0:T(8,128)S(1)}, f32[256,128]{1,0:T(8,128)}, u32[]{:S(2)}) copy-start(f32[256,128]{1,0:T(8,128)} %refs_15_.1) | copy-start | bytes 393220
  96.7 22.2 %copy-start.4 = (f32[256,128]{1,0:T(8,128)S(1)}, f32[256,128]{1,0:T(8,128)}, u32[]{:S(2)}) copy-start(f32[256,128]{1,0:T(8,128)} %refs_16_.1) | copy-start | bytes 393220
  96.7 22.2 %copy-start.5 = (f32[256,128]{1,0:T(8,128)S(1)}, f32[256,128]{1,0:T(8,128)}, u32[]{:S(2)}) copy-start(f32[256,128]{1,0:T(8,128)} %refs_17_.1) | copy-start | bytes 393220
  96.7 22.2 %copy-start.6 = (f32[128,256]{1,0:T(8,128)S(1)}, f32[128,256]{1,0:T(8,128)}, u32[]{:S(2)}) copy-start(f32[128,256]{1,0:T(8,128)} %refs_14_.1) | copy-start | bytes 393220
  99.6 11.7 %collective-permute-start.26 = (f32[640,256]{1,0:T(8,128)S(1)}, f32[640,256]{1,0:T(8,128)S(1)}, u32[]{:S(2)}, u32[]{:S(2)}) collective-permute-start(f32[640,256]{1,0:T(8,128)S(1)} %constant_dynamic-update-slice_fusion.29), channel_id=1, source_target_pairs={{0,2},{2,0},{4,6},{6,4},{8,10},{10,8},{12,14},{14,12},{16,18},{18,... | collective-permute-start | bytes 1966088 | tf_op jit(solution)/shard_map/ppermute | solution.py:384
  99.7 11.6 %collective-permute-start.25 = (f32[384,256]{1,0:T(8,128)S(1)}, f32[384,256]{1,0:T(8,128)S(1)}, u32[]{:S(2)}, u32[]{:S(2)}) collective-permute-start(f32[384,256]{1,0:T(8,128)S(1)} %constant_dynamic-slice_fusion.2), channel_id=1, source_target_pairs={{0,1},{1,0},{2,3},{3,2},{4,5},{5,4},{6,7},{7,6},{8,9},{9,8},{10,11... | collective-permute-start | bytes 1179656 | tf_op jit(solution)/shard_map/ppermute | solution.py:404
  100.3 11.0 %collective-permute-start.27 = (f32[384,256]{1,0:T(8,128)}, f32[384,256]{1,0:T(8,128)S(1)}, u32[]{:S(2)}, u32[]{:S(2)}) collective-permute-start(f32[384,256]{1,0:T(8,128)} %copy-done.30), channel_id=1, source_target_pairs={{0,2},{2,0},{4,6},{6,4},{8,10},{10,8},{12,14},{14,12},{16,18},{18,... | collective-permute-start | bytes 1179656 | tf_op jit(solution)/shard_map/ppermute | solution.py:384
  100.5 10.8 %collective-permute-start.28 = (f32[384,256]{1,0:T(8,128)}, f32[384,256]{1,0:T(8,128)S(1)}, u32[]{:S(2)}, u32[]{:S(2)}) collective-permute-start(f32[384,256]{1,0:T(8,128)} %collective-permute-done.20), channel_id=1, source_target_pairs={{0,2},{2,0},{4,6},{6,4},{8,10},{10,8},{12,14},{14,12},{16,18},{18,... | collective-permute-start | bytes 1179656 | tf_op jit(solution)/shard_map/ppermute | solution.py:384
  111.3 1.8 collective-permute-start.29
  113.1 5.8 %copy-start.7 = (f32[16384,256]{1,0:T(8,128)}, f32[16384,256]{1,0:T(8,128)S(1)}, u32[]{:S(2)}) copy-start(f32[16384,256]{1,0:T(8,128)S(1)} %constant_dynamic-update-slice_fusion.refs_0_.refs_1_.refs_2_.refs_3_.refs_4_.refs_5_.refs_6_.refs_7_) | copy-start | bytes 50331652
  118.9 93.3 %copy-start = (f32[1024,256]{1,0:T(8,128)S(1)}, f32[1024,256]{1,0:T(8,128)}, u32[]{:S(2)}) copy-start(f32[1024,256]{1,0:T(8,128)} %refs_12_.3) | copy-start | bytes 3145732
  169.9 1.4 collective-permute-start.32
  171.4 5.6 %collective-permute-start.33 = (f32[256,128]{1,0:T(8,128)S(1)}, f32[256,128]{1,0:T(8,128)S(1)}, u32[]{:S(2)}, u32[]{:S(2)}) collective-permute-start(f32[256,128]{1,0:T(8,128)S(1)} %select_add_fusion.1), channel_id=1, source_target_pairs={{0,4},{2,6},{4,0},{6,2},{8,12},{10,14},{12,8},{14,10},{16,20},{18,... | collective-permute-start | bytes 393224 | tf_op jit(solution)/shard_map/ppermute | solution.py:339
  172.7 105.9 %collective-permute-start.30 = (f32[1024,128]{1,0:T(8,128)}, f32[1024,128]{1,0:T(8,128)}, u32[]{:S(2)}, u32[]{:S(2)}) collective-permute-start(f32[1024,128]{1,0:T(8,128)} %constant_dynamic-slice_fusion.1), channel_id=1, source_target_pairs={{0,1},{1,0},{2,3},{3,2},{4,5},{5,4},{6,7},{7,6},{8,9},{9,8},{10,11... | collective-permute-start | bytes 1572872 | tf_op jit(solution)/shard_map/ppermute | solution.py:331
  177.0 22.6 %collective-permute-start.34 = (f32[256,128]{1,0:T(8,128)S(1)}, f32[256,128]{1,0:T(8,128)S(1)}, u32[]{:S(2)}, u32[]{:S(2)}) collective-permute-start(f32[256,128]{1,0:T(8,128)S(1)} %add.420), channel_id=1, source_target_pairs={{0,8},{2,10},{4,12},{6,14},{8,0},{10,2},{12,4},{14,6},{16,24},{18,... | collective-permute-start | bytes 393224 | tf_op jit(solution)/shard_map/ppermute | solution.py:339
  200.3 74.9 %collective-permute-start.35 = (f32[256,128]{1,0:T(8,128)}, f32[256,128]{1,0:T(8,128)}, u32[]{:S(2)}, u32[]{:S(2)}) collective-permute-start(f32[256,128]{1,0:T(8,128)} %add.421), channel_id=1, source_target_pairs={{0,16},{2,18},{4,20},{6,22},{8,24},{10,26},{12,28},{14,30},{16,0},... | collective-permute-start | bytes 393224 | tf_op jit(solution)/shard_map/ppermute | solution.py:339
  267.4 8.8 %collective-permute-start.37 = (f32[256,128]{1,0:T(8,128)S(1)}, f32[256,128]{1,0:T(8,128)S(1)}, u32[]{:S(2)}, u32[]{:S(2)}) collective-permute-start(f32[256,128]{1,0:T(8,128)S(1)} %broadcast_select_fusion.3), channel_id=1, source_target_pairs={{0,2},{2,0},{4,6},{6,4},{8,10},{10,8},{12,14},{14,12},{16,18},{18,... | collective-permute-start | bytes 393224 | tf_op jit(solution)/shard_map/ppermute | solution.py:339
  276.2 10.0 %collective-permute-start.36 = (f32[256,128]{1,0:T(8,128)S(1)}, f32[256,128]{1,0:T(8,128)S(1)}, u32[]{:S(2)}, u32[]{:S(2)}) collective-permute-start(f32[256,128]{1,0:T(8,128)S(1)} %add.422), channel_id=1, source_target_pairs={{0,2},{2,0},{4,6},{6,4},{8,10},{10,8},{12,14},{14,12},{16,18},{18,... | collective-permute-start | bytes 393224 | tf_op jit(solution)/shard_map/ppermute | solution.py:339
  276.3 6.5 %collective-permute-start.38 = (f32[256,128]{1,0:T(8,128)S(1)}, f32[256,128]{1,0:T(8,128)S(1)}, u32[]{:S(2)}, u32[]{:S(2)}) collective-permute-start(f32[256,128]{1,0:T(8,128)S(1)} %select_add_fusion), channel_id=1, source_target_pairs={{0,4},{2,6},{4,0},{6,2},{8,12},{10,14},{12,8},{14,10},{16,20},{18,... | collective-permute-start | bytes 393224 | tf_op jit(solution)/shard_map/ppermute | solution.py:339
  281.6 16.8 %collective-permute-start.31 = (f32[1024,128]{1,0:T(8,128)S(1)}, f32[1024,128]{1,0:T(8,128)S(1)}, u32[]{:S(2)}, u32[]{:S(2)}) collective-permute-start(f32[1024,128]{1,0:T(8,128)S(1)} %constant_dynamic-slice_fusion), channel_id=1, source_target_pairs={{0,1},{1,0},{2,3},{3,2},{4,5},{5,4},{6,7},{7,6},{8,9},{9,8},{10,11... | collective-permute-start | bytes 1572872 | tf_op jit(solution)/shard_map/ppermute | solution.py:331
  282.8 6.9 %collective-permute-start.39 = (f32[256,128]{1,0:T(8,128)S(1)}, f32[256,128]{1,0:T(8,128)S(1)}, u32[]{:S(2)}, u32[]{:S(2)}) collective-permute-start(f32[256,128]{1,0:T(8,128)S(1)} %add.424), channel_id=1, source_target_pairs={{0,8},{2,10},{4,12},{6,14},{8,0},{10,2},{12,4},{14,6},{16,24},{18,... | collective-permute-start | bytes 393224 | tf_op jit(solution)/shard_map/ppermute | solution.py:339
  289.8 8.5 %collective-permute-start.40 = (f32[256,128]{1,0:T(8,128)S(1)}, f32[256,128]{1,0:T(8,128)S(1)}, u32[]{:S(2)}, u32[]{:S(2)}) collective-permute-start(f32[256,128]{1,0:T(8,128)S(1)} %add.425), channel_id=1, source_target_pairs={{0,16},{2,18},{4,20},{6,22},{8,24},{10,26},{12,28},{14,30},{16,0},... | collective-permute-start | bytes 393224 | tf_op jit(solution)/shard_map/ppermute | solution.py:339
  298.3 2.0 collective-permute-start.41
  (16 other events, 37.0 us)
Sparse Core Ops, SparseCore 0:
  94.2 80.2 all-gather.1

commit v4 on v3

--- a/solution.py
+++ b/solution.py
@@ -45,14 +45,63 @@
     return value[:, :half] + value[:, half:]
 
 
-def forward_kernel(entries, ids, *refs):
-    feats = refs[:entries]
+def choose(index, sources, use, base=0):
+    if len(sources) == 1:
+        use(sources[0])
+        return
+    half = len(sources) // 2
+
+    @pl.when(index < base + half)
+    def _():
+        choose(index, sources[:half], use, base)
+
+    @pl.when(index >= base + half)
+    def _():
+        choose(index, sources[half:], use, base + half)
+
+
+def fetch(code_of, count, total, sources, target, sem):
+    rows = target.shape[0] // count
+
+    def one(at, carry):
+        code = code_of(at)
+        place = pl.ds(pl.multiple_of(code % total * rows, rows), rows)
+        to = target.at[pl.ds(pl.multiple_of(at * rows, rows), rows), :]
+
+        def use(source):
+            pltpu.make_async_copy(source.at[place, :], to, sem).start()
+
+        choose(code // total, sources, use)
+        return carry
+
+    lax.fori_loop(0, count, one, 0)
+
+
+def forward_kernel(entries, total, source_count, ids, *refs):
+    sources = refs[:source_count]
     (cot_ref, grad_ref, bias_ref, wq_ref, wk_ref, wv_ref, wo_ref,
-     out_ref, feat_ref, stat_ref, gq_ref, go_ref) = refs[entries:]
+     out_ref, feat_ref, stat_ref, gq_ref, go_ref, buffer, sems) = refs[source_count:]
     rows = cot_ref.shape[0]
+    step = pl.program_id(0)
+    turn = step % 2
+
+    def load(at, into):
+        fetch(
+            lambda entry: ids[at, entry], entries, total, sources, buffer.at[into], sems.at[into]
+        )
+
+    @pl.when(step == 0)
+    def _():
+        load(0, 0)
+
+    @pl.when(step + 1 < pl.num_programs(0))
+    def _():
+        load(step + 1, 1 - turn)
+
+    pltpu.make_async_copy(buffer.at[turn], buffer.at[turn], sems.at[turn]).wait()
     cols = wq_ref.shape[1]
     heads = cols // HEAD_SIZE
-    inputs = split(jnp.concatenate([ref[...] for ref in feats], axis=0))
+    inputs = split(buffer[turn])
     w_query = split(wq_ref[...])
     w_out = split(wo_ref[...])
     pairs = mul3(inputs, split(wide(wk_ref[...], wv_ref[...])))
@@ -106,16 +155,13 @@
     go_ref[...] += mul3(mixed, cot, 0, 0)
 
 
-def attend_forward(ids, all_feats, out_cotangent, grad_mixed, bias, w_query, w_key, w_value, w_out):
+def attend_forward(ids, sources, total, out_cotangent, grad_mixed, bias, w_query, w_key, w_value, w_out):
     block_count, entries = ids.shape
     node_rows, width = out_cotangent.shape
     rows = node_rows // block_count
     cols = w_query.shape[1]
     heads = cols // HEAD_SIZE
 
-    def picked(entry):
-        return pl.BlockSpec((rows, width), lambda b, ids: (ids[b, entry], 0))
-
     def whole(array):
         return pl.BlockSpec(array.shape, lambda b, ids: (0,) * array.ndim)
 
@@ -124,7 +170,7 @@
     out_shape = jax.ShapeDtypeStruct((cols, width), F32)
     node_shape = jax.ShapeDtypeStruct((node_rows, width), F32)
     return pl.pallas_call(
-        functools.partial(forward_kernel, entries),
+        functools.partial(forward_kernel, entries, total, len(sources)),
         out_shape=(
             node_shape,
             node_shape,
@@ -135,7 +181,7 @@
         grid_spec=pltpu.PrefetchScalarGridSpec(
             num_scalar_prefetch=1,
             grid=(block_count,),
-            in_specs=[picked(entry) for entry in range(entries)]
+            in_specs=[pl.BlockSpec(memory_space=pl.ANY) for _ in sources]
             + [own, pl.BlockSpec((rows, cols), lambda b, ids: (b, 0))]
             + [pl.BlockSpec((1, 1, entries * rows), lambda b, ids: (b, 0, 0))]
             + [whole(w) for w in (w_query, w_key, w_value, w_out)],
@@ -146,24 +192,46 @@
                 whole(grad_shape),
                 whole(out_shape),
             ),
+            scratch_shapes=[
+                pltpu.VMEM((2, entries * rows, width), F32),
+                pltpu.SemaphoreType.DMA((2,)),
+            ],
         ),
         compiler_params=pltpu.CompilerParams(
             dimension_semantics=("arbitrary",), vmem_limit_bytes=50 * 1024 * 1024
         ),
         name="attend_forward",
-    )(ids, *([all_feats] * entries), out_cotangent, grad_mixed, bias, w_query, w_key, w_value, w_out)
-
-
-def backward_kernel(steps_ref, readers_ref, *refs):
-    feats, cots, stats = refs[:GROUP], refs[GROUP:2 * GROUP], refs[2 * GROUP:3 * GROUP]
-    (own_ref, bias_ref, part_ref, wq_ref, wk_ref, wv_ref,
-     feat_ref, gk_ref, gv_ref, key_mem, value_mem, dk_mem, dv_mem) = refs[3 * GROUP:]
+    )(ids, *sources, out_cotangent, grad_mixed, bias, w_query, w_key, w_value, w_out)
+
+
+def backward_kernel(total, source_count, steps_ref, readers_ref, *refs):
+    cots, stats, refs = refs[:GROUP], refs[GROUP:2 * GROUP], refs[2 * GROUP:]
+    sources = refs[:source_count]
+    (own_ref, bias_ref, part_ref, wq_ref, wk_ref, wv_ref, feat_ref, gk_ref, gv_ref,
+     key_mem, value_mem, dk_mem, dv_mem, buffer, sems) = refs[source_count:]
     step = pl.program_id(0)
     rows = own_ref.shape[0]
     cols = wq_ref.shape[1]
     heads = cols // HEAD_SIZE
     lane = lax.broadcasted_iota(jnp.int32, (rows, cols), 1) // HEAD_SIZE
     kind = steps_ref[1, step]
+    turn = step % 2
+
+    def load(at, into):
+        fetch(
+            lambda reader: readers_ref[1, at * GROUP + reader],
+            GROUP, total, sources, buffer.at[into], sems.at[into],
+        )
+
+    @pl.when(step == 0)
+    def _():
+        load(0, 0)
+
+    following = jnp.minimum(step + 1, pl.num_programs(0) - 1)
+
+    @pl.when((following > step) & (steps_ref[1, following] >= 4))
+    def _():
+        load(step + 1, 1 - turn)
 
     @pl.when(step == 0)
     def _():
@@ -183,7 +251,8 @@
 
     @pl.when(kind >= 4)
     def _():
-        inputs = split(jnp.concatenate([ref[...] for ref in feats], axis=0))
+        pltpu.make_async_copy(buffer.at[turn], buffer.at[turn], sems.at[turn]).wait()
+        inputs = split(buffer[turn])
         q_high, q_low = split(mul3(inputs, split(wq_ref[...])) * SCALE)
         g_high, g_low = split(jnp.concatenate([ref[...] for ref in cots], axis=0))
         q_twice, q_both = wide(q_high, q_high), wide(q_high, q_low)
@@ -226,7 +295,7 @@
 
 
 def attend_backward(
-    steps, readers, all_feats, all_cots, all_stats, own_feats, bias, part,
+    steps, readers, sources, total, all_cots, all_stats, own_feats, bias, part,
     w_query, w_key, w_value, rows,
 ):
     count = steps.shape[1]
@@ -250,14 +319,14 @@
     own = pl.BlockSpec((rows, width), lambda s, steps, readers: (steps[0, s], 0))
     grad_shape = jax.ShapeDtypeStruct((width, cols), F32)
     return pl.pallas_call(
-        backward_kernel,
+        functools.partial(backward_kernel, total, len(sources)),
         out_shape=(jax.ShapeDtypeStruct((node_rows, width), F32), grad_shape, grad_shape),
         grid_spec=pltpu.PrefetchScalarGridSpec(
             num_scalar_prefetch=2,
             grid=(count,),
-            in_specs=[picked(at, width, 1) for at in range(GROUP)]
-            + [picked(at, cols, 2) for at in range(GROUP)]
+            in_specs=[picked(at, cols, 0) for at in range(GROUP)]
             + [picked_stat(at) for at in range(GROUP)]
+            + [pl.BlockSpec(memory_space=pl.ANY) for _ in sources]
             + [own, pl.BlockSpec((1, 8, rows), lambda s, steps, readers: (s, 0, 0)), own]
             + [whole(w) for w in (w_query, w_key, w_value)],
             out_specs=(own, whole(grad_shape), whole(grad_shape)),
@@ -266,6 +335,8 @@
                 pltpu.VMEM((heads * rows, 2 * cols), BF16),
                 pltpu.VMEM((rows, cols), F32),
                 pltpu.VMEM((rows, cols), F32),
+                pltpu.VMEM((2, GROUP * rows, width), F32),
+                pltpu.SemaphoreType.DMA((2,)),
             ],
         ),
         compiler_params=pltpu.CompilerParams(
@@ -273,7 +344,7 @@
         ),
         name="attend_backward",
     )(
-        steps, readers, *([all_feats] * GROUP), *([all_cots] * GROUP), *([all_stats] * GROUP),
+        steps, readers, *([all_cots] * GROUP), *([all_stats] * GROUP), *sources,
         own_feats, bias, part, w_query, w_key, w_value,
     )
 
@@ -347,10 +418,21 @@
     return jnp.where(odd, other, mine), jnp.where(odd, mine, other)
 
 
-def gather_feats(part, block_count):
+def double(value, bit):
+    size, me = lax.axis_size("dom"), lax.axis_index("dom")
+    other = lax.ppermute(value, "dom", [(at, at ^ bit) for at in range(size)])
+    upper = me & bit != 0
+    low, high = jnp.where(upper, other, value), jnp.where(upper, value, other)
+    return jnp.concatenate([low, high], axis=0)
+
+
+def gather_feats(part, lists, block_count):
     size, me = lax.axis_size("dom"), lax.axis_index("dom")
     if size != 16 or lax.axis_size("head") != 2 or block_count != 8:
-        return lax.all_gather(part, "dom", axis=0, tiled=True), lambda ids: ids, part
+        bit = 1
+        while bit < size:
+            lists, bit = double(lists, bit), bit * 2
+        return (lax.all_gather(part, "dom", axis=0, tiled=True),), lambda ids: ids, part, lists
     side = lax.axis_index("head")
     rows = part.shape[0] // block_count
     total = size * block_count
@@ -371,24 +453,22 @@
     def lacking(value):
         return lax.dynamic_slice_in_dim(value, 2 * side * rows, 3 * rows, axis=0)
 
-    result = jnp.zeros((total * rows, part.shape[1]), F32)
-
-    def put(value, start):
-        nonlocal result
-        result = lax.dynamic_update_slice_in_dim(result, value, start * rows, axis=0)
-
-    half = total // 2
-    put(part, 0)
-
     def swap(value):
         return lax.ppermute(value, "dom", across)
 
     start = lax.dynamic_slice_in_dim(part, 3 * side * rows, 5 * rows, axis=0)
     held = (lax.ppermute(start, "dom", onward), lax.ppermute(start, "dom", back))
     twin = swap(part)
-    held, twin = lax.optimization_barrier((held, twin))
-    put(twin, half)
+    lists = double(lists, 1)
+    held, twin, lists = lax.optimization_barrier((held, twin, lists))
+    sources = [None] * 30
+    sources[0], sources[1] = part, twin
     slots, lack, lack_slots = (1, 2), (), ()
+
+    def keep(slot, value, swapped, offset):
+        sources[4 * slot - 2 + offset] = value
+        sources[4 * slot + offset] = swapped
+
     for step in range(1, 5):
         if step < 3:
             coming = (
@@ -404,23 +484,22 @@
         more = tuple(lax.ppermute(lacking(value), "head", other_head) for value in held)
         swapped = tuple(swap(value) for value in held)
         swapped_lack = tuple(swap(value) for value in lack)
-        coming, held, more, swapped, lack, swapped_lack = lax.optimization_barrier(
-            (coming, held, more, swapped, lack, swapped_lack)
+        if step < 4:
+            lists = double(lists, 1 << step)
+        coming, held, more, swapped, lack, swapped_lack, lists = lax.optimization_barrier(
+            (coming, held, more, swapped, lack, swapped_lack, lists)
         )
         for at, slot in enumerate(slots):
-            put(held[at], slot * block_count)
-            put(swapped[at], half + slot * block_count)
+            keep(slot, held[at], swapped[at], 0)
         for at, slot in enumerate(lack_slots):
-            put(lack[at], slot * block_count + 5)
-            put(swapped_lack[at], half + slot * block_count + 5)
+            keep(slot, lack[at], swapped_lack[at], 1)
         lack, lack_slots = more, slots
         if step == 3:
             held, slots = (jnp.concatenate(coming, axis=0),), (7,)
             late = held[0]
         else:
             held, slots = coming, (2 * step + 1, 2 * step + 2)
-    put(lack[0], 7 * block_count + 5)
-    put(swap(lack[0]), half + 7 * block_count + 5)
+    keep(7, lack[0], swap(lack[0]), 1)
 
     def chip_place(chip):
         level, column = chip // 2, chip % 2
@@ -430,11 +509,14 @@
         owner, block = ids // block_count, ids % block_count
         gap = (chip_place(owner // 2) - chip_place(me // 2)) % 8
         slot = jnp.where(gap < 4, 2 * gap, 2 * (8 - gap) - 1)
-        moved = jnp.where(gap == 0, block, (block + 5 * side) % block_count)
-        spot = slot * block_count + moved
-        return spot + jnp.where(owner % 2 == me % 2, 0, half)
-
-    return result, place, late
+        moved = (block + 5 * side) % block_count
+        far = owner % 2 != me % 2
+        source = 4 * slot - 2 + 2 * far + (moved >= 5)
+        inside = jnp.where(moved < 5, moved, moved - 5)
+        source = jnp.where(gap == 0, far, source)
+        return source * total + jnp.where(gap == 0, block, inside)
+
+    return tuple(sources), place, late, lists
 
 
 def per_device(
@@ -450,30 +532,27 @@
     ids = jnp.concatenate([self_ids, nbr_part * block_count + nbr_slot], axis=1)
     mask = jnp.concatenate([jnp.ones((block_count, 1, rows), jnp.int32), key_mask], axis=1)
     bias = jnp.where(mask > 0, 0.0, MASKED).reshape(block_count, 1, (list_len + 1) * rows)
-    all_feats, place, late = gather_feats(node_features, block_count)
+    names = jnp.pad(ids, ((0, 0), (0, rows - list_len - 1))).astype(F32)[:, None]
+    lists = jnp.concatenate([names, key_mask.astype(F32)], axis=1)
+    sources, place, late, lists = gather_feats(node_features, lists, block_count)
+    all_ids = lists[:, 0, : list_len + 1].astype(jnp.int32)
+    all_mask = jnp.concatenate([jnp.ones_like(lists[:, :1]), lists[:, 1:]], axis=1)
+    steps, readers, back_bias = plan_backward(
+        all_ids, all_mask, me, block_count, dom_count * slot_cap
+    )
+    spots = jnp.stack([readers, place(readers)])
     grad_mixed = lax.dot_general(
         out_cotangent, w_out, (((1,), (1,)), ((), ())), precision=lax.Precision.HIGHEST
     )
+    sent, late = lax.optimization_barrier((grad_mixed, late))
+    all_grads = lax.all_gather(sent, "dom", axis=0, tiled=True)
+    sources, steps, spots, back_bias = lax.optimization_barrier(
+        (sources, steps, spots, back_bias)
+    )
+    total = dom_count * block_count
     cols = w_query.shape[1]
-    names = jnp.pad(ids, ((0, 0), (0, rows - list_len - 1))).astype(F32)
-    extra = jnp.concatenate([names, key_mask.reshape(-1, rows).astype(F32)], axis=0)
-    extra = extra.reshape(-1, cols)
-    extra_blocks = -(-extra.shape[0] // rows)
-    extra = jnp.pad(extra, ((0, extra_blocks * rows - extra.shape[0]), (0, 0)))
-    sent = jnp.concatenate([grad_mixed, extra], axis=0)
-    sent, late = lax.optimization_barrier((sent, late))
-    all_grads = lax.all_gather(sent, "dom", axis=0, tiled=True)
-    extra = all_grads.reshape(dom_count, -1, cols)[:, node_rows:].reshape(dom_count, -1, rows)
-    all_ids = extra[:, :block_count, : list_len + 1].astype(jnp.int32)
-    all_ids = all_ids.reshape(-1, list_len + 1)
-    all_mask = extra[:, block_count:(list_len + 1) * block_count].reshape(-1, list_len, rows)
-    all_mask = jnp.concatenate([jnp.ones_like(all_mask[:, :1]), all_mask], axis=1)
-    steps, readers, back_bias = plan_backward(
-        all_ids, all_mask, me, block_count, dom_count * slot_cap
-    )
-    grad_spots = readers + readers // block_count * extra_blocks
     out_part, feat_part, stats, grad_query, grad_out = attend_forward(
-        place(ids), all_feats, out_cotangent, grad_mixed, bias, w_query, w_key, w_value, w_out
+        place(ids), sources, total, out_cotangent, grad_mixed, bias, w_query, w_key, w_value, w_out
     )
     layer_out = head_scatter(out_part)
     pieces = [grad_out[:, at:at + cols] for at in range(0, width, cols)]
@@ -482,7 +561,7 @@
     grad_out = jnp.concatenate(pieces, axis=1)
     all_stats = lax.all_gather(stats, "dom", axis=0, tiled=True)
     feats_part, grad_key, grad_value = attend_backward(
-        steps, jnp.stack([readers, place(readers), grad_spots]), all_feats, all_grads, all_stats, node_features, back_bias, feat_part,
+        steps, spots, sources, total, all_grads, all_stats, node_features, back_bias, feat_part,
         w_query, w_key, w_value, rows,
     )
     grad_features = head_scatter(feats_part)

time: 309 us -> 342 us (1.11)
  Pallas kernels: 104 us -> 129 us
  waiting for transfers between devices: 76.3 us -> 87.2 us
  starting transfers between devices: 39.8 us -> 35.5 us
    pallas_call x2, Pallas kernels: 104 us -> 129 us  [the longest x1 74.5 us: attend_backward(): pl.pallas_call(functools.partial(backward_kernel, total, len(sources)), o...]
    ppermute x0 -> x4, waiting for transfers between devices: none -> 17.4 us  [double(): other = lax.ppermute(value, 'dom', [(at, at ^ bit) for at in range(size)])]
    ppermute x10, starting transfers between devices: 19 us -> 5.84 us  [from_across(): return lax.ppermute(value, 'dom', [(at, at ^ bit) for at in range(size)])]
    dynamic_update_slice x30 -> x0, local copies, waits for them, and re-layouts: 11.8 us -> none  [put(): lax.dynamic_update_slice_in_dim(result, value, start * rows, axis=0)]
    ppermute x7, waiting for transfers between devices: 39.4 us -> 31.3 us  [gather_feats(): lax.ppermute(lacking(value), 'head', other_head)]
    ppermute x2, waiting for transfers between devices: 0.06 us -> 5.29 us  [gather_feats(): lax.ppermute(held[1], 'dom', back)]
    ppermute x0 -> x4, starting transfers between devices: none -> 5.19 us  [double(): other = lax.ppermute(value, 'dom', [(at, at ^ bit) for at in range(size)])]
    ppermute x2, starting transfers between devices: 1.08 us -> 5.85 us  [head_scatter(): return kept + lax.ppermute(sent, 'head', [(0, 1), (1, 0)])]
  transfers between devices with their start and end apart: 43 -> 47, of which waited for: 16 -> 22; matrix products, arithmetic and copies ran while one was open for 13% -> 12% of each run, Pallas kernels for 34% -> 38%
where the time goes in v4:
time: 342 us; the launch traced here: 340 us
  Pallas kernels  129 us (38%)
  waiting for transfers between devices  87.2 us (25%)
  starting transfers between devices  35.5 us (10%)
  local copies, waits for them, and re-layouts  31.4 us (9%)
  blocking collectives  22.5 us (7%)
  other arithmetic  18.8 us (5%)
  between operations  14.5 us (4%)
    pallas_call x1, Pallas kernels, attend_backward(): pl.pallas_call(functools.partial(backward_kernel, total, len(sources)), o...  74.5 us
    pallas_call x1, Pallas kernels, attend_forward(): pl.pallas_call(functools.partial(forward_kernel, entries, total, len(sour...  54.3 us
    ppermute x7, waiting for transfers between devices, gather_feats(): lax.ppermute(lacking(value), 'head', other_head)  31.3 us
    all_gather x1, blocking collectives, per_device(): all_stats = lax.all_gather(stats, 'dom', axis=0, tiled=True)  22.5 us
    ppermute x4, waiting for transfers between devices, double(): other = lax.ppermute(value, 'dom', [(at, at ^ bit) for at in range(size)])  17.4 us
    ppermute x10, waiting for transfers between devices, from_across(): return lax.ppermute(value, 'dom', [(at, at ^ bit) for at in range(size)])  13.8 us
    ppermute x1, waiting for transfers between devices, gather_feats(): lax.ppermute(start, 'dom', onward)  11.6 us
    unnamed x46, local copies, waits for them, and re-layouts  8.96 us
  transfers between devices with their start and end apart: 47, of which 22 were waited for; matrix products, arithmetic and copies ran while one was open for 12% of the time, Pallas kernels for 38%

profile of v4, /device:TPU:0, one launch (start us, length us, event | category | flops | bytes accessed | tf_op | source)
XLA Modules:
  0.0 340.5 jit_solution(17647962908532147050)
XLA Ops:
  7.2 1.1 constant_dynamic-slice_fusion.9
  8.4 3.1 collective-permute-start
  14.5 11.6 %collective-permute-done.refs_2_.refs_10_ = f32[640,256]{1,0:T(8,128)S(1)} collective-permute-done((f32[640,256]{1,0:T(8,128)S(1)}, f32[640,256]{1,0:T(8,128)S(1)}, u32[]{:S(2)}, u32[]{:S(2)}) %collective-permute-start) | collective-permute-done | bytes 655392 | tf_op jit(solution)/shard_map/ppermute | solution.py:460
  26.1 1.5 collective-permute-done.1.refs_6_.refs_14_
  27.7 1.6 collective-permute-start.6
  29.7 1.5 collective-permute-start.4
  31.7 2.5 collective-permute-done.10
  35.1 2.3 collective-permute-done.6.refs_3_.refs_11_
  37.4 1.5 collective-permute-start.7
  39.0 7.8 %collective-permute-done.7.refs_7_.refs_15_ = f32[384,256]{1,0:T(8,128)S(1)} collective-permute-done((f32[384,256]{1,0:T(8,128)}, f32[384,256]{1,0:T(8,128)S(1)}, u32[]{:S(2)}, u32[]{:S(2)}) %collective-permute-start.7) | collective-permute-done | bytes 393248 | tf_op jit(solution)/shard_map/ppermute | solution.py:484
  46.8 1.6 collective-permute-done.5.refs_14_.refs_22_
  48.5 1.0 collective-permute-start.13
  49.5 1.0 constant_dynamic-slice_fusion.5
  50.5 1.2 collective-permute-start.14
  51.7 1.6 collective-permute-start.19
  53.7 3.9 %collective-permute-done.19 = f32[32,8,128]{2,0,1:T(8,128)S(1)} collective-permute-done((f32[32,8,128]{2,0,1:T(8,128)S(1)}, f32[32,8,128]{2,0,1:T(8,128)S(1)}, u32[]{:S(2)}, u32[]{:S(2)}) %collective-permute-start.19) | collective-permute-done | bytes 131104 | tf_op jit(solution)/shard_map/ppermute | solution.py:423
  57.6 0.9 collective-permute-start.12
  58.5 2.1 collective-permute-done.13.refs_11_.refs_19_
  60.6 7.2 %collective-permute-done.14.refs_15_.refs_23_ = f32[384,256]{1,0:T(8,128)S(1)} collective-permute-done((f32[384,256]{1,0:T(8,128)S(1)}, f32[384,256]{1,0:T(8,128)S(1)}, u32[]{:S(2)}, u32[]{:S(2)}) %collective-permute-start.14) | collective-permute-done | bytes 393248 | tf_op jit(solution)/shard_map/ppermute | solution.py:484
  68.3 1.8 collective-permute-done.18.refs_9_.refs_17_
  70.8 3.6 %collective-permute-done.12.refs_22_.refs_30_ = f32[640,256]{1,0:T(8,128)} collective-permute-done((f32[640,256]{1,0:T(8,128)}, f32[640,256]{1,0:T(8,128)}, u32[]{:S(2)}, u32[]{:S(2)}) %collective-permute-start.12) | collective-permute-done | bytes 655392 | tf_op jit(solution)/shard_map/ppermute | solution.py:475
  74.4 1.2 constant_dynamic-slice_fusion.4
  75.6 1.5 collective-permute-start.20
  77.1 0.9 collective-permute-start.22
  78.0 1.0 slice.25
  79.8 2.6 collective-permute-start.28
  82.4 3.8 %collective-permute-done.21 = f32[256,256]{1,0:T(8,128)S(1)} collective-permute-done((f32[256,256]{1,0:T(8,128)S(1)}, f32[256,256]{1,0:T(8,128)S(1)}, u32[]{:S(2)}, u32[]{:S(2)}) %collective-permute-start.21) | collective-permute-done | bytes 262176 | tf_op jit(solution)/shard_map/ppermute | solution.py:480
  86.2 1.9 constant_dynamic-slice_fusion.3
  88.1 10.1 %collective-permute-done.28 = f32[64,8,128]{2,0,1:T(8,128)S(1)} collective-permute-done((f32[64,8,128]{2,0,1:T(8,128)S(1)}, f32[64,8,128]{2,0,1:T(8,128)S(1)}, u32[]{:S(2)}, u32[]{:S(2)}) %collective-permute-start.28) | collective-permute-done | bytes 262176 | tf_op jit(solution)/shard_map/ppermute | solution.py:423
  98.2 1.1 collective-permute-start.23
  100.2 1.8 fusion.32.refs_31_
  101.9 1.1 broadcast_select_fusion.1
  103.9 3.1 collective-permute-done.23.refs_23_.refs_31_
  107.0 1.8 constant_dynamic-update-slice_fusion.1
  108.8 1.7 constant_dynamic-update-slice_fusion.refs_26_.refs_34_
  110.6 1.8 constant_dynamic-slice_fusion.2
  112.3 1.2 collective-permute-start.29
  115.4 8.8 %collective-permute-done.29.refs_27_.refs_35_ = f32[384,256]{1,0:T(8,128)} collective-permute-done((f32[384,256]{1,0:T(8,128)}, f32[384,256]{1,0:T(8,128)}, u32[]{:S(2)}, u32[]{:S(2)}) %collective-permute-start.29) | collective-permute-done | bytes 393248 | tf_op jit(solution)/shard_map/ppermute | solution.py:484
  124.3 1.8 slice.27
  126.1 1.5 slice_convert_fusion
  127.6 0.9 convert_element_type.89
  128.5 2.1 copy.23
  133.5 1.9 pad_bitcast_fusion
  135.5 2.3 gather_fusion
  141.5 0.9 copy-done.6
  143.2 54.3 %attend_forward.1 = (f32[1024,256]{1,0:T(8,128)}, f32[1024,256]{1,0:T(8,128)}, f32[8,8,128]{2,1,0:T(8,128)S(1)}, f32[256,128]{1,0:T(8,128)S(1)}, f32[128,256]{1,0:T(8,128)S(1)}) custom-call(s32[8,8]{1,0:T(8,128)S(1)} %get-tuple-element.186.ids, f32[1024,256]{1,0:T(8,128)} %refs_38_.1, f32[1024,256]{1,0:T(8,128)} %copy-done.13, f32[640,256]{1,0:T(8,128)} %copy-done.10, ...), custom_call_target="tpu_custom_call" | custom-call | tf_op jit(solution)/shard_map/attend_forward/pallas_call | solution.py:172
  197.7 1.3 collective-permute-done.36
  199.0 1.6 collective-permute-start.37
  200.7 1.9 constant_dynamic-slice_fusion
  202.9 1.8 collective-permute-done.37
  204.7 0.9 add.430
  205.7 2.1 collective-permute-start.38
  207.8 22.5 %all_gather.7.refs_4_.refs_5_.refs_6_.refs_7_ = f32[128,8,128]{2,1,0:T(8,128)} all-gather(f32[8,8,128]{2,1,0:T(8,128)} %copy-done.9), channel_id=1, replica_groups=mesh['dom'=16,'head'=2] {'dom'}, dimensions={0}, use_global_device_ids=true | all-gather | bytes 557056 | tf_op jit(solution)/shard_map/all_gather | solution.py:562
  231.0 0.9 copy-done.2
  231.9 0.9 copy-done.4
  232.8 0.9 copy-done.7
  233.7 74.5 %attend_backward.1 = (f32[1024,256]{1,0:T(8,128)}, f32[256,128]{1,0:T(8,128)S(1)}, f32[256,128]{1,0:T(8,128)S(1)}) custom-call(s32[2,24]{1,0:T(2,128)S(1)} %pad_add_fusion.1.steps_ref, s32[2,96]{1,0:T(2,128)S(1)} %pad_add_fusion.2.readers_ref, f32[16384,128]{1,0:T(8,128)} %all-gather.2.cloned.1.call-done.refs_0_.refs_1_.refs_2_.refs_3_, ...), custom_call_target="tpu_custom_call" | custom-call | tf_op jit(solution)/shard_map/attend_backward/pallas_call | solution.py:321
  308.3 1.1 add.432
  310.0 2.1 dynamic-slice_add_fusion.1
  312.1 1.1 constant_dynamic-slice_fusion.1
  313.1 5.4 %collective-permute-start.35 = (f32[1024,128]{1,0:T(8,128)S(1)}, f32[1024,128]{1,0:T(8,128)S(1)}, u32[]{:S(2)}, u32[]{:S(2)}) collective-permute-start(f32[1024,128]{1,0:T(8,128)S(1)} %constant_dynamic-slice_fusion.1), channel_id=1, source_target_pairs={{0,1},{1,0},{2,3},{3,2},{4,5},{5,4},{6,7},{7,6},{8,9},{9,8},{10,11... | collective-permute-start | bytes 1572872 | tf_op jit(solution)/shard_map/ppermute | solution.py:402
  318.6 1.2 collective-permute-start.43
  320.5 3.1 collective-permute-done.43
  324.4 7.1 %collective-permute-done.44 = f32[256,128]{1,0:T(8,128)S(1)} collective-permute-done((f32[256,128]{1,0:T(8,128)S(1)}, f32[256,128]{1,0:T(8,128)S(1)}, u32[]{:S(2)}, u32[]{:S(2)}) %collective-permute-start.44) | collective-permute-done | bytes 131104 | tf_op jit(solution)/shard_map/ppermute | solution.py:410
  (153 shorter events, 24.0 us)
Async XLA Ops:
  7.2 223.8 %all-gather.2.cloned.1.call-start = ((), (), s32[]{:S(2)}) async-start(), calls=%async_computation | async-start | bytes 8912896 | tf_op jit(solution)/shard_map/all_gather | solution.py:548
  8.4 91.8 %copy-start.5 = (f32[128,256]{1,0:T(8,128)S(1)}, f32[128,256]{1,0:T(8,128)}, u32[]{:S(2)}) copy-start(f32[128,256]{1,0:T(8,128)} %refs_36_.1) | copy-start | bytes 393220
  8.4 17.7 %collective-permute-start = (f32[640,256]{1,0:T(8,128)S(1)}, f32[640,256]{1,0:T(8,128)S(1)}, u32[]{:S(2)}, u32[]{:S(2)}) collective-permute-start(f32[640,256]{1,0:T(8,128)S(1)} %constant_dynamic-slice_fusion.9), channel_id=1, source_target_pairs={{0,8},{2,10},{8,16},{10,18},{16,24},{18,26},{24,28},{26,30},{28,20... | collective-permute-start | bytes 1966088 | tf_op jit(solution)/shard_map/ppermute | solution.py:460
  11.4 16.2 %collective-permute-start.1 = (f32[640,256]{1,0:T(8,128)S(1)}, f32[640,256]{1,0:T(8,128)S(1)}, u32[]{:S(2)}, u32[]{:S(2)}) collective-permute-start(f32[640,256]{1,0:T(8,128)S(1)} %constant_dynamic-slice_fusion.9), channel_id=1, source_target_pairs={{8,0},{10,2},{16,8},{18,10},{24,16},{26,18},{28,24},{30,26},{20,28... | collective-permute-start | bytes 1966088 | tf_op jit(solution)/shard_map/ppermute | solution.py:460
  11.4 16.2 %collective-permute-start.2 = (f32[1024,256]{1,0:T(8,128)}, f32[1024,256]{1,0:T(8,128)S(1)}, u32[]{:S(2)}, u32[]{:S(2)}) collective-permute-start(f32[1024,256]{1,0:T(8,128)} %refs_38_.1), channel_id=1, source_target_pairs={{0,2},{2,0},{4,6},{6,4},{8,10},{10,8},{12,14},{14,12},{16,18},{18,... | collective-permute-start | bytes 3145736 | tf_op jit(solution)/shard_map/ppermute | solution.py:457
  13.1 1.4 collective-permute-start.3
  26.1 22.4 %copy-start.10 = (f32[640,256]{1,0:T(8,128)}, f32[640,256]{1,0:T(8,128)S(1)}, u32[]{:S(2)}) copy-start(f32[640,256]{1,0:T(8,128)S(1)} %collective-permute-done.refs_2_.refs_10_) | copy-start | bytes 1966084
  27.6 21.9 %copy-start.11 = (f32[640,256]{1,0:T(8,128)}, f32[640,256]{1,0:T(8,128)S(1)}, u32[]{:S(2)}) copy-start(f32[640,256]{1,0:T(8,128)S(1)} %collective-permute-done.1.refs_6_.refs_14_) | copy-start | bytes 1966084
  27.6 1.6 copy-start.13
  27.7 9.7 %collective-permute-start.6 = (f32[384,256]{1,0:T(8,128)S(1)}, f32[384,256]{1,0:T(8,128)S(1)}, u32[]{:S(2)}, u32[]{:S(2)}) collective-permute-start(f32[384,256]{1,0:T(8,128)S(1)} %constant_dynamic-slice_fusion.8), channel_id=1, source_target_pairs={{0,1},{1,0},{2,3},{3,2},{4,5},{5,4},{6,7},{7,6},{8,9},{9,8},{10,11... | collective-permute-start | bytes 1179656 | tf_op jit(solution)/shard_map/ppermute | solution.py:484
  29.3 5.0 %collective-permute-start.10 = (f32[16,8,128]{2,0,1:T(8,128)S(1)}, f32[16,8,128]{2,0,1:T(8,128)S(1)}, u32[]{:S(2)}, u32[]{:S(2)}) collective-permute-start(f32[16,8,128]{2,0,1:T(8,128)S(1)} %pad_maximum_fusion.5), channel_id=1, source_target_pairs={{0,4},{2,6},{4,0},{6,2},{8,12},{10,14},{12,8},{14,10},{16,20},{18,... | collective-permute-start | bytes 196616 | tf_op jit(solution)/shard_map/ppermute | solution.py:423
  29.7 17.1 %collective-permute-start.4 = (f32[640,256]{1,0:T(8,128)S(1)}, f32[640,256]{1,0:T(8,128)S(1)}, u32[]{:S(2)}, u32[]{:S(2)}) collective-permute-start(f32[640,256]{1,0:T(8,128)S(1)} %collective-permute-done.refs_2_.refs_10_), channel_id=1, source_target_pairs={{0,8},{2,10},{8,16},{10,18},{16,24},{18,26},{24,28},{26,30},{28,20... | collective-permute-start | bytes 1966088 | tf_op jit(solution)/shard_map/ppermute | solution.py:475
  31.2 17.3 %collective-permute-start.8 = (f32[640,256]{1,0:T(8,128)S(1)}, f32[640,256]{1,0:T(8,128)}, u32[]{:S(2)}, u32[]{:S(2)}) collective-permute-start(f32[640,256]{1,0:T(8,128)S(1)} %collective-permute-done.refs_2_.refs_10_), channel_id=1, source_target_pairs={{0,2},{2,0},{4,6},{6,4},{8,10},{10,8},{12,14},{14,12},{16,18},{18,... | collective-permute-start | bytes 1966088 | tf_op jit(solution)/shard_map/ppermute | solution.py:457
  31.2 17.3 %collective-permute-start.5 = (f32[640,256]{1,0:T(8,128)S(1)}, f32[640,256]{1,0:T(8,128)}, u32[]{:S(2)}, u32[]{:S(2)}) collective-permute-start(f32[640,256]{1,0:T(8,128)S(1)} %collective-permute-done.1.refs_6_.refs_14_), channel_id=1, source_target_pairs={{8,0},{10,2},{16,8},{18,10},{24,16},{26,18},{28,24},{30,26},{20,28... | collective-permute-start | bytes 1966088 | tf_op jit(solution)/shard_map/ppermute | solution.py:475
  34.3 14.2 %collective-permute-start.9 = (f32[640,256]{1,0:T(8,128)S(1)}, f32[640,256]{1,0:T(8,128)}, u32[]{:S(2)}, u32[]{:S(2)}) collective-permute-start(f32[640,256]{1,0:T(8,128)S(1)} %collective-permute-done.1.refs_6_.refs_14_), channel_id=1, source_target_pairs={{0,2},{2,0},{4,6},{6,4},{8,10},{10,8},{12,14},{14,12},{16,18},{18,... | collective-permute-start | bytes 1966088 | tf_op jit(solution)/shard_map/ppermute | solution.py:457
  37.4 9.4 %collective-permute-start.7 = (f32[384,256]{1,0:T(8,128)}, f32[384,256]{1,0:T(8,128)S(1)}, u32[]{:S(2)}, u32[]{:S(2)}) collective-permute-start(f32[384,256]{1,0:T(8,128)} %constant_dynamic-slice_fusion.7), channel_id=1, source_target_pairs={{0,1},{1,0},{2,3},{3,2},{4,5},{5,4},{6,7},{7,6},{8,9},{9,8},{10,11... | collective-permute-start | bytes 1179656 | tf_op jit(solution)/shard_map/ppermute | solution.py:484
  46.8 52.5 %copy-start.12 = (f32[640,256]{1,0:T(8,128)}, f32[640,256]{1,0:T(8,128)S(1)}, u32[]{:S(2)}) copy-start(f32[640,256]{1,0:T(8,128)S(1)} %collective-permute-done.4.refs_10_.refs_18_) | copy-start | bytes 1966084
  48.5 12.1 %collective-permute-start.13 = (f32[384,256]{1,0:T(8,128)S(1)}, f32[384,256]{1,0:T(8,128)S(1)}, u32[]{:S(2)}, u32[]{:S(2)}) collective-permute-start(f32[384,256]{1,0:T(8,128)S(1)} %constant_dynamic-slice_fusion.6), channel_id=1, source_target_pairs={{0,1},{1,0},{2,3},{3,2},{4,5},{5,4},{6,7},{7,6},{8,9},{9,8},{10,11... | collective-permute-start | bytes 1179656 | tf_op jit(solution)/shard_map/ppermute | solution.py:484
  50.5 17.2 %collective-permute-start.14 = (f32[384,256]{1,0:T(8,128)S(1)}, f32[384,256]{1,0:T(8,128)S(1)}, u32[]{:S(2)}, u32[]{:S(2)}) collective-permute-start(f32[384,256]{1,0:T(8,128)S(1)} %constant_dynamic-slice_fusion.5), channel_id=1, source_target_pairs={{0,1},{1,0},{2,3},{3,2},{4,5},{5,4},{6,7},{7,6},{8,9},{9,8},{10,11... | collective-permute-start | bytes 1179656 | tf_op jit(solution)/shard_map/ppermute | solution.py:484
  51.7 16.1 %collective-permute-start.17 = (f32[384,256]{1,0:T(8,128)S(1)}, f32[384,256]{1,0:T(8,128)S(1)}, u32[]{:S(2)}, u32[]{:S(2)}) collective-permute-start(f32[384,256]{1,0:T(8,128)S(1)} %collective-permute-done.6.refs_3_.refs_11_), channel_id=1, source_target_pairs={{0,2},{2,0},{4,6},{6,4},{8,10},{10,8},{12,14},{14,12},{16,18},{18,... | collective-permute-start | bytes 1179656 | tf_op jit(solution)/shard_map/ppermute | solution.py:457
  51.7 5.9 %collective-permute-start.19 = (f32[32,8,128]{2,0,1:T(8,128)S(1)}, f32[32,8,128]{2,0,1:T(8,128)S(1)}, u32[]{:S(2)}, u32[]{:S(2)}) collective-permute-start(f32[32,8,128]{2,0,1:T(8,128)S(1)} %pad_maximum_fusion.2), channel_id=1, source_target_pairs={{0,8},{2,10},{4,12},{6,14},{8,0},{10,2},{12,4},{14,6},{16,24},{18,... | collective-permute-start | bytes 393224 | tf_op jit(solution)/shard_map/ppermute | solution.py:423
  53.3 17.5 %collective-permute-start.11 = (f32[640,256]{1,0:T(8,128)S(1)}, f32[640,256]{1,0:T(8,128)}, u32[]{:S(2)}, u32[]{:S(2)}) collective-permute-start(f32[640,256]{1,0:T(8,128)S(1)} %collective-permute-done.4.refs_10_.refs_18_), channel_id=1, source_target_pairs={{0,8},{2,10},{8,16},{10,18},{16,24},{18,26},{24,28},{26,30},{28,20... | collective-permute-start | bytes 1966088 | tf_op jit(solution)/shard_map/ppermute | solution.py:475
  57.6 16.8 %collective-permute-start.12 = (f32[640,256]{1,0:T(8,128)}, f32[640,256]{1,0:T(8,128)}, u32[]{:S(2)}, u32[]{:S(2)}) collective-permute-start(f32[640,256]{1,0:T(8,128)} %collective-permute-done.5.refs_14_.refs_22_), channel_id=1, source_target_pairs={{8,0},{10,2},{16,8},{18,10},{24,16},{26,18},{28,24},{30,26},{20,28... | collective-permute-start | bytes 1966088 | tf_op jit(solution)/shard_map/ppermute | solution.py:475
  60.6 13.8 %collective-permute-start.15 = (f32[640,256]{1,0:T(8,128)S(1)}, f32[640,256]{1,0:T(8,128)}, u32[]{:S(2)}, u32[]{:S(2)}) collective-permute-start(f32[640,256]{1,0:T(8,128)S(1)} %collective-permute-done.4.refs_10_.refs_18_), channel_id=1, source_target_pairs={{0,2},{2,0},{4,6},{6,4},{8,10},{10,8},{12,14},{14,12},{16,18},{18,... | collective-permute-start | bytes 1966088 | tf_op jit(solution)/shard_map/ppermute | solution.py:457
  67.8 6.7 %collective-permute-start.16 = (f32[640,256]{1,0:T(8,128)}, f32[640,256]{1,0:T(8,128)}, u32[]{:S(2)}, u32[]{:S(2)}) collective-permute-start(f32[640,256]{1,0:T(8,128)} %collective-permute-done.5.refs_14_.refs_22_), channel_id=1, source_target_pairs={{0,2},{2,0},{4,6},{6,4},{8,10},{10,8},{12,14},{14,12},{16,18},{18,... | collective-permute-start | bytes 1966088 | tf_op jit(solution)/shard_map/ppermute | solution.py:457
  67.8 2.4 collective-permute-start.18
  68.3 31.9 %copy-start.14 = (f32[1024,256]{1,0:T(8,128)S(1)}, f32[1024,256]{1,0:T(8,128)}, u32[]{:S(2)}) copy-start(f32[1024,256]{1,0:T(8,128)} %refs_30_.1) | copy-start | bytes 3145732
  68.3 33.6 %copy-start.16 = (f32[64,8,128]{2,0,1:T(8,128)}, f32[64,8,128]{2,0,1:T(8,128)S(1)}, u32[]{:S(2)}) copy-start(f32[64,8,128]{2,0,1:T(8,128)S(1)} %pad_maximum_fusion.1) | copy-start | bytes 786436
  75.6 23.7 %collective-permute-start.20 = (f32[384,256]{1,0:T(8,128)S(1)}, f32[384,256]{1,0:T(8,128)S(1)}, u32[]{:S(2)}, u32[]{:S(2)}) collective-permute-start(f32[384,256]{1,0:T(8,128)S(1)} %get-tuple-element.189), channel_id=1, source_target_pairs={{0,8},{2,10},{8,16},{10,18},{16,24},{18,26},{24,28},{26,30},{28,20... | collective-permute-start | bytes 1179656 | tf_op jit(solution)/shard_map/ppermute | solution.py:479
  77.1 22.9 %collective-permute-start.22 = (f32[384,256]{1,0:T(8,128)S(1)}, f32[384,256]{1,0:T(8,128)}, u32[]{:S(2)}, u32[]{:S(2)}) collective-permute-start(f32[384,256]{1,0:T(8,128)S(1)} %get-tuple-element.188), channel_id=1, source_target_pairs={{0,1},{1,0},{2,3},{3,2},{4,5},{5,4},{6,7},{7,6},{8,9},{9,8},{10,11... | collective-permute-start | bytes 1179656 | tf_op jit(solution)/shard_map/ppermute | solution.py:484
  79.0 7.2 %collective-permute-start.21 = (f32[256,256]{1,0:T(8,128)S(1)}, f32[256,256]{1,0:T(8,128)S(1)}, u32[]{:S(2)}, u32[]{:S(2)}) collective-permute-start(f32[256,256]{1,0:T(8,128)S(1)} %slice.25), channel_id=1, source_target_pairs={{8,0},{10,2},{16,8},{18,10},{24,16},{26,18},{28,24},{30,26},{20,28... | collective-permute-start | bytes 786440 | tf_op jit(solution)/shard_map/ppermute | solution.py:480
  79.8 18.4 %collective-permute-start.28 = (f32[64,8,128]{2,0,1:T(8,128)S(1)}, f32[64,8,128]{2,0,1:T(8,128)S(1)}, u32[]{:S(2)}, u32[]{:S(2)}) collective-permute-start(f32[64,8,128]{2,0,1:T(8,128)S(1)} %pad_maximum_fusion.1), channel_id=1, source_target_pairs={{0,16},{2,18},{4,20},{6,22},{8,24},{10,26},{12,28},{14,30},{16,0},... | collective-permute-start | bytes 786440 | tf_op jit(solution)/shard_map/ppermute | solution.py:423
  82.4 24.6 %collective-permute-start.24 = (f32[640,256]{1,0:T(8,128)}, f32[640,256]{1,0:T(8,128)}, u32[]{:S(2)}, u32[]{:S(2)}) collective-permute-start(f32[640,256]{1,0:T(8,128)} %collective-permute-done.11.refs_18_.refs_26_), channel_id=1, source_target_pairs={{0,2},{2,0},{4,6},{6,4},{8,10},{10,8},{12,14},{14,12},{16,18},{18,... | collective-permute-start | bytes 1966088 | tf_op jit(solution)/shard_map/ppermute | solution.py:457
  86.2 13.9 %copy-start.18 = (f32[256,256]{1,0:T(8,128)}, f32[256,256]{1,0:T(8,128)S(1)}, u32[]{:S(2)}) copy-start(f32[256,256]{1,0:T(8,128)S(1)} %collective-permute-done.21) | copy-start | bytes 786436
  86.2 20.8 %collective-permute-start.25 = (f32[640,256]{1,0:T(8,128)}, f32[640,256]{1,0:T(8,128)}, u32[]{:S(2)}, u32[]{:S(2)}) collective-permute-start(f32[640,256]{1,0:T(8,128)} %collective-permute-done.12.refs_22_.refs_30_), channel_id=1, source_target_pairs={{0,2},{2,0},{4,6},{6,4},{8,10},{10,8},{12,14},{14,12},{16,18},{18,... | collective-permute-start | bytes 1966088 | tf_op jit(solution)/shard_map/ppermute | solution.py:457
  98.2 1.9 copy-start.19
  98.2 8.8 %collective-permute-start.23 = (f32[384,256]{1,0:T(8,128)}, f32[384,256]{1,0:T(8,128)}, u32[]{:S(2)}, u32[]{:S(2)}) collective-permute-start(f32[384,256]{1,0:T(8,128)} %constant_dynamic-slice_fusion.3), channel_id=1, source_target_pairs={{0,1},{1,0},{2,3},{3,2},{4,5},{5,4},{6,7},{7,6},{8,9},{9,8},{10,11... | collective-permute-start | bytes 1179656 | tf_op jit(solution)/shard_map/ppermute | solution.py:484
  99.3 7.7 %collective-permute-start.26 = (f32[384,256]{1,0:T(8,128)S(1)}, f32[384,256]{1,0:T(8,128)S(1)}, u32[]{:S(2)}, u32[]{:S(2)}) collective-permute-start(f32[384,256]{1,0:T(8,128)S(1)} %collective-permute-done.13.refs_11_.refs_19_), channel_id=1, source_target_pairs={{0,2},{2,0},{4,6},{6,4},{8,10},{10,8},{12,14},{14,12},{16,18},{18,... | collective-permute-start | bytes 1179656 | tf_op jit(solution)/shard_map/ppermute | solution.py:457
  100.1 6.9 %collective-permute-start.27 = (f32[384,256]{1,0:T(8,128)S(1)}, f32[384,256]{1,0:T(8,128)S(1)}, u32[]{:S(2)}, u32[]{:S(2)}) collective-permute-start(f32[384,256]{1,0:T(8,128)S(1)} %collective-permute-done.14.refs_15_.refs_23_), channel_id=1, source_target_pairs={{0,2},{2,0},{4,6},{6,4},{8,10},{10,8},{12,14},{14,12},{16,18},{18,... | collective-permute-start | bytes 1179656 | tf_op jit(solution)/shard_map/ppermute | solution.py:457
  101.9 39.5 %copy-start = (f32[256,128]{1,0:T(8,128)S(1)}, f32[256,128]{1,0:T(8,128)}, u32[]{:S(2)}) copy-start(f32[256,128]{1,0:T(8,128)} %refs_41_.1) | copy-start | bytes 393220
  101.9 39.5 %copy-start.1 = (f32[256,128]{1,0:T(8,128)S(1)}, f32[256,128]{1,0:T(8,128)}, u32[]{:S(2)}) copy-start(f32[256,128]{1,0:T(8,128)} %refs_42_.1) | copy-start | bytes 393220
  101.9 39.5 %copy-start.3 = (f32[256,128]{1,0:T(8,128)S(1)}, f32[256,128]{1,0:T(8,128)}, u32[]{:S(2)}) copy-start(f32[256,128]{1,0:T(8,128)} %refs_43_.1) | copy-start | bytes 393220
  110.5 13.7 %collective-permute-start.30 = (f32[640,256]{1,0:T(8,128)}, f32[640,256]{1,0:T(8,128)}, u32[]{:S(2)}, u32[]{:S(2)}) collective-permute-start(f32[640,256]{1,0:T(8,128)} %constant_dynamic-update-slice_fusion.refs_26_.refs_34_), channel_id=1, source_target_pairs={{0,2},{2,0},{4,6},{6,4},{8,10},{10,8},{12,14},{14,12},{16,18},{18,... | collective-permute-start | bytes 1966088 | tf_op jit(solution)/shard_map/ppermute | solution.py:457
  112.3 11.8 %collective-permute-start.29 = (f32[384,256]{1,0:T(8,128)}, f32[384,256]{1,0:T(8,128)}, u32[]{:S(2)}, u32[]{:S(2)}) collective-permute-start(f32[384,256]{1,0:T(8,128)} %constant_dynamic-slice_fusion.2), channel_id=1, source_target_pairs={{0,1},{1,0},{2,3},{3,2},{4,5},{5,4},{6,7},{7,6},{8,9},{9,8},{10,11... | collective-permute-start | bytes 1179656 | tf_op jit(solution)/shard_map/ppermute | solution.py:484
  113.5 10.7 %collective-permute-start.31 = (f32[384,256]{1,0:T(8,128)}, f32[384,256]{1,0:T(8,128)}, u32[]{:S(2)}, u32[]{:S(2)}) collective-permute-start(f32[384,256]{1,0:T(8,128)} %collective-permute-done.22.refs_19_.refs_27_), channel_id=1, source_target_pairs={{0,2},{2,0},{4,6},{6,4},{8,10},{10,8},{12,14},{14,12},{16,18},{18,... | collective-permute-start | bytes 1179656 | tf_op jit(solution)/shard_map/ppermute | solution.py:457
  113.7 10.5 %collective-permute-start.32 = (f32[384,256]{1,0:T(8,128)}, f32[384,256]{1,0:T(8,128)}, u32[]{:S(2)}, u32[]{:S(2)}) collective-permute-start(f32[384,256]{1,0:T(8,128)} %collective-permute-done.23.refs_23_.refs_31_), channel_id=1, source_target_pairs={{0,2},{2,0},{4,6},{6,4},{8,10},{10,8},{12,14},{14,12},{16,18},{18,... | collective-permute-start | bytes 1179656 | tf_op jit(solution)/shard_map/ppermute | solution.py:457
  124.2 17.3 %collective-permute-start.33 = (f32[384,256]{1,0:T(8,128)}, f32[384,256]{1,0:T(8,128)}, u32[]{:S(2)}, u32[]{:S(2)}) collective-permute-start(f32[384,256]{1,0:T(8,128)} %collective-permute-done.29.refs_27_.refs_35_), channel_id=1, source_target_pairs={{0,2},{2,0},{4,6},{6,4},{8,10},{10,8},{12,14},{14,12},{16,18},{18,... | collective-permute-start | bytes 1179656 | tf_op jit(solution)/shard_map/ppermute | solution.py:457
  132.2 1.3 copy-start.20
  141.5 0.9 copy-start.6
  197.5 1.5 copy-start.9
  197.6 1.4 collective-permute-start.36
  199.0 5.7 %collective-permute-start.37 = (f32[256,128]{1,0:T(8,128)S(1)}, f32[256,128]{1,0:T(8,128)}, u32[]{:S(2)}, u32[]{:S(2)}) collective-permute-start(f32[256,128]{1,0:T(8,128)S(1)} %select_add_fusion.1), channel_id=1, source_target_pairs={{0,4},{2,6},{4,0},{6,2},{8,12},{10,14},{12,8},{14,10},{16,20},{18,... | collective-permute-start | bytes 393224 | tf_op jit(solution)/shard_map/ppermute | solution.py:410
  202.5 107.5 %collective-permute-start.34 = (f32[1024,128]{1,0:T(8,128)}, f32[1024,128]{1,0:T(8,128)}, u32[]{:S(2)}, u32[]{:S(2)}) collective-permute-start(f32[1024,128]{1,0:T(8,128)} %constant_dynamic-slice_fusion), channel_id=1, source_target_pairs={{0,1},{1,0},{2,3},{3,2},{4,5},{5,4},{6,7},{7,6},{8,9},{9,8},{10,11... | collective-permute-start | bytes 1572872 | tf_op jit(solution)/shard_map/ppermute | solution.py:402
  205.7 24.7 %collective-permute-start.38 = (f32[256,128]{1,0:T(8,128)S(1)}, f32[256,128]{1,0:T(8,128)S(1)}, u32[]{:S(2)}, u32[]{:S(2)}) collective-permute-start(f32[256,128]{1,0:T(8,128)S(1)} %add.430), channel_id=1, source_target_pairs={{0,8},{2,10},{4,12},{6,14},{8,0},{10,2},{12,4},{14,6},{16,24},{18,... | collective-permute-start | bytes 393224 | tf_op jit(solution)/shard_map/ppermute | solution.py:410
  231.0 77.3 %collective-permute-start.39 = (f32[256,128]{1,0:T(8,128)}, f32[256,128]{1,0:T(8,128)}, u32[]{:S(2)}, u32[]{:S(2)}) collective-permute-start(f32[256,128]{1,0:T(8,128)} %add.431), channel_id=1, source_target_pairs={{0,16},{2,18},{4,20},{6,22},{8,24},{10,26},{12,28},{14,30},{16,0},... | collective-permute-start | bytes 393224 | tf_op jit(solution)/shard_map/ppermute | solution.py:410
  231.0 0.9 copy-start.2
  308.2 23.4 %copy-start.15 = (f32[1024,256]{1,0:T(8,128)S(1)}, f32[1024,256]{1,0:T(8,128)}, u32[]{:S(2)}) copy-start(f32[1024,256]{1,0:T(8,128)} %get-tuple-element.179) | copy-start | bytes 3145732
  308.2 1.6 collective-permute-start.41
  309.4 10.4 %collective-permute-start.40 = (f32[256,128]{1,0:T(8,128)S(1)}, f32[256,128]{1,0:T(8,128)S(1)}, u32[]{:S(2)}, u32[]{:S(2)}) collective-permute-start(f32[256,128]{1,0:T(8,128)S(1)} %add.432), channel_id=1, source_target_pairs={{0,2},{2,0},{4,6},{6,4},{8,10},{10,8},{12,14},{14,12},{16,18},{18,... | collective-permute-start | bytes 393224 | tf_op jit(solution)/shard_map/ppermute | solution.py:410
  309.9 8.7 %collective-permute-start.42 = (f32[256,128]{1,0:T(8,128)S(1)}, f32[256,128]{1,0:T(8,128)S(1)}, u32[]{:S(2)}, u32[]{:S(2)}) collective-permute-start(f32[256,128]{1,0:T(8,128)S(1)} %select_add_fusion), channel_id=1, source_target_pairs={{0,4},{2,6},{4,0},{6,2},{8,12},{10,14},{12,8},{14,10},{16,20},{18,... | collective-permute-start | bytes 393224 | tf_op jit(solution)/shard_map/ppermute | solution.py:410
  313.1 18.5 %collective-permute-start.35 = (f32[1024,128]{1,0:T(8,128)S(1)}, f32[1024,128]{1,0:T(8,128)S(1)}, u32[]{:S(2)}, u32[]{:S(2)}) collective-permute-start(f32[1024,128]{1,0:T(8,128)S(1)} %constant_dynamic-slice_fusion.1), channel_id=1, source_target_pairs={{0,1},{1,0},{2,3},{3,2},{4,5},{5,4},{6,7},{7,6},{8,9},{9,8},{10,11... | collective-permute-start | bytes 1572872 | tf_op jit(solution)/shard_map/ppermute | solution.py:402
  318.6 5.0 %collective-permute-start.43 = (f32[256,128]{1,0:T(8,128)S(1)}, f32[256,128]{1,0:T(8,128)S(1)}, u32[]{:S(2)}, u32[]{:S(2)}) collective-permute-start(f32[256,128]{1,0:T(8,128)S(1)} %add.434), channel_id=1, source_target_pairs={{0,8},{2,10},{4,12},{6,14},{8,0},{10,2},{12,4},{14,6},{16,24},{18,... | collective-permute-start | bytes 393224 | tf_op jit(solution)/shard_map/ppermute | solution.py:410
  323.6 7.8 %collective-permute-start.44 = (f32[256,128]{1,0:T(8,128)S(1)}, f32[256,128]{1,0:T(8,128)S(1)}, u32[]{:S(2)}, u32[]{:S(2)}) collective-permute-start(f32[256,128]{1,0:T(8,128)S(1)} %add.435), channel_id=1, source_target_pairs={{0,16},{2,18},{4,20},{6,22},{8,24},{10,26},{12,28},{14,30},{16,0},... | collective-permute-start | bytes 393224 | tf_op jit(solution)/shard_map/ppermute | solution.py:410
  331.5 1.4 collective-permute-start.45
  (5 other events, 3.9 us)
Sparse Core Ops, SparseCore 0:
  110.6 73.7 all-gather.1

commit v5 on v2

--- a/solution.py
+++ b/solution.py
@@ -45,14 +45,39 @@
     return value[:, :half] + value[:, half:]
 
 
-def forward_kernel(entries, ids, *refs):
-    feats = refs[:entries]
+def forward_kernel(entries, layout, ids, *refs):
+    sources = refs[:len(layout)]
     (cot_ref, grad_ref, bias_ref, wq_ref, wk_ref, wv_ref, wo_ref,
-     out_ref, feat_ref, stat_ref, gq_ref, go_ref) = refs[entries:]
+     all_ref, out_ref, feat_ref, stat_ref, gq_ref, go_ref,
+     feats, sems, all_sem) = refs[len(layout):]
     rows = cot_ref.shape[0]
+    step = pl.program_id(0)
+    keep = pltpu.make_async_copy(feats, all_ref, all_sem)
+
+    @pl.when(step == 0)
+    def _():
+        copies = []
+        for at, (count, block) in enumerate(layout):
+            copies.append(
+                pltpu.make_async_copy(
+                    sources[at].at[pl.ds(0, count), :],
+                    feats.at[pl.ds(block * rows, count), :],
+                    sems.at[at],
+                )
+            )
+        for copy in copies:
+            copy.start()
+        for copy in copies:
+            copy.wait()
+        keep.start()
+
+    listed = [
+        feats[pl.ds(pl.multiple_of(ids[step, entry] * rows, rows), rows), :]
+        for entry in range(entries)
+    ]
     cols = wq_ref.shape[1]
     heads = cols // HEAD_SIZE
-    inputs = split(jnp.concatenate([ref[...] for ref in feats], axis=0))
+    inputs = split(jnp.concatenate(listed, axis=0))
     w_query = split(wq_ref[...])
     w_out = split(wo_ref[...])
     pairs = mul3(inputs, split(wide(wk_ref[...], wv_ref[...])))
@@ -105,16 +130,20 @@
     gq_ref[...] += mul3(own, grad_query, 0, 0)
     go_ref[...] += mul3(mixed, cot, 0, 0)
 
-
-def attend_forward(ids, all_feats, out_cotangent, grad_mixed, bias, w_query, w_key, w_value, w_out):
+    @pl.when(step == pl.num_programs(0) - 1)
+    def _():
+        keep.wait()
+
+
+def attend_forward(ids, pieces, total, out_cotangent, grad_mixed, bias, w_query, w_key, w_value, w_out):
     block_count, entries = ids.shape
     node_rows, width = out_cotangent.shape
     rows = node_rows // block_count
     cols = w_query.shape[1]
     heads = cols // HEAD_SIZE
 
-    def picked(entry):
-        return pl.BlockSpec((rows, width), lambda b, ids: (ids[b, entry], 0))
+    layout = [(count, block) for _, count, block in pieces]
+    all_shape = jax.ShapeDtypeStruct((total * rows, width), F32)
 
     def whole(array):
         return pl.BlockSpec(array.shape, lambda b, ids: (0,) * array.ndim)
@@ -124,8 +153,9 @@
     out_shape = jax.ShapeDtypeStruct((cols, width), F32)
     node_shape = jax.ShapeDtypeStruct((node_rows, width), F32)
     return pl.pallas_call(
-        functools.partial(forward_kernel, entries),
+        functools.partial(forward_kernel, entries, layout),
         out_shape=(
+            all_shape,
             node_shape,
             node_shape,
             jax.ShapeDtypeStruct((block_count, 2 * heads, rows), F32),
@@ -135,29 +165,36 @@
         grid_spec=pltpu.PrefetchScalarGridSpec(
             num_scalar_prefetch=1,
             grid=(block_count,),
-            in_specs=[picked(entry) for entry in range(entries)]
+            in_specs=[pl.BlockSpec(memory_space=pl.ANY) for _ in pieces]
             + [own, pl.BlockSpec((rows, cols), lambda b, ids: (b, 0))]
             + [pl.BlockSpec((1, 1, entries * rows), lambda b, ids: (b, 0, 0))]
             + [whole(w) for w in (w_query, w_key, w_value, w_out)],
             out_specs=(
+                pl.BlockSpec(memory_space=pl.ANY),
                 own,
                 own,
                 pl.BlockSpec((1, 2 * heads, rows), lambda b, ids: (b, 0, 0)),
                 whole(grad_shape),
                 whole(out_shape),
             ),
+            scratch_shapes=[
+                pltpu.VMEM((total * rows, width), F32),
+                pltpu.SemaphoreType.DMA((len(layout),)),
+                pltpu.SemaphoreType.DMA,
+            ],
         ),
         compiler_params=pltpu.CompilerParams(
-            dimension_semantics=("arbitrary",), vmem_limit_bytes=50 * 1024 * 1024
+            dimension_semantics=("arbitrary",), vmem_limit_bytes=56 * 1024 * 1024
         ),
         name="attend_forward",
-    )(ids, *([all_feats] * entries), out_cotangent, grad_mixed, bias, w_query, w_key, w_value, w_out)
+    )(ids, *[array for array, _, _ in pieces], out_cotangent, grad_mixed, bias, w_query, w_key, w_value, w_out)
 
 
 def backward_kernel(steps_ref, readers_ref, *refs):
     feats, cots, stats = refs[:GROUP], refs[GROUP:2 * GROUP], refs[2 * GROUP:3 * GROUP]
-    (own_ref, bias_ref, part_ref, wq_ref, wk_ref, wv_ref,
-     feat_ref, gk_ref, gv_ref, key_mem, value_mem, dk_mem, dv_mem) = refs[3 * GROUP:]
+    lists = refs[3 * GROUP:4 * GROUP]
+    (own_ref, part_ref, wq_ref, wk_ref, wv_ref,
+     feat_ref, gk_ref, gv_ref, key_mem, value_mem, dk_mem, dv_mem) = refs[4 * GROUP:]
     step = pl.program_id(0)
     rows = own_ref.shape[0]
     cols = wq_ref.shape[1]
@@ -191,7 +228,14 @@
         mark_row = lax.broadcasted_iota(jnp.int32, (8, GROUP * rows), 0)
         mark_col = lax.broadcasted_iota(jnp.int32, (8, GROUP * rows), 1)
         marks = (mark_row == mark_col // rows).astype(BF16)
-        bias = mul(bias_ref[0].astype(BF16), marks, 0, 0)
+        masks = []
+        for at, ref in enumerate(lists):
+            entry = readers_ref[2, step * GROUP + at]
+            row = ref[0, pl.ds(jnp.maximum(entry, 0), 1), :]
+            kept = ((row > 0) | (entry == 0)) & (entry >= 0)
+            masks.append(jnp.where(kept, 0.0, MASKED))
+        masks.append(jnp.zeros((8 - GROUP, rows), F32))
+        bias = mul(jnp.concatenate(masks, axis=0).astype(BF16), marks, 0, 0)
         stat = jnp.concatenate([ref[0] for ref in stats], axis=1)
         grad_key = dk_mem[...]
         grad_value = dv_mem[...]
@@ -226,7 +270,7 @@
 
 
 def attend_backward(
-    steps, readers, all_feats, all_cots, all_stats, own_feats, bias, part,
+    steps, readers, all_feats, all_cots, all_stats, lists, own_feats, part,
     w_query, w_key, w_value, rows,
 ):
     count = steps.shape[1]
@@ -234,12 +278,15 @@
     cols = w_query.shape[1]
     heads = cols // HEAD_SIZE
 
-    def picked(at, lanes):
-        return pl.BlockSpec((rows, lanes), lambda s, steps, readers: (readers[s * GROUP + at], 0))
-
-    def picked_stat(at):
+    def picked(at, lanes, kind):
         return pl.BlockSpec(
-            (1, 2 * heads, rows), lambda s, steps, readers: (readers[s * GROUP + at], 0, 0)
+            (rows, lanes), lambda s, steps, readers: (readers[kind, s * GROUP + at], 0)
+        )
+
+    def picked_row(at, array, kind):
+        return pl.BlockSpec(
+            (1,) + array.shape[1:],
+            lambda s, steps, readers: (readers[kind, s * GROUP + at], 0, 0),
         )
 
     def whole(array):
@@ -253,10 +300,11 @@
         grid_spec=pltpu.PrefetchScalarGridSpec(
             num_scalar_prefetch=2,
             grid=(count,),
-            in_specs=[picked(at, width) for at in range(GROUP)]
-            + [picked(at, cols) for at in range(GROUP)]
-            + [picked_stat(at) for at in range(GROUP)]
-            + [own, pl.BlockSpec((1, 8, rows), lambda s, steps, readers: (s, 0, 0)), own]
+            in_specs=[picked(at, width, 1) for at in range(GROUP)]
+            + [picked(at, cols, 0) for at in range(GROUP)]
+            + [picked_row(at, all_stats, 0) for at in range(GROUP)]
+            + [picked_row(at, lists, 3) for at in range(GROUP)]
+            + [own, own]
             + [whole(w) for w in (w_query, w_key, w_value)],
             out_specs=(own, whole(grad_shape), whole(grad_shape)),
             scratch_shapes=[
@@ -272,11 +320,11 @@
         name="attend_backward",
     )(
         steps, readers, *([all_feats] * GROUP), *([all_cots] * GROUP), *([all_stats] * GROUP),
-        own_feats, bias, part, w_query, w_key, w_value,
-    )
-
-
-def plan_backward(all_ids, all_mask, me, block_count, pair_limit):
+        *([lists] * GROUP), own_feats, part, w_query, w_key, w_value,
+    )
+
+
+def plan_backward(all_ids, me, block_count, pair_limit):
     blocks, entries = all_ids.shape
     candidates = blocks * entries
     flat = all_ids.reshape(-1)
@@ -302,10 +350,7 @@
     source = jnp.sum(jnp.where(hit, order[None, :], 0), axis=1)
     filled = jnp.sum(hit.astype(jnp.int32), axis=1) > 0
     readers = source // entries
-    mask = all_mask.reshape(candidates, -1)[source]
-    bias = jnp.where((mask > 0) & filled[:, None], 0.0, MASKED)
-    bias = bias.reshape(count, GROUP, -1)
-    bias = jnp.concatenate([bias, jnp.zeros((count, 8 - GROUP, bias.shape[2]), F32)], axis=1)
+    entry = jnp.where(filled, source % entries, -1)
     step = jnp.arange(count, dtype=jnp.int32)
     block = jnp.sum((step[:, None] >= ends[None, :]).astype(jnp.int32), axis=1)
     live = block < block_count
@@ -315,7 +360,7 @@
     kind = jnp.where(
         live, first.astype(jnp.int32) + 2 * last.astype(jnp.int32) + 4, 0
     )
-    return jnp.stack([block, kind]), readers, bias
+    return jnp.stack([block, kind]), readers, entry
 
 
 def head_scatter(part):
@@ -343,6 +388,115 @@
         bit *= 2
     other = from_across(mine, 1)
     return jnp.where(odd, other, mine), jnp.where(odd, mine, other)
+
+
+def double(value, bit):
+    size, me = lax.axis_size("dom"), lax.axis_index("dom")
+    other = lax.ppermute(value, "dom", [(at, at ^ bit) for at in range(size)])
+    upper = me & bit != 0
+    low, high = jnp.where(upper, other, value), jnp.where(upper, value, other)
+    return jnp.concatenate([low, high], axis=0)
+
+
+def gather_feats(part, lists, block_count, make_plan):
+    size, me = lax.axis_size("dom"), lax.axis_index("dom")
+    if size != 16 or lax.axis_size("head") != 2 or block_count != 8:
+        plan = make_plan(lax.all_gather(lists, "dom", axis=0, tiled=True), lambda ids: ids)
+        everything = lax.all_gather(part, "dom", axis=0, tiled=True)
+        return [(everything, everything.shape[0], 0)], lambda ids: ids, part, plan
+    side = lax.axis_index("head")
+    rows = part.shape[0] // block_count
+    total = size * block_count
+
+    ring = [0, 2, 4, 6, 7, 5, 3, 1]
+    onward, back = [], []
+    for at in range(8):
+        for core in range(2):
+            here, there = 2 * ring[at] + core, 2 * ring[(at + 1) % 8] + core
+            onward.append((here, there))
+            back.append((there, here))
+    across = [(at, at ^ 1) for at in range(size)]
+    other_head = [(0, 1), (1, 0)]
+
+    def lacking(value):
+        return lax.dynamic_slice_in_dim(value, 2 * side * rows, 3 * rows, axis=0)
+
+    half = total // 2
+
+    def swap(value):
+        return lax.ppermute(value, "dom", across)
+
+    def chip_place(chip):
+        level, column = chip // 2, chip % 2
+        return jnp.where(column == 0, level, 7 - level)
+
+    def place(ids):
+        owner, block = ids // block_count, ids % block_count
+        gap = (chip_place(owner // 2) - chip_place(me // 2)) % 8
+        slot = jnp.where(gap < 4, 2 * gap, 2 * (8 - gap) - 1)
+        moved = jnp.where(gap == 0, block, (block + 5 * side) % block_count)
+        spot = slot * block_count + moved
+        return spot + jnp.where(owner % 2 == me % 2, 0, half)
+
+    notes = lists.reshape(-1, lists.shape[2])
+    below = notes.shape[0] // 2
+    notes = jnp.concatenate([notes[:below], notes[below:]], axis=1)
+
+    start = lax.dynamic_slice_in_dim(part, 3 * side * rows, 5 * rows, axis=0)
+    start = jnp.concatenate([start, notes], axis=0)
+    held = (lax.ppermute(start, "dom", onward), lax.ppermute(start, "dom", back))
+    twin = swap(part)
+    all_notes = [notes, swap(notes)]
+    held, twin = lax.optimization_barrier((held, twin))
+    pieces = [(part, block_count * rows, 0), (twin, block_count * rows, half)]
+
+    def keep(value, swapped, slot, offset, count):
+        pieces.append((value, count * rows, slot * block_count + offset))
+        pieces.append((swapped, count * rows, half + slot * block_count + offset))
+        if offset == 0:
+            all_notes.extend([value[count * rows:], swapped[count * rows:]])
+
+    slots, lack, lack_slots = (1, 2), (), ()
+    for step in range(1, 5):
+        if step < 3:
+            coming = (
+                lax.ppermute(held[0], "dom", onward), lax.ppermute(held[1], "dom", back)
+            )
+        elif step == 3:
+            coming = (
+                lax.ppermute(held[0][: 3 * rows], "dom", onward),
+                lax.ppermute(held[1][3 * rows:], "dom", back),
+            )
+        else:
+            coming = ()
+        more = tuple(lax.ppermute(lacking(value), "head", other_head) for value in held)
+        swapped = tuple(swap(value) for value in held)
+        swapped_lack = tuple(swap(value) for value in lack)
+        if step < 4:
+            coming, held, more, swapped, lack, swapped_lack = lax.optimization_barrier(
+                (coming, held, more, swapped, lack, swapped_lack)
+            )
+        else:
+            held, swapped, lack, swapped_lack = lax.optimization_barrier(
+                (held, swapped, lack, swapped_lack)
+            )
+        for at, slot in enumerate(slots):
+            keep(held[at], swapped[at], slot, 0, 5)
+        for at, slot in enumerate(lack_slots):
+            keep(lack[at], swapped_lack[at], slot, 5, 3)
+        lack, lack_slots = more, slots
+        if step == 3:
+            held, slots = (jnp.concatenate(coming, axis=0),), (7,)
+            late = held[0]
+        else:
+            held, slots = coming, (2 * step + 1, 2 * step + 2)
+    every = jnp.concatenate(all_notes, axis=0)
+    width = lists.shape[2]
+    every = jnp.concatenate([every[:, :width], every[:, width:]], axis=0)
+    plan = make_plan(every.reshape((-1,) + lists.shape[1:]), place)
+    lack, plan = lax.optimization_barrier((lack, plan))
+    keep(lack[0], swap(lack[0]), 7, 5, 3)
+    return pieces, place, late, plan
 
 
 def per_device(
@@ -358,28 +512,37 @@
     ids = jnp.concatenate([self_ids, nbr_part * block_count + nbr_slot], axis=1)
     mask = jnp.concatenate([jnp.ones((block_count, 1, rows), jnp.int32), key_mask], axis=1)
     bias = jnp.where(mask > 0, 0.0, MASKED).reshape(block_count, 1, (list_len + 1) * rows)
-    all_feats = lax.all_gather(node_features, "dom", axis=0, tiled=True)
+    names = jnp.pad(ids, ((0, 0), (0, rows - list_len - 1))).astype(F32)[:, None]
+    lists = jnp.concatenate([names, key_mask.astype(F32)], axis=1)
+
+    def make_plan(lists, place):
+        all_ids = lists[:, 0, : list_len + 1].astype(jnp.int32)
+        steps, rows_of, entry = plan_backward(
+            all_ids, me, block_count, dom_count * slot_cap
+        )
+        readers = all_ids[:, 0][rows_of]
+        return steps, jnp.stack([readers, place(readers), entry, rows_of]), lists
+
+    pieces, place, late, (steps, spots, lists) = gather_feats(
+        node_features, lists, block_count, make_plan
+    )
     grad_mixed = lax.dot_general(
         out_cotangent, w_out, (((1,), (1,)), ((), ())), precision=lax.Precision.HIGHEST
     )
-    all_grads = lax.all_gather(grad_mixed, "dom", axis=0, tiled=True)
-    all_ids = lax.all_gather(ids, "dom", axis=0, tiled=True)
-    all_mask = lax.all_gather(mask, "dom", axis=0, tiled=True)
-    steps, readers, back_bias = plan_backward(
-        all_ids, all_mask, me, block_count, dom_count * slot_cap
-    )
-    out_part, feat_part, stats, grad_query, grad_out = attend_forward(
-        ids, all_feats, out_cotangent, grad_mixed, bias, w_query, w_key, w_value, w_out
+    sent, late = lax.optimization_barrier((grad_mixed, late))
+    all_grads = lax.all_gather(sent, "dom", axis=0, tiled=True)
+    cols = w_query.shape[1]
+    all_feats, out_part, feat_part, stats, grad_query, grad_out = attend_forward(
+        place(ids), pieces, dom_count * block_count, out_cotangent, grad_mixed, bias, w_query, w_key, w_value, w_out
     )
     layer_out = head_scatter(out_part)
-    cols = w_query.shape[1]
     pieces = [grad_out[:, at:at + cols] for at in range(0, width, cols)]
     grad_query, grad_out = dom_sum(grad_query, jnp.concatenate(pieces, axis=0))
     pieces = [grad_out[at:at + cols] for at in range(0, width, cols)]
     grad_out = jnp.concatenate(pieces, axis=1)
     all_stats = lax.all_gather(stats, "dom", axis=0, tiled=True)
     feats_part, grad_key, grad_value = attend_backward(
-        steps, readers, all_feats, all_grads, all_stats, node_features, back_bias, feat_part,
+        steps, spots, all_feats, all_grads, all_stats, lists, node_features, feat_part,
         w_query, w_key, w_value, rows,
     )
     grad_features = head_scatter(feats_part)

time: 324 us -> 313 us (0.966)
  blocking collectives: 67.4 us -> 21.1 us
  local copies, waits for them, and re-layouts: 4.72 us -> 20.6 us
  starting transfers between devices: 12.7 us -> 28.2 us
  waiting for transfers between devices: 99.5 us -> 89.1 us
  Pallas kernels: 113 us -> 123 us
  other arithmetic: 8.57 us -> 13.4 us
    all_gather x2 -> x1, waiting for transfers between devices: 83.2 us -> 0.01 us  [per_device(): all_grads = lax.all_gather(sent, 'dom', axis=0, tiled=True)]
    ppermute x0 -> x31, waiting for transfers between devices: none -> 74.4 us  [the longest x7 37.5 us: gather_feats(): lax.ppermute(lacking(value), 'head', other_head)]
    all_gather x2 -> x0, blocking collectives: 45.5 us -> none  [the longest x1 23.7 us: per_device(): all_ids = lax.all_gather(ids, 'dom', axis=0, tiled=True)]
    ppermute x0 -> x31, starting transfers between devices: none -> 20.9 us  [the longest x7 8.7 us: gather_feats(): lax.ppermute(lacking(value), 'head', other_head)]
    unnamed x18 -> x73, local copies, waits for them, and re-layouts: 1.07 us -> 12.6 us
    pallas_call x1, Pallas kernels: 50 us -> 56.6 us  [attend_forward(): pl.pallas_call(functools.partial(forward_kernel, entries, layout), out_sh...]
    ppermute x10, starting transfers between devices: 9.81 us -> 4.6 us  [from_across(): return lax.ppermute(value, 'dom', [(at, at ^ bit) for at in range(size)])]
    pallas_call x1, Pallas kernels: 63.2 us -> 66.5 us  [attend_backward(): pl.pallas_call(backward_kernel, out_shape=(jax.ShapeDtypeStruct((node_row...]
  transfers between devices with their start and end apart: 14 -> 44, of which waited for: 8 -> 20; matrix products, arithmetic and copies ran while one was open for 4% -> 10% of each run, Pallas kernels for 35% -> 39%
where the time goes in v5:
time: 313 us; the launch traced here: 312 us
  Pallas kernels  123 us (39%)
  waiting for transfers between devices  89.1 us (28%)
  starting transfers between devices  28.2 us (9%)
  blocking collectives  21.1 us (7%)
  local copies, waits for them, and re-layouts  20.6 us (7%)
  between operations  14.6 us (5%)
  other arithmetic  13.4 us (4%)
    pallas_call x1, Pallas kernels, attend_backward(): pl.pallas_call(backward_kernel, out_shape=(jax.ShapeDtypeStruct((node_row...  66.5 us
    pallas_call x1, Pallas kernels, attend_forward(): pl.pallas_call(functools.partial(forward_kernel, entries, layout), out_sh...  56.6 us
    ppermute x7, waiting for transfers between devices, gather_feats(): lax.ppermute(lacking(value), 'head', other_head)  37.5 us
    all_gather x1, blocking collectives, per_device(): all_stats = lax.all_gather(stats, 'dom', axis=0, tiled=True)  21.1 us
    ppermute x1, waiting for transfers between devices, gather_feats(): lax.ppermute(start, 'dom', onward)  16.1 us
    ppermute x10, waiting for transfers between devices, from_across(): return lax.ppermute(value, 'dom', [(at, at ^ bit) for at in range(size)])  14.7 us
    unnamed x73, local copies, waits for them, and re-layouts  12.6 us
    ppermute x2, waiting for transfers between devices, gather_feats(): lax.ppermute(held[0], 'dom', onward)  10 us
  transfers between devices with their start and end apart: 44, of which 20 were waited for; matrix products, arithmetic and copies ran while one was open for 10% of the time, Pallas kernels for 39%

profile of v5, /device:TPU:0, one launch (start us, length us, event | category | flops | bytes accessed | tf_op | source)
XLA Modules:
  0.0 311.9 jit_solution(12558371457002849573)
XLA Ops:
  9.1 0.8 convert_element_type.58
  9.9 1.2 constant_dynamic-slice_fusion.9
  11.2 0.9 maximum_maximum_fusion
  12.1 2.7 collective-permute-start
  14.7 16.1 %collective-permute-done.refs_2_ = f32[672,256]{1,0:T(8,128)S(1)} collective-permute-done((f32[672,256]{1,0:T(8,128)}, f32[672,256]{1,0:T(8,128)S(1)}, u32[]{:S(2)}, u32[]{:S(2)}) %collective-permute-start) | collective-permute-done | bytes 688160 | tf_op jit(solution)/shard_map/ppermute | solution.py:447
  30.9 1.6 collective-permute-done.1.refs_4_
  32.5 1.6 collective-permute-start.5
  34.1 1.6 collective-permute-start.3
  36.6 6.3 %collective-permute-done.5.refs_10_ = f32[384,256]{1,0:T(8,128)S(1)} collective-permute-done((f32[384,256]{1,0:T(8,128)S(1)}, f32[384,256]{1,0:T(8,128)S(1)}, u32[]{:S(2)}, u32[]{:S(2)}) %collective-permute-start.5) | collective-permute-done | bytes 393248 | tf_op jit(solution)/shard_map/ppermute | solution.py:472
  42.9 1.5 collective-permute-start.6
  44.4 7.9 %collective-permute-done.6.refs_12_ = f32[384,256]{1,0:T(8,128)S(1)} collective-permute-done((f32[384,256]{1,0:T(8,128)S(1)}, f32[384,256]{1,0:T(8,128)S(1)}, u32[]{:S(2)}, u32[]{:S(2)}) %collective-permute-start.6) | collective-permute-done | bytes 393248 | tf_op jit(solution)/shard_map/ppermute | solution.py:472
  52.4 1.6 collective-permute-start.11
  54.6 1.0 collective-permute-start.10
  55.8 8.8 %collective-permute-done.11.refs_18_ = f32[384,256]{1,0:T(8,128)} collective-permute-done((f32[384,256]{1,0:T(8,128)S(1)}, f32[384,256]{1,0:T(8,128)}, u32[]{:S(2)}, u32[]{:S(2)}) %collective-permute-start.11) | collective-permute-done | bytes 393248 | tf_op jit(solution)/shard_map/ppermute | solution.py:472
  64.7 4.9 %collective-permute-done.12.refs_20_ = f32[384,256]{1,0:T(8,128)} collective-permute-done((f32[384,256]{1,0:T(8,128)S(1)}, f32[384,256]{1,0:T(8,128)}, u32[]{:S(2)}, u32[]{:S(2)}) %collective-permute-start.12) | collective-permute-done | bytes 393248 | tf_op jit(solution)/shard_map/ppermute | solution.py:472
  69.5 1.6 collective-permute-start.9
  71.1 1.7 collective-permute-done.16.refs_13_
  73.8 0.9 copy-done.17
  74.7 10.0 %collective-permute-done.9.refs_14_ = f32[672,256]{1,0:T(8,128)S(1)} collective-permute-done((f32[672,256]{1,0:T(8,128)S(1)}, f32[672,256]{1,0:T(8,128)S(1)}, u32[]{:S(2)}, u32[]{:S(2)}) %collective-permute-start.9) | collective-permute-done | bytes 688160 | tf_op jit(solution)/shard_map/ppermute | solution.py:463
  84.8 1.9 collective-permute-start.17
  86.7 1.5 collective-permute-start.19
  89.3 0.8 constant_dynamic-slice_fusion.3
  90.0 5.0 %collective-permute-done.18 = f32[288,256]{1,0:T(8,128)S(1)} collective-permute-done((f32[288,256]{1,0:T(8,128)S(1)}, f32[288,256]{1,0:T(8,128)S(1)}, u32[]{:S(2)}, u32[]{:S(2)}) %collective-permute-start.18) | collective-permute-done | bytes 294944 | tf_op jit(solution)/shard_map/ppermute | solution.py:468
  95.5 0.8 collective-permute-done.19.refs_24_
  96.3 0.8 copy-done.24
  97.1 1.8 fusion.34.refs_31_
  98.9 4.2 %collective-permute-done.20.refs_26_ = f32[384,256]{1,0:T(8,128)} collective-permute-done((f32[384,256]{1,0:T(8,128)}, f32[384,256]{1,0:T(8,128)}, u32[]{:S(2)}, u32[]{:S(2)}) %collective-permute-start.20) | collective-permute-done | bytes 393248 | tf_op jit(solution)/shard_map/ppermute | solution.py:472
  103.3 1.2 collective-permute-done.29
  104.5 0.8 constant_dynamic-update-slice_fusion.15
  105.3 0.8 constant_dynamic-update-slice_fusion.14
  106.1 0.8 constant_dynamic-update-slice_fusion.13
  106.8 0.8 constant_dynamic-update-slice_fusion.12
  107.6 0.8 constant_dynamic-update-slice_fusion.11
  108.3 0.8 constant_dynamic-update-slice_fusion.10
  109.1 0.8 constant_dynamic-update-slice_fusion.9
  109.9 0.8 constant_dynamic-update-slice_fusion.8
  111.3 0.8 constant_dynamic-slice_fusion.2
  112.1 1.4 collective-permute-start.28
  113.5 0.8 constant_dynamic-update-slice_fusion.6
  114.3 0.8 constant_dynamic-update-slice_fusion.4
  117.6 1.2 gather_fusion
  119.2 4.6 %collective-permute-done.28.refs_28_ = f32[384,256]{1,0:T(8,128)} collective-permute-done((f32[384,256]{1,0:T(8,128)}, f32[384,256]{1,0:T(8,128)}, u32[]{:S(2)}, u32[]{:S(2)}) %collective-permute-start.28) | collective-permute-done | bytes 393248 | tf_op jit(solution)/shard_map/ppermute | solution.py:472
  124.4 1.3 collective-permute-done.30.refs_29_
  125.7 0.8 copy-done.27
  126.5 56.6 %attend_forward.1 = (f32[16384,256]{1,0:T(8,128)}, f32[1024,256]{1,0:T(8,128)}, f32[1024,256]{1,0:T(8,128)}, f32[8,8,128]{2,1,0:T(8,128)}, f32[256,128]{1,0:T(8,128)}, /*index=5*/f32[128,256]{1,0:T(8,128)}) custom-call(s32[8,8]{1,0:T(8,128)} %get-tuple-element.118.ids, f32[1024,256]{1,0:T(8,128)} %refs_16_.1, f32[1024,256]{1,0:T(8,128)} %collective-permute-done.2.refs_1_, ...), custom_call_target="tpu_custom_call" | custom-call | tf_op jit(solution)/shard_map/attend_forward/pallas_call | solution.py:155
  183.2 1.0 fusion.33
  184.2 1.1 collective-permute-start.33
  185.3 1.0 collective-permute-done.33
  186.3 0.9 select_add_fusion.1
  187.7 1.9 constant_dynamic-slice_fusion
  189.6 1.4 collective-permute-start.31
  191.0 1.2 collective-permute-done.34
  192.2 1.6 collective-permute-start.35
  193.9 21.1 %all_gather.7.refs_8_.refs_9_.refs_10_.refs_11_ = f32[128,8,128]{2,1,0:T(8,128)S(1)} all-gather(f32[8,8,128]{2,1,0:T(8,128)} %get-tuple-element.108), channel_id=1, replica_groups=mesh['dom'=16,'head'=2] {'dom'}, dimensions={0}, use_global_device_ids=true | all-gather | bytes 557056 | tf_op jit(solution)/shard_map/all_gather | solution.py:543
  215.7 66.5 %attend_backward.1 = (f32[1024,256]{1,0:T(8,128)S(1)}, f32[256,128]{1,0:T(8,128)S(1)}, f32[256,128]{1,0:T(8,128)S(1)}) custom-call(s32[2,24]{1,0:T(2,128)S(1)} %pad_add_fusion.2.steps_ref, s32[4,96]{1,0:T(4,128)S(1)} %pad_add_fusion.1.readers_ref, f32[16384,256]{1,0:T(8,128)} %get-tuple-element.106.refs_0_.refs_1_.refs_2_.refs_3_, ...), custom_call_target="tpu_custom_call" | custom-call | tf_op jit(solution)/shard_map/attend_backward/pallas_call | solution.py:297
  283.0 1.0 add.410
  284.5 0.9 select_add_fusion
  285.5 2.1 dynamic-slice_add_fusion.1
  287.6 1.3 collective-permute-start.32
  288.9 2.0 collective-permute-done.39
  291.7 4.3 %collective-permute-done.40 = f32[256,128]{1,0:T(8,128)S(1)} collective-permute-done((f32[256,128]{1,0:T(8,128)S(1)}, f32[256,128]{1,0:T(8,128)S(1)}, u32[]{:S(2)}, u32[]{:S(2)}) %collective-permute-start.40) | collective-permute-done | bytes 131104 | tf_op jit(solution)/shard_map/ppermute | solution.py:382
  297.2 5.7 %collective-permute-done.41 = f32[256,128]{1,0:T(8,128)S(1)} collective-permute-done((f32[256,128]{1,0:T(8,128)S(1)}, f32[256,128]{1,0:T(8,128)S(1)}, u32[]{:S(2)}, u32[]{:S(2)}) %collective-permute-start.41) | collective-permute-done | bytes 131104 | tf_op jit(solution)/shard_map/ppermute | solution.py:382
  303.0 0.9 dynamic-slice_add_fusion
  304.4 0.7 broadcast_select_fusion.1
  (169 shorter events, 15.9 us)
Async XLA Ops:
  7.2 208.5 %all-gather.2.cloned.1.call-start = ((), (), s32[]{:S(2)}) async-start(), calls=%async_computation | async-start | bytes 8912896 | tf_op jit(solution)/shard_map/all_gather | solution.py:533
  7.2 25.2 %collective-permute-start.2 = (f32[1024,256]{1,0:T(8,128)}, f32[1024,256]{1,0:T(8,128)}, u32[]{:S(2)}, u32[]{:S(2)}) collective-permute-start(f32[1024,256]{1,0:T(8,128)} %refs_16_.1), channel_id=1, source_target_pairs={{0,2},{2,0},{4,6},{6,4},{8,10},{10,8},{12,14},{14,12},{16,18},{18,... | collective-permute-start | bytes 3145736 | tf_op jit(solution)/shard_map/ppermute | solution.py:427
  9.9 87.2 %copy-start.6 = (f32[1024,256]{1,0:T(8,128)S(1)}, f32[1024,256]{1,0:T(8,128)}, u32[]{:S(2)}) copy-start(f32[1024,256]{1,0:T(8,128)} %refs_30_.1) | copy-start | bytes 3145732
  9.9 87.2 %copy-start.19 = (f32[128,256]{1,0:T(8,128)S(1)}, f32[128,256]{1,0:T(8,128)}, u32[]{:S(2)}) copy-start(f32[128,256]{1,0:T(8,128)} %refs_36_.1) | copy-start | bytes 393220
  12.1 18.8 %collective-permute-start = (f32[672,256]{1,0:T(8,128)}, f32[672,256]{1,0:T(8,128)S(1)}, u32[]{:S(2)}, u32[]{:S(2)}) collective-permute-start(f32[672,256]{1,0:T(8,128)} %maximum_maximum_fusion), channel_id=1, source_target_pairs={{0,8},{2,10},{8,16},{10,18},{16,24},{18,26},{24,28},{26,30},{28,20... | collective-permute-start | bytes 2064392 | tf_op jit(solution)/shard_map/ppermute | solution.py:447
  14.7 17.7 %collective-permute-start.1 = (f32[672,256]{1,0:T(8,128)}, f32[672,256]{1,0:T(8,128)S(1)}, u32[]{:S(2)}, u32[]{:S(2)}) collective-permute-start(f32[672,256]{1,0:T(8,128)} %maximum_maximum_fusion), channel_id=1, source_target_pairs={{8,0},{10,2},{16,8},{18,10},{24,16},{26,18},{28,24},{30,26},{20,28... | collective-permute-start | bytes 2064392 | tf_op jit(solution)/shard_map/ppermute | solution.py:447
  30.9 33.8 %copy-start.10 = (f32[672,256]{1,0:T(8,128)}, f32[672,256]{1,0:T(8,128)S(1)}, u32[]{:S(2)}) copy-start(f32[672,256]{1,0:T(8,128)S(1)} %collective-permute-done.refs_2_) | copy-start | bytes 2064388
  32.4 22.2 %copy-start.11 = (f32[672,256]{1,0:T(8,128)}, f32[672,256]{1,0:T(8,128)S(1)}, u32[]{:S(2)}) copy-start(f32[672,256]{1,0:T(8,128)S(1)} %collective-permute-done.1.refs_4_) | copy-start | bytes 2064388
  32.5 10.4 %collective-permute-start.5 = (f32[384,256]{1,0:T(8,128)S(1)}, f32[384,256]{1,0:T(8,128)S(1)}, u32[]{:S(2)}, u32[]{:S(2)}) collective-permute-start(f32[384,256]{1,0:T(8,128)S(1)} %constant_dynamic-slice_fusion.8), channel_id=1, source_target_pairs={{0,1},{1,0},{2,3},{3,2},{4,5},{5,4},{6,7},{7,6},{8,9},{9,8},{10,11... | collective-permute-start | bytes 1179656 | tf_op jit(solution)/shard_map/ppermute | solution.py:472
  34.1 18.3 %collective-permute-start.3 = (f32[672,256]{1,0:T(8,128)S(1)}, f32[672,256]{1,0:T(8,128)S(1)}, u32[]{:S(2)}, u32[]{:S(2)}) collective-permute-start(f32[672,256]{1,0:T(8,128)S(1)} %collective-permute-done.refs_2_), channel_id=1, source_target_pairs={{0,8},{2,10},{8,16},{10,18},{16,24},{18,26},{24,28},{26,30},{28,20... | collective-permute-start | bytes 2064392 | tf_op jit(solution)/shard_map/ppermute | solution.py:463
  35.6 16.7 %collective-permute-start.4 = (f32[672,256]{1,0:T(8,128)S(1)}, f32[672,256]{1,0:T(8,128)S(1)}, u32[]{:S(2)}, u32[]{:S(2)}) collective-permute-start(f32[672,256]{1,0:T(8,128)S(1)} %collective-permute-done.1.refs_4_), channel_id=1, source_target_pairs={{8,0},{10,2},{16,8},{18,10},{24,16},{26,18},{28,24},{30,26},{20,28... | collective-permute-start | bytes 2064392 | tf_op jit(solution)/shard_map/ppermute | solution.py:463
  36.1 16.3 %collective-permute-start.7 = (f32[672,256]{1,0:T(8,128)S(1)}, f32[672,256]{1,0:T(8,128)S(1)}, u32[]{:S(2)}, u32[]{:S(2)}) collective-permute-start(f32[672,256]{1,0:T(8,128)S(1)} %collective-permute-done.refs_2_), channel_id=1, source_target_pairs={{0,2},{2,0},{4,6},{6,4},{8,10},{10,8},{12,14},{14,12},{16,18},{18,... | collective-permute-start | bytes 2064392 | tf_op jit(solution)/shard_map/ppermute | solution.py:427
  36.1 16.3 %collective-permute-start.8 = (f32[672,256]{1,0:T(8,128)S(1)}, f32[672,256]{1,0:T(8,128)S(1)}, u32[]{:S(2)}, u32[]{:S(2)}) collective-permute-start(f32[672,256]{1,0:T(8,128)S(1)} %collective-permute-done.1.refs_4_), channel_id=1, source_target_pairs={{0,2},{2,0},{4,6},{6,4},{8,10},{10,8},{12,14},{14,12},{16,18},{18,... | collective-permute-start | bytes 2064392 | tf_op jit(solution)/shard_map/ppermute | solution.py:427
  42.9 53.5 %copy-start.20 = (f32[384,256]{1,0:T(8,128)}, f32[384,256]{1,0:T(8,128)S(1)}, u32[]{:S(2)}) copy-start(f32[384,256]{1,0:T(8,128)S(1)} %collective-permute-done.5.refs_10_) | copy-start | bytes 1179652
  42.9 9.4 %collective-permute-start.6 = (f32[384,256]{1,0:T(8,128)S(1)}, f32[384,256]{1,0:T(8,128)S(1)}, u32[]{:S(2)}, u32[]{:S(2)}) collective-permute-start(f32[384,256]{1,0:T(8,128)S(1)} %constant_dynamic-slice_fusion.7), channel_id=1, source_target_pairs={{0,1},{1,0},{2,3},{3,2},{4,5},{5,4},{6,7},{7,6},{8,9},{9,8},{10,11... | collective-permute-start | bytes 1179656 | tf_op jit(solution)/shard_map/ppermute | solution.py:472
  52.3 44.0 %copy-start.21 = (f32[384,256]{1,0:T(8,128)}, f32[384,256]{1,0:T(8,128)S(1)}, u32[]{:S(2)}) copy-start(f32[384,256]{1,0:T(8,128)S(1)} %collective-permute-done.6.refs_12_) | copy-start | bytes 1179652
  52.3 20.5 %copy-start.12 = (f32[672,256]{1,0:T(8,128)}, f32[672,256]{1,0:T(8,128)S(1)}, u32[]{:S(2)}) copy-start(f32[672,256]{1,0:T(8,128)S(1)} %collective-permute-done.3.refs_6_) | copy-start | bytes 2064388
  52.3 20.5 %copy-start.13 = (f32[672,256]{1,0:T(8,128)}, f32[672,256]{1,0:T(8,128)S(1)}, u32[]{:S(2)}) copy-start(f32[672,256]{1,0:T(8,128)S(1)} %collective-permute-done.4.refs_8_) | copy-start | bytes 2064388
  52.3 20.5 %copy-start.14 = (f32[672,256]{1,0:T(8,128)}, f32[672,256]{1,0:T(8,128)S(1)}, u32[]{:S(2)}) copy-start(f32[672,256]{1,0:T(8,128)S(1)} %collective-permute-done.7.refs_3_) | copy-start | bytes 2064388
  52.4 36.4 %copy-start.15 = (f32[672,256]{1,0:T(8,128)}, f32[672,256]{1,0:T(8,128)S(1)}, u32[]{:S(2)}) copy-start(f32[672,256]{1,0:T(8,128)S(1)} %collective-permute-done.8.refs_5_) | copy-start | bytes 2064388
  52.4 12.2 %collective-permute-start.11 = (f32[384,256]{1,0:T(8,128)S(1)}, f32[384,256]{1,0:T(8,128)}, u32[]{:S(2)}, u32[]{:S(2)}) collective-permute-start(f32[384,256]{1,0:T(8,128)S(1)} %constant_dynamic-slice_fusion.6), channel_id=1, source_target_pairs={{0,1},{1,0},{2,3},{3,2},{4,5},{5,4},{6,7},{7,6},{8,9},{9,8},{10,11... | collective-permute-start | bytes 1179656 | tf_op jit(solution)/shard_map/ppermute | solution.py:472
  54.0 15.5 %collective-permute-start.12 = (f32[384,256]{1,0:T(8,128)S(1)}, f32[384,256]{1,0:T(8,128)}, u32[]{:S(2)}, u32[]{:S(2)}) collective-permute-start(f32[384,256]{1,0:T(8,128)S(1)} %constant_dynamic-slice_fusion.5), channel_id=1, source_target_pairs={{0,1},{1,0},{2,3},{3,2},{4,5},{5,4},{6,7},{7,6},{8,9},{9,8},{10,11... | collective-permute-start | bytes 1179656 | tf_op jit(solution)/shard_map/ppermute | solution.py:472
  54.6 16.5 %collective-permute-start.15 = (f32[384,256]{1,0:T(8,128)S(1)}, f32[384,256]{1,0:T(8,128)S(1)}, u32[]{:S(2)}, u32[]{:S(2)}) collective-permute-start(f32[384,256]{1,0:T(8,128)S(1)} %collective-permute-done.5.refs_10_), channel_id=1, source_target_pairs={{0,2},{2,0},{4,6},{6,4},{8,10},{10,8},{12,14},{14,12},{16,18},{18,... | collective-permute-start | bytes 1179656 | tf_op jit(solution)/shard_map/ppermute | solution.py:427
  54.6 18.2 %collective-permute-start.10 = (f32[672,256]{1,0:T(8,128)S(1)}, f32[672,256]{1,0:T(8,128)S(1)}, u32[]{:S(2)}, u32[]{:S(2)}) collective-permute-start(f32[672,256]{1,0:T(8,128)S(1)} %collective-permute-done.4.refs_8_), channel_id=1, source_target_pairs={{8,0},{10,2},{16,8},{18,10},{24,16},{26,18},{28,24},{30,26},{20,28... | collective-permute-start | bytes 2064392 | tf_op jit(solution)/shard_map/ppermute | solution.py:463
  55.6 17.2 %collective-permute-start.13 = (f32[672,256]{1,0:T(8,128)S(1)}, f32[672,256]{1,0:T(8,128)S(1)}, u32[]{:S(2)}, u32[]{:S(2)}) collective-permute-start(f32[672,256]{1,0:T(8,128)S(1)} %collective-permute-done.3.refs_6_), channel_id=1, source_target_pairs={{0,2},{2,0},{4,6},{6,4},{8,10},{10,8},{12,14},{14,12},{16,18},{18,... | collective-permute-start | bytes 2064392 | tf_op jit(solution)/shard_map/ppermute | solution.py:427
  64.6 8.2 %collective-permute-start.14 = (f32[672,256]{1,0:T(8,128)S(1)}, f32[672,256]{1,0:T(8,128)S(1)}, u32[]{:S(2)}, u32[]{:S(2)}) collective-permute-start(f32[672,256]{1,0:T(8,128)S(1)} %collective-permute-done.4.refs_8_), channel_id=1, source_target_pairs={{0,2},{2,0},{4,6},{6,4},{8,10},{10,8},{12,14},{14,12},{16,18},{18,... | collective-permute-start | bytes 2064392 | tf_op jit(solution)/shard_map/ppermute | solution.py:427
  69.5 15.2 %collective-permute-start.9 = (f32[672,256]{1,0:T(8,128)S(1)}, f32[672,256]{1,0:T(8,128)S(1)}, u32[]{:S(2)}, u32[]{:S(2)}) collective-permute-start(f32[672,256]{1,0:T(8,128)S(1)} %collective-permute-done.3.refs_6_), channel_id=1, source_target_pairs={{0,8},{2,10},{8,16},{10,18},{16,24},{18,26},{24,28},{26,30},{28,20... | collective-permute-start | bytes 2064392 | tf_op jit(solution)/shard_map/ppermute | solution.py:463
  71.1 1.8 copy-start.22
  71.1 1.7 collective-permute-start.16
  72.8 43.1 %copy-start.9 = (f32[672,256]{1,0:T(8,128)}, f32[672,256]{1,0:T(8,128)S(1)}, u32[]{:S(2)}) copy-start(f32[672,256]{1,0:T(8,128)S(1)} %collective-permute-done.10.refs_16_) | copy-start | bytes 2064388
  84.8 31.2 %copy-start.7 = (f32[672,256]{1,0:T(8,128)}, f32[672,256]{1,0:T(8,128)S(1)}, u32[]{:S(2)}) copy-start(f32[672,256]{1,0:T(8,128)S(1)} %collective-permute-done.9.refs_14_) | copy-start | bytes 2064388
  84.8 10.7 %collective-permute-start.17 = (f32[384,256]{1,0:T(8,128)S(1)}, f32[384,256]{1,0:T(8,128)S(1)}, u32[]{:S(2)}, u32[]{:S(2)}) collective-permute-start(f32[384,256]{1,0:T(8,128)S(1)} %get-tuple-element.121), channel_id=1, source_target_pairs={{0,8},{2,10},{8,16},{10,18},{16,24},{18,26},{24,28},{26,30},{28,20... | collective-permute-start | bytes 1179656 | tf_op jit(solution)/shard_map/ppermute | solution.py:467
  86.7 9.6 %collective-permute-start.19 = (f32[384,256]{1,0:T(8,128)S(1)}, f32[384,256]{1,0:T(8,128)S(1)}, u32[]{:S(2)}, u32[]{:S(2)}) collective-permute-start(f32[384,256]{1,0:T(8,128)S(1)} %get-tuple-element.120), channel_id=1, source_target_pairs={{0,1},{1,0},{2,3},{3,2},{4,5},{5,4},{6,7},{7,6},{8,9},{9,8},{10,11... | collective-permute-start | bytes 1179656 | tf_op jit(solution)/shard_map/ppermute | solution.py:472
  88.2 6.8 %collective-permute-start.18 = (f32[288,256]{1,0:T(8,128)S(1)}, f32[288,256]{1,0:T(8,128)S(1)}, u32[]{:S(2)}, u32[]{:S(2)}) collective-permute-start(f32[288,256]{1,0:T(8,128)S(1)} %slice.89), channel_id=1, source_target_pairs={{8,0},{10,2},{16,8},{18,10},{24,16},{26,18},{28,24},{30,26},{20,28... | collective-permute-start | bytes 884744 | tf_op jit(solution)/shard_map/ppermute | solution.py:468
  88.7 14.4 %collective-permute-start.21 = (f32[672,256]{1,0:T(8,128)S(1)}, f32[672,256]{1,0:T(8,128)}, u32[]{:S(2)}, u32[]{:S(2)}) collective-permute-start(f32[672,256]{1,0:T(8,128)S(1)} %collective-permute-done.9.refs_14_), channel_id=1, source_target_pairs={{0,2},{2,0},{4,6},{6,4},{8,10},{10,8},{12,14},{14,12},{16,18},{18,... | collective-permute-start | bytes 2064392 | tf_op jit(solution)/shard_map/ppermute | solution.py:427
  88.8 14.4 %collective-permute-start.22 = (f32[672,256]{1,0:T(8,128)S(1)}, f32[672,256]{1,0:T(8,128)}, u32[]{:S(2)}, u32[]{:S(2)}) collective-permute-start(f32[672,256]{1,0:T(8,128)S(1)} %collective-permute-done.10.refs_16_), channel_id=1, source_target_pairs={{0,2},{2,0},{4,6},{6,4},{8,10},{10,8},{12,14},{14,12},{16,18},{18,... | collective-permute-start | bytes 2064392 | tf_op jit(solution)/shard_map/ppermute | solution.py:427
  90.0 33.8 %copy-start.28 = (s32[8,7,128]{2,0,1:T(8,128)S(1)}, s32[8,7,128]{2,0,1:T(8,128)}, u32[]{:S(2)}) copy-start(s32[8,7,128]{2,0,1:T(8,128)} %param.16) | copy-start | bytes 86020
  95.0 8.1 %collective-permute-start.20 = (f32[384,256]{1,0:T(8,128)}, f32[384,256]{1,0:T(8,128)}, u32[]{:S(2)}, u32[]{:S(2)}) collective-permute-start(f32[384,256]{1,0:T(8,128)} %constant_dynamic-slice_fusion.3), channel_id=1, source_target_pairs={{0,1},{1,0},{2,3},{3,2},{4,5},{5,4},{6,7},{7,6},{8,9},{9,8},{10,11... | collective-permute-start | bytes 1179656 | tf_op jit(solution)/shard_map/ppermute | solution.py:472
  95.5 7.6 %collective-permute-start.23 = (f32[384,256]{1,0:T(8,128)}, f32[384,256]{1,0:T(8,128)}, u32[]{:S(2)}, u32[]{:S(2)}) collective-permute-start(f32[384,256]{1,0:T(8,128)} %collective-permute-done.11.refs_18_), channel_id=1, source_target_pairs={{0,2},{2,0},{4,6},{6,4},{8,10},{10,8},{12,14},{14,12},{16,18},{18,... | collective-permute-start | bytes 1179656 | tf_op jit(solution)/shard_map/ppermute | solution.py:427
  96.3 6.8 %collective-permute-start.24 = (f32[384,256]{1,0:T(8,128)}, f32[384,256]{1,0:T(8,128)}, u32[]{:S(2)}, u32[]{:S(2)}) collective-permute-start(f32[384,256]{1,0:T(8,128)} %collective-permute-done.12.refs_20_), channel_id=1, source_target_pairs={{0,2},{2,0},{4,6},{6,4},{8,10},{10,8},{12,14},{14,12},{16,18},{18,... | collective-permute-start | bytes 1179656 | tf_op jit(solution)/shard_map/ppermute | solution.py:427
  103.2 22.5 %copy-start.8 = (f32[672,256]{1,0:T(8,128)}, f32[672,256]{1,0:T(8,128)S(1)}, u32[]{:S(2)}) copy-start(f32[672,256]{1,0:T(8,128)S(1)} %constant_dynamic-update-slice_fusion.refs_22_) | copy-start | bytes 2064388
  103.2 1.3 collective-permute-start.29
  110.6 4.4 %collective-permute-start.25 = (f32[672,256]{1,0:T(8,128)S(1)}, f32[672,256]{1,0:T(8,128)S(1)}, u32[]{:S(2)}, u32[]{:S(2)}) collective-permute-start(f32[672,256]{1,0:T(8,128)S(1)} %constant_dynamic-update-slice_fusion.refs_22_), channel_id=1, source_target_pairs={{0,2},{2,0},{4,6},{6,4},{8,10},{10,8},{12,14},{14,12},{16,18},{18,... | collective-permute-start | bytes 2064392 | tf_op jit(solution)/shard_map/ppermute | solution.py:427
  110.8 4.3 %collective-permute-start.26 = (f32[384,256]{1,0:T(8,128)}, f32[384,256]{1,0:T(8,128)S(1)}, u32[]{:S(2)}, u32[]{:S(2)}) collective-permute-start(f32[384,256]{1,0:T(8,128)} %copy-done.24), channel_id=1, source_target_pairs={{0,2},{2,0},{4,6},{6,4},{8,10},{10,8},{12,14},{14,12},{16,18},{18,... | collective-permute-start | bytes 1179656 | tf_op jit(solution)/shard_map/ppermute | solution.py:427
  111.1 3.9 %collective-permute-start.27 = (f32[384,256]{1,0:T(8,128)}, f32[384,256]{1,0:T(8,128)S(1)}, u32[]{:S(2)}, u32[]{:S(2)}) collective-permute-start(f32[384,256]{1,0:T(8,128)} %collective-permute-done.20.refs_26_), channel_id=1, source_target_pairs={{0,2},{2,0},{4,6},{6,4},{8,10},{10,8},{12,14},{14,12},{16,18},{18,... | collective-permute-start | bytes 1179656 | tf_op jit(solution)/shard_map/ppermute | solution.py:427
  112.1 11.7 %collective-permute-start.28 = (f32[384,256]{1,0:T(8,128)}, f32[384,256]{1,0:T(8,128)}, u32[]{:S(2)}, u32[]{:S(2)}) collective-permute-start(f32[384,256]{1,0:T(8,128)} %constant_dynamic-slice_fusion.2), channel_id=1, source_target_pairs={{0,1},{1,0},{2,3},{3,2},{4,5},{5,4},{6,7},{7,6},{8,9},{9,8},{10,11... | collective-permute-start | bytes 1179656 | tf_op jit(solution)/shard_map/ppermute | solution.py:472
  115.1 10.7 %copy-start.18 = (f32[672,256]{1,0:T(8,128)}, f32[672,256]{1,0:T(8,128)S(1)}, u32[]{:S(2)}) copy-start(f32[672,256]{1,0:T(8,128)S(1)} %collective-permute-done.25.refs_23_) | copy-start | bytes 2064388
  123.8 1.9 collective-permute-start.30
  126.5 89.1 %copy-start.1 = (f32[256,128]{1,0:T(8,128)S(1)}, f32[256,128]{1,0:T(8,128)}, u32[]{:S(2)}) copy-start(f32[256,128]{1,0:T(8,128)} %refs_18_.1) | copy-start | bytes 393220
  126.5 89.2 %copy-start.2 = (f32[256,128]{1,0:T(8,128)S(1)}, f32[256,128]{1,0:T(8,128)}, u32[]{:S(2)}) copy-start(f32[256,128]{1,0:T(8,128)} %refs_19_.1) | copy-start | bytes 393220
  126.5 89.2 %copy-start.3 = (f32[256,128]{1,0:T(8,128)S(1)}, f32[256,128]{1,0:T(8,128)}, u32[]{:S(2)}) copy-start(f32[256,128]{1,0:T(8,128)} %refs_20_.1) | copy-start | bytes 393220
  183.1 32.5 %copy-start = (f32[1024,256]{1,0:T(8,128)S(1)}, f32[1024,256]{1,0:T(8,128)}, u32[]{:S(2)}) copy-start(f32[1024,256]{1,0:T(8,128)} %refs_16_.1) | copy-start | bytes 3145732
  184.2 2.1 collective-permute-start.33
  187.2 5.0 %collective-permute-start.34 = (f32[256,128]{1,0:T(8,128)S(1)}, f32[256,128]{1,0:T(8,128)S(1)}, u32[]{:S(2)}, u32[]{:S(2)}) collective-permute-start(f32[256,128]{1,0:T(8,128)S(1)} %select_add_fusion.1), channel_id=1, source_target_pairs={{0,4},{2,6},{4,0},{6,2},{8,12},{10,14},{12,8},{14,10},{16,20},{18,... | collective-permute-start | bytes 393224 | tf_op jit(solution)/shard_map/ppermute | solution.py:382
  189.6 96.0 %collective-permute-start.31 = (f32[1024,128]{1,0:T(8,128)}, f32[1024,128]{1,0:T(8,128)}, u32[]{:S(2)}, u32[]{:S(2)}) collective-permute-start(f32[1024,128]{1,0:T(8,128)} %constant_dynamic-slice_fusion), channel_id=1, source_target_pairs={{0,1},{1,0},{2,3},{3,2},{4,5},{5,4},{6,7},{7,6},{8,9},{9,8},{10,11... | collective-permute-start | bytes 1572872 | tf_op jit(solution)/shard_map/ppermute | solution.py:374
  192.2 22.7 %collective-permute-start.35 = (f32[256,128]{1,0:T(8,128)S(1)}, f32[256,128]{1,0:T(8,128)S(1)}, u32[]{:S(2)}, u32[]{:S(2)}) collective-permute-start(f32[256,128]{1,0:T(8,128)S(1)} %add.408), channel_id=1, source_target_pairs={{0,8},{2,10},{4,12},{6,14},{8,0},{10,2},{12,4},{14,6},{16,24},{18,... | collective-permute-start | bytes 393224 | tf_op jit(solution)/shard_map/ppermute | solution.py:382
  215.7 67.3 %collective-permute-start.36 = (f32[256,128]{1,0:T(8,128)}, f32[256,128]{1,0:T(8,128)}, u32[]{:S(2)}, u32[]{:S(2)}) collective-permute-start(f32[256,128]{1,0:T(8,128)} %add.409), channel_id=1, source_target_pairs={{0,16},{2,18},{4,20},{6,22},{8,24},{10,26},{12,28},{14,30},{16,0},... | collective-permute-start | bytes 393224 | tf_op jit(solution)/shard_map/ppermute | solution.py:382
  282.9 1.6 collective-permute-start.38
  284.0 7.1 %collective-permute-start.37 = (f32[256,128]{1,0:T(8,128)S(1)}, f32[256,128]{1,0:T(8,128)S(1)}, u32[]{:S(2)}, u32[]{:S(2)}) collective-permute-start(f32[256,128]{1,0:T(8,128)S(1)} %add.410), channel_id=1, source_target_pairs={{0,2},{2,0},{4,6},{6,4},{8,10},{10,8},{12,14},{14,12},{16,18},{18,... | collective-permute-start | bytes 393224 | tf_op jit(solution)/shard_map/ppermute | solution.py:382
  285.4 5.5 %collective-permute-start.39 = (f32[256,128]{1,0:T(8,128)S(1)}, f32[256,128]{1,0:T(8,128)S(1)}, u32[]{:S(2)}, u32[]{:S(2)}) collective-permute-start(f32[256,128]{1,0:T(8,128)S(1)} %select_add_fusion), channel_id=1, source_target_pairs={{0,4},{2,6},{4,0},{6,2},{8,12},{10,14},{12,8},{14,10},{16,20},{18,... | collective-permute-start | bytes 393224 | tf_op jit(solution)/shard_map/ppermute | solution.py:382
  287.6 15.4 %collective-permute-start.32 = (f32[1024,128]{1,0:T(8,128)S(1)}, f32[1024,128]{1,0:T(8,128)S(1)}, u32[]{:S(2)}, u32[]{:S(2)}) collective-permute-start(f32[1024,128]{1,0:T(8,128)S(1)} %constant_dynamic-slice_fusion.1), channel_id=1, source_target_pairs={{0,1},{1,0},{2,3},{3,2},{4,5},{5,4},{6,7},{7,6},{8,9},{9,8},{10,11... | collective-permute-start | bytes 1572872 | tf_op jit(solution)/shard_map/ppermute | solution.py:374
  291.0 5.0 %collective-permute-start.40 = (f32[256,128]{1,0:T(8,128)S(1)}, f32[256,128]{1,0:T(8,128)S(1)}, u32[]{:S(2)}, u32[]{:S(2)}) collective-permute-start(f32[256,128]{1,0:T(8,128)S(1)} %add.412), channel_id=1, source_target_pairs={{0,8},{2,10},{4,12},{6,14},{8,0},{10,2},{12,4},{14,6},{16,24},{18,... | collective-permute-start | bytes 393224 | tf_op jit(solution)/shard_map/ppermute | solution.py:382
  296.0 6.9 %collective-permute-start.41 = (f32[256,128]{1,0:T(8,128)S(1)}, f32[256,128]{1,0:T(8,128)S(1)}, u32[]{:S(2)}, u32[]{:S(2)}) collective-permute-start(f32[256,128]{1,0:T(8,128)S(1)} %add.413), channel_id=1, source_target_pairs={{0,16},{2,18},{4,20},{6,22},{8,24},{10,26},{12,28},{14,30},{16,0},... | collective-permute-start | bytes 393224 | tf_op jit(solution)/shard_map/ppermute | solution.py:382
  303.0 1.4 collective-permute-start.42
  (9 other events, 7.2 us)
Sparse Core Ops, SparseCore 0:
  103.4 74.4 all-gather.1

commit v6 on v5

--- a/solution.py
+++ b/solution.py
@@ -45,22 +45,22 @@
     return value[:, :half] + value[:, half:]
 
 
-def forward_kernel(entries, layout, ids, *refs):
-    sources = refs[:len(layout)]
+def forward_kernel(entries, layout, source_count, ids, *refs):
+    sources = refs[:source_count]
     (cot_ref, grad_ref, bias_ref, wq_ref, wk_ref, wv_ref, wo_ref,
      all_ref, out_ref, feat_ref, stat_ref, gq_ref, go_ref,
-     feats, sems, all_sem) = refs[len(layout):]
-    rows = cot_ref.shape[0]
+     feats, mixed_mem, grad_mem, sems, all_sem) = refs[source_count:]
+    rows = grad_ref.shape[0]
     step = pl.program_id(0)
     keep = pltpu.make_async_copy(feats, all_ref, all_sem)
 
     @pl.when(step == 0)
     def _():
         copies = []
-        for at, (count, block) in enumerate(layout):
+        for at, (source, row, count, block) in enumerate(layout):
             copies.append(
                 pltpu.make_async_copy(
-                    sources[at].at[pl.ds(0, count), :],
+                    sources[source].at[pl.ds(row, count), :],
                     feats.at[pl.ds(block * rows, count), :],
                     sems.at[at],
                 )
@@ -83,55 +83,62 @@
     pairs = mul3(inputs, split(wide(wk_ref[...], wv_ref[...])))
     key_high, key_low = split(pairs[:, :cols])
     value_high, value_low = split(pairs[:, cols:])
-    key_twice, key_both = wide(key_high, key_high), wide(key_high, key_low)
-    value_twice, value_both = wide(value_high, value_high), wide(value_high, value_low)
+    key_both, value_both = wide(key_high, key_low), wide(value_high, value_low)
+    turned_high, turned_low = split(jnp.transpose(pairs))
+    turned_keys = jnp.concatenate([turned_high[:cols], turned_high[:cols]], axis=0)
+    turned_values = jnp.concatenate([turned_high[cols:], turned_high[cols:]], axis=0)
     own = (inputs[0][:rows], inputs[1][:rows])
     query = mul3(own, w_query) * SCALE
-    cot = split(cot_ref[...])
     grad_mixed = grad_ref[...]
-    bias = bias_ref[0]
     lane = lax.broadcasted_iota(jnp.int32, (rows, cols), 1) // HEAD_SIZE
+    here = [lane == head for head in range(heads)]
+
+    def spread(value):
+        return jnp.concatenate([jnp.where(mask, value, 0.0) for mask in here], axis=0)
+
+    def gather(value):
+        parts = [
+            jnp.where(mask, value[head * rows:(head + 1) * rows], 0.0)
+            for head, mask in enumerate(here)
+        ]
+        return sum(parts[1:], parts[0])
+
+    q_high, q_low = split(spread(query))
+    scores = mul(wide(q_high, q_low), turned_keys) + mul(q_high, turned_low[:cols]) + bias_ref[0]
+    top = jnp.max(scores, axis=1, keepdims=True)
+    probs = jnp.exp(scores - top)
+    total = jnp.sum(probs, axis=1, keepdims=True)
+    inverse = 1.0 / total
+    p_high, p_low = split(probs)
+    weighted = (fold(mul(p_high, value_both)) + mul(p_low, value_high)) * inverse
+    mixed = gather(weighted)
+    grad_part = spread(grad_mixed)
+    delta = jnp.sum(grad_part * weighted, axis=1, keepdims=True)
+    g_high, g_low = split(grad_part)
+    grad_probs = mul(wide(g_high, g_low), turned_values) + mul(g_high, turned_low[cols:])
+    s_high, s_low = split(probs * (grad_probs - delta))
+    back = (fold(mul(s_high, key_both)) + mul(s_low, key_high)) * (inverse * SCALE)
+    grad_query = gather(back)
+    log_total = top + jnp.log(total)
     stat_lane = lax.broadcasted_iota(jnp.int32, (rows, rows), 1)
-    mixed = jnp.zeros((rows, cols), F32)
-    grad_query = jnp.zeros((rows, cols), F32)
     stats = jnp.zeros((rows, rows), F32)
     for head in range(heads):
-        here = lane == head
-        q_high, q_low = split(jnp.where(here, query, 0.0))
-        scores = mul(wide(q_high, q_low), key_twice, 1, 1) + mul(q_high, key_low, 1, 1) + bias
-        top = jnp.max(scores, axis=1, keepdims=True)
-        probs = jnp.exp(scores - top)
-        total = jnp.sum(probs, axis=1, keepdims=True)
-        p_high, p_low = split(probs)
-        weighted = fold(mul(p_high, value_both)) + mul(p_low, value_high)
-        inverse = 1.0 / total
-        part = jnp.where(here, weighted * inverse, 0.0)
-        mixed = mixed + part
-        grad_part = jnp.where(here, grad_mixed, 0.0)
-        delta = jnp.sum(grad_part * part, axis=1, keepdims=True)
-        g_high, g_low = split(grad_part)
-        grad_probs = mul(wide(g_high, g_low), value_twice, 1, 1) + mul(g_high, value_low, 1, 1)
-        s_high, s_low = split(probs * (grad_probs - delta))
-        back = fold(mul(s_high, key_both)) + mul(s_low, key_high)
-        grad_query = grad_query + jnp.where(here, back * (inverse * SCALE), 0.0)
-        stats = jnp.where(stat_lane == head, top + jnp.log(total), stats)
-        stats = jnp.where(stat_lane == heads + head, delta, stats)
-    mixed = split(mixed)
-    grad_query = split(grad_query)
-    out_ref[...] = mul3(mixed, w_out)
-    feat_ref[...] = mul3(grad_query, w_query, 1, 1)
+        at = slice(head * rows, (head + 1) * rows)
+        stats = jnp.where(stat_lane == head, log_total[at], stats)
+        stats = jnp.where(stat_lane == heads + head, delta[at], stats)
+    block = pl.ds(pl.multiple_of(step * rows, rows), rows)
+    mixed_mem[block, :] = mixed
+    grad_mem[block, :] = grad_query
     stat_ref[0] = jnp.transpose(stats)[: 2 * heads]
-
-    @pl.when(pl.program_id(0) == 0)
-    def _():
-        gq_ref[...] = jnp.zeros_like(gq_ref)
-        go_ref[...] = jnp.zeros_like(go_ref)
-
-    gq_ref[...] += mul3(own, grad_query, 0, 0)
-    go_ref[...] += mul3(mixed, cot, 0, 0)
 
     @pl.when(step == pl.num_programs(0) - 1)
     def _():
+        mixed, grad_query = split(mixed_mem[...]), split(grad_mem[...])
+        first = pl.ds(pl.multiple_of(ids[0, 0] * rows, rows), mixed_mem.shape[0])
+        out_ref[...] = mul3(mixed, w_out)
+        feat_ref[...] = mul3(grad_query, w_query, 1, 1)
+        gq_ref[...] = mul3(split(feats[first, :]), grad_query, 0, 0)
+        go_ref[...] = mul3(mixed, split(cot_ref[...]), 0, 0)
         keep.wait()
 
 
@@ -142,18 +149,23 @@
     cols = w_query.shape[1]
     heads = cols // HEAD_SIZE
 
-    layout = [(count, block) for _, count, block in pieces]
+    arrays = []
+    for array, *_ in pieces:
+        if not any(array is known for known in arrays):
+            arrays.append(array)
+    layout = [
+        ([array is known for known in arrays].index(True), *rest) for array, *rest in pieces
+    ]
     all_shape = jax.ShapeDtypeStruct((total * rows, width), F32)
 
     def whole(array):
         return pl.BlockSpec(array.shape, lambda b, ids: (0,) * array.ndim)
 
-    own = pl.BlockSpec((rows, width), lambda b, ids: (b, 0))
     grad_shape = jax.ShapeDtypeStruct((width, cols), F32)
     out_shape = jax.ShapeDtypeStruct((cols, width), F32)
     node_shape = jax.ShapeDtypeStruct((node_rows, width), F32)
     return pl.pallas_call(
-        functools.partial(forward_kernel, entries, layout),
+        functools.partial(forward_kernel, entries, layout, len(arrays)),
         out_shape=(
             all_shape,
             node_shape,
@@ -165,20 +177,22 @@
         grid_spec=pltpu.PrefetchScalarGridSpec(
             num_scalar_prefetch=1,
             grid=(block_count,),
-            in_specs=[pl.BlockSpec(memory_space=pl.ANY) for _ in pieces]
-            + [own, pl.BlockSpec((rows, cols), lambda b, ids: (b, 0))]
+            in_specs=[pl.BlockSpec(memory_space=pl.ANY) for _ in arrays]
+            + [whole(out_cotangent), pl.BlockSpec((rows, cols), lambda b, ids: (b, 0))]
             + [pl.BlockSpec((1, 1, entries * rows), lambda b, ids: (b, 0, 0))]
             + [whole(w) for w in (w_query, w_key, w_value, w_out)],
             out_specs=(
                 pl.BlockSpec(memory_space=pl.ANY),
-                own,
-                own,
+                whole(node_shape),
+                whole(node_shape),
                 pl.BlockSpec((1, 2 * heads, rows), lambda b, ids: (b, 0, 0)),
                 whole(grad_shape),
                 whole(out_shape),
             ),
             scratch_shapes=[
                 pltpu.VMEM((total * rows, width), F32),
+                pltpu.VMEM((node_rows, cols), F32),
+                pltpu.VMEM((node_rows, cols), F32),
                 pltpu.SemaphoreType.DMA((len(layout),)),
                 pltpu.SemaphoreType.DMA,
             ],
@@ -187,140 +201,154 @@
             dimension_semantics=("arbitrary",), vmem_limit_bytes=56 * 1024 * 1024
         ),
         name="attend_forward",
-    )(ids, *[array for array, _, _ in pieces], out_cotangent, grad_mixed, bias, w_query, w_key, w_value, w_out)
-
-
-def backward_kernel(steps_ref, readers_ref, *refs):
-    feats, cots, stats = refs[:GROUP], refs[GROUP:2 * GROUP], refs[2 * GROUP:3 * GROUP]
-    lists = refs[3 * GROUP:4 * GROUP]
-    (own_ref, part_ref, wq_ref, wk_ref, wv_ref,
-     feat_ref, gk_ref, gv_ref, key_mem, value_mem, dk_mem, dv_mem) = refs[4 * GROUP:]
-    step = pl.program_id(0)
-    rows = own_ref.shape[0]
+    )(ids, *arrays, out_cotangent, grad_mixed, bias, w_query, w_key, w_value, w_out)
+
+
+def backward_kernel(
+    steps_ref, readers_ref, feats_ref, cots_ref, stats_ref, lists_ref, own_ref, part_ref,
+    wq_ref, wk_ref, wv_ref, feat_ref, gk_ref, gv_ref,
+    pair_mem, key_mem, value_mem, dk_mem, dv_mem, buffer, grads, sems,
+):
+    rows = buffer.shape[1] // GROUP
     cols = wq_ref.shape[1]
     heads = cols // HEAD_SIZE
     lane = lax.broadcasted_iota(jnp.int32, (rows, cols), 1) // HEAD_SIZE
-    kind = steps_ref[1, step]
-
-    @pl.when(step == 0)
-    def _():
-        gk_ref[...] = jnp.zeros_like(gk_ref)
-        gv_ref[...] = jnp.zeros_like(gv_ref)
-
-    @pl.when(kind % 2 == 1)
-    def _():
-        pairs = mul3(split(own_ref[...]), split(wide(wk_ref[...], wv_ref[...])))
-        for head in range(heads):
-            here = lane == head
-            at = pl.ds(head * rows, rows)
-            key_mem[at, :] = wide(*split(jnp.where(here, pairs[:, :cols], 0.0)))
-            value_mem[at, :] = wide(*split(jnp.where(here, pairs[:, cols:], 0.0)))
-        dk_mem[...] = jnp.zeros_like(dk_mem)
-        dv_mem[...] = jnp.zeros_like(dv_mem)
-
-    @pl.when(kind >= 4)
-    def _():
-        inputs = split(jnp.concatenate([ref[...] for ref in feats], axis=0))
-        q_high, q_low = split(mul3(inputs, split(wq_ref[...])) * SCALE)
-        g_high, g_low = split(jnp.concatenate([ref[...] for ref in cots], axis=0))
-        q_twice, q_both = wide(q_high, q_high), wide(q_high, q_low)
-        g_twice, g_both = wide(g_high, g_high), wide(g_high, g_low)
-        mark_row = lax.broadcasted_iota(jnp.int32, (8, GROUP * rows), 0)
-        mark_col = lax.broadcasted_iota(jnp.int32, (8, GROUP * rows), 1)
-        marks = (mark_row == mark_col // rows).astype(BF16)
-        masks = []
-        for at, ref in enumerate(lists):
+    count = steps_ref[2, 0]
+
+    def load(step, into):
+        for at in range(GROUP):
+            to = pl.ds(at * rows, rows)
+            spot = readers_ref[1, step * GROUP + at]
+            start = pl.ds(pl.multiple_of(spot * rows, rows), rows)
+            pltpu.make_async_copy(
+                feats_ref.at[start, :], buffer.at[into, to, :], sems.at[0, into]
+            ).start()
+            spot = readers_ref[0, step * GROUP + at]
+            start = pl.ds(pl.multiple_of(spot * rows, rows), rows)
+            pltpu.make_async_copy(
+                cots_ref.at[start, :], grads.at[into, to, :], sems.at[1, into]
+            ).start()
+
+    load(0, 0)
+    own = split(own_ref[...])
+    pair_mem[...] = mul3(own, split(wide(wk_ref[...], wv_ref[...])))
+    dk_mem[...] = jnp.zeros_like(dk_mem)
+    dv_mem[...] = jnp.zeros_like(dv_mem)
+    w_query = split(wq_ref[...])
+    mark_row = lax.broadcasted_iota(jnp.int32, (8, GROUP * rows), 0)
+    mark_col = lax.broadcasted_iota(jnp.int32, (8, GROUP * rows), 1)
+    marks = (mark_row == mark_col // rows).astype(BF16)
+
+    def chunk(step, carry):
+        turn = step % 2
+        kind = steps_ref[1, step]
+        block = pl.ds(pl.multiple_of(steps_ref[0, step] * rows, rows), rows)
+
+        @pl.when(step + 1 < count)
+        def _():
+            load(step + 1, 1 - turn)
+
+        @pl.when(kind % 2 == 1)
+        def _():
+            pairs = pair_mem[block, :]
+            for head in range(heads):
+                here = lane == head
+                at = pl.ds(head * rows, rows)
+                key_mem[at, :] = wide(*split(jnp.where(here, pairs[:, :cols], 0.0)))
+                value_mem[at, :] = wide(*split(jnp.where(here, pairs[:, cols:], 0.0)))
+
+        pltpu.make_async_copy(buffer.at[turn], buffer.at[turn], sems.at[0, turn]).wait()
+        pltpu.make_async_copy(grads.at[turn], grads.at[turn], sems.at[1, turn]).wait()
+        query = mul3(split(buffer[turn]), w_query) * SCALE
+        grad = grads[turn]
+        q_high, q_low = split(query)
+        g_high, g_low = split(grad)
+        q_both, g_both = wide(q_high, q_low), wide(g_high, g_low)
+        turned_high, turned_low = split(jnp.transpose(wide(query, grad)))
+        turned_q = jnp.concatenate([turned_high[:cols], turned_high[:cols]], axis=0)
+        turned_g = jnp.concatenate([turned_high[cols:], turned_high[cols:]], axis=0)
+        masks, stats = [], []
+        for at in range(GROUP):
             entry = readers_ref[2, step * GROUP + at]
-            row = ref[0, pl.ds(jnp.maximum(entry, 0), 1), :]
+            row = lists_ref[readers_ref[3, step * GROUP + at], pl.ds(jnp.maximum(entry, 0), 1), :]
             kept = ((row > 0) | (entry == 0)) & (entry >= 0)
             masks.append(jnp.where(kept, 0.0, MASKED))
+            stats.append(stats_ref[readers_ref[0, step * GROUP + at]])
         masks.append(jnp.zeros((8 - GROUP, rows), F32))
         bias = mul(jnp.concatenate(masks, axis=0).astype(BF16), marks, 0, 0)
-        stat = jnp.concatenate([ref[0] for ref in stats], axis=1)
-        grad_key = dk_mem[...]
-        grad_value = dv_mem[...]
-        for head in range(heads):
-            here = lane == head
-            keys = key_mem[pl.ds(head * rows, rows), :]
-            values = value_mem[pl.ds(head * rows, rows), :]
-            scores = mul(keys, q_twice, 1, 1) + mul(keys[:, :cols], q_low, 1, 1)
-            probs = jnp.exp(scores + (bias - stat[head:head + 1]))
-            grad_probs = mul(values, g_twice, 1, 1) + mul(values[:, :cols], g_low, 1, 1)
-            grad_scores = probs * (grad_probs - stat[heads + head:heads + head + 1])
-            p_high, p_low = split(probs)
-            term = fold(mul(p_high, g_both)) + mul(p_low, g_high)
-            grad_value = grad_value + jnp.where(here, term, 0.0)
-            s_high, s_low = split(grad_scores)
-            term = fold(mul(s_high, q_both)) + mul(s_low, q_high)
-            grad_key = grad_key + jnp.where(here, term, 0.0)
-        dk_mem[...] = grad_key
-        dv_mem[...] = grad_value
-
-    @pl.when((kind // 2) % 2 == 1)
-    def _():
-        grad_key, grad_value = split(dk_mem[...]), split(dv_mem[...])
-        own = split(own_ref[...])
-        feat_ref[...] = (
-            part_ref[...]
-            + mul3(grad_key, split(wk_ref[...]), 1, 1)
-            + mul3(grad_value, split(wv_ref[...]), 1, 1)
-        )
-        gk_ref[...] += mul3(own, grad_key, 0, 0)
-        gv_ref[...] += mul3(own, grad_value, 0, 0)
+        stat = jnp.concatenate(stats, axis=1)
+        keys, values = key_mem[...], value_mem[...]
+        scores = mul(keys, turned_q) + mul(keys[:, :cols], turned_low[:cols])
+        grad_probs = mul(values, turned_g) + mul(values[:, :cols], turned_low[cols:])
+
+        def rows_of(first):
+            return [
+                jnp.broadcast_to(stat[first + head:first + head + 1], bias.shape)
+                for head in range(heads)
+            ]
+
+        shift = jnp.concatenate([bias - each for each in rows_of(0)], axis=0)
+        probs = jnp.exp(scores + shift)
+        grad_scores = probs * (grad_probs - jnp.concatenate(rows_of(heads), axis=0))
+        p_high, p_low = split(probs)
+        grad_value = fold(mul(p_high, g_both)) + mul(p_low, g_high)
+        s_high, s_low = split(grad_scores)
+        grad_key = fold(mul(s_high, q_both)) + mul(s_low, q_high)
+
+        def gathered(value):
+            parts = [
+                jnp.where(lane == head, value[head * rows:(head + 1) * rows], 0.0)
+                for head in range(heads)
+            ]
+            return sum(parts[1:], parts[0])
+
+        dv_mem[block, :] += gathered(grad_value)
+        dk_mem[block, :] += gathered(grad_key)
+        return carry
+
+    lax.fori_loop(0, count, chunk, 0)
+    grad_key, grad_value = split(dk_mem[...]), split(dv_mem[...])
+    feat_ref[...] = (
+        part_ref[...]
+        + mul3(grad_key, split(wk_ref[...]), 1, 1)
+        + mul3(grad_value, split(wv_ref[...]), 1, 1)
+    )
+    own = split(own_ref[...])
+    gk_ref[...] = mul3(own, grad_key, 0, 0)
+    gv_ref[...] = mul3(own, grad_value, 0, 0)
 
 
 def attend_backward(
     steps, readers, all_feats, all_cots, all_stats, lists, own_feats, part,
     w_query, w_key, w_value, rows,
 ):
-    count = steps.shape[1]
     node_rows, width = own_feats.shape
     cols = w_query.shape[1]
     heads = cols // HEAD_SIZE
-
-    def picked(at, lanes, kind):
-        return pl.BlockSpec(
-            (rows, lanes), lambda s, steps, readers: (readers[kind, s * GROUP + at], 0)
-        )
-
-    def picked_row(at, array, kind):
-        return pl.BlockSpec(
-            (1,) + array.shape[1:],
-            lambda s, steps, readers: (readers[kind, s * GROUP + at], 0, 0),
-        )
-
-    def whole(array):
-        return pl.BlockSpec(array.shape, lambda s, steps, readers: (0,) * array.ndim)
-
-    own = pl.BlockSpec((rows, width), lambda s, steps, readers: (steps[0, s], 0))
+    held = pl.BlockSpec(memory_space=pltpu.VMEM)
+    scalars = pl.BlockSpec(memory_space=pltpu.SMEM)
+    afar = pl.BlockSpec(memory_space=pl.ANY)
     grad_shape = jax.ShapeDtypeStruct((width, cols), F32)
     return pl.pallas_call(
         backward_kernel,
         out_shape=(jax.ShapeDtypeStruct((node_rows, width), F32), grad_shape, grad_shape),
-        grid_spec=pltpu.PrefetchScalarGridSpec(
-            num_scalar_prefetch=2,
-            grid=(count,),
-            in_specs=[picked(at, width, 1) for at in range(GROUP)]
-            + [picked(at, cols, 0) for at in range(GROUP)]
-            + [picked_row(at, all_stats, 0) for at in range(GROUP)]
-            + [picked_row(at, lists, 3) for at in range(GROUP)]
-            + [own, own]
-            + [whole(w) for w in (w_query, w_key, w_value)],
-            out_specs=(own, whole(grad_shape), whole(grad_shape)),
-            scratch_shapes=[
-                pltpu.VMEM((heads * rows, 2 * cols), BF16),
-                pltpu.VMEM((heads * rows, 2 * cols), BF16),
-                pltpu.VMEM((rows, cols), F32),
-                pltpu.VMEM((rows, cols), F32),
-            ],
-        ),
-        compiler_params=pltpu.CompilerParams(
-            dimension_semantics=("arbitrary",), vmem_limit_bytes=50 * 1024 * 1024
-        ),
+        in_specs=[scalars, scalars, afar, afar] + [held] * 7,
+        out_specs=(held, held, held),
+        scratch_shapes=[
+            pltpu.VMEM((node_rows, 2 * cols), F32),
+            pltpu.VMEM((heads * rows, 2 * cols), BF16),
+            pltpu.VMEM((heads * rows, 2 * cols), BF16),
+            pltpu.VMEM((node_rows, cols), F32),
+            pltpu.VMEM((node_rows, cols), F32),
+            pltpu.VMEM((2, GROUP * rows, width), F32),
+            pltpu.VMEM((2, GROUP * rows, cols), F32),
+            pltpu.SemaphoreType.DMA((2, 2)),
+        ],
+        compiler_params=pltpu.CompilerParams(vmem_limit_bytes=50 * 1024 * 1024),
         name="attend_backward",
     )(
-        steps, readers, *([all_feats] * GROUP), *([all_cots] * GROUP), *([all_stats] * GROUP),
-        *([lists] * GROUP), own_feats, part, w_query, w_key, w_value,
+        steps, readers, all_feats, all_cots, all_stats, lists, own_feats, part,
+        w_query, w_key, w_value,
     )
 
 
@@ -360,7 +388,7 @@
     kind = jnp.where(
         live, first.astype(jnp.int32) + 2 * last.astype(jnp.int32) + 4, 0
     )
-    return jnp.stack([block, kind]), readers, entry
+    return jnp.stack([block, kind, jnp.full_like(kind, ends[-1])]), readers, entry
 
 
 def head_scatter(part):
@@ -403,7 +431,7 @@
     if size != 16 or lax.axis_size("head") != 2 or block_count != 8:
         plan = make_plan(lax.all_gather(lists, "dom", axis=0, tiled=True), lambda ids: ids)
         everything = lax.all_gather(part, "dom", axis=0, tiled=True)
-        return [(everything, everything.shape[0], 0)], lambda ids: ids, part, plan
+        return [(everything, 0, everything.shape[0], 0)], lambda ids: ids, part, plan
     side = lax.axis_index("head")
     rows = part.shape[0] // block_count
     total = size * block_count
@@ -419,7 +447,10 @@
     other_head = [(0, 1), (1, 0)]
 
     def lacking(value):
-        return lax.dynamic_slice_in_dim(value, 2 * side * rows, 3 * rows, axis=0)
+        parts = [
+            lax.dynamic_slice_in_dim(each, 2 * side * rows, 3 * rows, axis=0) for each in value
+        ]
+        return jnp.concatenate(parts, axis=0)
 
     half = total // 2
 
@@ -448,15 +479,15 @@
     twin = swap(part)
     all_notes = [notes, swap(notes)]
     held, twin = lax.optimization_barrier((held, twin))
-    pieces = [(part, block_count * rows, 0), (twin, block_count * rows, half)]
-
-    def keep(value, swapped, slot, offset, count):
-        pieces.append((value, count * rows, slot * block_count + offset))
-        pieces.append((swapped, count * rows, half + slot * block_count + offset))
-        if offset == 0:
-            all_notes.extend([value[count * rows:], swapped[count * rows:]])
-
-    slots, lack, lack_slots = (1, 2), (), ()
+    pieces = [(part, 0, block_count * rows, 0), (twin, 0, block_count * rows, half)]
+
+    def keep(value, swapped, slots):
+        for at, slot in enumerate(slots):
+            first = slot * block_count + 5
+            pieces.append((value, 3 * at * rows, 3 * rows, first))
+            pieces.append((swapped, 3 * at * rows, 3 * rows, half + first))
+
+    slots, lack, lack_slots, notes = (1, 2), (), (), ()
     for step in range(1, 5):
         if step < 3:
             coming = (
@@ -467,35 +498,41 @@
                 lax.ppermute(held[0][: 3 * rows], "dom", onward),
                 lax.ppermute(held[1][3 * rows:], "dom", back),
             )
+            notes = jnp.concatenate(all_notes, axis=0)
+            all_notes = []
         else:
             coming = ()
-        more = tuple(lax.ppermute(lacking(value), "head", other_head) for value in held)
+        more = (lax.ppermute(lacking(held), "head", other_head),)
         swapped = tuple(swap(value) for value in held)
         swapped_lack = tuple(swap(value) for value in lack)
         if step < 4:
-            coming, held, more, swapped, lack, swapped_lack = lax.optimization_barrier(
-                (coming, held, more, swapped, lack, swapped_lack)
+            coming, held, more, swapped, lack, swapped_lack, notes = lax.optimization_barrier(
+                (coming, held, more, swapped, lack, swapped_lack, notes)
             )
         else:
             held, swapped, lack, swapped_lack = lax.optimization_barrier(
                 (held, swapped, lack, swapped_lack)
             )
         for at, slot in enumerate(slots):
-            keep(held[at], swapped[at], slot, 0, 5)
-        for at, slot in enumerate(lack_slots):
-            keep(lack[at], swapped_lack[at], slot, 5, 3)
+            first = slot * block_count
+            pieces.append((held[at], 0, 5 * rows, first))
+            pieces.append((swapped[at], 0, 5 * rows, half + first))
+            all_notes.extend([held[at][5 * rows:], swapped[at][5 * rows:]])
+        if lack:
+            keep(lack[0], swapped_lack[0], lack_slots)
         lack, lack_slots = more, slots
         if step == 3:
             held, slots = (jnp.concatenate(coming, axis=0),), (7,)
             late = held[0]
         else:
             held, slots = coming, (2 * step + 1, 2 * step + 2)
+    all_notes.insert(0, notes)
     every = jnp.concatenate(all_notes, axis=0)
     width = lists.shape[2]
     every = jnp.concatenate([every[:, :width], every[:, width:]], axis=0)
     plan = make_plan(every.reshape((-1,) + lists.shape[1:]), place)
     lack, plan = lax.optimization_barrier((lack, plan))
-    keep(lack[0], swap(lack[0]), 7, 5, 3)
+    keep(lack[0], swap(lack[0]), (7,))
     return pieces, place, late, plan
 
 

time: 313 us -> 280 us (0.89)
  Pallas kernels: 123 us -> 95.4 us
  waiting for transfers between devices: 89.1 us -> 81.2 us
  starting transfers between devices: 28.2 us -> 22.6 us
  local copies, waits for them, and re-layouts: 20.6 us -> 26.1 us
    ppermute x7 -> x4, waiting for transfers between devices: 37.5 us -> 6.83 us  [gather_feats(): more = (lax.ppermute(lacking(held), 'head', other_head),)]
    pallas_call x1, Pallas kernels: 66.5 us -> 50.9 us  [attend_backward(): pl.pallas_call(backward_kernel, out_shape=(jax.ShapeDtypeStruct((node_row...]
    pallas_call x1, Pallas kernels: 56.6 us -> 44.5 us  [attend_forward(): pl.pallas_call(functools.partial(forward_kernel, entries, layout, len(arr...]
    ppermute x2, waiting for transfers between devices: 10 us -> 21.5 us  [gather_feats(): lax.ppermute(held[0], 'dom', onward)]
    ppermute x1, waiting for transfers between devices: 0.01 us -> 8.4 us  [gather_feats(): lax.ppermute(held[0][:3 * rows], 'dom', onward)]
    ppermute x7 -> x4, starting transfers between devices: 8.7 us -> 4.25 us  [gather_feats(): more = (lax.ppermute(lacking(held), 'head', other_head),)]
    unnamed x73 -> x69, local copies, waits for them, and re-layouts: 12.6 us -> 15.6 us
  transfers between devices with their start and end apart: 44 -> 38, of which waited for: 20 -> 17; matrix products, arithmetic and copies ran while one was open for 10% -> 13% of each run, Pallas kernels for 39% -> 34%
where the time goes in v6:
time: 280 us; the launch traced here: 277 us
  Pallas kernels  95.4 us (34%)
  waiting for transfers between devices  81.2 us (29%)
  local copies, waits for them, and re-layouts  26.1 us (9%)
  starting transfers between devices  22.6 us (8%)
  blocking collectives  21 us (8%)
  between operations  14.6 us (5%)
  other arithmetic  14.2 us (5%)
    pallas_call x1, Pallas kernels, attend_backward(): pl.pallas_call(backward_kernel, out_shape=(jax.ShapeDtypeStruct((node_row...  50.9 us
    pallas_call x1, Pallas kernels, attend_forward(): pl.pallas_call(functools.partial(forward_kernel, entries, layout, len(arr...  44.5 us
    ppermute x2, waiting for transfers between devices, gather_feats(): lax.ppermute(held[0], 'dom', onward)  21.5 us
    all_gather x1, blocking collectives, per_device(): all_stats = lax.all_gather(stats, 'dom', axis=0, tiled=True)  21 us
    ppermute x1, waiting for transfers between devices, gather_feats(): lax.ppermute(start, 'dom', onward)  16 us
    unnamed x69, local copies, waits for them, and re-layouts  15.6 us
    ppermute x10, waiting for transfers between devices, from_across(): return lax.ppermute(value, 'dom', [(at, at ^ bit) for at in range(size)])  15.3 us
    ppermute x1, waiting for transfers between devices, gather_feats(): lax.ppermute(held[0][:3 * rows], 'dom', onward)  8.4 us
  transfers between devices with their start and end apart: 38, of which 17 were waited for; matrix products, arithmetic and copies ran while one was open for 13% of the time, Pallas kernels for 34%

profile of v6, /device:TPU:0, one launch (start us, length us, event | category | flops | bytes accessed | tf_op | source)
XLA Modules:
  0.0 276.9 jit_solution(10558860922125365478)
XLA Ops:
  7.8 0.7 multiply_add_fusion
  8.5 0.7 fusion.10
  9.2 0.8 convert_element_type.58
  9.9 1.1 constant_dynamic-slice_fusion.9
  11.1 0.9 maximum_maximum_fusion
  12.0 2.8 %collective-permute-start = (f32[672,256]{1,0:T(8,128)}, f32[672,256]{1,0:T(8,128)S(1)}, u32[]{:S(2)}, u32[]{:S(2)}) collective-permute-start(f32[672,256]{1,0:T(8,128)} %maximum_maximum_fusion), channel_id=1, source_target_pairs={{0,8},{2,10},{8,16},{10,18},{16,24},{18,26},{24,28},{26,30},{28,20... | collective-permute-start | bytes 2064392 | tf_op jit(solution)/shard_map/ppermute | solution.py:478
  14.8 16.0 %collective-permute-done.refs_2_ = f32[672,256]{1,0:T(8,128)S(1)} collective-permute-done((f32[672,256]{1,0:T(8,128)}, f32[672,256]{1,0:T(8,128)S(1)}, u32[]{:S(2)}, u32[]{:S(2)}) %collective-permute-start) | collective-permute-done | bytes 688160 | tf_op jit(solution)/shard_map/ppermute | solution.py:478
  30.8 1.5 collective-permute-done.1.refs_4_
  32.5 1.6 collective-permute-start.5
  34.1 1.6 collective-permute-start.3
  37.2 13.2 %collective-permute-done.3.refs_6_ = f32[672,256]{1,0:T(8,128)} collective-permute-done((f32[672,256]{1,0:T(8,128)S(1)}, f32[672,256]{1,0:T(8,128)}, u32[]{:S(2)}, u32[]{:S(2)}) %collective-permute-start.3) | collective-permute-done | bytes 688160 | tf_op jit(solution)/shard_map/ppermute | solution.py:494
  50.4 1.3 collective-permute-done.4.refs_8_
  51.7 0.8 copy-done.17
  52.8 0.9 copy-done.12
  53.7 1.8 fusion.34.refs_25_
  56.1 1.6 collective-permute-start.8
  58.4 1.1 constant_dynamic-slice_fusion.5
  59.4 1.0 constant_dynamic-slice_fusion.6
  61.7 1.4 constant_dynamic-update-slice_fusion.6
  63.1 1.4 constant_dynamic-update-slice_fusion.5
  64.4 1.4 constant_dynamic-update-slice_fusion.4
  65.8 8.3 %collective-permute-done.8.refs_12_ = f32[672,256]{1,0:T(8,128)S(1)} collective-permute-done((f32[672,256]{1,0:T(8,128)}, f32[672,256]{1,0:T(8,128)S(1)}, u32[]{:S(2)}, u32[]{:S(2)}) %collective-permute-start.8) | collective-permute-done | bytes 688160 | tf_op jit(solution)/shard_map/ppermute | solution.py:494
  74.2 1.6 collective-permute-done.9.refs_14_
  75.7 4.3 %collective-permute-done.10.refs_16_ = f32[768,256]{1,0:T(8,128)S(1)} collective-permute-done((f32[768,256]{1,0:T(8,128)S(1)}, f32[768,256]{1,0:T(8,128)S(1)}, u32[]{:S(2)}, u32[]{:S(2)}) %collective-permute-start.10) | collective-permute-done | bytes 786464 | tf_op jit(solution)/shard_map/ppermute | solution.py:505
  81.9 0.8 constant_dynamic-update-slice_fusion.3
  82.6 0.8 constant_dynamic-update-slice_fusion.2
  83.4 7.4 %collective-permute-done.15 = f32[288,256]{1,0:T(8,128)S(1)} collective-permute-done((f32[288,256]{1,0:T(8,128)S(1)}, f32[288,256]{1,0:T(8,128)S(1)}, u32[]{:S(2)}, u32[]{:S(2)}) %collective-permute-start.15) | collective-permute-done | bytes 294944 | tf_op jit(solution)/shard_map/ppermute | solution.py:499
  90.9 1.6 collective-permute-start.14
  92.4 0.8 constant_dynamic-update-slice_fusion.1
  93.2 8.4 %collective-permute-done.14 = f32[384,256]{1,0:T(8,128)S(1)} collective-permute-done((f32[384,256]{1,0:T(8,128)S(1)}, f32[384,256]{1,0:T(8,128)S(1)}, u32[]{:S(2)}, u32[]{:S(2)}) %collective-permute-start.14) | collective-permute-done | bytes 393248 | tf_op jit(solution)/shard_map/ppermute | solution.py:498
  101.6 1.0 copy-done.14
  104.1 0.8 constant_dynamic-slice_fusion.2
  104.9 1.5 collective-permute-start.23
  106.5 0.8 constant_dynamic-update-slice_fusion.16
  107.2 0.8 constant_dynamic-update-slice_fusion.14
  108.0 0.8 copy-done.22
  110.4 0.7 pad.16.clone
  112.1 1.2 gather_fusion
  113.8 2.5 collective-permute-done.23.refs_22_
  116.9 1.3 collective-permute-done.24.refs_23_
  118.2 0.7 copy-done.25
  119.0 44.5 %attend_forward.1 = (f32[16384,256]{1,0:T(8,128)}, f32[1024,256]{1,0:T(8,128)}, f32[1024,256]{1,0:T(8,128)}, f32[8,8,128]{2,1,0:T(8,128)}, f32[256,128]{1,0:T(8,128)}, /*index=5*/f32[128,256]{1,0:T(8,128)}) custom-call(s32[8,8]{1,0:T(8,128)} %get-tuple-element.102.ids, f32[1024,256]{1,0:T(8,128)} %own_ref.1, f32[1024,256]{1,0:T(8,128)} %collective-permute-done.2.refs_1_, ...), custom_call_target="tpu_custom_call" | custom-call | tf_op jit(solution)/shard_map/attend_forward/pallas_call | solution.py:167
  163.5 1.0 fusion.33
  164.5 1.1 collective-permute-start.27
  165.6 1.0 collective-permute-done.27
  166.6 0.9 select_add_fusion.1
  168.1 1.9 constant_dynamic-slice_fusion
  169.9 1.5 collective-permute-start.25
  171.5 1.1 collective-permute-done.28
  172.6 1.7 collective-permute-start.29
  174.2 21.0 %all_gather.7.stats_ref = f32[128,8,128]{2,1,0:T(8,128)S(1)} all-gather(f32[8,8,128]{2,1,0:T(8,128)} %get-tuple-element.92), channel_id=1, replica_groups=mesh['dom'=16,'head'=2] {'dom'}, dimensions={0}, use_global_device_ids=true | all-gather | bytes 557056 | tf_op jit(solution)/shard_map/all_gather | solution.py:580
  195.3 0.7 add.409
  196.0 50.9 %attend_backward.1 = (f32[1024,256]{1,0:T(8,128)S(1)}, f32[256,128]{1,0:T(8,128)S(1)}, f32[256,128]{1,0:T(8,128)S(1)}) custom-call(s32[3,24]{1,0:T(4,128)S(1)} %add_add_fusion.steps_ref, s32[4,96]{1,0:T(4,128)S(1)} %pad_add_fusion.1.readers_ref, f32[16384,256]{1,0:T(8,128)} %get-tuple-element.90.feats_ref, ...), custom_call_target="tpu_custom_call" | custom-call | tf_op jit(solution)/shard_map/attend_backward/pallas_call | solution.py:332
  247.6 1.0 add.410
  249.2 0.9 select_add_fusion
  250.2 2.1 dynamic-slice_add_fusion.1
  252.3 1.3 collective-permute-start.26
  253.6 2.0 collective-permute-done.33
  255.7 0.7 broadcast_select_fusion
  256.4 4.3 %collective-permute-done.34 = f32[256,128]{1,0:T(8,128)S(1)} collective-permute-done((f32[256,128]{1,0:T(8,128)S(1)}, f32[256,128]{1,0:T(8,128)S(1)}, u32[]{:S(2)}, u32[]{:S(2)}) %collective-permute-start.34) | collective-permute-done | bytes 131104 | tf_op jit(solution)/shard_map/ppermute | solution.py:410
  260.8 0.7 pad_maximum_fusion.4
  261.5 6.5 %collective-permute-done.35 = f32[256,128]{1,0:T(8,128)S(1)} collective-permute-done((f32[256,128]{1,0:T(8,128)S(1)}, f32[256,128]{1,0:T(8,128)S(1)}, u32[]{:S(2)}, u32[]{:S(2)}) %collective-permute-start.35) | collective-permute-done | bytes 131104 | tf_op jit(solution)/shard_map/ppermute | solution.py:410
  268.0 0.9 dynamic-slice_add_fusion
  269.3 0.7 broadcast_select_fusion.1
  (159 shorter events, 14.7 us)
Async XLA Ops:
  7.2 46.5 %copy-start.23 = (f32[128,256]{1,0:T(8,128)S(1)}, f32[128,256]{1,0:T(8,128)}, u32[]{:S(2)}) copy-start(f32[128,256]{1,0:T(8,128)} %refs_30_.1) | copy-start | bytes 393220
  7.2 46.5 %copy-start.6 = (f32[1024,256]{1,0:T(8,128)S(1)}, f32[1024,256]{1,0:T(8,128)}, u32[]{:S(2)}) copy-start(f32[1024,256]{1,0:T(8,128)} %refs_24_.1) | copy-start | bytes 3145732
  7.2 188.8 %all-gather.2.cloned.1.call-start = ((), (), s32[]{:S(2)}) async-start(), calls=%async_computation | async-start | bytes 8912896 | tf_op jit(solution)/shard_map/all_gather | solution.py:570
  7.2 25.1 %collective-permute-start.2 = (f32[1024,256]{1,0:T(8,128)}, f32[1024,256]{1,0:T(8,128)}, u32[]{:S(2)}, u32[]{:S(2)}) collective-permute-start(f32[1024,256]{1,0:T(8,128)} %own_ref.1), channel_id=1, source_target_pairs={{0,2},{2,0},{4,6},{6,4},{8,10},{10,8},{12,14},{14,12},{16,18},{18,... | collective-permute-start | bytes 3145736 | tf_op jit(solution)/shard_map/ppermute | solution.py:458
  12.0 18.8 %collective-permute-start = (f32[672,256]{1,0:T(8,128)}, f32[672,256]{1,0:T(8,128)S(1)}, u32[]{:S(2)}, u32[]{:S(2)}) collective-permute-start(f32[672,256]{1,0:T(8,128)} %maximum_maximum_fusion), channel_id=1, source_target_pairs={{0,8},{2,10},{8,16},{10,18},{16,24},{18,26},{24,28},{26,30},{28,20... | collective-permute-start | bytes 2064392 | tf_op jit(solution)/shard_map/ppermute | solution.py:478
  14.8 17.5 %collective-permute-start.1 = (f32[672,256]{1,0:T(8,128)}, f32[672,256]{1,0:T(8,128)S(1)}, u32[]{:S(2)}, u32[]{:S(2)}) collective-permute-start(f32[672,256]{1,0:T(8,128)} %maximum_maximum_fusion), channel_id=1, source_target_pairs={{8,0},{10,2},{16,8},{18,10},{24,16},{26,18},{28,24},{30,26},{20,28... | collective-permute-start | bytes 2064392 | tf_op jit(solution)/shard_map/ppermute | solution.py:478
  30.8 35.0 %copy-start.10 = (f32[672,256]{1,0:T(8,128)}, f32[672,256]{1,0:T(8,128)S(1)}, u32[]{:S(2)}) copy-start(f32[672,256]{1,0:T(8,128)S(1)} %collective-permute-done.refs_2_) | copy-start | bytes 2064388
  32.3 23.1 %copy-start.11 = (f32[672,256]{1,0:T(8,128)}, f32[672,256]{1,0:T(8,128)S(1)}, u32[]{:S(2)}) copy-start(f32[672,256]{1,0:T(8,128)S(1)} %collective-permute-done.1.refs_4_) | copy-start | bytes 2064388
  32.5 19.2 %collective-permute-start.5 = (f32[768,256]{1,0:T(8,128)S(1)}, f32[768,256]{1,0:T(8,128)S(1)}, u32[]{:S(2)}, u32[]{:S(2)}) collective-permute-start(f32[768,256]{1,0:T(8,128)S(1)} %pad_maximum_fusion), channel_id=1, source_target_pairs={{0,1},{1,0},{2,3},{3,2},{4,5},{5,4},{6,7},{7,6},{8,9},{9,8},{10,11... | collective-permute-start | bytes 2359304 | tf_op jit(solution)/shard_map/ppermute | solution.py:505
  34.1 16.3 %collective-permute-start.3 = (f32[672,256]{1,0:T(8,128)S(1)}, f32[672,256]{1,0:T(8,128)}, u32[]{:S(2)}, u32[]{:S(2)}) collective-permute-start(f32[672,256]{1,0:T(8,128)S(1)} %collective-permute-done.refs_2_), channel_id=1, source_target_pairs={{0,8},{2,10},{8,16},{10,18},{16,24},{18,26},{24,28},{26,30},{28,20... | collective-permute-start | bytes 2064392 | tf_op jit(solution)/shard_map/ppermute | solution.py:494
  35.6 16.0 %collective-permute-start.4 = (f32[672,256]{1,0:T(8,128)S(1)}, f32[672,256]{1,0:T(8,128)}, u32[]{:S(2)}, u32[]{:S(2)}) collective-permute-start(f32[672,256]{1,0:T(8,128)S(1)} %collective-permute-done.1.refs_4_), channel_id=1, source_target_pairs={{8,0},{10,2},{16,8},{18,10},{24,16},{26,18},{28,24},{30,26},{20,28... | collective-permute-start | bytes 2064392 | tf_op jit(solution)/shard_map/ppermute | solution.py:494
  36.1 15.6 %collective-permute-start.6 = (f32[672,256]{1,0:T(8,128)S(1)}, f32[672,256]{1,0:T(8,128)S(1)}, u32[]{:S(2)}, u32[]{:S(2)}) collective-permute-start(f32[672,256]{1,0:T(8,128)S(1)} %collective-permute-done.refs_2_), channel_id=1, source_target_pairs={{0,2},{2,0},{4,6},{6,4},{8,10},{10,8},{12,14},{14,12},{16,18},{18,... | collective-permute-start | bytes 2064392 | tf_op jit(solution)/shard_map/ppermute | solution.py:458
  36.1 15.6 %collective-permute-start.7 = (f32[672,256]{1,0:T(8,128)S(1)}, f32[672,256]{1,0:T(8,128)S(1)}, u32[]{:S(2)}, u32[]{:S(2)}) collective-permute-start(f32[672,256]{1,0:T(8,128)S(1)} %collective-permute-done.1.refs_4_), channel_id=1, source_target_pairs={{0,2},{2,0},{4,6},{6,4},{8,10},{10,8},{12,14},{14,12},{16,18},{18,... | collective-permute-start | bytes 2064392 | tf_op jit(solution)/shard_map/ppermute | solution.py:458
  50.4 5.1 %collective-permute-start.20 = (f32[32,256]{1,0:T(8,128)S(1)}, f32[32,256]{1,0:T(8,128)S(1)}, u32[]{:S(2)}, u32[]{:S(2)}) collective-permute-start(f32[32,256]{1,0:T(8,128)S(1)} %get-tuple-element.116), channel_id=1, source_target_pairs={{0,2},{2,0},{4,6},{6,4},{8,10},{10,8},{12,14},{14,12},{16,18},{18,... | collective-permute-start | bytes 98312 | tf_op jit(solution)/shard_map/ppermute | solution.py:458
  51.7 0.9 copy-start.17
  51.7 1.1 copy-start.18
  52.8 0.9 copy-start.12
  53.7 7.4 %collective-permute-start.11 = (f32[672,256]{1,0:T(8,128)}, f32[672,256]{1,0:T(8,128)}, u32[]{:S(2)}, u32[]{:S(2)}) collective-permute-start(f32[672,256]{1,0:T(8,128)} %collective-permute-done.3.refs_6_), channel_id=1, source_target_pairs={{0,2},{2,0},{4,6},{6,4},{8,10},{10,8},{12,14},{14,12},{16,18},{18,... | collective-permute-start | bytes 2064392 | tf_op jit(solution)/shard_map/ppermute | solution.py:458
  56.1 18.1 %collective-permute-start.8 = (f32[672,256]{1,0:T(8,128)}, f32[672,256]{1,0:T(8,128)S(1)}, u32[]{:S(2)}, u32[]{:S(2)}) collective-permute-start(f32[672,256]{1,0:T(8,128)} %collective-permute-done.3.refs_6_), channel_id=1, source_target_pairs={{0,8},{2,10},{8,16},{10,18},{16,24},{18,26},{24,28},{26,30},{28,20... | collective-permute-start | bytes 2064392 | tf_op jit(solution)/shard_map/ppermute | solution.py:494
  57.7 8.1 %collective-permute-start.12 = (f32[672,256]{1,0:T(8,128)}, f32[672,256]{1,0:T(8,128)S(1)}, u32[]{:S(2)}, u32[]{:S(2)}) collective-permute-start(f32[672,256]{1,0:T(8,128)} %collective-permute-done.4.refs_8_), channel_id=1, source_target_pairs={{0,2},{2,0},{4,6},{6,4},{8,10},{10,8},{12,14},{14,12},{16,18},{18,... | collective-permute-start | bytes 2064392 | tf_op jit(solution)/shard_map/ppermute | solution.py:458
  57.9 17.8 %collective-permute-start.9 = (f32[672,256]{1,0:T(8,128)}, f32[672,256]{1,0:T(8,128)S(1)}, u32[]{:S(2)}, u32[]{:S(2)}) collective-permute-start(f32[672,256]{1,0:T(8,128)} %collective-permute-done.4.refs_8_), channel_id=1, source_target_pairs={{8,0},{10,2},{16,8},{18,10},{24,16},{26,18},{28,24},{30,26},{20,28... | collective-permute-start | bytes 2064392 | tf_op jit(solution)/shard_map/ppermute | solution.py:494
  60.5 19.5 %collective-permute-start.10 = (f32[768,256]{1,0:T(8,128)S(1)}, f32[768,256]{1,0:T(8,128)S(1)}, u32[]{:S(2)}, u32[]{:S(2)}) collective-permute-start(f32[768,256]{1,0:T(8,128)S(1)} %pad_maximum_fusion.1), channel_id=1, source_target_pairs={{0,1},{1,0},{2,3},{3,2},{4,5},{5,4},{6,7},{7,6},{8,9},{9,8},{10,11... | collective-permute-start | bytes 2359304 | tf_op jit(solution)/shard_map/ppermute | solution.py:505
  61.1 18.9 %collective-permute-start.13 = (f32[768,256]{1,0:T(8,128)}, f32[768,256]{1,0:T(8,128)}, u32[]{:S(2)}, u32[]{:S(2)}) collective-permute-start(f32[768,256]{1,0:T(8,128)} %copy-done.12), channel_id=1, source_target_pairs={{0,2},{2,0},{4,6},{6,4},{8,10},{10,8},{12,14},{14,12},{16,18},{18,... | collective-permute-start | bytes 2359304 | tf_op jit(solution)/shard_map/ppermute | solution.py:458
  65.8 16.1 %copy-start.24 = (f32[320,256]{1,0:T(8,128)S(1)}, f32[320,256]{1,0:T(8,128)}, u32[]{:S(2)}) copy-start(f32[320,256]{1,0:T(8,128)} %constant_dynamic-update-slice_fusion.4) | copy-start | bytes 983044
  65.8 36.8 %copy-start.19 = (f32[672,256]{1,0:T(8,128)}, f32[672,256]{1,0:T(8,128)S(1)}, u32[]{:S(2)}) copy-start(f32[672,256]{1,0:T(8,128)S(1)} %collective-permute-done.12.refs_9_) | copy-start | bytes 2064388
  74.2 33.8 %copy-start.7 = (f32[672,256]{1,0:T(8,128)}, f32[672,256]{1,0:T(8,128)S(1)}, u32[]{:S(2)}) copy-start(f32[672,256]{1,0:T(8,128)S(1)} %collective-permute-done.8.refs_12_) | copy-start | bytes 2064388
  75.7 32.2 %copy-start.9 = (f32[672,256]{1,0:T(8,128)}, f32[672,256]{1,0:T(8,128)S(1)}, u32[]{:S(2)}) copy-start(f32[672,256]{1,0:T(8,128)S(1)} %collective-permute-done.9.refs_14_) | copy-start | bytes 2064388
  80.0 22.6 %copy-start.13 = (f32[768,256]{1,0:T(8,128)}, f32[768,256]{1,0:T(8,128)S(1)}, u32[]{:S(2)}) copy-start(f32[768,256]{1,0:T(8,128)S(1)} %collective-permute-done.10.refs_16_) | copy-start | bytes 2359300
  80.1 21.5 %collective-permute-start.17 = (f32[672,256]{1,0:T(8,128)S(1)}, f32[672,256]{1,0:T(8,128)S(1)}, u32[]{:S(2)}, u32[]{:S(2)}) collective-permute-start(f32[672,256]{1,0:T(8,128)S(1)} %collective-permute-done.8.refs_12_), channel_id=1, source_target_pairs={{0,2},{2,0},{4,6},{6,4},{8,10},{10,8},{12,14},{14,12},{16,18},{18,... | collective-permute-start | bytes 2064392 | tf_op jit(solution)/shard_map/ppermute | solution.py:458
  80.2 21.4 %collective-permute-start.18 = (f32[672,256]{1,0:T(8,128)S(1)}, f32[672,256]{1,0:T(8,128)S(1)}, u32[]{:S(2)}, u32[]{:S(2)}) collective-permute-start(f32[672,256]{1,0:T(8,128)S(1)} %collective-permute-done.9.refs_14_), channel_id=1, source_target_pairs={{0,2},{2,0},{4,6},{6,4},{8,10},{10,8},{12,14},{14,12},{16,18},{18,... | collective-permute-start | bytes 2064392 | tf_op jit(solution)/shard_map/ppermute | solution.py:458
  80.8 35.5 %copy-start.26 = (s32[8,7,128]{2,0,1:T(8,128)S(1)}, s32[8,7,128]{2,0,1:T(8,128)}, u32[]{:S(2)}) copy-start(s32[8,7,128]{2,0,1:T(8,128)} %param.16) | copy-start | bytes 86020
  80.9 20.8 %collective-permute-start.16 = (f32[768,256]{1,0:T(8,128)S(1)}, f32[768,256]{1,0:T(8,128)S(1)}, u32[]{:S(2)}, u32[]{:S(2)}) collective-permute-start(f32[768,256]{1,0:T(8,128)S(1)} %pad_maximum_fusion.2), channel_id=1, source_target_pairs={{0,1},{1,0},{2,3},{3,2},{4,5},{5,4},{6,7},{7,6},{8,9},{9,8},{10,11... | collective-permute-start | bytes 2359304 | tf_op jit(solution)/shard_map/ppermute | solution.py:505
  81.4 21.2 %collective-permute-start.19 = (f32[768,256]{1,0:T(8,128)S(1)}, f32[768,256]{1,0:T(8,128)S(1)}, u32[]{:S(2)}, u32[]{:S(2)}) collective-permute-start(f32[768,256]{1,0:T(8,128)S(1)} %collective-permute-done.10.refs_16_), channel_id=1, source_target_pairs={{0,2},{2,0},{4,6},{6,4},{8,10},{10,8},{12,14},{14,12},{16,18},{18,... | collective-permute-start | bytes 2359304 | tf_op jit(solution)/shard_map/ppermute | solution.py:458
  81.4 9.4 %collective-permute-start.15 = (f32[288,256]{1,0:T(8,128)S(1)}, f32[288,256]{1,0:T(8,128)S(1)}, u32[]{:S(2)}, u32[]{:S(2)}) collective-permute-start(f32[288,256]{1,0:T(8,128)S(1)} %slice.92), channel_id=1, source_target_pairs={{8,0},{10,2},{16,8},{18,10},{24,16},{26,18},{28,24},{30,26},{20,28... | collective-permute-start | bytes 884744 | tf_op jit(solution)/shard_map/ppermute | solution.py:499
  90.9 10.7 %collective-permute-start.14 = (f32[384,256]{1,0:T(8,128)S(1)}, f32[384,256]{1,0:T(8,128)S(1)}, u32[]{:S(2)}, u32[]{:S(2)}) collective-permute-start(f32[384,256]{1,0:T(8,128)S(1)} %get-tuple-element.105), channel_id=1, source_target_pairs={{0,8},{2,10},{8,16},{10,18},{16,24},{18,26},{24,28},{26,30},{28,20... | collective-permute-start | bytes 1179656 | tf_op jit(solution)/shard_map/ppermute | solution.py:498
  101.6 1.2 copy-start.20
  101.6 1.3 copy-start.21
  101.6 1.0 copy-start.14
  102.6 0.9 copy-start.15
  103.5 14.7 %copy-start.8 = (f32[672,256]{1,0:T(8,128)}, f32[672,256]{1,0:T(8,128)S(1)}, u32[]{:S(2)}) copy-start(f32[672,256]{1,0:T(8,128)S(1)} %constant_dynamic-update-slice_fusion.10.refs_18_) | copy-start | bytes 2064388
  103.5 4.4 %collective-permute-start.21 = (f32[672,256]{1,0:T(8,128)S(1)}, f32[672,256]{1,0:T(8,128)S(1)}, u32[]{:S(2)}, u32[]{:S(2)}) collective-permute-start(f32[672,256]{1,0:T(8,128)S(1)} %constant_dynamic-update-slice_fusion.10.refs_18_), channel_id=1, source_target_pairs={{0,2},{2,0},{4,6},{6,4},{8,10},{10,8},{12,14},{14,12},{16,18},{18,... | collective-permute-start | bytes 2064392 | tf_op jit(solution)/shard_map/ppermute | solution.py:458
  103.6 4.4 %collective-permute-start.22 = (f32[768,256]{1,0:T(8,128)}, f32[768,256]{1,0:T(8,128)S(1)}, u32[]{:S(2)}, u32[]{:S(2)}) collective-permute-start(f32[768,256]{1,0:T(8,128)} %copy-done.14), channel_id=1, source_target_pairs={{0,2},{2,0},{4,6},{6,4},{8,10},{10,8},{12,14},{14,12},{16,18},{18,... | collective-permute-start | bytes 2359304 | tf_op jit(solution)/shard_map/ppermute | solution.py:458
  104.9 11.4 %collective-permute-start.23 = (f32[384,256]{1,0:T(8,128)}, f32[384,256]{1,0:T(8,128)}, u32[]{:S(2)}, u32[]{:S(2)}) collective-permute-start(f32[384,256]{1,0:T(8,128)} %constant_dynamic-slice_fusion.2), channel_id=1, source_target_pairs={{0,1},{1,0},{2,3},{3,2},{4,5},{5,4},{6,7},{7,6},{8,9},{9,8},{10,11... | collective-permute-start | bytes 1179656 | tf_op jit(solution)/shard_map/ppermute | solution.py:505
  108.0 0.9 copy-start.22
  108.0 1.1 copy-start.16
  116.3 1.9 collective-permute-start.24
  118.2 0.7 copy-start.25
  119.0 77.0 %copy-start.1 = (f32[256,128]{1,0:T(8,128)S(1)}, f32[256,128]{1,0:T(8,128)}, u32[]{:S(2)}) copy-start(f32[256,128]{1,0:T(8,128)} %wq_ref.1) | copy-start | bytes 393220
  119.0 77.0 %copy-start.2 = (f32[256,128]{1,0:T(8,128)S(1)}, f32[256,128]{1,0:T(8,128)}, u32[]{:S(2)}) copy-start(f32[256,128]{1,0:T(8,128)} %wk_ref.1) | copy-start | bytes 393220
  119.0 77.0 %copy-start.3 = (f32[256,128]{1,0:T(8,128)S(1)}, f32[256,128]{1,0:T(8,128)}, u32[]{:S(2)}) copy-start(f32[256,128]{1,0:T(8,128)} %wv_ref.1) | copy-start | bytes 393220
  163.5 32.4 %copy-start = (f32[1024,256]{1,0:T(8,128)S(1)}, f32[1024,256]{1,0:T(8,128)}, u32[]{:S(2)}) copy-start(f32[1024,256]{1,0:T(8,128)} %own_ref.1) | copy-start | bytes 3145732
  164.5 2.1 collective-permute-start.27
  167.5 5.0 %collective-permute-start.28 = (f32[256,128]{1,0:T(8,128)S(1)}, f32[256,128]{1,0:T(8,128)S(1)}, u32[]{:S(2)}, u32[]{:S(2)}) collective-permute-start(f32[256,128]{1,0:T(8,128)S(1)} %select_add_fusion.1), channel_id=1, source_target_pairs={{0,4},{2,6},{4,0},{6,2},{8,12},{10,14},{12,8},{14,10},{16,20},{18,... | collective-permute-start | bytes 393224 | tf_op jit(solution)/shard_map/ppermute | solution.py:410
  169.9 80.3 %collective-permute-start.25 = (f32[1024,128]{1,0:T(8,128)}, f32[1024,128]{1,0:T(8,128)}, u32[]{:S(2)}, u32[]{:S(2)}) collective-permute-start(f32[1024,128]{1,0:T(8,128)} %constant_dynamic-slice_fusion), channel_id=1, source_target_pairs={{0,1},{1,0},{2,3},{3,2},{4,5},{5,4},{6,7},{7,6},{8,9},{9,8},{10,11... | collective-permute-start | bytes 1572872 | tf_op jit(solution)/shard_map/ppermute | solution.py:402
  172.6 22.7 %collective-permute-start.29 = (f32[256,128]{1,0:T(8,128)S(1)}, f32[256,128]{1,0:T(8,128)S(1)}, u32[]{:S(2)}, u32[]{:S(2)}) collective-permute-start(f32[256,128]{1,0:T(8,128)S(1)} %add.408), channel_id=1, source_target_pairs={{0,8},{2,10},{4,12},{6,14},{8,0},{10,2},{12,4},{14,6},{16,24},{18,... | collective-permute-start | bytes 393224 | tf_op jit(solution)/shard_map/ppermute | solution.py:410
  195.9 51.7 %collective-permute-start.30 = (f32[256,128]{1,0:T(8,128)}, f32[256,128]{1,0:T(8,128)}, u32[]{:S(2)}, u32[]{:S(2)}) collective-permute-start(f32[256,128]{1,0:T(8,128)} %add.409), channel_id=1, source_target_pairs={{0,16},{2,18},{4,20},{6,22},{8,24},{10,26},{12,28},{14,30},{16,0},... | collective-permute-start | bytes 393224 | tf_op jit(solution)/shard_map/ppermute | solution.py:410
  246.9 0.7 copy-start.5
  247.6 1.6 collective-permute-start.32
  248.6 7.1 %collective-permute-start.31 = (f32[256,128]{1,0:T(8,128)S(1)}, f32[256,128]{1,0:T(8,128)S(1)}, u32[]{:S(2)}, u32[]{:S(2)}) collective-permute-start(f32[256,128]{1,0:T(8,128)S(1)} %add.410), channel_id=1, source_target_pairs={{0,2},{2,0},{4,6},{6,4},{8,10},{10,8},{12,14},{14,12},{16,18},{18,... | collective-permute-start | bytes 393224 | tf_op jit(solution)/shard_map/ppermute | solution.py:410
  250.1 5.5 %collective-permute-start.33 = (f32[256,128]{1,0:T(8,128)S(1)}, f32[256,128]{1,0:T(8,128)S(1)}, u32[]{:S(2)}, u32[]{:S(2)}) collective-permute-start(f32[256,128]{1,0:T(8,128)S(1)} %select_add_fusion), channel_id=1, source_target_pairs={{0,4},{2,6},{4,0},{6,2},{8,12},{10,14},{12,8},{14,10},{16,20},{18,... | collective-permute-start | bytes 393224 | tf_op jit(solution)/shard_map/ppermute | solution.py:410
  252.3 15.7 %collective-permute-start.26 = (f32[1024,128]{1,0:T(8,128)S(1)}, f32[1024,128]{1,0:T(8,128)S(1)}, u32[]{:S(2)}, u32[]{:S(2)}) collective-permute-start(f32[1024,128]{1,0:T(8,128)S(1)} %constant_dynamic-slice_fusion.1), channel_id=1, source_target_pairs={{0,1},{1,0},{2,3},{3,2},{4,5},{5,4},{6,7},{7,6},{8,9},{9,8},{10,11... | collective-permute-start | bytes 1572872 | tf_op jit(solution)/shard_map/ppermute | solution.py:402
  255.6 5.0 %collective-permute-start.34 = (f32[256,128]{1,0:T(8,128)S(1)}, f32[256,128]{1,0:T(8,128)S(1)}, u32[]{:S(2)}, u32[]{:S(2)}) collective-permute-start(f32[256,128]{1,0:T(8,128)S(1)} %add.412), channel_id=1, source_target_pairs={{0,8},{2,10},{4,12},{6,14},{8,0},{10,2},{12,4},{14,6},{16,24},{18,... | collective-permute-start | bytes 393224 | tf_op jit(solution)/shard_map/ppermute | solution.py:410
  260.7 7.2 %collective-permute-start.35 = (f32[256,128]{1,0:T(8,128)S(1)}, f32[256,128]{1,0:T(8,128)S(1)}, u32[]{:S(2)}, u32[]{:S(2)}) collective-permute-start(f32[256,128]{1,0:T(8,128)S(1)} %add.413), channel_id=1, source_target_pairs={{0,16},{2,18},{4,20},{6,22},{8,24},{10,26},{12,28},{14,30},{16,0},... | collective-permute-start | bytes 393224 | tf_op jit(solution)/shard_map/ppermute | solution.py:410
  267.9 1.4 collective-permute-start.36
  (1 other events, 0.7 us)
Sparse Core Ops, SparseCore 0:
  103.7 74.2 all-gather.1

commit v7 on v6

--- a/solution.py
+++ b/solution.py
@@ -8,7 +8,7 @@
 from jax.sharding import PartitionSpec as P
 
 HEAD_SIZE = 32
-GROUP = 4
+GROUP = 2
 SCALE = HEAD_SIZE ** (-0.5)
 MASKED = -1e30
 F32 = jnp.float32
@@ -38,6 +38,29 @@
 
 def wide(first, second):
     return jnp.concatenate([first, second], axis=1)
+
+
+def pair_left(value):
+    rows, cols = value.shape
+    span = min(cols, 2 * HEAD_SIZE)
+    lane = lax.broadcasted_iota(jnp.int32, (rows, span), 1) // HEAD_SIZE
+    result = []
+    for first in range(0, cols, span):
+        part = value[:, first:first + span]
+        parts = [jnp.where(lane == head, part, 0.0) for head in range(span // HEAD_SIZE)]
+        high, low = split(jnp.concatenate(parts, axis=0))
+        result.append(jnp.concatenate([high, low, high], axis=1))
+    return result
+
+
+def pair_products(lefts, high, low):
+    span = high.shape[0] // len(lefts)
+    result = []
+    for at, left in enumerate(lefts):
+        here = slice(at * span, (at + 1) * span)
+        right = jnp.concatenate([high[here], high[here], low[here]], axis=0)
+        result.append(mul(left, right))
+    return jnp.concatenate(result, axis=0)
 
 
 def fold(value):
@@ -85,8 +108,6 @@
     value_high, value_low = split(pairs[:, cols:])
     key_both, value_both = wide(key_high, key_low), wide(value_high, value_low)
     turned_high, turned_low = split(jnp.transpose(pairs))
-    turned_keys = jnp.concatenate([turned_high[:cols], turned_high[:cols]], axis=0)
-    turned_values = jnp.concatenate([turned_high[cols:], turned_high[cols:]], axis=0)
     own = (inputs[0][:rows], inputs[1][:rows])
     query = mul3(own, w_query) * SCALE
     grad_mixed = grad_ref[...]
@@ -103,8 +124,8 @@
         ]
         return sum(parts[1:], parts[0])
 
-    q_high, q_low = split(spread(query))
-    scores = mul(wide(q_high, q_low), turned_keys) + mul(q_high, turned_low[:cols]) + bias_ref[0]
+    scores = pair_products(pair_left(query), turned_high[:cols], turned_low[:cols])
+    scores = scores + bias_ref[0]
     top = jnp.max(scores, axis=1, keepdims=True)
     probs = jnp.exp(scores - top)
     total = jnp.sum(probs, axis=1, keepdims=True)
@@ -114,8 +135,7 @@
     mixed = gather(weighted)
     grad_part = spread(grad_mixed)
     delta = jnp.sum(grad_part * weighted, axis=1, keepdims=True)
-    g_high, g_low = split(grad_part)
-    grad_probs = mul(wide(g_high, g_low), turned_values) + mul(g_high, turned_low[cols:])
+    grad_probs = pair_products(pair_left(grad_mixed), turned_high[cols:], turned_low[cols:])
     s_high, s_low = split(probs * (grad_probs - delta))
     back = (fold(mul(s_high, key_both)) + mul(s_low, key_high)) * (inverse * SCALE)
     grad_query = gather(back)
@@ -251,11 +271,9 @@
         @pl.when(kind % 2 == 1)
         def _():
             pairs = pair_mem[block, :]
-            for head in range(heads):
-                here = lane == head
-                at = pl.ds(head * rows, rows)
-                key_mem[at, :] = wide(*split(jnp.where(here, pairs[:, :cols], 0.0)))
-                value_mem[at, :] = wide(*split(jnp.where(here, pairs[:, cols:], 0.0)))
+            for memory, value in ((key_mem, pairs[:, :cols]), (value_mem, pairs[:, cols:])):
+                for at, left in enumerate(pair_left(value)):
+                    memory[at] = left
 
         pltpu.make_async_copy(buffer.at[turn], buffer.at[turn], sems.at[0, turn]).wait()
         pltpu.make_async_copy(grads.at[turn], grads.at[turn], sems.at[1, turn]).wait()
@@ -265,8 +283,6 @@
         g_high, g_low = split(grad)
         q_both, g_both = wide(q_high, q_low), wide(g_high, g_low)
         turned_high, turned_low = split(jnp.transpose(wide(query, grad)))
-        turned_q = jnp.concatenate([turned_high[:cols], turned_high[:cols]], axis=0)
-        turned_g = jnp.concatenate([turned_high[cols:], turned_high[cols:]], axis=0)
         masks, stats = [], []
         for at in range(GROUP):
             entry = readers_ref[2, step * GROUP + at]
@@ -277,9 +293,13 @@
         masks.append(jnp.zeros((8 - GROUP, rows), F32))
         bias = mul(jnp.concatenate(masks, axis=0).astype(BF16), marks, 0, 0)
         stat = jnp.concatenate(stats, axis=1)
-        keys, values = key_mem[...], value_mem[...]
-        scores = mul(keys, turned_q) + mul(keys[:, :cols], turned_low[:cols])
-        grad_probs = mul(values, turned_g) + mul(values[:, :cols], turned_low[cols:])
+        each = range(key_mem.shape[0])
+        scores = pair_products(
+            [key_mem[at] for at in each], turned_high[:cols], turned_low[:cols]
+        )
+        grad_probs = pair_products(
+            [value_mem[at] for at in each], turned_high[cols:], turned_low[cols:]
+        )
 
         def rows_of(first):
             return [
@@ -324,7 +344,7 @@
 ):
     node_rows, width = own_feats.shape
     cols = w_query.shape[1]
-    heads = cols // HEAD_SIZE
+    span = min(cols, 2 * HEAD_SIZE)
     held = pl.BlockSpec(memory_space=pltpu.VMEM)
     scalars = pl.BlockSpec(memory_space=pltpu.SMEM)
     afar = pl.BlockSpec(memory_space=pl.ANY)
@@ -336,8 +356,8 @@
         out_specs=(held, held, held),
         scratch_shapes=[
             pltpu.VMEM((node_rows, 2 * cols), F32),
-            pltpu.VMEM((heads * rows, 2 * cols), BF16),
-            pltpu.VMEM((heads * rows, 2 * cols), BF16),
+            pltpu.VMEM((cols // span, span // HEAD_SIZE * rows, 3 * span), BF16),
+            pltpu.VMEM((cols // span, span // HEAD_SIZE * rows, 3 * span), BF16),
             pltpu.VMEM((node_rows, cols), F32),
             pltpu.VMEM((node_rows, cols), F32),
             pltpu.VMEM((2, GROUP * rows, width), F32),
@@ -486,6 +506,13 @@
             first = slot * block_count + 5
             pieces.append((value, 3 * at * rows, 3 * rows, first))
             pieces.append((swapped, 3 * at * rows, 3 * rows, half + first))
+
+    def keep_ring(values, swapped, slots):
+        for at, slot in enumerate(slots):
+            first = slot * block_count
+            pieces.append((values[at], 0, 5 * rows, first))
+            pieces.append((swapped[at], 0, 5 * rows, half + first))
+            all_notes.extend([values[at][5 * rows:], swapped[at][5 * rows:]])
 
     slots, lack, lack_slots, notes = (1, 2), (), (), ()
     for step in range(1, 5):
@@ -503,23 +530,30 @@
         else:
             coming = ()
         more = (lax.ppermute(lacking(held), "head", other_head),)
-        swapped = tuple(swap(value) for value in held)
-        swapped_lack = tuple(swap(value) for value in lack)
-        if step < 4:
-            coming, held, more, swapped, lack, swapped_lack, notes = lax.optimization_barrier(
-                (coming, held, more, swapped, lack, swapped_lack, notes)
-            )
+        if step == 3:
+            waiting = (held, slots, lack, lack_slots)
+            coming, held, more, notes = lax.optimization_barrier((coming, held, more, notes))
         else:
-            held, swapped, lack, swapped_lack = lax.optimization_barrier(
-                (held, swapped, lack, swapped_lack)
-            )
-        for at, slot in enumerate(slots):
-            first = slot * block_count
-            pieces.append((held[at], 0, 5 * rows, first))
-            pieces.append((swapped[at], 0, 5 * rows, half + first))
-            all_notes.extend([held[at][5 * rows:], swapped[at][5 * rows:]])
-        if lack:
-            keep(lack[0], swapped_lack[0], lack_slots)
+            swapped = tuple(swap(value) for value in held)
+            swapped_lack = tuple(swap(value) for value in lack)
+            if step < 3:
+                coming, held, more, swapped, lack, swapped_lack = lax.optimization_barrier(
+                    (coming, held, more, swapped, lack, swapped_lack)
+                )
+            else:
+                old, old_slots, old_lack, old_lack_slots = waiting
+                old_swapped = tuple(swap(value) for value in old)
+                old_swapped_lack = tuple(swap(value) for value in old_lack)
+                held, swapped, lack, swapped_lack, old_swapped, old_swapped_lack = (
+                    lax.optimization_barrier(
+                        (held, swapped, lack, swapped_lack, old_swapped, old_swapped_lack)
+                    )
+                )
+                keep_ring(old, old_swapped, old_slots)
+                keep(old_lack[0], old_swapped_lack[0], old_lack_slots)
+            keep_ring(held, swapped, slots)
+            if lack:
+                keep(lack[0], swapped_lack[0], lack_slots)
         lack, lack_slots = more, slots
         if step == 3:
             held, slots = (jnp.concatenate(coming, axis=0),), (7,)

time: 280 us -> 266 us (0.950)
  Pallas kernels: 95.4 us -> 73.2 us
  starting transfers between devices: 22.6 us -> 31 us
  waiting for transfers between devices: 81.2 us -> 84.8 us
    pallas_call x1, Pallas kernels: 50.9 us -> 34.7 us  [attend_backward(): pl.pallas_call(backward_kernel, out_shape=(jax.ShapeDtypeStruct((node_row...]
    ppermute x10, starting transfers between devices: 4.17 us -> 14.2 us  [from_across(): return lax.ppermute(value, 'dom', [(at, at ^ bit) for at in range(size)])]
    ppermute x4, waiting for transfers between devices: 6.83 us -> 16.3 us  [gather_feats(): more = (lax.ppermute(lacking(held), 'head', other_head),)]
    ppermute x1, waiting for transfers between devices: 8.4 us -> 0.81 us  [gather_feats(): lax.ppermute(held[0][:3 * rows], 'dom', onward)]
    pallas_call x1, Pallas kernels: 44.5 us -> 38.5 us  [attend_forward(): pl.pallas_call(functools.partial(forward_kernel, entries, layout, len(arr...]
    ppermute x13, waiting for transfers between devices: 1.33 us -> 5.25 us  [swap(): return lax.ppermute(value, 'dom', across)]
  transfers between devices with their start and end apart: 38 -> 38, of which waited for: 17 -> 21; matrix products, arithmetic and copies ran while one was open for 13% -> 13% of each run, Pallas kernels for 34% -> 28%
where the time goes in v7:
time: 266 us; the launch traced here: 265 us
  waiting for transfers between devices  84.8 us (32%)
  Pallas kernels  73.2 us (28%)
  starting transfers between devices  31 us (12%)
  local copies, waits for them, and re-layouts  23.8 us (9%)
  blocking collectives  21.4 us (8%)
  between operations  14.6 us (5%)
  other arithmetic  14.2 us (5%)
    pallas_call x1, Pallas kernels, attend_forward(): pl.pallas_call(functools.partial(forward_kernel, entries, layout, len(arr...  38.5 us
    pallas_call x1, Pallas kernels, attend_backward(): pl.pallas_call(backward_kernel, out_shape=(jax.ShapeDtypeStruct((node_row...  34.7 us
    ppermute x2, waiting for transfers between devices, gather_feats(): lax.ppermute(held[0], 'dom', onward)  21.5 us
    all_gather x1, blocking collectives, per_device(): all_stats = lax.all_gather(stats, 'dom', axis=0, tiled=True)  21.4 us
    ppermute x4, waiting for transfers between devices, gather_feats(): more = (lax.ppermute(lacking(held), 'head', other_head),)  16.3 us
    ppermute x1, waiting for transfers between devices, gather_feats(): lax.ppermute(start, 'dom', onward)  16 us
    ppermute x10, waiting for transfers between devices, from_across(): return lax.ppermute(value, 'dom', [(at, at ^ bit) for at in range(size)])  15.8 us
    ppermute x10, starting transfers between devices, from_across(): return lax.ppermute(value, 'dom', [(at, at ^ bit) for at in range(size)])  14.2 us
  transfers between devices with their start and end apart: 38, of which 21 were waited for; matrix products, arithmetic and copies ran while one was open for 13% of the time, Pallas kernels for 28%

profile of v7, /device:TPU:0, one launch (start us, length us, event | category | flops | bytes accessed | tf_op | source)
XLA Modules:
  0.0 264.7 jit_solution(2430334173951318065)
XLA Ops:
  7.8 0.7 multiply_add_fusion
  8.5 0.7 fusion.10
  9.2 0.8 convert_element_type.58
  9.9 1.1 constant_dynamic-slice_fusion.9
  11.1 0.9 maximum_maximum_fusion
  12.0 2.8 %collective-permute-start = (f32[672,256]{1,0:T(8,128)}, f32[672,256]{1,0:T(8,128)S(1)}, u32[]{:S(2)}, u32[]{:S(2)}) collective-permute-start(f32[672,256]{1,0:T(8,128)} %maximum_maximum_fusion), channel_id=1, source_target_pairs={{0,8},{2,10},{8,16},{10,18},{16,24},{18,26},{24,28},{26,30},{28,20... | collective-permute-start | bytes 2064392 | tf_op jit(solution)/shard_map/ppermute | solution.py:498
  14.8 16.0 %collective-permute-done.refs_2_ = f32[672,256]{1,0:T(8,128)S(1)} collective-permute-done((f32[672,256]{1,0:T(8,128)}, f32[672,256]{1,0:T(8,128)S(1)}, u32[]{:S(2)}, u32[]{:S(2)}) %collective-permute-start) | collective-permute-done | bytes 688160 | tf_op jit(solution)/shard_map/ppermute | solution.py:498
  30.8 1.5 collective-permute-done.1.refs_4_
  32.5 1.6 collective-permute-start.5
  34.1 1.6 collective-permute-start.3
  37.2 13.2 %collective-permute-done.3.refs_6_ = f32[672,256]{1,0:T(8,128)} collective-permute-done((f32[672,256]{1,0:T(8,128)S(1)}, f32[672,256]{1,0:T(8,128)}, u32[]{:S(2)}, u32[]{:S(2)}) %collective-permute-start.3) | collective-permute-done | bytes 688160 | tf_op jit(solution)/shard_map/ppermute | solution.py:521
  50.4 1.3 collective-permute-done.4.refs_8_
  51.7 0.8 copy-done.17
  52.8 0.9 copy-done.12
  53.7 1.8 fusion.34.refs_25_
  56.1 1.6 collective-permute-start.8
  58.4 1.1 constant_dynamic-slice_fusion.5
  59.4 1.0 constant_dynamic-slice_fusion.6
  61.7 1.4 constant_dynamic-update-slice_fusion.6
  63.1 1.4 constant_dynamic-update-slice_fusion.5
  64.4 1.4 constant_dynamic-update-slice_fusion.4
  65.8 8.3 %collective-permute-done.8.refs_12_ = f32[672,256]{1,0:T(8,128)S(1)} collective-permute-done((f32[672,256]{1,0:T(8,128)}, f32[672,256]{1,0:T(8,128)S(1)}, u32[]{:S(2)}, u32[]{:S(2)}) %collective-permute-start.8) | collective-permute-done | bytes 688160 | tf_op jit(solution)/shard_map/ppermute | solution.py:521
  74.2 1.6 collective-permute-done.9.refs_14_
  75.7 4.3 %collective-permute-done.10.refs_16_ = f32[768,256]{1,0:T(8,128)S(1)} collective-permute-done((f32[768,256]{1,0:T(8,128)S(1)}, f32[768,256]{1,0:T(8,128)S(1)}, u32[]{:S(2)}, u32[]{:S(2)}) %collective-permute-start.10) | collective-permute-done | bytes 786464 | tf_op jit(solution)/shard_map/ppermute | solution.py:532
  80.1 0.8 copy-done.13
  81.9 1.6 collective-permute-start.14
  84.0 0.8 constant_dynamic-update-slice_fusion.3
  84.7 0.8 constant_dynamic-update-slice_fusion.2
  85.5 0.8 constant_dynamic-update-slice_fusion.1
  86.2 4.8 %collective-permute-done.15 = f32[288,256]{1,0:T(8,128)S(1)} collective-permute-done((f32[288,256]{1,0:T(8,128)S(1)}, f32[288,256]{1,0:T(8,128)S(1)}, u32[]{:S(2)}, u32[]{:S(2)}) %collective-permute-start.15) | collective-permute-done | bytes 294944 | tf_op jit(solution)/shard_map/ppermute | solution.py:526
  91.0 0.8 collective-permute-done.14
  91.8 8.3 %collective-permute-done.16.refs_20_ = f32[768,256]{1,0:T(8,128)} collective-permute-done((f32[768,256]{1,0:T(8,128)S(1)}, f32[768,256]{1,0:T(8,128)}, u32[]{:S(2)}, u32[]{:S(2)}) %collective-permute-start.16) | collective-permute-done | bytes 786464 | tf_op jit(solution)/shard_map/ppermute | solution.py:532
  101.4 0.8 constant_dynamic-slice_fusion.2
  102.2 2.3 collective-permute-done.20.refs_13_
  105.7 1.0 collective-permute-done.18.refs_19_
  106.7 0.9 copy-done.16
  109.0 0.7 pad.16.clone
  110.7 1.2 gather_fusion
  112.3 3.7 %collective-permute-done.23.refs_22_ = f32[384,256]{1,0:T(8,128)} collective-permute-done((f32[384,256]{1,0:T(8,128)}, f32[384,256]{1,0:T(8,128)}, u32[]{:S(2)}, u32[]{:S(2)}) %collective-permute-start.23) | collective-permute-done | bytes 393248 | tf_op jit(solution)/shard_map/ppermute | solution.py:532
  116.6 1.3 collective-permute-done.24.refs_23_
  118.0 0.7 copy-done.25
  118.7 38.5 %attend_forward.1 = (f32[16384,256]{1,0:T(8,128)}, f32[1024,256]{1,0:T(8,128)}, f32[1024,256]{1,0:T(8,128)}, f32[8,8,128]{2,1,0:T(8,128)}, f32[256,128]{1,0:T(8,128)}, /*index=5*/f32[128,256]{1,0:T(8,128)}) custom-call(s32[8,8]{1,0:T(8,128)} %get-tuple-element.96.ids, f32[1024,256]{1,0:T(8,128)} %own_ref.1, f32[1024,256]{1,0:T(8,128)} %collective-permute-done.2.refs_1_, ...), custom_call_target="tpu_custom_call" | custom-call | tf_op jit(solution)/shard_map/attend_forward/pallas_call | solution.py:187
  157.2 1.0 fusion.33
  158.2 1.1 collective-permute-start.27
  159.4 1.0 collective-permute-done.27
  160.3 0.9 select_add_fusion.1
  161.8 1.9 constant_dynamic-slice_fusion
  163.7 0.7 collective-permute-start.25
  164.4 2.0 collective-permute-done.28
  166.3 1.6 collective-permute-start.29
  168.0 21.4 %all_gather.7.stats_ref = f32[128,8,128]{2,1,0:T(8,128)S(1)} all-gather(f32[8,8,128]{2,1,0:T(8,128)} %get-tuple-element.86), channel_id=1, replica_groups=mesh['dom'=16,'head'=2] {'dom'}, dimensions={0}, use_global_device_ids=true | all-gather | bytes 557056 | tf_op jit(solution)/shard_map/all_gather | solution.py:614
  190.1 34.7 %attend_backward.1 = (f32[1024,256]{1,0:T(8,128)S(1)}, f32[256,128]{1,0:T(8,128)S(1)}, f32[256,128]{1,0:T(8,128)S(1)}) custom-call(s32[3,40]{1,0:T(4,128)S(1)} %add_add_fusion.steps_ref, s32[4,80]{1,0:T(4,128)S(1)} %pad_add_fusion.1.readers_ref, f32[16384,256]{1,0:T(8,128)} %get-tuple-element.84.feats_ref, ...), custom_call_target="tpu_custom_call" | custom-call | tf_op jit(solution)/shard_map/attend_backward/pallas_call | solution.py:352
  225.5 9.0 %collective-permute-start.32 = (f32[256,128]{1,0:T(8,128)S(1)}, f32[256,128]{1,0:T(8,128)S(1)}, u32[]{:S(2)}, u32[]{:S(2)}) collective-permute-start(f32[256,128]{1,0:T(8,128)S(1)} %broadcast_select_fusion.3), channel_id=1, source_target_pairs={{0,2},{2,0},{4,6},{6,4},{8,10},{10,8},{12,14},{14,12},{16,18},{18,... | collective-permute-start | bytes 393224 | tf_op jit(solution)/shard_map/ppermute | solution.py:430
  234.5 1.0 add.414
  235.6 0.9 select_add_fusion
  236.7 2.1 dynamic-slice_add_fusion.1
  238.7 1.5 collective-permute-start.26
  240.2 2.3 collective-permute-done.33
  242.6 0.7 broadcast_select_fusion
  243.3 4.4 %collective-permute-done.34 = f32[256,128]{1,0:T(8,128)S(1)} collective-permute-done((f32[256,128]{1,0:T(8,128)S(1)}, f32[256,128]{1,0:T(8,128)S(1)}, u32[]{:S(2)}, u32[]{:S(2)}) %collective-permute-start.34) | collective-permute-done | bytes 131104 | tf_op jit(solution)/shard_map/ppermute | solution.py:430
  247.7 1.6 collective-permute-start.35
  250.0 5.7 %collective-permute-done.35 = f32[256,128]{1,0:T(8,128)S(1)} collective-permute-done((f32[256,128]{1,0:T(8,128)S(1)}, f32[256,128]{1,0:T(8,128)S(1)}, u32[]{:S(2)}, u32[]{:S(2)}) %collective-permute-start.35) | collective-permute-done | bytes 131104 | tf_op jit(solution)/shard_map/ppermute | solution.py:430
  255.8 0.9 dynamic-slice_add_fusion
  257.1 0.7 broadcast_select_fusion.1
  (159 shorter events, 15.7 us)
Async XLA Ops:
  7.2 46.5 %copy-start.23 = (f32[128,256]{1,0:T(8,128)S(1)}, f32[128,256]{1,0:T(8,128)}, u32[]{:S(2)}) copy-start(f32[128,256]{1,0:T(8,128)} %refs_30_.1) | copy-start | bytes 393220
  7.2 46.5 %copy-start.6 = (f32[1024,256]{1,0:T(8,128)S(1)}, f32[1024,256]{1,0:T(8,128)}, u32[]{:S(2)}) copy-start(f32[1024,256]{1,0:T(8,128)} %refs_24_.1) | copy-start | bytes 3145732
  7.2 182.9 %all-gather.2.cloned.1.call-start = ((), (), s32[]{:S(2)}) async-start(), calls=%async_computation | async-start | bytes 8912896 | tf_op jit(solution)/shard_map/all_gather | solution.py:604
  7.2 25.1 %collective-permute-start.2 = (f32[1024,256]{1,0:T(8,128)}, f32[1024,256]{1,0:T(8,128)}, u32[]{:S(2)}, u32[]{:S(2)}) collective-permute-start(f32[1024,256]{1,0:T(8,128)} %own_ref.1), channel_id=1, source_target_pairs={{0,2},{2,0},{4,6},{6,4},{8,10},{10,8},{12,14},{14,12},{16,18},{18,... | collective-permute-start | bytes 3145736 | tf_op jit(solution)/shard_map/ppermute | solution.py:478
  12.0 18.8 %collective-permute-start = (f32[672,256]{1,0:T(8,128)}, f32[672,256]{1,0:T(8,128)S(1)}, u32[]{:S(2)}, u32[]{:S(2)}) collective-permute-start(f32[672,256]{1,0:T(8,128)} %maximum_maximum_fusion), channel_id=1, source_target_pairs={{0,8},{2,10},{8,16},{10,18},{16,24},{18,26},{24,28},{26,30},{28,20... | collective-permute-start | bytes 2064392 | tf_op jit(solution)/shard_map/ppermute | solution.py:498
  14.8 17.5 %collective-permute-start.1 = (f32[672,256]{1,0:T(8,128)}, f32[672,256]{1,0:T(8,128)S(1)}, u32[]{:S(2)}, u32[]{:S(2)}) collective-permute-start(f32[672,256]{1,0:T(8,128)} %maximum_maximum_fusion), channel_id=1, source_target_pairs={{8,0},{10,2},{16,8},{18,10},{24,16},{26,18},{28,24},{30,26},{20,28... | collective-permute-start | bytes 2064392 | tf_op jit(solution)/shard_map/ppermute | solution.py:498
  30.8 35.0 %copy-start.10 = (f32[672,256]{1,0:T(8,128)}, f32[672,256]{1,0:T(8,128)S(1)}, u32[]{:S(2)}) copy-start(f32[672,256]{1,0:T(8,128)S(1)} %collective-permute-done.refs_2_) | copy-start | bytes 2064388
  32.3 23.1 %copy-start.11 = (f32[672,256]{1,0:T(8,128)}, f32[672,256]{1,0:T(8,128)S(1)}, u32[]{:S(2)}) copy-start(f32[672,256]{1,0:T(8,128)S(1)} %collective-permute-done.1.refs_4_) | copy-start | bytes 2064388
  32.5 19.2 %collective-permute-start.5 = (f32[768,256]{1,0:T(8,128)S(1)}, f32[768,256]{1,0:T(8,128)S(1)}, u32[]{:S(2)}, u32[]{:S(2)}) collective-permute-start(f32[768,256]{1,0:T(8,128)S(1)} %pad_maximum_fusion), channel_id=1, source_target_pairs={{0,1},{1,0},{2,3},{3,2},{4,5},{5,4},{6,7},{7,6},{8,9},{9,8},{10,11... | collective-permute-start | bytes 2359304 | tf_op jit(solution)/shard_map/ppermute | solution.py:532
  34.1 16.3 %collective-permute-start.3 = (f32[672,256]{1,0:T(8,128)S(1)}, f32[672,256]{1,0:T(8,128)}, u32[]{:S(2)}, u32[]{:S(2)}) collective-permute-start(f32[672,256]{1,0:T(8,128)S(1)} %collective-permute-done.refs_2_), channel_id=1, source_target_pairs={{0,8},{2,10},{8,16},{10,18},{16,24},{18,26},{24,28},{26,30},{28,20... | collective-permute-start | bytes 2064392 | tf_op jit(solution)/shard_map/ppermute | solution.py:521
  35.6 16.0 %collective-permute-start.4 = (f32[672,256]{1,0:T(8,128)S(1)}, f32[672,256]{1,0:T(8,128)}, u32[]{:S(2)}, u32[]{:S(2)}) collective-permute-start(f32[672,256]{1,0:T(8,128)S(1)} %collective-permute-done.1.refs_4_), channel_id=1, source_target_pairs={{8,0},{10,2},{16,8},{18,10},{24,16},{26,18},{28,24},{30,26},{20,28... | collective-permute-start | bytes 2064392 | tf_op jit(solution)/shard_map/ppermute | solution.py:521
  36.1 15.6 %collective-permute-start.6 = (f32[672,256]{1,0:T(8,128)S(1)}, f32[672,256]{1,0:T(8,128)S(1)}, u32[]{:S(2)}, u32[]{:S(2)}) collective-permute-start(f32[672,256]{1,0:T(8,128)S(1)} %collective-permute-done.refs_2_), channel_id=1, source_target_pairs={{0,2},{2,0},{4,6},{6,4},{8,10},{10,8},{12,14},{14,12},{16,18},{18,... | collective-permute-start | bytes 2064392 | tf_op jit(solution)/shard_map/ppermute | solution.py:478
  36.1 15.6 %collective-permute-start.7 = (f32[672,256]{1,0:T(8,128)S(1)}, f32[672,256]{1,0:T(8,128)S(1)}, u32[]{:S(2)}, u32[]{:S(2)}) collective-permute-start(f32[672,256]{1,0:T(8,128)S(1)} %collective-permute-done.1.refs_4_), channel_id=1, source_target_pairs={{0,2},{2,0},{4,6},{6,4},{8,10},{10,8},{12,14},{14,12},{16,18},{18,... | collective-permute-start | bytes 2064392 | tf_op jit(solution)/shard_map/ppermute | solution.py:478
  50.4 5.1 %collective-permute-start.17 = (f32[32,256]{1,0:T(8,128)S(1)}, f32[32,256]{1,0:T(8,128)S(1)}, u32[]{:S(2)}, u32[]{:S(2)}) collective-permute-start(f32[32,256]{1,0:T(8,128)S(1)} %get-tuple-element.110), channel_id=1, source_target_pairs={{0,2},{2,0},{4,6},{6,4},{8,10},{10,8},{12,14},{14,12},{16,18},{18,... | collective-permute-start | bytes 98312 | tf_op jit(solution)/shard_map/ppermute | solution.py:478
  51.7 0.9 copy-start.17
  51.7 1.1 copy-start.18
  52.8 0.9 copy-start.12
  53.7 7.4 %collective-permute-start.11 = (f32[672,256]{1,0:T(8,128)}, f32[672,256]{1,0:T(8,128)}, u32[]{:S(2)}, u32[]{:S(2)}) collective-permute-start(f32[672,256]{1,0:T(8,128)} %collective-permute-done.3.refs_6_), channel_id=1, source_target_pairs={{0,2},{2,0},{4,6},{6,4},{8,10},{10,8},{12,14},{14,12},{16,18},{18,... | collective-permute-start | bytes 2064392 | tf_op jit(solution)/shard_map/ppermute | solution.py:478
  56.1 18.1 %collective-permute-start.8 = (f32[672,256]{1,0:T(8,128)}, f32[672,256]{1,0:T(8,128)S(1)}, u32[]{:S(2)}, u32[]{:S(2)}) collective-permute-start(f32[672,256]{1,0:T(8,128)} %collective-permute-done.3.refs_6_), channel_id=1, source_target_pairs={{0,8},{2,10},{8,16},{10,18},{16,24},{18,26},{24,28},{26,30},{28,20... | collective-permute-start | bytes 2064392 | tf_op jit(solution)/shard_map/ppermute | solution.py:521
  57.7 8.1 %collective-permute-start.12 = (f32[672,256]{1,0:T(8,128)}, f32[672,256]{1,0:T(8,128)S(1)}, u32[]{:S(2)}, u32[]{:S(2)}) collective-permute-start(f32[672,256]{1,0:T(8,128)} %collective-permute-done.4.refs_8_), channel_id=1, source_target_pairs={{0,2},{2,0},{4,6},{6,4},{8,10},{10,8},{12,14},{14,12},{16,18},{18,... | collective-permute-start | bytes 2064392 | tf_op jit(solution)/shard_map/ppermute | solution.py:478
  57.9 17.8 %collective-permute-start.9 = (f32[672,256]{1,0:T(8,128)}, f32[672,256]{1,0:T(8,128)S(1)}, u32[]{:S(2)}, u32[]{:S(2)}) collective-permute-start(f32[672,256]{1,0:T(8,128)} %collective-permute-done.4.refs_8_), channel_id=1, source_target_pairs={{8,0},{10,2},{16,8},{18,10},{24,16},{26,18},{28,24},{30,26},{20,28... | collective-permute-start | bytes 2064392 | tf_op jit(solution)/shard_map/ppermute | solution.py:521
  60.5 19.5 %collective-permute-start.10 = (f32[768,256]{1,0:T(8,128)S(1)}, f32[768,256]{1,0:T(8,128)S(1)}, u32[]{:S(2)}, u32[]{:S(2)}) collective-permute-start(f32[768,256]{1,0:T(8,128)S(1)} %pad_maximum_fusion.1), channel_id=1, source_target_pairs={{0,1},{1,0},{2,3},{3,2},{4,5},{5,4},{6,7},{7,6},{8,9},{9,8},{10,11... | collective-permute-start | bytes 2359304 | tf_op jit(solution)/shard_map/ppermute | solution.py:532
  61.1 18.9 %collective-permute-start.13 = (f32[768,256]{1,0:T(8,128)}, f32[768,256]{1,0:T(8,128)S(1)}, u32[]{:S(2)}, u32[]{:S(2)}) collective-permute-start(f32[768,256]{1,0:T(8,128)} %copy-done.12), channel_id=1, source_target_pairs={{0,2},{2,0},{4,6},{6,4},{8,10},{10,8},{12,14},{14,12},{16,18},{18,... | collective-permute-start | bytes 2359304 | tf_op jit(solution)/shard_map/ppermute | solution.py:478
  65.8 18.1 %copy-start.24 = (f32[320,256]{1,0:T(8,128)S(1)}, f32[320,256]{1,0:T(8,128)}, u32[]{:S(2)}) copy-start(f32[320,256]{1,0:T(8,128)} %constant_dynamic-update-slice_fusion.4) | copy-start | bytes 983044
  65.8 34.3 %copy-start.19 = (f32[672,256]{1,0:T(8,128)}, f32[672,256]{1,0:T(8,128)S(1)}, u32[]{:S(2)}) copy-start(f32[672,256]{1,0:T(8,128)S(1)} %collective-permute-done.12.refs_9_) | copy-start | bytes 2064388
  74.2 32.5 %copy-start.7 = (f32[672,256]{1,0:T(8,128)}, f32[672,256]{1,0:T(8,128)S(1)}, u32[]{:S(2)}) copy-start(f32[672,256]{1,0:T(8,128)S(1)} %collective-permute-done.8.refs_12_) | copy-start | bytes 2064388
  75.7 31.0 %copy-start.9 = (f32[672,256]{1,0:T(8,128)}, f32[672,256]{1,0:T(8,128)S(1)}, u32[]{:S(2)}) copy-start(f32[672,256]{1,0:T(8,128)S(1)} %collective-permute-done.9.refs_14_) | copy-start | bytes 2064388
  80.0 0.9 copy-start.13
  80.0 1.2 copy-start.14
  81.3 34.7 %copy-start.26 = (s32[8,7,128]{2,0,1:T(8,128)S(1)}, s32[8,7,128]{2,0,1:T(8,128)}, u32[]{:S(2)}) copy-start(s32[8,7,128]{2,0,1:T(8,128)} %param.16) | copy-start | bytes 86020
  81.3 18.8 %collective-permute-start.16 = (f32[768,256]{1,0:T(8,128)S(1)}, f32[768,256]{1,0:T(8,128)}, u32[]{:S(2)}, u32[]{:S(2)}) collective-permute-start(f32[768,256]{1,0:T(8,128)S(1)} %pad_maximum_fusion.2), channel_id=1, source_target_pairs={{0,1},{1,0},{2,3},{3,2},{4,5},{5,4},{6,7},{7,6},{8,9},{9,8},{10,11... | collective-permute-start | bytes 2359304 | tf_op jit(solution)/shard_map/ppermute | solution.py:532
  81.9 9.9 %collective-permute-start.14 = (f32[384,256]{1,0:T(8,128)S(1)}, f32[384,256]{1,0:T(8,128)S(1)}, u32[]{:S(2)}, u32[]{:S(2)}) collective-permute-start(f32[384,256]{1,0:T(8,128)S(1)} %get-tuple-element.99), channel_id=1, source_target_pairs={{0,8},{2,10},{8,16},{10,18},{16,24},{18,26},{24,28},{26,30},{28,20... | collective-permute-start | bytes 1179656 | tf_op jit(solution)/shard_map/ppermute | solution.py:525
  83.5 7.5 %collective-permute-start.15 = (f32[288,256]{1,0:T(8,128)S(1)}, f32[288,256]{1,0:T(8,128)S(1)}, u32[]{:S(2)}, u32[]{:S(2)}) collective-permute-start(f32[288,256]{1,0:T(8,128)S(1)} %slice.92), channel_id=1, source_target_pairs={{8,0},{10,2},{16,8},{18,10},{24,16},{26,18},{28,24},{30,26},{20,28... | collective-permute-start | bytes 884744 | tf_op jit(solution)/shard_map/ppermute | solution.py:526
  100.2 17.8 %copy-start.8 = (f32[672,256]{1,0:T(8,128)}, f32[672,256]{1,0:T(8,128)S(1)}, u32[]{:S(2)}) copy-start(f32[672,256]{1,0:T(8,128)S(1)} %constant_dynamic-update-slice_fusion.10.refs_18_) | copy-start | bytes 2064388
  100.2 5.4 %collective-permute-start.22 = (f32[768,256]{1,0:T(8,128)}, f32[768,256]{1,0:T(8,128)S(1)}, u32[]{:S(2)}, u32[]{:S(2)}) collective-permute-start(f32[768,256]{1,0:T(8,128)} %copy-done.13), channel_id=1, source_target_pairs={{0,2},{2,0},{4,6},{6,4},{8,10},{10,8},{12,14},{14,12},{16,18},{18,... | collective-permute-start | bytes 2359304 | tf_op jit(solution)/shard_map/ppermute | solution.py:478
  100.3 6.4 %collective-permute-start.19 = (f32[768,256]{1,0:T(8,128)}, f32[768,256]{1,0:T(8,128)S(1)}, u32[]{:S(2)}, u32[]{:S(2)}) collective-permute-start(f32[768,256]{1,0:T(8,128)} %collective-permute-done.16.refs_20_), channel_id=1, source_target_pairs={{0,2},{2,0},{4,6},{6,4},{8,10},{10,8},{12,14},{14,12},{16,18},{18,... | collective-permute-start | bytes 2359304 | tf_op jit(solution)/shard_map/ppermute | solution.py:478
  100.8 3.7 %collective-permute-start.20 = (f32[672,256]{1,0:T(8,128)S(1)}, f32[672,256]{1,0:T(8,128)S(1)}, u32[]{:S(2)}, u32[]{:S(2)}) collective-permute-start(f32[672,256]{1,0:T(8,128)S(1)} %collective-permute-done.8.refs_12_), channel_id=1, source_target_pairs={{0,2},{2,0},{4,6},{6,4},{8,10},{10,8},{12,14},{14,12},{16,18},{18,... | collective-permute-start | bytes 2064392 | tf_op jit(solution)/shard_map/ppermute | solution.py:478
  100.9 4.8 %collective-permute-start.21 = (f32[672,256]{1,0:T(8,128)S(1)}, f32[672,256]{1,0:T(8,128)S(1)}, u32[]{:S(2)}, u32[]{:S(2)}) collective-permute-start(f32[672,256]{1,0:T(8,128)S(1)} %collective-permute-done.9.refs_14_), channel_id=1, source_target_pairs={{0,2},{2,0},{4,6},{6,4},{8,10},{10,8},{12,14},{14,12},{16,18},{18,... | collective-permute-start | bytes 2064392 | tf_op jit(solution)/shard_map/ppermute | solution.py:478
  101.3 5.3 %collective-permute-start.18 = (f32[672,256]{1,0:T(8,128)S(1)}, f32[672,256]{1,0:T(8,128)S(1)}, u32[]{:S(2)}, u32[]{:S(2)}) collective-permute-start(f32[672,256]{1,0:T(8,128)S(1)} %constant_dynamic-update-slice_fusion.10.refs_18_), channel_id=1, source_target_pairs={{0,2},{2,0},{4,6},{6,4},{8,10},{10,8},{12,14},{14,12},{16,18},{18,... | collective-permute-start | bytes 2064392 | tf_op jit(solution)/shard_map/ppermute | solution.py:478
  104.5 2.2 copy-start.20
  104.5 11.5 %collective-permute-start.23 = (f32[384,256]{1,0:T(8,128)}, f32[384,256]{1,0:T(8,128)}, u32[]{:S(2)}, u32[]{:S(2)}) collective-permute-start(f32[384,256]{1,0:T(8,128)} %constant_dynamic-slice_fusion.2), channel_id=1, source_target_pairs={{0,1},{1,0},{2,3},{3,2},{4,5},{5,4},{6,7},{7,6},{8,9},{9,8},{10,11... | collective-permute-start | bytes 1179656 | tf_op jit(solution)/shard_map/ppermute | solution.py:532
  105.7 2.1 copy-start.21
  105.7 1.1 copy-start.15
  106.6 1.2 copy-start.22
  106.7 1.0 copy-start.16
  116.0 1.9 collective-permute-start.24
  117.9 0.7 copy-start.25
  118.7 71.4 %copy-start.1 = (f32[256,128]{1,0:T(8,128)S(1)}, f32[256,128]{1,0:T(8,128)}, u32[]{:S(2)}) copy-start(f32[256,128]{1,0:T(8,128)} %wq_ref.1) | copy-start | bytes 393220
  118.7 71.4 %copy-start.2 = (f32[256,128]{1,0:T(8,128)S(1)}, f32[256,128]{1,0:T(8,128)}, u32[]{:S(2)}) copy-start(f32[256,128]{1,0:T(8,128)} %wk_ref.1) | copy-start | bytes 393220
  118.7 71.4 %copy-start.3 = (f32[256,128]{1,0:T(8,128)S(1)}, f32[256,128]{1,0:T(8,128)}, u32[]{:S(2)}) copy-start(f32[256,128]{1,0:T(8,128)} %wv_ref.1) | copy-start | bytes 393220
  157.2 32.9 %copy-start = (f32[1024,256]{1,0:T(8,128)S(1)}, f32[1024,256]{1,0:T(8,128)}, u32[]{:S(2)}) copy-start(f32[1024,256]{1,0:T(8,128)} %own_ref.1) | copy-start | bytes 3145732
  158.2 2.1 collective-permute-start.27
  161.3 5.0 %collective-permute-start.28 = (f32[256,128]{1,0:T(8,128)S(1)}, f32[256,128]{1,0:T(8,128)S(1)}, u32[]{:S(2)}, u32[]{:S(2)}) collective-permute-start(f32[256,128]{1,0:T(8,128)S(1)} %select_add_fusion.1), channel_id=1, source_target_pairs={{0,4},{2,6},{4,0},{6,2},{8,12},{10,14},{12,8},{14,10},{16,20},{18,... | collective-permute-start | bytes 393224 | tf_op jit(solution)/shard_map/ppermute | solution.py:430
  163.7 73.0 %collective-permute-start.25 = (f32[1024,128]{1,0:T(8,128)}, f32[1024,128]{1,0:T(8,128)}, u32[]{:S(2)}, u32[]{:S(2)}) collective-permute-start(f32[1024,128]{1,0:T(8,128)} %constant_dynamic-slice_fusion), channel_id=1, source_target_pairs={{0,1},{1,0},{2,3},{3,2},{4,5},{5,4},{6,7},{7,6},{8,9},{9,8},{10,11... | collective-permute-start | bytes 1572872 | tf_op jit(solution)/shard_map/ppermute | solution.py:422
  166.3 23.1 %collective-permute-start.29 = (f32[256,128]{1,0:T(8,128)S(1)}, f32[256,128]{1,0:T(8,128)S(1)}, u32[]{:S(2)}, u32[]{:S(2)}) collective-permute-start(f32[256,128]{1,0:T(8,128)S(1)} %add.412), channel_id=1, source_target_pairs={{0,8},{2,10},{4,12},{6,14},{8,0},{10,2},{12,4},{14,6},{16,24},{18,... | collective-permute-start | bytes 393224 | tf_op jit(solution)/shard_map/ppermute | solution.py:430
  190.1 44.5 %collective-permute-start.30 = (f32[256,128]{1,0:T(8,128)}, f32[256,128]{1,0:T(8,128)}, u32[]{:S(2)}, u32[]{:S(2)}) collective-permute-start(f32[256,128]{1,0:T(8,128)} %add.413), channel_id=1, source_target_pairs={{0,16},{2,18},{4,20},{6,22},{8,24},{10,26},{12,28},{14,30},{16,0},... | collective-permute-start | bytes 393224 | tf_op jit(solution)/shard_map/ppermute | solution.py:430
  224.8 0.7 copy-start.5
  225.5 10.1 %collective-permute-start.32 = (f32[256,128]{1,0:T(8,128)S(1)}, f32[256,128]{1,0:T(8,128)S(1)}, u32[]{:S(2)}, u32[]{:S(2)}) collective-permute-start(f32[256,128]{1,0:T(8,128)S(1)} %broadcast_select_fusion.3), channel_id=1, source_target_pairs={{0,2},{2,0},{4,6},{6,4},{8,10},{10,8},{12,14},{14,12},{16,18},{18,... | collective-permute-start | bytes 393224 | tf_op jit(solution)/shard_map/ppermute | solution.py:430
  235.5 7.1 %collective-permute-start.31 = (f32[256,128]{1,0:T(8,128)S(1)}, f32[256,128]{1,0:T(8,128)S(1)}, u32[]{:S(2)}, u32[]{:S(2)}) collective-permute-start(f32[256,128]{1,0:T(8,128)S(1)} %add.414), channel_id=1, source_target_pairs={{0,2},{2,0},{4,6},{6,4},{8,10},{10,8},{12,14},{14,12},{16,18},{18,... | collective-permute-start | bytes 393224 | tf_op jit(solution)/shard_map/ppermute | solution.py:430
  236.6 5.9 %collective-permute-start.33 = (f32[256,128]{1,0:T(8,128)S(1)}, f32[256,128]{1,0:T(8,128)S(1)}, u32[]{:S(2)}, u32[]{:S(2)}) collective-permute-start(f32[256,128]{1,0:T(8,128)S(1)} %select_add_fusion), channel_id=1, source_target_pairs={{0,4},{2,6},{4,0},{6,2},{8,12},{10,14},{12,8},{14,10},{16,20},{18,... | collective-permute-start | bytes 393224 | tf_op jit(solution)/shard_map/ppermute | solution.py:430
  238.7 17.0 %collective-permute-start.26 = (f32[1024,128]{1,0:T(8,128)S(1)}, f32[1024,128]{1,0:T(8,128)S(1)}, u32[]{:S(2)}, u32[]{:S(2)}) collective-permute-start(f32[1024,128]{1,0:T(8,128)S(1)} %constant_dynamic-slice_fusion.1), channel_id=1, source_target_pairs={{0,1},{1,0},{2,3},{3,2},{4,5},{5,4},{6,7},{7,6},{8,9},{9,8},{10,11... | collective-permute-start | bytes 1572872 | tf_op jit(solution)/shard_map/ppermute | solution.py:422
  242.5 5.2 %collective-permute-start.34 = (f32[256,128]{1,0:T(8,128)S(1)}, f32[256,128]{1,0:T(8,128)S(1)}, u32[]{:S(2)}, u32[]{:S(2)}) collective-permute-start(f32[256,128]{1,0:T(8,128)S(1)} %add.416), channel_id=1, source_target_pairs={{0,8},{2,10},{4,12},{6,14},{8,0},{10,2},{12,4},{14,6},{16,24},{18,... | collective-permute-start | bytes 393224 | tf_op jit(solution)/shard_map/ppermute | solution.py:430
  247.7 8.0 %collective-permute-start.35 = (f32[256,128]{1,0:T(8,128)S(1)}, f32[256,128]{1,0:T(8,128)S(1)}, u32[]{:S(2)}, u32[]{:S(2)}) collective-permute-start(f32[256,128]{1,0:T(8,128)S(1)} %add.417), channel_id=1, source_target_pairs={{0,16},{2,18},{4,20},{6,22},{8,24},{10,26},{12,28},{14,30},{16,0},... | collective-permute-start | bytes 393224 | tf_op jit(solution)/shard_map/ppermute | solution.py:430
  255.7 1.4 collective-permute-start.36
  (1 other events, 0.7 us)
Sparse Core Ops, SparseCore 0:
  100.3 74.6 all-gather.1

commit v8 on v7

--- a/solution.py
+++ b/solution.py
@@ -9,6 +9,7 @@
 
 HEAD_SIZE = 32
 GROUP = 2
+RING = 6
 SCALE = HEAD_SIZE ** (-0.5)
 MASKED = -1e30
 F32 = jnp.float32
@@ -453,6 +454,7 @@
         everything = lax.all_gather(part, "dom", axis=0, tiled=True)
         return [(everything, 0, everything.shape[0], 0)], lambda ids: ids, part, plan
     side = lax.axis_index("head")
+    lacked = block_count - RING
     rows = part.shape[0] // block_count
     total = size * block_count
 
@@ -468,7 +470,8 @@
 
     def lacking(value):
         parts = [
-            lax.dynamic_slice_in_dim(each, 2 * side * rows, 3 * rows, axis=0) for each in value
+            lax.dynamic_slice_in_dim(each, (RING - lacked) * side * rows, lacked * rows, axis=0)
+            for each in value
         ]
         return jnp.concatenate(parts, axis=0)
 
@@ -485,7 +488,7 @@
         owner, block = ids // block_count, ids % block_count
         gap = (chip_place(owner // 2) - chip_place(me // 2)) % 8
         slot = jnp.where(gap < 4, 2 * gap, 2 * (8 - gap) - 1)
-        moved = jnp.where(gap == 0, block, (block + 5 * side) % block_count)
+        moved = jnp.where(gap == 0, block, (block + RING * side) % block_count)
         spot = slot * block_count + moved
         return spot + jnp.where(owner % 2 == me % 2, 0, half)
 
@@ -493,7 +496,7 @@
     below = notes.shape[0] // 2
     notes = jnp.concatenate([notes[:below], notes[below:]], axis=1)
 
-    start = lax.dynamic_slice_in_dim(part, 3 * side * rows, 5 * rows, axis=0)
+    start = lax.dynamic_slice_in_dim(part, lacked * side * rows, RING * rows, axis=0)
     start = jnp.concatenate([start, notes], axis=0)
     held = (lax.ppermute(start, "dom", onward), lax.ppermute(start, "dom", back))
     twin = swap(part)
@@ -503,16 +506,16 @@
 
     def keep(value, swapped, slots):
         for at, slot in enumerate(slots):
-            first = slot * block_count + 5
-            pieces.append((value, 3 * at * rows, 3 * rows, first))
-            pieces.append((swapped, 3 * at * rows, 3 * rows, half + first))
+            first = slot * block_count + RING
+            pieces.append((value, lacked * at * rows, lacked * rows, first))
+            pieces.append((swapped, lacked * at * rows, lacked * rows, half + first))
 
     def keep_ring(values, swapped, slots):
         for at, slot in enumerate(slots):
             first = slot * block_count
-            pieces.append((values[at], 0, 5 * rows, first))
-            pieces.append((swapped[at], 0, 5 * rows, half + first))
-            all_notes.extend([values[at][5 * rows:], swapped[at][5 * rows:]])
+            pieces.append((values[at], 0, RING * rows, first))
+            pieces.append((swapped[at], 0, RING * rows, half + first))
+            all_notes.extend([values[at][RING * rows:], swapped[at][RING * rows:]])
 
     slots, lack, lack_slots, notes = (1, 2), (), (), ()
     for step in range(1, 5):
@@ -522,8 +525,8 @@
             )
         elif step == 3:
             coming = (
-                lax.ppermute(held[0][: 3 * rows], "dom", onward),
-                lax.ppermute(held[1][3 * rows:], "dom", back),
+                lax.ppermute(held[0][: RING // 2 * rows], "dom", onward),
+                lax.ppermute(held[1][RING // 2 * rows:], "dom", back),
             )
             notes = jnp.concatenate(all_notes, axis=0)
             all_notes = []
@@ -607,11 +610,11 @@
         place(ids), pieces, dom_count * block_count, out_cotangent, grad_mixed, bias, w_query, w_key, w_value, w_out
     )
     layer_out = head_scatter(out_part)
+    all_stats = lax.all_gather(stats, "dom", axis=0, tiled=True)
     pieces = [grad_out[:, at:at + cols] for at in range(0, width, cols)]
     grad_query, grad_out = dom_sum(grad_query, jnp.concatenate(pieces, axis=0))
     pieces = [grad_out[at:at + cols] for at in range(0, width, cols)]
     grad_out = jnp.concatenate(pieces, axis=1)
-    all_stats = lax.all_gather(stats, "dom", axis=0, tiled=True)
     feats_part, grad_key, grad_value = attend_backward(
         steps, spots, all_feats, all_grads, all_stats, lists, node_features, feat_part,
         w_query, w_key, w_value, rows,

time: 266 us -> 263 us (0.989)
  waiting for transfers between devices: 84.8 us -> 80.4 us
    ppermute x2, waiting for transfers between devices: 21.5 us -> 10.3 us  [gather_feats(): lax.ppermute(held[0], 'dom', onward)]
    ppermute x4, waiting for transfers between devices: 16.3 us -> 22.8 us  [gather_feats(): more = (lax.ppermute(lacking(held), 'head', other_head),)]
    ppermute x1, waiting for transfers between devices: 16 us -> 18.8 us  [gather_feats(): lax.ppermute(start, 'dom', onward)]
    unnamed x69 -> x73, local copies, waits for them, and re-layouts: 13.3 us -> 13.1 us
  transfers between devices with their start and end apart: 38 -> 38, of which waited for: 21 -> 20; matrix products, arithmetic and copies ran while one was open for 13% -> 14% of each run, Pallas kernels for 28% -> 28%
where the time goes in v8:
time: 263 us; the launch traced here: 262 us
  waiting for transfers between devices  80.4 us (31%)
  Pallas kernels  73.1 us (28%)
  starting transfers between devices  32 us (12%)
  local copies, waits for them, and re-layouts  23.9 us (9%)
  blocking collectives  21.2 us (8%)
  other arithmetic  15 us (6%)
  between operations  14.6 us (6%)
    pallas_call x1, Pallas kernels, attend_forward(): pl.pallas_call(functools.partial(forward_kernel, entries, layout, len(arr...  38.5 us
    pallas_call x1, Pallas kernels, attend_backward(): pl.pallas_call(backward_kernel, out_shape=(jax.ShapeDtypeStruct((node_row...  34.6 us
    ppermute x4, waiting for transfers between devices, gather_feats(): more = (lax.ppermute(lacking(held), 'head', other_head),)  22.8 us
    all_gather x1, blocking collectives, per_device(): all_stats = lax.all_gather(stats, 'dom', axis=0, tiled=True)  21.2 us
    ppermute x1, waiting for transfers between devices, gather_feats(): lax.ppermute(start, 'dom', onward)  18.8 us
    ppermute x10, waiting for transfers between devices, from_across(): return lax.ppermute(value, 'dom', [(at, at ^ bit) for at in range(size)])  14.9 us
    ppermute x10, starting transfers between devices, from_across(): return lax.ppermute(value, 'dom', [(at, at ^ bit) for at in range(size)])  14.5 us
    unnamed x73, local copies, waits for them, and re-layouts  13.1 us
  transfers between devices with their start and end apart: 38, of which 20 were waited for; matrix products, arithmetic and copies ran while one was open for 14% of the time, Pallas kernels for 28%

profile of v8, /device:TPU:0, one launch (start us, length us, event | category | flops | bytes accessed | tf_op | source)
XLA Modules:
  0.0 262.0 jit_solution(14561297592165973978)
XLA Ops:
  7.8 0.7 multiply_add_fusion
  8.5 0.7 fusion.10
  9.2 0.8 convert_element_type.58
  10.0 1.2 constant_dynamic-slice_fusion.9
  11.1 1.0 maximum_maximum_fusion
  12.1 2.8 %collective-permute-start = (f32[800,256]{1,0:T(8,128)}, f32[800,256]{1,0:T(8,128)S(1)}, u32[]{:S(2)}, u32[]{:S(2)}) collective-permute-start(f32[800,256]{1,0:T(8,128)} %maximum_maximum_fusion), channel_id=1, source_target_pairs={{0,8},{2,10},{8,16},{10,18},{16,24},{18,26},{24,28},{26,30},{28,20... | collective-permute-start | bytes 2457608 | tf_op jit(solution)/shard_map/ppermute | solution.py:501
  14.9 18.8 %collective-permute-done.refs_2_ = f32[800,256]{1,0:T(8,128)S(1)} collective-permute-done((f32[800,256]{1,0:T(8,128)}, f32[800,256]{1,0:T(8,128)S(1)}, u32[]{:S(2)}, u32[]{:S(2)}) %collective-permute-start) | collective-permute-done | bytes 819232 | tf_op jit(solution)/shard_map/ppermute | solution.py:501
  33.7 1.5 collective-permute-done.1.refs_4_
  35.3 1.6 collective-permute-start.3
  37.6 1.6 collective-permute-start.5
  39.8 12.0 %collective-permute-done.5.refs_10_ = f32[512,256]{1,0:T(8,128)S(1)} collective-permute-done((f32[512,256]{1,0:T(8,128)S(1)}, f32[512,256]{1,0:T(8,128)S(1)}, u32[]{:S(2)}, u32[]{:S(2)}) %collective-permute-start.5) | collective-permute-done | bytes 524320 | tf_op jit(solution)/shard_map/ppermute | solution.py:535
  51.8 2.8 %collective-permute-done.3.refs_6_ = f32[800,256]{1,0:T(8,128)S(1)} collective-permute-done((f32[800,256]{1,0:T(8,128)S(1)}, f32[800,256]{1,0:T(8,128)S(1)}, u32[]{:S(2)}, u32[]{:S(2)}) %collective-permute-start.3) | collective-permute-done | bytes 819232 | tf_op jit(solution)/shard_map/ppermute | solution.py:524
  54.6 2.9 %collective-permute-done.4.refs_8_ = f32[800,256]{1,0:T(8,128)S(1)} collective-permute-done((f32[800,256]{1,0:T(8,128)S(1)}, f32[800,256]{1,0:T(8,128)S(1)}, u32[]{:S(2)}, u32[]{:S(2)}) %collective-permute-start.4) | collective-permute-done | bytes 819232 | tf_op jit(solution)/shard_map/ppermute | solution.py:524
  57.6 0.8 copy-done.12
  58.4 0.8 pad_maximum_fusion.1
  59.3 1.5 collective-permute-start.10
  60.8 1.8 fusion.34.refs_25_
  63.7 1.6 collective-permute-start.8
  66.3 6.8 %collective-permute-done.10.refs_16_ = f32[512,256]{1,0:T(8,128)} collective-permute-done((f32[512,256]{1,0:T(8,128)}, f32[512,256]{1,0:T(8,128)}, u32[]{:S(2)}, u32[]{:S(2)}) %collective-permute-start.10) | collective-permute-done | bytes 524320 | tf_op jit(solution)/shard_map/ppermute | solution.py:535
  73.1 1.4 constant_dynamic-update-slice_fusion.6
  75.1 1.4 constant_dynamic-update-slice_fusion.4
  76.5 7.5 %collective-permute-done.8.refs_12_ = f32[800,256]{1,0:T(8,128)S(1)} collective-permute-done((f32[800,256]{1,0:T(8,128)}, f32[800,256]{1,0:T(8,128)S(1)}, u32[]{:S(2)}, u32[]{:S(2)}) %collective-permute-start.8) | collective-permute-done | bytes 819232 | tf_op jit(solution)/shard_map/ppermute | solution.py:524
  84.1 1.3 collective-permute-done.9.refs_14_
  86.6 1.6 collective-permute-start.14
  88.2 1.4 constant_dynamic-update-slice_fusion.3
  90.1 1.4 constant_dynamic-update-slice_fusion.1
  92.1 3.8 %collective-permute-done.14 = f32[384,256]{1,0:T(8,128)S(1)} collective-permute-done((f32[384,256]{1,0:T(8,128)S(1)}, f32[384,256]{1,0:T(8,128)S(1)}, u32[]{:S(2)}, u32[]{:S(2)}) %collective-permute-start.14) | collective-permute-done | bytes 393248 | tf_op jit(solution)/shard_map/ppermute | solution.py:528
  96.4 1.9 collective-permute-done.16.refs_20_
  98.3 0.8 constant_dynamic-update-slice_fusion.11
  99.1 0.8 constant_dynamic-update-slice_fusion.10.refs_18_
  101.1 1.7 constant_dynamic-slice_fusion.2
  102.8 1.0 constant_dynamic-update-slice_fusion.18
  103.8 2.6 collective-permute-done.22.refs_17_
  107.0 0.8 constant_dynamic-update-slice_fusion.13
  109.8 1.2 gather_fusion
  112.0 0.7 pad.16.clone
  112.8 2.2 collective-permute-done.23.refs_22_
  115.0 0.7 copy.26
  115.7 0.8 collective-permute-done.24.refs_23_
  116.5 0.7 copy-done.27
  117.2 38.5 %attend_forward.1 = (f32[16384,256]{1,0:T(8,128)}, f32[1024,256]{1,0:T(8,128)}, f32[1024,256]{1,0:T(8,128)}, f32[8,8,128]{2,1,0:T(8,128)}, f32[256,128]{1,0:T(8,128)}, /*index=5*/f32[128,256]{1,0:T(8,128)}) custom-call(s32[8,8]{1,0:T(8,128)} %get-tuple-element.96.ids, f32[1024,256]{1,0:T(8,128)} %own_ref.1, f32[1024,256]{1,0:T(8,128)} %collective-permute-done.2.refs_1_, ...), custom_call_target="tpu_custom_call" | custom-call | tf_op jit(solution)/shard_map/attend_forward/pallas_call | solution.py:188
  155.7 1.0 fusion.33
  156.8 1.1 collective-permute-start.27
  157.9 1.0 collective-permute-done.27
  158.9 0.9 select_add_fusion.1
  160.3 1.9 constant_dynamic-slice_fusion
  162.7 2.1 collective-permute-done.28
  164.8 1.6 collective-permute-start.29
  166.4 21.2 %all_gather.7.stats_ref = f32[128,8,128]{2,1,0:T(8,128)S(1)} all-gather(f32[8,8,128]{2,1,0:T(8,128)} %get-tuple-element.86), channel_id=1, replica_groups=mesh['dom'=16,'head'=2] {'dom'}, dimensions={0}, use_global_device_ids=true | all-gather | bytes 557056 | tf_op jit(solution)/shard_map/all_gather | solution.py:613
  187.6 0.7 add.413
  188.3 34.6 %attend_backward.1 = (f32[1024,256]{1,0:T(8,128)S(1)}, f32[256,128]{1,0:T(8,128)S(1)}, f32[256,128]{1,0:T(8,128)S(1)}) custom-call(s32[3,40]{1,0:T(4,128)S(1)} %add_add_fusion.steps_ref, s32[4,80]{1,0:T(4,128)S(1)} %pad_add_fusion.1.readers_ref, f32[16384,256]{1,0:T(8,128)} %get-tuple-element.84.feats_ref, ...), custom_call_target="tpu_custom_call" | custom-call | tf_op jit(solution)/shard_map/attend_backward/pallas_call | solution.py:353
  223.6 8.3 %collective-permute-start.32 = (f32[256,128]{1,0:T(8,128)S(1)}, f32[256,128]{1,0:T(8,128)S(1)}, u32[]{:S(2)}, u32[]{:S(2)}) collective-permute-start(f32[256,128]{1,0:T(8,128)S(1)} %broadcast_select_fusion.3), channel_id=1, source_target_pairs={{0,2},{2,0},{4,6},{6,4},{8,10},{10,8},{12,14},{14,12},{16,18},{18,... | collective-permute-start | bytes 393224 | tf_op jit(solution)/shard_map/ppermute | solution.py:431
  231.9 1.0 add.414
  232.9 0.9 select_add_fusion
  234.0 2.1 dynamic-slice_add_fusion.1
  236.1 1.5 collective-permute-start.26
  237.6 2.2 collective-permute-done.33
  240.0 0.7 broadcast_select_fusion
  240.6 4.4 %collective-permute-done.34 = f32[256,128]{1,0:T(8,128)S(1)} collective-permute-done((f32[256,128]{1,0:T(8,128)S(1)}, f32[256,128]{1,0:T(8,128)S(1)}, u32[]{:S(2)}, u32[]{:S(2)}) %collective-permute-start.34) | collective-permute-done | bytes 131104 | tf_op jit(solution)/shard_map/ppermute | solution.py:431
  245.0 2.6 %collective-permute-start.35 = (f32[256,128]{1,0:T(8,128)S(1)}, f32[256,128]{1,0:T(8,128)S(1)}, u32[]{:S(2)}, u32[]{:S(2)}) collective-permute-start(f32[256,128]{1,0:T(8,128)S(1)} %add.417), channel_id=1, source_target_pairs={{0,16},{2,18},{4,20},{6,22},{8,24},{10,26},{12,28},{14,30},{16,0},... | collective-permute-start | bytes 393224 | tf_op jit(solution)/shard_map/ppermute | solution.py:431
  247.7 0.7 pad_maximum_fusion.4
  248.3 4.7 %collective-permute-done.35 = f32[256,128]{1,0:T(8,128)S(1)} collective-permute-done((f32[256,128]{1,0:T(8,128)S(1)}, f32[256,128]{1,0:T(8,128)S(1)}, u32[]{:S(2)}, u32[]{:S(2)}) %collective-permute-start.35) | collective-permute-done | bytes 131104 | tf_op jit(solution)/shard_map/ppermute | solution.py:431
  253.1 0.9 dynamic-slice_add_fusion
  254.4 0.7 broadcast_select_fusion.1
  (164 shorter events, 15.1 us)
Async XLA Ops:
  7.2 53.6 %copy-start.20 = (f32[128,256]{1,0:T(8,128)S(1)}, f32[128,256]{1,0:T(8,128)}, u32[]{:S(2)}) copy-start(f32[128,256]{1,0:T(8,128)} %refs_30_.1) | copy-start | bytes 393220
  7.2 53.6 %copy-start.6 = (f32[1024,256]{1,0:T(8,128)S(1)}, f32[1024,256]{1,0:T(8,128)}, u32[]{:S(2)}) copy-start(f32[1024,256]{1,0:T(8,128)} %refs_24_.1) | copy-start | bytes 3145732
  7.2 181.1 %all-gather.2.cloned.1.call-start = ((), (), s32[]{:S(2)}) async-start(), calls=%async_computation | async-start | bytes 8912896 | tf_op jit(solution)/shard_map/all_gather | solution.py:607
  7.2 28.1 %collective-permute-start.2 = (f32[1024,256]{1,0:T(8,128)}, f32[1024,256]{1,0:T(8,128)}, u32[]{:S(2)}, u32[]{:S(2)}) collective-permute-start(f32[1024,256]{1,0:T(8,128)} %own_ref.1), channel_id=1, source_target_pairs={{0,2},{2,0},{4,6},{6,4},{8,10},{10,8},{12,14},{14,12},{16,18},{18,... | collective-permute-start | bytes 3145736 | tf_op jit(solution)/shard_map/ppermute | solution.py:481
  12.1 21.6 %collective-permute-start = (f32[800,256]{1,0:T(8,128)}, f32[800,256]{1,0:T(8,128)S(1)}, u32[]{:S(2)}, u32[]{:S(2)}) collective-permute-start(f32[800,256]{1,0:T(8,128)} %maximum_maximum_fusion), channel_id=1, source_target_pairs={{0,8},{2,10},{8,16},{10,18},{16,24},{18,26},{24,28},{26,30},{28,20... | collective-permute-start | bytes 2457608 | tf_op jit(solution)/shard_map/ppermute | solution.py:501
  14.9 20.4 %collective-permute-start.1 = (f32[800,256]{1,0:T(8,128)}, f32[800,256]{1,0:T(8,128)S(1)}, u32[]{:S(2)}, u32[]{:S(2)}) collective-permute-start(f32[800,256]{1,0:T(8,128)} %maximum_maximum_fusion), channel_id=1, source_target_pairs={{8,0},{10,2},{16,8},{18,10},{24,16},{26,18},{28,24},{30,26},{20,28... | collective-permute-start | bytes 2457608 | tf_op jit(solution)/shard_map/ppermute | solution.py:501
  33.7 51.8 %copy-start.9 = (f32[800,256]{1,0:T(8,128)}, f32[800,256]{1,0:T(8,128)S(1)}, u32[]{:S(2)}) copy-start(f32[800,256]{1,0:T(8,128)S(1)} %collective-permute-done.refs_2_) | copy-start | bytes 2457604
  35.3 50.2 %copy-start.10 = (f32[800,256]{1,0:T(8,128)}, f32[800,256]{1,0:T(8,128)S(1)}, u32[]{:S(2)}) copy-start(f32[800,256]{1,0:T(8,128)S(1)} %collective-permute-done.1.refs_4_) | copy-start | bytes 2457604
  35.3 19.3 %collective-permute-start.3 = (f32[800,256]{1,0:T(8,128)S(1)}, f32[800,256]{1,0:T(8,128)S(1)}, u32[]{:S(2)}, u32[]{:S(2)}) collective-permute-start(f32[800,256]{1,0:T(8,128)S(1)} %collective-permute-done.refs_2_), channel_id=1, source_target_pairs={{0,8},{2,10},{8,16},{10,18},{16,24},{18,26},{24,28},{26,30},{28,20... | collective-permute-start | bytes 2457608 | tf_op jit(solution)/shard_map/ppermute | solution.py:524
  36.9 20.7 %collective-permute-start.6 = (f32[800,256]{1,0:T(8,128)S(1)}, f32[800,256]{1,0:T(8,128)S(1)}, u32[]{:S(2)}, u32[]{:S(2)}) collective-permute-start(f32[800,256]{1,0:T(8,128)S(1)} %collective-permute-done.refs_2_), channel_id=1, source_target_pairs={{0,2},{2,0},{4,6},{6,4},{8,10},{10,8},{12,14},{14,12},{16,18},{18,... | collective-permute-start | bytes 2457608 | tf_op jit(solution)/shard_map/ppermute | solution.py:481
  36.9 20.7 %collective-permute-start.4 = (f32[800,256]{1,0:T(8,128)S(1)}, f32[800,256]{1,0:T(8,128)S(1)}, u32[]{:S(2)}, u32[]{:S(2)}) collective-permute-start(f32[800,256]{1,0:T(8,128)S(1)} %collective-permute-done.1.refs_4_), channel_id=1, source_target_pairs={{8,0},{10,2},{16,8},{18,10},{24,16},{26,18},{28,24},{30,26},{20,28... | collective-permute-start | bytes 2457608 | tf_op jit(solution)/shard_map/ppermute | solution.py:524
  37.3 20.2 %collective-permute-start.7 = (f32[800,256]{1,0:T(8,128)S(1)}, f32[800,256]{1,0:T(8,128)S(1)}, u32[]{:S(2)}, u32[]{:S(2)}) collective-permute-start(f32[800,256]{1,0:T(8,128)S(1)} %collective-permute-done.1.refs_4_), channel_id=1, source_target_pairs={{0,2},{2,0},{4,6},{6,4},{8,10},{10,8},{12,14},{14,12},{16,18},{18,... | collective-permute-start | bytes 2457608 | tf_op jit(solution)/shard_map/ppermute | solution.py:481
  37.6 14.2 %collective-permute-start.5 = (f32[512,256]{1,0:T(8,128)S(1)}, f32[512,256]{1,0:T(8,128)S(1)}, u32[]{:S(2)}, u32[]{:S(2)}) collective-permute-start(f32[512,256]{1,0:T(8,128)S(1)} %pad_maximum_fusion), channel_id=1, source_target_pairs={{0,1},{1,0},{2,3},{3,2},{4,5},{5,4},{6,7},{7,6},{8,9},{9,8},{10,11... | collective-permute-start | bytes 1572872 | tf_op jit(solution)/shard_map/ppermute | solution.py:535
  51.8 5.7 %copy-start.21 = (f32[512,256]{1,0:T(8,128)}, f32[512,256]{1,0:T(8,128)S(1)}, u32[]{:S(2)}) copy-start(f32[512,256]{1,0:T(8,128)S(1)} %collective-permute-done.5.refs_10_) | copy-start | bytes 1572868
  51.8 10.7 %collective-permute-start.17 = (f32[32,256]{1,0:T(8,128)S(1)}, f32[32,256]{1,0:T(8,128)S(1)}, u32[]{:S(2)}, u32[]{:S(2)}) collective-permute-start(f32[32,256]{1,0:T(8,128)S(1)} %get-tuple-element.108), channel_id=1, source_target_pairs={{0,2},{2,0},{4,6},{6,4},{8,10},{10,8},{12,14},{14,12},{16,18},{18,... | collective-permute-start | bytes 98312 | tf_op jit(solution)/shard_map/ppermute | solution.py:481
  54.6 3.0 %copy-start.11 = (f32[800,256]{1,0:T(8,128)}, f32[800,256]{1,0:T(8,128)S(1)}, u32[]{:S(2)}) copy-start(f32[800,256]{1,0:T(8,128)S(1)} %collective-permute-done.3.refs_6_) | copy-start | bytes 2457604
  57.5 0.9 copy-start.12
  57.5 1.7 copy-start.13
  57.6 3.2 %copy-start.14 = (f32[800,256]{1,0:T(8,128)}, f32[800,256]{1,0:T(8,128)S(1)}, u32[]{:S(2)}) copy-start(f32[800,256]{1,0:T(8,128)S(1)} %collective-permute-done.7.refs_5_) | copy-start | bytes 2457604
  59.3 13.9 %collective-permute-start.10 = (f32[512,256]{1,0:T(8,128)}, f32[512,256]{1,0:T(8,128)}, u32[]{:S(2)}, u32[]{:S(2)}) collective-permute-start(f32[512,256]{1,0:T(8,128)} %pad_maximum_fusion.1), channel_id=1, source_target_pairs={{0,1},{1,0},{2,3},{3,2},{4,5},{5,4},{6,7},{7,6},{8,9},{9,8},{10,11... | collective-permute-start | bytes 1572872 | tf_op jit(solution)/shard_map/ppermute | solution.py:535
  63.2 13.3 %collective-permute-start.11 = (f32[800,256]{1,0:T(8,128)}, f32[800,256]{1,0:T(8,128)S(1)}, u32[]{:S(2)}, u32[]{:S(2)}) collective-permute-start(f32[800,256]{1,0:T(8,128)} %copy-done.11), channel_id=1, source_target_pairs={{0,2},{2,0},{4,6},{6,4},{8,10},{10,8},{12,14},{14,12},{16,18},{18,... | collective-permute-start | bytes 2457608 | tf_op jit(solution)/shard_map/ppermute | solution.py:481
  63.2 13.3 %collective-permute-start.12 = (f32[800,256]{1,0:T(8,128)}, f32[800,256]{1,0:T(8,128)S(1)}, u32[]{:S(2)}, u32[]{:S(2)}) collective-permute-start(f32[800,256]{1,0:T(8,128)} %copy-done.12), channel_id=1, source_target_pairs={{0,2},{2,0},{4,6},{6,4},{8,10},{10,8},{12,14},{14,12},{16,18},{18,... | collective-permute-start | bytes 2457608 | tf_op jit(solution)/shard_map/ppermute | solution.py:481
  63.7 20.4 %collective-permute-start.8 = (f32[800,256]{1,0:T(8,128)}, f32[800,256]{1,0:T(8,128)S(1)}, u32[]{:S(2)}, u32[]{:S(2)}) collective-permute-start(f32[800,256]{1,0:T(8,128)} %copy-done.11), channel_id=1, source_target_pairs={{0,8},{2,10},{8,16},{10,18},{16,24},{18,26},{24,28},{26,30},{28,20... | collective-permute-start | bytes 2457608 | tf_op jit(solution)/shard_map/ppermute | solution.py:524
  65.3 20.1 %collective-permute-start.9 = (f32[800,256]{1,0:T(8,128)}, f32[800,256]{1,0:T(8,128)S(1)}, u32[]{:S(2)}, u32[]{:S(2)}) collective-permute-start(f32[800,256]{1,0:T(8,128)} %copy-done.12), channel_id=1, source_target_pairs={{8,0},{10,2},{16,8},{18,10},{24,16},{26,18},{28,24},{30,26},{20,28... | collective-permute-start | bytes 2457608 | tf_op jit(solution)/shard_map/ppermute | solution.py:524
  73.1 3.3 %collective-permute-start.13 = (f32[512,256]{1,0:T(8,128)}, f32[512,256]{1,0:T(8,128)S(1)}, u32[]{:S(2)}, u32[]{:S(2)}) collective-permute-start(f32[512,256]{1,0:T(8,128)} %copy-done.21), channel_id=1, source_target_pairs={{0,2},{2,0},{4,6},{6,4},{8,10},{10,8},{12,14},{14,12},{16,18},{18,... | collective-permute-start | bytes 1572872 | tf_op jit(solution)/shard_map/ppermute | solution.py:481
  76.5 8.9 %copy-start.22 = (f32[512,256]{1,0:T(8,128)}, f32[512,256]{1,0:T(8,128)S(1)}, u32[]{:S(2)}) copy-start(f32[512,256]{1,0:T(8,128)S(1)} %collective-permute-done.13.refs_11_) | copy-start | bytes 1572868
  76.5 13.0 %copy-start.15 = (f32[800,256]{1,0:T(8,128)}, f32[800,256]{1,0:T(8,128)S(1)}, u32[]{:S(2)}) copy-start(f32[800,256]{1,0:T(8,128)S(1)} %collective-permute-done.11.refs_7_) | copy-start | bytes 2457604
  76.5 15.0 %copy-start.16 = (f32[800,256]{1,0:T(8,128)}, f32[800,256]{1,0:T(8,128)S(1)}, u32[]{:S(2)}) copy-start(f32[800,256]{1,0:T(8,128)S(1)} %collective-permute-done.12.refs_9_) | copy-start | bytes 2457604
  84.1 24.1 %copy-start.8 = (f32[800,256]{1,0:T(8,128)}, f32[800,256]{1,0:T(8,128)S(1)}, u32[]{:S(2)}) copy-start(f32[800,256]{1,0:T(8,128)S(1)} %collective-permute-done.8.refs_12_) | copy-start | bytes 2457604
  85.4 22.8 %copy-start.7 = (f32[800,256]{1,0:T(8,128)}, f32[800,256]{1,0:T(8,128)S(1)}, u32[]{:S(2)}) copy-start(f32[800,256]{1,0:T(8,128)S(1)} %collective-permute-done.9.refs_14_) | copy-start | bytes 2457604
  85.5 29.5 %copy-start.28 = (s32[8,7,128]{2,0,1:T(8,128)S(1)}, s32[8,7,128]{2,0,1:T(8,128)}, u32[]{:S(2)}) copy-start(s32[8,7,128]{2,0,1:T(8,128)} %param.16) | copy-start | bytes 86020
  85.6 12.7 %collective-permute-start.16 = (f32[512,256]{1,0:T(8,128)S(1)}, f32[512,256]{1,0:T(8,128)S(1)}, u32[]{:S(2)}, u32[]{:S(2)}) collective-permute-start(f32[512,256]{1,0:T(8,128)S(1)} %pad_maximum_fusion.2), channel_id=1, source_target_pairs={{0,1},{1,0},{2,3},{3,2},{4,5},{5,4},{6,7},{7,6},{8,9},{9,8},{10,11... | collective-permute-start | bytes 1572872 | tf_op jit(solution)/shard_map/ppermute | solution.py:535
  86.1 10.3 %collective-permute-start.15 = (f32[416,256]{1,0:T(8,128)S(1)}, f32[416,256]{1,0:T(8,128)S(1)}, u32[]{:S(2)}, u32[]{:S(2)}) collective-permute-start(f32[416,256]{1,0:T(8,128)S(1)} %slice.92), channel_id=1, source_target_pairs={{8,0},{10,2},{16,8},{18,10},{24,16},{26,18},{28,24},{30,26},{20,28... | collective-permute-start | bytes 1277960 | tf_op jit(solution)/shard_map/ppermute | solution.py:529
  86.6 9.3 %collective-permute-start.14 = (f32[384,256]{1,0:T(8,128)S(1)}, f32[384,256]{1,0:T(8,128)S(1)}, u32[]{:S(2)}, u32[]{:S(2)}) collective-permute-start(f32[384,256]{1,0:T(8,128)S(1)} %slice.91), channel_id=1, source_target_pairs={{0,8},{2,10},{8,16},{10,18},{16,24},{18,26},{24,28},{26,30},{28,20... | collective-permute-start | bytes 1179656 | tf_op jit(solution)/shard_map/ppermute | solution.py:528
  98.3 18.2 %copy-start.23 = (f32[512,256]{1,0:T(8,128)}, f32[512,256]{1,0:T(8,128)S(1)}, u32[]{:S(2)}) copy-start(f32[512,256]{1,0:T(8,128)S(1)} %collective-permute-done.16.refs_20_) | copy-start | bytes 1572868
  100.0 7.0 %collective-permute-start.20 = (f32[800,256]{1,0:T(8,128)S(1)}, f32[800,256]{1,0:T(8,128)S(1)}, u32[]{:S(2)}, u32[]{:S(2)}) collective-permute-start(f32[800,256]{1,0:T(8,128)S(1)} %collective-permute-done.8.refs_12_), channel_id=1, source_target_pairs={{0,2},{2,0},{4,6},{6,4},{8,10},{10,8},{12,14},{14,12},{16,18},{18,... | collective-permute-start | bytes 2457608 | tf_op jit(solution)/shard_map/ppermute | solution.py:481
  100.0 6.9 %collective-permute-start.21 = (f32[800,256]{1,0:T(8,128)S(1)}, f32[800,256]{1,0:T(8,128)S(1)}, u32[]{:S(2)}, u32[]{:S(2)}) collective-permute-start(f32[800,256]{1,0:T(8,128)S(1)} %collective-permute-done.9.refs_14_), channel_id=1, source_target_pairs={{0,2},{2,0},{4,6},{6,4},{8,10},{10,8},{12,14},{14,12},{16,18},{18,... | collective-permute-start | bytes 2457608 | tf_op jit(solution)/shard_map/ppermute | solution.py:481
  100.5 6.4 %collective-permute-start.18 = (f32[800,256]{1,0:T(8,128)}, f32[800,256]{1,0:T(8,128)S(1)}, u32[]{:S(2)}, u32[]{:S(2)}) collective-permute-start(f32[800,256]{1,0:T(8,128)} %constant_dynamic-update-slice_fusion.10.refs_18_), channel_id=1, source_target_pairs={{0,2},{2,0},{4,6},{6,4},{8,10},{10,8},{12,14},{14,12},{16,18},{18,... | collective-permute-start | bytes 2457608 | tf_op jit(solution)/shard_map/ppermute | solution.py:481
  100.6 5.8 %collective-permute-start.22 = (f32[512,256]{1,0:T(8,128)}, f32[512,256]{1,0:T(8,128)S(1)}, u32[]{:S(2)}, u32[]{:S(2)}) collective-permute-start(f32[512,256]{1,0:T(8,128)} %collective-permute-done.10.refs_16_), channel_id=1, source_target_pairs={{0,2},{2,0},{4,6},{6,4},{8,10},{10,8},{12,14},{14,12},{16,18},{18,... | collective-permute-start | bytes 1572872 | tf_op jit(solution)/shard_map/ppermute | solution.py:481
  101.0 5.9 %collective-permute-start.19 = (f32[512,256]{1,0:T(8,128)S(1)}, f32[512,256]{1,0:T(8,128)S(1)}, u32[]{:S(2)}, u32[]{:S(2)}) collective-permute-start(f32[512,256]{1,0:T(8,128)S(1)} %collective-permute-done.16.refs_20_), channel_id=1, source_target_pairs={{0,2},{2,0},{4,6},{6,4},{8,10},{10,8},{12,14},{14,12},{16,18},{18,... | collective-permute-start | bytes 1572872 | tf_op jit(solution)/shard_map/ppermute | solution.py:481
  106.4 1.4 copy-start.24
  106.4 8.6 %collective-permute-start.23 = (f32[256,256]{1,0:T(8,128)}, f32[256,256]{1,0:T(8,128)S(1)}, u32[]{:S(2)}, u32[]{:S(2)}) collective-permute-start(f32[256,256]{1,0:T(8,128)} %constant_dynamic-slice_fusion.2), channel_id=1, source_target_pairs={{0,1},{1,0},{2,3},{3,2},{4,5},{5,4},{6,7},{7,6},{8,9},{9,8},{10,11... | collective-permute-start | bytes 786440 | tf_op jit(solution)/shard_map/ppermute | solution.py:535
  106.9 9.6 %copy-start.17 = (f32[800,256]{1,0:T(8,128)}, f32[800,256]{1,0:T(8,128)S(1)}, u32[]{:S(2)}) copy-start(f32[800,256]{1,0:T(8,128)S(1)} %collective-permute-done.20.refs_13_) | copy-start | bytes 2457604
  106.9 1.2 copy-start.18
  106.9 1.4 copy-start.25
  107.0 1.1 copy-start.19
  115.0 1.5 copy-start.26
  115.0 1.5 collective-permute-start.24
  117.2 71.0 %copy-start.1 = (f32[256,128]{1,0:T(8,128)S(1)}, f32[256,128]{1,0:T(8,128)}, u32[]{:S(2)}) copy-start(f32[256,128]{1,0:T(8,128)} %wq_ref.1) | copy-start | bytes 393220
  117.2 71.0 %copy-start.2 = (f32[256,128]{1,0:T(8,128)S(1)}, f32[256,128]{1,0:T(8,128)}, u32[]{:S(2)}) copy-start(f32[256,128]{1,0:T(8,128)} %wk_ref.1) | copy-start | bytes 393220
  117.2 71.1 %copy-start.3 = (f32[256,128]{1,0:T(8,128)S(1)}, f32[256,128]{1,0:T(8,128)}, u32[]{:S(2)}) copy-start(f32[256,128]{1,0:T(8,128)} %wv_ref.1) | copy-start | bytes 393220
  155.7 32.5 %copy-start = (f32[1024,256]{1,0:T(8,128)S(1)}, f32[1024,256]{1,0:T(8,128)}, u32[]{:S(2)}) copy-start(f32[1024,256]{1,0:T(8,128)} %own_ref.1) | copy-start | bytes 3145732
  156.8 2.1 collective-permute-start.27
  159.8 5.0 %collective-permute-start.28 = (f32[256,128]{1,0:T(8,128)S(1)}, f32[256,128]{1,0:T(8,128)S(1)}, u32[]{:S(2)}, u32[]{:S(2)}) collective-permute-start(f32[256,128]{1,0:T(8,128)S(1)} %select_add_fusion.1), channel_id=1, source_target_pairs={{0,4},{2,6},{4,0},{6,2},{8,12},{10,14},{12,8},{14,10},{16,20},{18,... | collective-permute-start | bytes 393224 | tf_op jit(solution)/shard_map/ppermute | solution.py:431
  162.2 71.8 %collective-permute-start.25 = (f32[1024,128]{1,0:T(8,128)}, f32[1024,128]{1,0:T(8,128)}, u32[]{:S(2)}, u32[]{:S(2)}) collective-permute-start(f32[1024,128]{1,0:T(8,128)} %constant_dynamic-slice_fusion), channel_id=1, source_target_pairs={{0,1},{1,0},{2,3},{3,2},{4,5},{5,4},{6,7},{7,6},{8,9},{9,8},{10,11... | collective-permute-start | bytes 1572872 | tf_op jit(solution)/shard_map/ppermute | solution.py:423
  164.8 22.7 %collective-permute-start.29 = (f32[256,128]{1,0:T(8,128)S(1)}, f32[256,128]{1,0:T(8,128)S(1)}, u32[]{:S(2)}, u32[]{:S(2)}) collective-permute-start(f32[256,128]{1,0:T(8,128)S(1)} %add.412), channel_id=1, source_target_pairs={{0,8},{2,10},{4,12},{6,14},{8,0},{10,2},{12,4},{14,6},{16,24},{18,... | collective-permute-start | bytes 393224 | tf_op jit(solution)/shard_map/ppermute | solution.py:431
  188.2 43.6 %collective-permute-start.30 = (f32[256,128]{1,0:T(8,128)}, f32[256,128]{1,0:T(8,128)}, u32[]{:S(2)}, u32[]{:S(2)}) collective-permute-start(f32[256,128]{1,0:T(8,128)} %add.413), channel_id=1, source_target_pairs={{0,16},{2,18},{4,20},{6,22},{8,24},{10,26},{12,28},{14,30},{16,0},... | collective-permute-start | bytes 393224 | tf_op jit(solution)/shard_map/ppermute | solution.py:431
  223.6 9.3 %collective-permute-start.32 = (f32[256,128]{1,0:T(8,128)S(1)}, f32[256,128]{1,0:T(8,128)S(1)}, u32[]{:S(2)}, u32[]{:S(2)}) collective-permute-start(f32[256,128]{1,0:T(8,128)S(1)} %broadcast_select_fusion.3), channel_id=1, source_target_pairs={{0,2},{2,0},{4,6},{6,4},{8,10},{10,8},{12,14},{14,12},{16,18},{18,... | collective-permute-start | bytes 393224 | tf_op jit(solution)/shard_map/ppermute | solution.py:431
  232.8 7.1 %collective-permute-start.31 = (f32[256,128]{1,0:T(8,128)S(1)}, f32[256,128]{1,0:T(8,128)S(1)}, u32[]{:S(2)}, u32[]{:S(2)}) collective-permute-start(f32[256,128]{1,0:T(8,128)S(1)} %add.414), channel_id=1, source_target_pairs={{0,2},{2,0},{4,6},{6,4},{8,10},{10,8},{12,14},{14,12},{16,18},{18,... | collective-permute-start | bytes 393224 | tf_op jit(solution)/shard_map/ppermute | solution.py:431
  233.9 5.9 %collective-permute-start.33 = (f32[256,128]{1,0:T(8,128)S(1)}, f32[256,128]{1,0:T(8,128)S(1)}, u32[]{:S(2)}, u32[]{:S(2)}) collective-permute-start(f32[256,128]{1,0:T(8,128)S(1)} %select_add_fusion), channel_id=1, source_target_pairs={{0,4},{2,6},{4,0},{6,2},{8,12},{10,14},{12,8},{14,10},{16,20},{18,... | collective-permute-start | bytes 393224 | tf_op jit(solution)/shard_map/ppermute | solution.py:431
  236.1 17.0 %collective-permute-start.26 = (f32[1024,128]{1,0:T(8,128)S(1)}, f32[1024,128]{1,0:T(8,128)S(1)}, u32[]{:S(2)}, u32[]{:S(2)}) collective-permute-start(f32[1024,128]{1,0:T(8,128)S(1)} %constant_dynamic-slice_fusion.1), channel_id=1, source_target_pairs={{0,1},{1,0},{2,3},{3,2},{4,5},{5,4},{6,7},{7,6},{8,9},{9,8},{10,11... | collective-permute-start | bytes 1572872 | tf_op jit(solution)/shard_map/ppermute | solution.py:423
  239.8 5.2 %collective-permute-start.34 = (f32[256,128]{1,0:T(8,128)S(1)}, f32[256,128]{1,0:T(8,128)S(1)}, u32[]{:S(2)}, u32[]{:S(2)}) collective-permute-start(f32[256,128]{1,0:T(8,128)S(1)} %add.416), channel_id=1, source_target_pairs={{0,8},{2,10},{4,12},{6,14},{8,0},{10,2},{12,4},{14,6},{16,24},{18,... | collective-permute-start | bytes 393224 | tf_op jit(solution)/shard_map/ppermute | solution.py:431
  245.0 8.0 %collective-permute-start.35 = (f32[256,128]{1,0:T(8,128)S(1)}, f32[256,128]{1,0:T(8,128)S(1)}, u32[]{:S(2)}, u32[]{:S(2)}) collective-permute-start(f32[256,128]{1,0:T(8,128)S(1)} %add.417), channel_id=1, source_target_pairs={{0,16},{2,18},{4,20},{6,22},{8,24},{10,26},{12,28},{14,30},{16,0},... | collective-permute-start | bytes 393224 | tf_op jit(solution)/shard_map/ppermute | solution.py:431
  253.0 1.4 collective-permute-start.36
  (3 other events, 2.0 us)
Sparse Core Ops, SparseCore 0:
  100.1 73.1 all-gather.1

commit v9 on v8

--- a/solution.py
+++ b/solution.py
@@ -290,7 +290,7 @@
             row = lists_ref[readers_ref[3, step * GROUP + at], pl.ds(jnp.maximum(entry, 0), 1), :]
             kept = ((row > 0) | (entry == 0)) & (entry >= 0)
             masks.append(jnp.where(kept, 0.0, MASKED))
-            stats.append(stats_ref[readers_ref[0, step * GROUP + at]])
+            stats.append(stats_ref[readers_ref[4, step * GROUP + at]])
         masks.append(jnp.zeros((8 - GROUP, rows), F32))
         bias = mul(jnp.concatenate(masks, axis=0).astype(BF16), marks, 0, 0)
         stat = jnp.concatenate(stats, axis=1)
@@ -447,12 +447,20 @@
     return jnp.concatenate([low, high], axis=0)
 
 
-def gather_feats(part, lists, block_count, make_plan):
+def doubled_place(device, size):
+    place, bit = jnp.zeros_like(device), 1
+    while bit < size:
+        place = 2 * place + device // bit % 2
+        bit *= 2
+    return place
+
+
+def gather_feats(part, lists, block_count, make_plan, early):
     size, me = lax.axis_size("dom"), lax.axis_index("dom")
     if size != 16 or lax.axis_size("head") != 2 or block_count != 8:
         plan = make_plan(lax.all_gather(lists, "dom", axis=0, tiled=True), lambda ids: ids)
         everything = lax.all_gather(part, "dom", axis=0, tiled=True)
-        return [(everything, 0, everything.shape[0], 0)], lambda ids: ids, part, plan
+        return [(everything, 0, everything.shape[0], 0)], lambda ids: ids, part, plan, early
     side = lax.axis_index("head")
     lacked = block_count - RING
     rows = part.shape[0] // block_count
@@ -501,7 +509,7 @@
     held = (lax.ppermute(start, "dom", onward), lax.ppermute(start, "dom", back))
     twin = swap(part)
     all_notes = [notes, swap(notes)]
-    held, twin = lax.optimization_barrier((held, twin))
+    held, twin, early = lax.optimization_barrier((held, twin, early))
     pieces = [(part, 0, block_count * rows, 0), (twin, 0, block_count * rows, half)]
 
     def keep(value, swapped, slots):
@@ -570,7 +578,7 @@
     plan = make_plan(every.reshape((-1,) + lists.shape[1:]), place)
     lack, plan = lax.optimization_barrier((lack, plan))
     keep(lack[0], swap(lack[0]), (7,))
-    return pieces, place, late, plan
+    return pieces, place, late, plan, early
 
 
 def per_device(
@@ -595,13 +603,15 @@
             all_ids, me, block_count, dom_count * slot_cap
         )
         readers = all_ids[:, 0][rows_of]
-        return steps, jnp.stack([readers, place(readers), entry, rows_of]), lists
-
-    pieces, place, late, (steps, spots, lists) = gather_feats(
-        node_features, lists, block_count, make_plan
-    )
+        stat_of = doubled_place(readers // block_count, dom_count) * block_count
+        stat_of = stat_of + readers % block_count
+        return steps, jnp.stack([readers, place(readers), entry, rows_of, stat_of]), lists
+
     grad_mixed = lax.dot_general(
         out_cotangent, w_out, (((1,), (1,)), ((), ())), precision=lax.Precision.HIGHEST
+    )
+    pieces, place, late, (steps, spots, lists), grad_mixed = gather_feats(
+        node_features, lists, block_count, make_plan, grad_mixed
     )
     sent, late = lax.optimization_barrier((grad_mixed, late))
     all_grads = lax.all_gather(sent, "dom", axis=0, tiled=True)
@@ -610,7 +620,11 @@
         place(ids), pieces, dom_count * block_count, out_cotangent, grad_mixed, bias, w_query, w_key, w_value, w_out
     )
     layer_out = head_scatter(out_part)
-    all_stats = lax.all_gather(stats, "dom", axis=0, tiled=True)
+    all_stats = stats
+    bit = dom_count // 2
+    while bit:
+        all_stats = double(all_stats, bit)
+        bit //= 2
     pieces = [grad_out[:, at:at + cols] for at in range(0, width, cols)]
     grad_query, grad_out = dom_sum(grad_query, jnp.concatenate(pieces, axis=0))
     pieces = [grad_out[at:at + cols] for at in range(0, width, cols)]

time: 263 us -> 258 us (0.981)
  waiting for transfers between devices: 80.4 us -> 105 us
  blocking collectives: 21.2 us -> 0 us
  local copies, waits for them, and re-layouts: 23.9 us -> 14 us
  Pallas kernels: 73.1 us -> 81.9 us
  starting transfers between devices: 32 us -> 23.3 us
    all_gather x1 -> x0, blocking collectives: 21.2 us -> none  [per_device(): all_stats = lax.all_gather(stats, 'dom', axis=0, tiled=True)]
    ppermute x0 -> x4, waiting for transfers between devices: none -> 15.1 us  [double(): other = lax.ppermute(value, 'dom', [(at, at ^ bit) for at in range(size)])]
    ppermute x10, starting transfers between devices: 14.5 us -> 4.39 us  [from_across(): return lax.ppermute(value, 'dom', [(at, at ^ bit) for at in range(size)])]
    pallas_call x1, Pallas kernels: 34.6 us -> 43.6 us  [attend_backward(): pl.pallas_call(backward_kernel, out_shape=(jax.ShapeDtypeStruct((node_row...]
    unnamed x73 -> x71, local copies, waits for them, and re-layouts: 13.1 us -> 4.71 us
    ppermute x1, waiting for transfers between devices: 3.78 us -> 7.85 us  [gather_feats(): lax.ppermute(held[0][:RING // 2 * rows], 'dom', onward)]
    ppermute x13, waiting for transfers between devices: 3.46 us -> 6.78 us  [swap(): return lax.ppermute(value, 'dom', across)]
    ppermute x10, waiting for transfers between devices: 14.9 us -> 18 us  [from_across(): return lax.ppermute(value, 'dom', [(at, at ^ bit) for at in range(size)])]
  transfers between devices with their start and end apart: 38 -> 42, of which waited for: 20 -> 25; matrix products, arithmetic and copies ran while one was open for 14% -> 11% of each run, Pallas kernels for 28% -> 32%
where the time goes in v9:
time: 258 us; the launch traced here: 257 us
  waiting for transfers between devices  105 us (41%)
  Pallas kernels  81.9 us (32%)
  starting transfers between devices  23.3 us (9%)
  between operations  14.8 us (6%)
  other arithmetic  14.5 us (6%)
  local copies, waits for them, and re-layouts  14 us (5%)
  matrix products  2.68 us (1%)
    pallas_call x1, Pallas kernels, attend_backward(): pl.pallas_call(backward_kernel, out_shape=(jax.ShapeDtypeStruct((node_row...  43.6 us
    pallas_call x1, Pallas kernels, attend_forward(): pl.pallas_call(functools.partial(forward_kernel, entries, layout, len(arr...  38.4 us
    ppermute x4, waiting for transfers between devices, gather_feats(): more = (lax.ppermute(lacking(held), 'head', other_head),)  24.9 us
    ppermute x10, waiting for transfers between devices, from_across(): return lax.ppermute(value, 'dom', [(at, at ^ bit) for at in range(size)])  18 us
    ppermute x1, waiting for transfers between devices, gather_feats(): lax.ppermute(start, 'dom', onward)  16.2 us
    ppermute x4, waiting for transfers between devices, double(): other = lax.ppermute(value, 'dom', [(at, at ^ bit) for at in range(size)])  15.1 us
    ppermute x2, waiting for transfers between devices, gather_feats(): lax.ppermute(held[0], 'dom', onward)  9.93 us
    ppermute x1, waiting for transfers between devices, gather_feats(): lax.ppermute(held[0][:RING // 2 * rows], 'dom', onward)  7.85 us
  transfers between devices with their start and end apart: 42, of which 25 were waited for; matrix products, arithmetic and copies ran while one was open for 11% of the time, Pallas kernels for 32%

profile of v9, /device:TPU:0, one launch (start us, length us, event | category | flops | bytes accessed | tf_op | source)
XLA Modules:
  0.0 256.7 jit_solution(17616328302075834786)
XLA Ops:
  7.7 0.7 multiply_add_fusion
  8.5 0.7 fusion.10
  9.2 0.8 convert_element_type.58
  9.9 1.2 constant_dynamic-slice_fusion.9
  11.1 1.0 maximum_maximum_fusion
  12.1 2.8 %collective-permute-start = (f32[800,256]{1,0:T(8,128)}, f32[800,256]{1,0:T(8,128)S(1)}, u32[]{:S(2)}, u32[]{:S(2)}) collective-permute-start(f32[800,256]{1,0:T(8,128)} %maximum_maximum_fusion), channel_id=1, source_target_pairs={{0,8},{2,10},{8,16},{10,18},{16,24},{18,26},{24,28},{26,30},{28,20... | collective-permute-start | bytes 2457608 | tf_op jit(solution)/shard_map/ppermute | solution.py:509
  14.9 2.7 %fusion.38.refs_25_ = f32[1024,128]{1,0:T(8,128)} fusion(f32[1024,256]{1,0:T(8,128)S(1)} %copy-done.6, f32[128,256]{1,0:T(8,128)} %refs_30_.1), kind=kOutput, calls=%fused_computation.222 | convolution fusion | flops 402653184 | bytes 1703936 | tf_op jit(solution)/shard_map/dot_general | solution.py:610
  17.5 16.2 %collective-permute-done.refs_2_ = f32[800,256]{1,0:T(8,128)S(1)} collective-permute-done((f32[800,256]{1,0:T(8,128)}, f32[800,256]{1,0:T(8,128)S(1)}, u32[]{:S(2)}, u32[]{:S(2)}) %collective-permute-start) | collective-permute-done | bytes 819232 | tf_op jit(solution)/shard_map/ppermute | solution.py:509
  33.7 1.7 collective-permute-done.1.refs_4_
  35.4 1.6 collective-permute-start.3
  37.6 1.0 constant_dynamic-slice_fusion.7
  38.7 1.6 collective-permute-start.5
  40.3 12.6 %collective-permute-done.5.refs_10_ = f32[512,256]{1,0:T(8,128)S(1)} collective-permute-done((f32[512,256]{1,0:T(8,128)S(1)}, f32[512,256]{1,0:T(8,128)S(1)}, u32[]{:S(2)}, u32[]{:S(2)}) %collective-permute-start.5) | collective-permute-done | bytes 524320 | tf_op jit(solution)/shard_map/ppermute | solution.py:543
  52.8 1.9 collective-permute-done.3.refs_6_
  54.7 3.1 %collective-permute-done.4.refs_8_ = f32[800,256]{1,0:T(8,128)S(1)} collective-permute-done((f32[800,256]{1,0:T(8,128)}, f32[800,256]{1,0:T(8,128)S(1)}, u32[]{:S(2)}, u32[]{:S(2)}) %collective-permute-start.4) | collective-permute-done | bytes 819232 | tf_op jit(solution)/shard_map/ppermute | solution.py:532
  57.9 1.6 collective-permute-start.10
  59.5 1.2 collective-permute-done.17
  61.3 1.6 collective-permute-start.8
  63.3 8.3 %collective-permute-done.10.refs_16_ = f32[512,256]{1,0:T(8,128)S(1)} collective-permute-done((f32[512,256]{1,0:T(8,128)S(1)}, f32[512,256]{1,0:T(8,128)S(1)}, u32[]{:S(2)}, u32[]{:S(2)}) %collective-permute-start.10) | collective-permute-done | bytes 524320 | tf_op jit(solution)/shard_map/ppermute | solution.py:543
  71.6 0.8 constant_dynamic-update-slice_fusion.5
  72.4 1.1 collective-permute-done.13.refs_11_
  73.5 8.1 %collective-permute-done.8.refs_12_ = f32[800,256]{1,0:T(8,128)S(1)} collective-permute-done((f32[800,256]{1,0:T(8,128)S(1)}, f32[800,256]{1,0:T(8,128)S(1)}, u32[]{:S(2)}, u32[]{:S(2)}) %collective-permute-start.8) | collective-permute-done | bytes 819232 | tf_op jit(solution)/shard_map/ppermute | solution.py:532
  81.6 1.3 collective-permute-done.9.refs_14_
  84.1 1.6 collective-permute-start.14
  85.7 7.8 %collective-permute-done.14 = f32[384,256]{1,0:T(8,128)S(1)} collective-permute-done((f32[384,256]{1,0:T(8,128)S(1)}, f32[384,256]{1,0:T(8,128)S(1)}, u32[]{:S(2)}, u32[]{:S(2)}) %collective-permute-start.14) | collective-permute-done | bytes 393248 | tf_op jit(solution)/shard_map/ppermute | solution.py:536
  94.1 2.0 collective-permute-done.16.refs_20_
  97.4 0.7 constant_dynamic-slice_fusion.2
  98.1 1.0 constant_dynamic-update-slice_fusion.18
  99.2 3.3 %collective-permute-done.22.refs_17_ = f32[512,256]{1,0:T(8,128)S(1)} collective-permute-done((f32[512,256]{1,0:T(8,128)S(1)}, f32[512,256]{1,0:T(8,128)S(1)}, u32[]{:S(2)}, u32[]{:S(2)}) %collective-permute-start.22) | collective-permute-done | bytes 524320 | tf_op jit(solution)/shard_map/ppermute | solution.py:489
  103.1 0.8 copy-done.17
  106.1 1.2 gather_fusion
  108.3 0.7 pad.20.clone
  109.1 2.0 collective-permute-done.23.refs_22_
  111.2 0.6 copy.23
  111.8 1.1 collective-permute-done.24.refs_23_
  112.9 0.7 copy-done.26
  113.6 38.4 %attend_forward.1 = (f32[16384,256]{1,0:T(8,128)}, f32[1024,256]{1,0:T(8,128)}, f32[1024,256]{1,0:T(8,128)}, f32[8,8,128]{2,1,0:T(8,128)}, f32[256,128]{1,0:T(8,128)}, /*index=5*/f32[128,256]{1,0:T(8,128)}) custom-call(s32[8,8]{1,0:T(8,128)} %get-tuple-element.98.ids, f32[1024,256]{1,0:T(8,128)} %own_ref.1, f32[1024,256]{1,0:T(8,128)} %collective-permute-done.2.refs_1_, ...), custom_call_target="tpu_custom_call" | custom-call | tf_op jit(solution)/shard_map/attend_forward/pallas_call | solution.py:188
  152.0 1.6 collective-permute-start.26
  153.7 0.9 fusion.37
  154.6 4.9 %collective-permute-done.26 = f32[8,8,128]{2,1,0:T(8,128)S(1)} collective-permute-done((f32[8,8,128]{2,1,0:T(8,128)}, f32[8,8,128]{2,1,0:T(8,128)S(1)}, u32[]{:S(2)}, u32[]{:S(2)}) %collective-permute-start.26) | collective-permute-done | bytes 32800 | tf_op jit(solution)/shard_map/ppermute | solution.py:444
  159.5 0.8 broadcast_select_fusion.12
  160.4 0.7 collective-permute-start.31
  161.1 6.9 %collective-permute-done.27 = f32[16,8,128]{2,1,0:T(8,128)S(1)} collective-permute-done((f32[16,8,128]{2,1,0:T(8,128)S(1)}, f32[16,8,128]{2,1,0:T(8,128)S(1)}, u32[]{:S(2)}, u32[]{:S(2)}) %collective-permute-start.27) | collective-permute-done | bytes 65568 | tf_op jit(solution)/shard_map/ppermute | solution.py:444
  168.5 1.0 select_add_fusion.1
  169.5 1.6 collective-permute-start.32
  171.0 3.4 %collective-permute-done.28 = f32[32,8,128]{2,1,0:T(8,128)S(1)} collective-permute-done((f32[32,8,128]{2,1,0:T(8,128)S(1)}, f32[32,8,128]{2,1,0:T(8,128)S(1)}, u32[]{:S(2)}, u32[]{:S(2)}) %collective-permute-start.28) | collective-permute-done | bytes 131104 | tf_op jit(solution)/shard_map/ppermute | solution.py:444
  174.5 1.5 collective-permute-done.32
  176.2 1.9 constant_dynamic-slice_fusion
  178.1 3.1 %collective-permute-done.33 = f32[256,128]{1,0:T(8,128)S(1)} collective-permute-done((f32[256,128]{1,0:T(8,128)S(1)}, f32[256,128]{1,0:T(8,128)S(1)}, u32[]{:S(2)}, u32[]{:S(2)}) %collective-permute-start.33) | collective-permute-done | bytes 131104 | tf_op jit(solution)/shard_map/ppermute | solution.py:431
  181.1 0.7 add.526
  181.8 1.1 collective-permute-start.34
  183.1 43.6 %attend_backward.1 = (f32[1024,256]{1,0:T(8,128)S(1)}, f32[256,128]{1,0:T(8,128)S(1)}, f32[256,128]{1,0:T(8,128)S(1)}) custom-call(s32[3,40]{1,0:T(4,128)S(1)} %add_add_fusion.steps_ref, s32[5,80]{1,0:T(8,128)S(1)} %stack.8.readers_ref, f32[16384,256]{1,0:T(8,128)} %get-tuple-element.86.feats_ref, f32[16384,128]{1,0:T(8,128)} %all-gather.2.cloned.1.call-done.cots_ref, ...), custom_call_target="tpu_custom_call" | custom-call | tf_op jit(solution)/shard_map/attend_backward/pallas_call | solution.py:353
  226.7 0.6 copy-done.4
  227.4 1.0 add.527
  228.9 0.9 select_add_fusion
  230.0 2.1 dynamic-slice_add_fusion.1
  232.1 1.0 collective-permute-start.30
  233.1 2.3 collective-permute-done.37
  235.5 0.7 broadcast_select_fusion.2
  236.2 4.2 %collective-permute-done.38 = f32[256,128]{1,0:T(8,128)S(1)} collective-permute-done((f32[256,128]{1,0:T(8,128)S(1)}, f32[256,128]{1,0:T(8,128)S(1)}, u32[]{:S(2)}, u32[]{:S(2)}) %collective-permute-start.38) | collective-permute-done | bytes 131104 | tf_op jit(solution)/shard_map/ppermute | solution.py:431
  240.5 0.7 pad_maximum_fusion.7
  241.2 6.5 %collective-permute-done.39 = f32[256,128]{1,0:T(8,128)S(1)} collective-permute-done((f32[256,128]{1,0:T(8,128)S(1)}, f32[256,128]{1,0:T(8,128)S(1)}, u32[]{:S(2)}, u32[]{:S(2)}) %collective-permute-start.39) | collective-permute-done | bytes 131104 | tf_op jit(solution)/shard_map/ppermute | solution.py:431
  247.8 0.9 dynamic-slice_add_fusion
  249.1 0.7 broadcast_select_fusion.3
  (177 shorter events, 11.7 us)
Async XLA Ops:
  7.2 7.7 %copy-start.6 = (f32[1024,256]{1,0:T(8,128)S(1)}, f32[1024,256]{1,0:T(8,128)}, u32[]{:S(2)}) copy-start(f32[1024,256]{1,0:T(8,128)} %refs_24_.1) | copy-start | bytes 3145732
  7.2 175.8 %all-gather.2.cloned.1.call-start = ((), (), s32[]{:S(2)}) async-start(), calls=%async_computation | async-start | bytes 8912896 | tf_op jit(solution)/shard_map/all_gather | solution.py:617
  7.2 28.1 %collective-permute-start.2 = (f32[1024,256]{1,0:T(8,128)}, f32[1024,256]{1,0:T(8,128)}, u32[]{:S(2)}, u32[]{:S(2)}) collective-permute-start(f32[1024,256]{1,0:T(8,128)} %own_ref.1), channel_id=1, source_target_pairs={{0,2},{2,0},{4,6},{6,4},{8,10},{10,8},{12,14},{14,12},{16,18},{18,... | collective-permute-start | bytes 3145736 | tf_op jit(solution)/shard_map/ppermute | solution.py:489
  12.1 21.6 %collective-permute-start = (f32[800,256]{1,0:T(8,128)}, f32[800,256]{1,0:T(8,128)S(1)}, u32[]{:S(2)}, u32[]{:S(2)}) collective-permute-start(f32[800,256]{1,0:T(8,128)} %maximum_maximum_fusion), channel_id=1, source_target_pairs={{0,8},{2,10},{8,16},{10,18},{16,24},{18,26},{24,28},{26,30},{28,20... | collective-permute-start | bytes 2457608 | tf_op jit(solution)/shard_map/ppermute | solution.py:509
  14.9 20.5 %collective-permute-start.1 = (f32[800,256]{1,0:T(8,128)}, f32[800,256]{1,0:T(8,128)}, u32[]{:S(2)}, u32[]{:S(2)}) collective-permute-start(f32[800,256]{1,0:T(8,128)} %maximum_maximum_fusion), channel_id=1, source_target_pairs={{8,0},{10,2},{16,8},{18,10},{24,16},{26,18},{28,24},{30,26},{20,28... | collective-permute-start | bytes 2457608 | tf_op jit(solution)/shard_map/ppermute | solution.py:509
  33.7 52.0 %copy-start.10 = (f32[800,256]{1,0:T(8,128)}, f32[800,256]{1,0:T(8,128)S(1)}, u32[]{:S(2)}) copy-start(f32[800,256]{1,0:T(8,128)S(1)} %collective-permute-done.refs_2_) | copy-start | bytes 2457604
  35.4 19.3 %collective-permute-start.3 = (f32[800,256]{1,0:T(8,128)S(1)}, f32[800,256]{1,0:T(8,128)S(1)}, u32[]{:S(2)}, u32[]{:S(2)}) collective-permute-start(f32[800,256]{1,0:T(8,128)S(1)} %collective-permute-done.refs_2_), channel_id=1, source_target_pairs={{0,8},{2,10},{8,16},{10,18},{16,24},{18,26},{24,28},{26,30},{28,20... | collective-permute-start | bytes 2457608 | tf_op jit(solution)/shard_map/ppermute | solution.py:532
  36.9 20.9 %collective-permute-start.6 = (f32[800,256]{1,0:T(8,128)S(1)}, f32[800,256]{1,0:T(8,128)S(1)}, u32[]{:S(2)}, u32[]{:S(2)}) collective-permute-start(f32[800,256]{1,0:T(8,128)S(1)} %collective-permute-done.refs_2_), channel_id=1, source_target_pairs={{0,2},{2,0},{4,6},{6,4},{8,10},{10,8},{12,14},{14,12},{16,18},{18,... | collective-permute-start | bytes 2457608 | tf_op jit(solution)/shard_map/ppermute | solution.py:489
  36.9 20.9 %collective-permute-start.4 = (f32[800,256]{1,0:T(8,128)}, f32[800,256]{1,0:T(8,128)S(1)}, u32[]{:S(2)}, u32[]{:S(2)}) collective-permute-start(f32[800,256]{1,0:T(8,128)} %collective-permute-done.1.refs_4_), channel_id=1, source_target_pairs={{8,0},{10,2},{16,8},{18,10},{24,16},{26,18},{28,24},{30,26},{20,28... | collective-permute-start | bytes 2457608 | tf_op jit(solution)/shard_map/ppermute | solution.py:532
  37.4 20.4 %collective-permute-start.7 = (f32[800,256]{1,0:T(8,128)}, f32[800,256]{1,0:T(8,128)S(1)}, u32[]{:S(2)}, u32[]{:S(2)}) collective-permute-start(f32[800,256]{1,0:T(8,128)} %collective-permute-done.1.refs_4_), channel_id=1, source_target_pairs={{0,2},{2,0},{4,6},{6,4},{8,10},{10,8},{12,14},{14,12},{16,18},{18,... | collective-permute-start | bytes 2457608 | tf_op jit(solution)/shard_map/ppermute | solution.py:489
  38.7 14.2 %collective-permute-start.5 = (f32[512,256]{1,0:T(8,128)S(1)}, f32[512,256]{1,0:T(8,128)S(1)}, u32[]{:S(2)}, u32[]{:S(2)}) collective-permute-start(f32[512,256]{1,0:T(8,128)S(1)} %pad_maximum_fusion), channel_id=1, source_target_pairs={{0,1},{1,0},{2,3},{3,2},{4,5},{5,4},{6,7},{7,6},{8,9},{9,8},{10,11... | collective-permute-start | bytes 1572872 | tf_op jit(solution)/shard_map/ppermute | solution.py:543
  52.8 43.4 %copy-start.20 = (f32[512,256]{1,0:T(8,128)}, f32[512,256]{1,0:T(8,128)S(1)}, u32[]{:S(2)}) copy-start(f32[512,256]{1,0:T(8,128)S(1)} %collective-permute-done.5.refs_10_) | copy-start | bytes 1572868
  54.7 41.4 %copy-start.11 = (f32[800,256]{1,0:T(8,128)}, f32[800,256]{1,0:T(8,128)S(1)}, u32[]{:S(2)}) copy-start(f32[800,256]{1,0:T(8,128)S(1)} %collective-permute-done.3.refs_6_) | copy-start | bytes 2457604
  57.8 38.3 %copy-start.12 = (f32[800,256]{1,0:T(8,128)}, f32[800,256]{1,0:T(8,128)S(1)}, u32[]{:S(2)}) copy-start(f32[800,256]{1,0:T(8,128)S(1)} %collective-permute-done.4.refs_8_) | copy-start | bytes 2457604
  57.8 38.3 %copy-start.13 = (f32[800,256]{1,0:T(8,128)}, f32[800,256]{1,0:T(8,128)S(1)}, u32[]{:S(2)}) copy-start(f32[800,256]{1,0:T(8,128)S(1)} %collective-permute-done.6.refs_3_) | copy-start | bytes 2457604
  57.8 38.3 %copy-start.14 = (f32[800,256]{1,0:T(8,128)}, f32[800,256]{1,0:T(8,128)S(1)}, u32[]{:S(2)}) copy-start(f32[800,256]{1,0:T(8,128)S(1)} %collective-permute-done.7.refs_5_) | copy-start | bytes 2457604
  57.9 13.6 %collective-permute-start.10 = (f32[512,256]{1,0:T(8,128)S(1)}, f32[512,256]{1,0:T(8,128)S(1)}, u32[]{:S(2)}, u32[]{:S(2)}) collective-permute-start(f32[512,256]{1,0:T(8,128)S(1)} %pad_maximum_fusion.1), channel_id=1, source_target_pairs={{0,1},{1,0},{2,3},{3,2},{4,5},{5,4},{6,7},{7,6},{8,9},{9,8},{10,11... | collective-permute-start | bytes 1572872 | tf_op jit(solution)/shard_map/ppermute | solution.py:543
  59.5 1.2 collective-permute-start.17
  60.8 12.7 %collective-permute-start.11 = (f32[800,256]{1,0:T(8,128)S(1)}, f32[800,256]{1,0:T(8,128)S(1)}, u32[]{:S(2)}, u32[]{:S(2)}) collective-permute-start(f32[800,256]{1,0:T(8,128)S(1)} %collective-permute-done.3.refs_6_), channel_id=1, source_target_pairs={{0,2},{2,0},{4,6},{6,4},{8,10},{10,8},{12,14},{14,12},{16,18},{18,... | collective-permute-start | bytes 2457608 | tf_op jit(solution)/shard_map/ppermute | solution.py:489
  60.9 12.6 %collective-permute-start.12 = (f32[800,256]{1,0:T(8,128)S(1)}, f32[800,256]{1,0:T(8,128)S(1)}, u32[]{:S(2)}, u32[]{:S(2)}) collective-permute-start(f32[800,256]{1,0:T(8,128)S(1)} %collective-permute-done.4.refs_8_), channel_id=1, source_target_pairs={{0,2},{2,0},{4,6},{6,4},{8,10},{10,8},{12,14},{14,12},{16,18},{18,... | collective-permute-start | bytes 2457608 | tf_op jit(solution)/shard_map/ppermute | solution.py:489
  61.3 20.3 %collective-permute-start.8 = (f32[800,256]{1,0:T(8,128)S(1)}, f32[800,256]{1,0:T(8,128)S(1)}, u32[]{:S(2)}, u32[]{:S(2)}) collective-permute-start(f32[800,256]{1,0:T(8,128)S(1)} %collective-permute-done.3.refs_6_), channel_id=1, source_target_pairs={{0,8},{2,10},{8,16},{10,18},{16,24},{18,26},{24,28},{26,30},{28,20... | collective-permute-start | bytes 2457608 | tf_op jit(solution)/shard_map/ppermute | solution.py:532
  62.8 20.0 %collective-permute-start.9 = (f32[800,256]{1,0:T(8,128)S(1)}, f32[800,256]{1,0:T(8,128)S(1)}, u32[]{:S(2)}, u32[]{:S(2)}) collective-permute-start(f32[800,256]{1,0:T(8,128)S(1)} %collective-permute-done.4.refs_8_), channel_id=1, source_target_pairs={{8,0},{10,2},{16,8},{18,10},{24,16},{26,18},{28,24},{30,26},{20,28... | collective-permute-start | bytes 2457608 | tf_op jit(solution)/shard_map/ppermute | solution.py:532
  71.6 32.8 %copy-start.21 = (f32[512,256]{1,0:T(8,128)}, f32[512,256]{1,0:T(8,128)S(1)}, u32[]{:S(2)}) copy-start(f32[512,256]{1,0:T(8,128)S(1)} %collective-permute-done.10.refs_16_) | copy-start | bytes 1572868
  71.6 1.9 collective-permute-start.13
  73.5 8.1 %copy-start.22 = (f32[512,256]{1,0:T(8,128)}, f32[512,256]{1,0:T(8,128)S(1)}, u32[]{:S(2)}) copy-start(f32[512,256]{1,0:T(8,128)S(1)} %collective-permute-done.13.refs_11_) | copy-start | bytes 1572868
  73.5 22.6 %copy-start.15 = (f32[800,256]{1,0:T(8,128)}, f32[800,256]{1,0:T(8,128)S(1)}, u32[]{:S(2)}) copy-start(f32[800,256]{1,0:T(8,128)S(1)} %collective-permute-done.11.refs_7_) | copy-start | bytes 2457604
  73.5 22.7 %copy-start.16 = (f32[800,256]{1,0:T(8,128)}, f32[800,256]{1,0:T(8,128)S(1)}, u32[]{:S(2)}) copy-start(f32[800,256]{1,0:T(8,128)S(1)} %collective-permute-done.12.refs_9_) | copy-start | bytes 2457604
  81.6 22.8 %copy-start.8 = (f32[800,256]{1,0:T(8,128)}, f32[800,256]{1,0:T(8,128)S(1)}, u32[]{:S(2)}) copy-start(f32[800,256]{1,0:T(8,128)S(1)} %collective-permute-done.8.refs_12_) | copy-start | bytes 2457604
  82.9 21.6 %copy-start.7 = (f32[800,256]{1,0:T(8,128)}, f32[800,256]{1,0:T(8,128)S(1)}, u32[]{:S(2)}) copy-start(f32[800,256]{1,0:T(8,128)S(1)} %collective-permute-done.9.refs_14_) | copy-start | bytes 2457604
  83.0 28.2 %copy-start.27 = (s32[8,7,128]{2,0,1:T(8,128)S(1)}, s32[8,7,128]{2,0,1:T(8,128)}, u32[]{:S(2)}) copy-start(s32[8,7,128]{2,0,1:T(8,128)} %param.16) | copy-start | bytes 86020
  83.1 13.0 %collective-permute-start.16 = (f32[512,256]{1,0:T(8,128)S(1)}, f32[512,256]{1,0:T(8,128)}, u32[]{:S(2)}, u32[]{:S(2)}) collective-permute-start(f32[512,256]{1,0:T(8,128)S(1)} %pad_maximum_fusion.2), channel_id=1, source_target_pairs={{0,1},{1,0},{2,3},{3,2},{4,5},{5,4},{6,7},{7,6},{8,9},{9,8},{10,11... | collective-permute-start | bytes 1572872 | tf_op jit(solution)/shard_map/ppermute | solution.py:543
  83.6 10.5 %collective-permute-start.15 = (f32[416,256]{1,0:T(8,128)S(1)}, f32[416,256]{1,0:T(8,128)S(1)}, u32[]{:S(2)}, u32[]{:S(2)}) collective-permute-start(f32[416,256]{1,0:T(8,128)S(1)} %slice.92), channel_id=1, source_target_pairs={{8,0},{10,2},{16,8},{18,10},{24,16},{26,18},{28,24},{30,26},{20,28... | collective-permute-start | bytes 1277960 | tf_op jit(solution)/shard_map/ppermute | solution.py:537
  84.1 9.5 %collective-permute-start.14 = (f32[384,256]{1,0:T(8,128)S(1)}, f32[384,256]{1,0:T(8,128)S(1)}, u32[]{:S(2)}, u32[]{:S(2)}) collective-permute-start(f32[384,256]{1,0:T(8,128)S(1)} %slice.91), channel_id=1, source_target_pairs={{0,8},{2,10},{8,16},{10,18},{16,24},{18,26},{24,28},{26,30},{28,20... | collective-permute-start | bytes 1179656 | tf_op jit(solution)/shard_map/ppermute | solution.py:536
  85.7 10.5 %copy-start.25 = (f32[320,256]{1,0:T(8,128)}, f32[320,256]{1,0:T(8,128)S(1)}, u32[]{:S(2)}) copy-start(f32[320,256]{1,0:T(8,128)S(1)} %constant_dynamic-update-slice_fusion) | copy-start | bytes 983044
  96.2 16.7 %copy-start.9 = (f32[800,256]{1,0:T(8,128)}, f32[800,256]{1,0:T(8,128)S(1)}, u32[]{:S(2)}) copy-start(f32[800,256]{1,0:T(8,128)S(1)} %constant_dynamic-update-slice_fusion.10.refs_18_) | copy-start | bytes 2457604
  96.2 6.8 %collective-permute-start.20 = (f32[800,256]{1,0:T(8,128)S(1)}, f32[800,256]{1,0:T(8,128)S(1)}, u32[]{:S(2)}, u32[]{:S(2)}) collective-permute-start(f32[800,256]{1,0:T(8,128)S(1)} %collective-permute-done.8.refs_12_), channel_id=1, source_target_pairs={{0,2},{2,0},{4,6},{6,4},{8,10},{10,8},{12,14},{14,12},{16,18},{18,... | collective-permute-start | bytes 2457608 | tf_op jit(solution)/shard_map/ppermute | solution.py:489
  96.3 6.7 %collective-permute-start.21 = (f32[800,256]{1,0:T(8,128)S(1)}, f32[800,256]{1,0:T(8,128)S(1)}, u32[]{:S(2)}, u32[]{:S(2)}) collective-permute-start(f32[800,256]{1,0:T(8,128)S(1)} %collective-permute-done.9.refs_14_), channel_id=1, source_target_pairs={{0,2},{2,0},{4,6},{6,4},{8,10},{10,8},{12,14},{14,12},{16,18},{18,... | collective-permute-start | bytes 2457608 | tf_op jit(solution)/shard_map/ppermute | solution.py:489
  96.8 6.2 %collective-permute-start.18 = (f32[800,256]{1,0:T(8,128)S(1)}, f32[800,256]{1,0:T(8,128)S(1)}, u32[]{:S(2)}, u32[]{:S(2)}) collective-permute-start(f32[800,256]{1,0:T(8,128)S(1)} %constant_dynamic-update-slice_fusion.10.refs_18_), channel_id=1, source_target_pairs={{0,2},{2,0},{4,6},{6,4},{8,10},{10,8},{12,14},{14,12},{16,18},{18,... | collective-permute-start | bytes 2457608 | tf_op jit(solution)/shard_map/ppermute | solution.py:489
  96.9 5.6 %collective-permute-start.22 = (f32[512,256]{1,0:T(8,128)S(1)}, f32[512,256]{1,0:T(8,128)S(1)}, u32[]{:S(2)}, u32[]{:S(2)}) collective-permute-start(f32[512,256]{1,0:T(8,128)S(1)} %collective-permute-done.10.refs_16_), channel_id=1, source_target_pairs={{0,2},{2,0},{4,6},{6,4},{8,10},{10,8},{12,14},{14,12},{16,18},{18,... | collective-permute-start | bytes 1572872 | tf_op jit(solution)/shard_map/ppermute | solution.py:489
  97.3 5.7 %collective-permute-start.19 = (f32[512,256]{1,0:T(8,128)}, f32[512,256]{1,0:T(8,128)S(1)}, u32[]{:S(2)}, u32[]{:S(2)}) collective-permute-start(f32[512,256]{1,0:T(8,128)} %collective-permute-done.16.refs_20_), channel_id=1, source_target_pairs={{0,2},{2,0},{4,6},{6,4},{8,10},{10,8},{12,14},{14,12},{16,18},{18,... | collective-permute-start | bytes 1572872 | tf_op jit(solution)/shard_map/ppermute | solution.py:489
  102.5 10.4 %copy-start.23 = (f32[512,256]{1,0:T(8,128)}, f32[512,256]{1,0:T(8,128)S(1)}, u32[]{:S(2)}) copy-start(f32[512,256]{1,0:T(8,128)S(1)} %collective-permute-done.22.refs_17_) | copy-start | bytes 1572868
  102.5 8.7 %collective-permute-start.23 = (f32[256,256]{1,0:T(8,128)}, f32[256,256]{1,0:T(8,128)}, u32[]{:S(2)}, u32[]{:S(2)}) collective-permute-start(f32[256,256]{1,0:T(8,128)} %constant_dynamic-slice_fusion.2), channel_id=1, source_target_pairs={{0,1},{1,0},{2,3},{3,2},{4,5},{5,4},{6,7},{7,6},{8,9},{9,8},{10,11... | collective-permute-start | bytes 786440 | tf_op jit(solution)/shard_map/ppermute | solution.py:543
  103.0 1.6 copy-start.19
  111.2 1.7 collective-permute-start.24
  152.0 31.0 %copy-start = (f32[1024,256]{1,0:T(8,128)S(1)}, f32[1024,256]{1,0:T(8,128)}, u32[]{:S(2)}) copy-start(f32[1024,256]{1,0:T(8,128)} %own_ref.1) | copy-start | bytes 3145732
  152.0 31.0 %copy-start.1 = (f32[256,128]{1,0:T(8,128)S(1)}, f32[256,128]{1,0:T(8,128)}, u32[]{:S(2)}) copy-start(f32[256,128]{1,0:T(8,128)} %wq_ref.1) | copy-start | bytes 393220
  152.0 31.0 %copy-start.2 = (f32[256,128]{1,0:T(8,128)S(1)}, f32[256,128]{1,0:T(8,128)}, u32[]{:S(2)}) copy-start(f32[256,128]{1,0:T(8,128)} %wk_ref.1) | copy-start | bytes 393220
  152.0 31.0 %copy-start.3 = (f32[256,128]{1,0:T(8,128)S(1)}, f32[256,128]{1,0:T(8,128)}, u32[]{:S(2)}) copy-start(f32[256,128]{1,0:T(8,128)} %wv_ref.1) | copy-start | bytes 393220
  152.0 7.4 %collective-permute-start.26 = (f32[8,8,128]{2,1,0:T(8,128)}, f32[8,8,128]{2,1,0:T(8,128)S(1)}, u32[]{:S(2)}, u32[]{:S(2)}) collective-permute-start(f32[8,8,128]{2,1,0:T(8,128)} %get-tuple-element.88), channel_id=1, source_target_pairs={{0,16},{2,18},{4,20},{6,22},{8,24},{10,26},{12,28},{14,30},{16,0},... | collective-permute-start | bytes 98312 | tf_op jit(solution)/shard_map/ppermute | solution.py:444
  160.3 7.7 %collective-permute-start.27 = (f32[16,8,128]{2,1,0:T(8,128)S(1)}, f32[16,8,128]{2,1,0:T(8,128)S(1)}, u32[]{:S(2)}, u32[]{:S(2)}) collective-permute-start(f32[16,8,128]{2,1,0:T(8,128)S(1)} %pad_maximum_fusion.8), channel_id=1, source_target_pairs={{0,8},{2,10},{4,12},{6,14},{8,0},{10,2},{12,4},{14,6},{16,24},{18,... | collective-permute-start | bytes 196616 | tf_op jit(solution)/shard_map/ppermute | solution.py:444
  160.4 8.1 %collective-permute-start.31 = (f32[256,128]{1,0:T(8,128)S(1)}, f32[256,128]{1,0:T(8,128)S(1)}, u32[]{:S(2)}, u32[]{:S(2)}) collective-permute-start(f32[256,128]{1,0:T(8,128)S(1)} %fusion.1), channel_id=1, source_target_pairs={{0,2},{2,0},{4,6},{6,4},{8,10},{10,8},{12,14},{14,12},{16,18},{18,... | collective-permute-start | bytes 393224 | tf_op jit(solution)/shard_map/ppermute | solution.py:431
  168.0 6.5 %collective-permute-start.28 = (f32[32,8,128]{2,1,0:T(8,128)S(1)}, f32[32,8,128]{2,1,0:T(8,128)S(1)}, u32[]{:S(2)}, u32[]{:S(2)}) collective-permute-start(f32[32,8,128]{2,1,0:T(8,128)S(1)} %pad_maximum_fusion.5), channel_id=1, source_target_pairs={{0,4},{2,6},{4,0},{6,2},{8,12},{10,14},{12,8},{14,10},{16,20},{18,... | collective-permute-start | bytes 393224 | tf_op jit(solution)/shard_map/ppermute | solution.py:444
  169.5 6.6 %collective-permute-start.32 = (f32[256,128]{1,0:T(8,128)S(1)}, f32[256,128]{1,0:T(8,128)S(1)}, u32[]{:S(2)}, u32[]{:S(2)}) collective-permute-start(f32[256,128]{1,0:T(8,128)S(1)} %select_add_fusion.1), channel_id=1, source_target_pairs={{0,4},{2,6},{4,0},{6,2},{8,12},{10,14},{12,8},{14,10},{16,20},{18,... | collective-permute-start | bytes 393224 | tf_op jit(solution)/shard_map/ppermute | solution.py:431
  174.5 8.4 %collective-permute-start.29 = (f32[64,8,128]{2,1,0:T(8,128)S(1)}, f32[64,8,128]{2,1,0:T(8,128)S(1)}, u32[]{:S(2)}, u32[]{:S(2)}) collective-permute-start(f32[64,8,128]{2,1,0:T(8,128)S(1)} %pad_maximum_fusion.4), channel_id=1, source_target_pairs={{0,2},{2,0},{4,6},{6,4},{8,10},{10,8},{12,14},{14,12},{16,18},{18,... | collective-permute-start | bytes 786440 | tf_op jit(solution)/shard_map/ppermute | solution.py:444
  176.1 5.0 %collective-permute-start.33 = (f32[256,128]{1,0:T(8,128)S(1)}, f32[256,128]{1,0:T(8,128)S(1)}, u32[]{:S(2)}, u32[]{:S(2)}) collective-permute-start(f32[256,128]{1,0:T(8,128)S(1)} %add.525), channel_id=1, source_target_pairs={{0,8},{2,10},{4,12},{6,14},{8,0},{10,2},{12,4},{14,6},{16,24},{18,... | collective-permute-start | bytes 393224 | tf_op jit(solution)/shard_map/ppermute | solution.py:431
  178.0 51.9 %collective-permute-start.25 = (f32[1024,128]{1,0:T(8,128)}, f32[1024,128]{1,0:T(8,128)}, u32[]{:S(2)}, u32[]{:S(2)}) collective-permute-start(f32[1024,128]{1,0:T(8,128)} %constant_dynamic-slice_fusion), channel_id=1, source_target_pairs={{0,1},{1,0},{2,3},{3,2},{4,5},{5,4},{6,7},{7,6},{8,9},{9,8},{10,11... | collective-permute-start | bytes 1572872 | tf_op jit(solution)/shard_map/ppermute | solution.py:423
  181.8 45.6 %collective-permute-start.34 = (f32[256,128]{1,0:T(8,128)}, f32[256,128]{1,0:T(8,128)}, u32[]{:S(2)}, u32[]{:S(2)}) collective-permute-start(f32[256,128]{1,0:T(8,128)} %add.526), channel_id=1, source_target_pairs={{0,16},{2,18},{4,20},{6,22},{8,24},{10,26},{12,28},{14,30},{16,0},... | collective-permute-start | bytes 393224 | tf_op jit(solution)/shard_map/ppermute | solution.py:431
  227.3 1.6 collective-permute-start.36
  228.4 7.1 %collective-permute-start.35 = (f32[256,128]{1,0:T(8,128)S(1)}, f32[256,128]{1,0:T(8,128)S(1)}, u32[]{:S(2)}, u32[]{:S(2)}) collective-permute-start(f32[256,128]{1,0:T(8,128)S(1)} %add.527), channel_id=1, source_target_pairs={{0,2},{2,0},{4,6},{6,4},{8,10},{10,8},{12,14},{14,12},{16,18},{18,... | collective-permute-start | bytes 393224 | tf_op jit(solution)/shard_map/ppermute | solution.py:431
  229.9 5.5 %collective-permute-start.37 = (f32[256,128]{1,0:T(8,128)S(1)}, f32[256,128]{1,0:T(8,128)S(1)}, u32[]{:S(2)}, u32[]{:S(2)}) collective-permute-start(f32[256,128]{1,0:T(8,128)S(1)} %select_add_fusion), channel_id=1, source_target_pairs={{0,4},{2,6},{4,0},{6,2},{8,12},{10,14},{12,8},{14,10},{16,20},{18,... | collective-permute-start | bytes 393224 | tf_op jit(solution)/shard_map/ppermute | solution.py:431
  232.1 15.7 %collective-permute-start.30 = (f32[1024,128]{1,0:T(8,128)S(1)}, f32[1024,128]{1,0:T(8,128)S(1)}, u32[]{:S(2)}, u32[]{:S(2)}) collective-permute-start(f32[1024,128]{1,0:T(8,128)S(1)} %constant_dynamic-slice_fusion.1), channel_id=1, source_target_pairs={{0,1},{1,0},{2,3},{3,2},{4,5},{5,4},{6,7},{7,6},{8,9},{9,8},{10,11... | collective-permute-start | bytes 1572872 | tf_op jit(solution)/shard_map/ppermute | solution.py:423
  235.4 5.0 %collective-permute-start.38 = (f32[256,128]{1,0:T(8,128)S(1)}, f32[256,128]{1,0:T(8,128)S(1)}, u32[]{:S(2)}, u32[]{:S(2)}) collective-permute-start(f32[256,128]{1,0:T(8,128)S(1)} %add.529), channel_id=1, source_target_pairs={{0,8},{2,10},{4,12},{6,14},{8,0},{10,2},{12,4},{14,6},{16,24},{18,... | collective-permute-start | bytes 393224 | tf_op jit(solution)/shard_map/ppermute | solution.py:431
  240.4 7.2 %collective-permute-start.39 = (f32[256,128]{1,0:T(8,128)S(1)}, f32[256,128]{1,0:T(8,128)S(1)}, u32[]{:S(2)}, u32[]{:S(2)}) collective-permute-start(f32[256,128]{1,0:T(8,128)S(1)} %add.530), channel_id=1, source_target_pairs={{0,16},{2,18},{4,20},{6,22},{8,24},{10,26},{12,28},{14,30},{16,0},... | collective-permute-start | bytes 393224 | tf_op jit(solution)/shard_map/ppermute | solution.py:431
  247.7 1.4 collective-permute-start.40
  (6 other events, 5.5 us)
Sparse Core Ops, SparseCore 0:
  96.4 73.5 all-gather.1

commit v10 on v9

--- a/solution.py
+++ b/solution.py
@@ -412,27 +412,35 @@
     return jnp.stack([block, kind, jnp.full_like(kind, ends[-1])]), readers, entry
 
 
-def head_scatter(part):
-    size = lax.axis_size("head")
-    if size != 2:
-        return lax.psum_scatter(part, "head", scatter_dimension=1, tiled=True)
+def head_parts(part):
     me = lax.axis_index("head")
     half = part.shape[1] // 2
     sent = lax.dynamic_slice_in_dim(part, (1 - me) * half, half, axis=1)
-    kept = lax.dynamic_slice_in_dim(part, me * half, half, axis=1)
+    return sent, lax.dynamic_slice_in_dim(part, me * half, half, axis=1)
+
+
+def head_scatter(part, parts=None):
+    if lax.axis_size("head") != 2:
+        return lax.psum_scatter(part, "head", scatter_dimension=1, tiled=True)
+    sent, kept = head_parts(part) if parts is None else parts
     return kept + lax.ppermute(sent, "head", [(0, 1), (1, 0)])
 
 
-def dom_sum(first, second):
-    size = lax.axis_size("dom")
+def from_across(value, bit):
+    pairs = [(at, at ^ bit) for at in range(lax.axis_size("dom"))]
+    return lax.ppermute(value, "dom", pairs)
+
+
+def dom_sum_start(first, second):
     odd = lax.axis_index("dom") % 2 == 1
-
-    def from_across(value, bit):
-        return lax.ppermute(value, "dom", [(at, at ^ bit) for at in range(size)])
-
     mine = jnp.where(odd, second, first) + from_across(jnp.where(odd, first, second), 1)
-    bit = 2
-    while bit < size:
+    return mine + from_across(mine, 2)
+
+
+def dom_sum_end(mine):
+    odd = lax.axis_index("dom") % 2 == 1
+    bit = 4
+    while bit < lax.axis_size("dom"):
         mine = mine + from_across(mine, bit)
         bit *= 2
     other = from_across(mine, 1)
@@ -540,30 +548,34 @@
             all_notes = []
         else:
             coming = ()
-        more = (lax.ppermute(lacking(held), "head", other_head),)
+        sent = lacking(held)
+        if step == 4:
+            held, sent, waiting = lax.optimization_barrier((held, sent, waiting))
+        more = (lax.ppermute(sent, "head", other_head),)
         if step == 3:
-            waiting = (held, slots, lack, lack_slots)
             coming, held, more, notes = lax.optimization_barrier((coming, held, more, notes))
+            waiting, waiting_slots = (held, lack), (slots, lack_slots)
         else:
             swapped = tuple(swap(value) for value in held)
-            swapped_lack = tuple(swap(value) for value in lack)
+            swapped_lack = tuple(swap(value) for value in lack) if step < 3 else ()
             if step < 3:
                 coming, held, more, swapped, lack, swapped_lack = lax.optimization_barrier(
                     (coming, held, more, swapped, lack, swapped_lack)
                 )
             else:
-                old, old_slots, old_lack, old_lack_slots = waiting
+                (old, old_lack), (old_slots, old_lack_slots) = waiting, waiting_slots
                 old_swapped = tuple(swap(value) for value in old)
                 old_swapped_lack = tuple(swap(value) for value in old_lack)
-                held, swapped, lack, swapped_lack, old_swapped, old_swapped_lack = (
+                held, swapped, lack, old_swapped, old_swapped_lack = (
                     lax.optimization_barrier(
-                        (held, swapped, lack, swapped_lack, old_swapped, old_swapped_lack)
+                        (held, swapped, lack, old_swapped, old_swapped_lack)
                     )
                 )
+                last, last_slots = lack, lack_slots
                 keep_ring(old, old_swapped, old_slots)
                 keep(old_lack[0], old_swapped_lack[0], old_lack_slots)
             keep_ring(held, swapped, slots)
-            if lack:
+            if swapped_lack:
                 keep(lack[0], swapped_lack[0], lack_slots)
         lack, lack_slots = more, slots
         if step == 3:
@@ -576,7 +588,8 @@
     width = lists.shape[2]
     every = jnp.concatenate([every[:, :width], every[:, width:]], axis=0)
     plan = make_plan(every.reshape((-1,) + lists.shape[1:]), place)
-    lack, plan = lax.optimization_barrier((lack, plan))
+    lack, last, plan = lax.optimization_barrier((lack, last, plan))
+    keep(last[0], swap(last[0]), last_slots)
     keep(lack[0], swap(lack[0]), (7,))
     return pieces, place, late, plan, early
 
@@ -619,22 +632,28 @@
     all_feats, out_part, feat_part, stats, grad_query, grad_out = attend_forward(
         place(ids), pieces, dom_count * block_count, out_cotangent, grad_mixed, bias, w_query, w_key, w_value, w_out
     )
-    layer_out = head_scatter(out_part)
-    all_stats = stats
-    bit = dom_count // 2
+    all_stats, bit, out_parts = stats, dom_count // 2, None
     while bit:
         all_stats = double(all_stats, bit)
+        if out_parts is None and lax.axis_size("head") == 2:
+            all_stats, out_parts = lax.optimization_barrier((all_stats, head_parts(out_part)))
         bit //= 2
+    layer_out = head_scatter(out_part, out_parts)
     pieces = [grad_out[:, at:at + cols] for at in range(0, width, cols)]
-    grad_query, grad_out = dom_sum(grad_query, jnp.concatenate(pieces, axis=0))
-    pieces = [grad_out[at:at + cols] for at in range(0, width, cols)]
-    grad_out = jnp.concatenate(pieces, axis=1)
+    early_sum = dom_sum_start(grad_query, jnp.concatenate(pieces, axis=0))
     feats_part, grad_key, grad_value = attend_backward(
         steps, spots, all_feats, all_grads, all_stats, lists, node_features, feat_part,
         w_query, w_key, w_value, rows,
     )
+    early_sum, feats_part, grad_key, grad_value = lax.optimization_barrier(
+        (early_sum, feats_part, grad_key, grad_value)
+    )
     grad_features = head_scatter(feats_part)
-    grad_key, grad_value = dom_sum(grad_key, grad_value)
+    late_sum = dom_sum_start(grad_key, grad_value)
+    grad_query, grad_out = dom_sum_end(early_sum)
+    pieces = [grad_out[at:at + cols] for at in range(0, width, cols)]
+    grad_out = jnp.concatenate(pieces, axis=1)
+    grad_key, grad_value = dom_sum_end(late_sum)
     return (layer_out, grad_features, grad_query, grad_key, grad_value, grad_out)
 
 

time: 258 us -> 261 us (1.012)
  waiting for transfers between devices: 105 us -> 110 us
  other arithmetic: 14.5 us -> 10.8 us
  starting transfers between devices: 23.3 us -> 26.7 us
    ppermute x2, waiting for transfers between devices: 0.01 us -> 4.51 us  [head_scatter(): return kept + lax.ppermute(sent, 'head', [(0, 1), (1, 0)])]
    add x9 -> x8, other arithmetic: 3.66 us -> 0.14 us  [the longest x4 0.06 us: dom_sum_end(): mine = mine + from_across(mine, bit)]
    unnamed x71 -> x75, local copies, waits for them, and re-layouts: 4.71 us -> 5.77 us
  transfers between devices with their start and end apart: 42 -> 42, of which waited for: 25 -> 24; matrix products, arithmetic and copies ran while one was open for 11% -> 9% of each run, Pallas kernels for 32% -> 31%
where the time goes in v10:
time: 261 us; the launch traced here: 259 us
  waiting for transfers between devices  110 us (42%)
  Pallas kernels  80 us (31%)
  starting transfers between devices  26.7 us (10%)
  between operations  14.8 us (6%)
  local copies, waits for them, and re-layouts  14.4 us (6%)
  other arithmetic  10.8 us (4%)
  matrix products  2.69 us (1%)
    pallas_call x1, Pallas kernels, attend_backward(): pl.pallas_call(backward_kernel, out_shape=(jax.ShapeDtypeStruct((node_row...  41.6 us
    pallas_call x1, Pallas kernels, attend_forward(): pl.pallas_call(functools.partial(forward_kernel, entries, layout, len(arr...  38.4 us
    ppermute x4, waiting for transfers between devices, gather_feats(): more = (lax.ppermute(sent, 'head', other_head),)  22 us
    ppermute x10, waiting for transfers between devices, from_across(): return lax.ppermute(value, 'dom', pairs)  21.6 us
    ppermute x1, waiting for transfers between devices, gather_feats(): lax.ppermute(start, 'dom', onward)  15.9 us
    ppermute x4, waiting for transfers between devices, double(): other = lax.ppermute(value, 'dom', [(at, at ^ bit) for at in range(size)])  14.5 us
    ppermute x2, waiting for transfers between devices, gather_feats(): lax.ppermute(held[0], 'dom', onward)  10.9 us
    ppermute x1, waiting for transfers between devices, gather_feats(): lax.ppermute(held[0][:RING // 2 * rows], 'dom', onward)  7.85 us
  transfers between devices with their start and end apart: 42, of which 24 were waited for; matrix products, arithmetic and copies ran while one was open for 9% of the time, Pallas kernels for 31%

profile of v10, /device:TPU:0, one launch (start us, length us, event | category | flops | bytes accessed | tf_op | source)
XLA Modules:
  0.0 259.5 jit_solution(15727862825244466320)
XLA Ops:
  7.7 0.7 multiply_add_fusion
  8.5 0.7 fusion.10
  9.2 0.8 convert_element_type.58
  9.9 1.2 constant_dynamic-slice_fusion.10
  11.2 2.8 %collective-permute-start = (f32[800,256]{1,0:T(8,128)S(1)}, f32[800,256]{1,0:T(8,128)S(1)}, u32[]{:S(2)}, u32[]{:S(2)}) collective-permute-start(f32[800,256]{1,0:T(8,128)S(1)} %maximum_maximum_fusion), channel_id=1, source_target_pairs={{0,8},{2,10},{8,16},{10,18},{16,24},{18,26},{24,28},{26,30},{28,20... | collective-permute-start | bytes 2457608 | tf_op jit(solution)/shard_map/ppermute | solution.py:517
  14.0 2.7 %fusion.38.refs_25_ = f32[1024,128]{1,0:T(8,128)} fusion(f32[1024,256]{1,0:T(8,128)S(1)} %copy-done.4, f32[128,256]{1,0:T(8,128)} %refs_30_.1), kind=kOutput, calls=%fused_computation.222 | convolution fusion | flops 402653184 | bytes 1703936 | tf_op jit(solution)/shard_map/dot_general | solution.py:623
  16.7 15.9 %collective-permute-done.refs_2_ = f32[800,256]{1,0:T(8,128)S(1)} collective-permute-done((f32[800,256]{1,0:T(8,128)S(1)}, f32[800,256]{1,0:T(8,128)S(1)}, u32[]{:S(2)}, u32[]{:S(2)}) %collective-permute-start) | collective-permute-done | bytes 819232 | tf_op jit(solution)/shard_map/ppermute | solution.py:517
  32.7 1.5 collective-permute-done.1.refs_4_
  34.2 1.6 collective-permute-start.3
  36.6 1.6 collective-permute-start.5
  38.2 12.6 %collective-permute-done.5.refs_10_ = f32[512,256]{1,0:T(8,128)S(1)} collective-permute-done((f32[512,256]{1,0:T(8,128)S(1)}, f32[512,256]{1,0:T(8,128)S(1)}, u32[]{:S(2)}, u32[]{:S(2)}) %collective-permute-start.5) | collective-permute-done | bytes 524320 | tf_op jit(solution)/shard_map/ppermute | solution.py:554
  50.7 2.8 %collective-permute-done.3.refs_6_ = f32[800,256]{1,0:T(8,128)S(1)} collective-permute-done((f32[800,256]{1,0:T(8,128)S(1)}, f32[800,256]{1,0:T(8,128)S(1)}, u32[]{:S(2)}, u32[]{:S(2)}) %collective-permute-start.3) | collective-permute-done | bytes 819232 | tf_op jit(solution)/shard_map/ppermute | solution.py:540
  53.6 2.9 %collective-permute-done.4.refs_8_ = f32[800,256]{1,0:T(8,128)S(1)} collective-permute-done((f32[800,256]{1,0:T(8,128)S(1)}, f32[800,256]{1,0:T(8,128)S(1)}, u32[]{:S(2)}, u32[]{:S(2)}) %collective-permute-start.4) | collective-permute-done | bytes 819232 | tf_op jit(solution)/shard_map/ppermute | solution.py:540
  56.6 1.6 collective-permute-start.10
  58.2 1.2 collective-permute-done.17
  59.9 1.6 collective-permute-start.8
  61.9 0.8 constant_dynamic-update-slice_fusion.7
  62.7 7.5 %collective-permute-done.10.refs_16_ = f32[512,256]{1,0:T(8,128)S(1)} collective-permute-done((f32[512,256]{1,0:T(8,128)S(1)}, f32[512,256]{1,0:T(8,128)S(1)}, u32[]{:S(2)}, u32[]{:S(2)}) %collective-permute-start.10) | collective-permute-done | bytes 524320 | tf_op jit(solution)/shard_map/ppermute | solution.py:554
  70.2 0.8 constant_dynamic-update-slice_fusion.5
  71.0 1.1 collective-permute-done.13.refs_11_
  72.1 8.1 %collective-permute-done.8.refs_12_ = f32[800,256]{1,0:T(8,128)S(1)} collective-permute-done((f32[800,256]{1,0:T(8,128)S(1)}, f32[800,256]{1,0:T(8,128)S(1)}, u32[]{:S(2)}, u32[]{:S(2)}) %collective-permute-start.8) | collective-permute-done | bytes 819232 | tf_op jit(solution)/shard_map/ppermute | solution.py:540
  80.2 1.3 collective-permute-done.9.refs_14_
  81.7 0.6 collective-permute-start.16
  82.7 1.6 collective-permute-start.14
  84.3 7.8 %collective-permute-done.14 = f32[384,256]{1,0:T(8,128)S(1)} collective-permute-done((f32[384,256]{1,0:T(8,128)S(1)}, f32[384,256]{1,0:T(8,128)S(1)}, u32[]{:S(2)}, u32[]{:S(2)}) %collective-permute-start.14) | collective-permute-done | bytes 393248 | tf_op jit(solution)/shard_map/ppermute | solution.py:544
  92.7 1.9 collective-permute-done.16.refs_20_
  94.7 0.7 copy-done.23
  95.5 0.8 constant_dynamic-slice_fusion.3
  97.8 1.0 constant_dynamic-update-slice_fusion.18
  98.8 2.9 %collective-permute-done.21.refs_17_ = f32[512,256]{1,0:T(8,128)S(1)} collective-permute-done((f32[512,256]{1,0:T(8,128)S(1)}, f32[512,256]{1,0:T(8,128)S(1)}, u32[]{:S(2)}, u32[]{:S(2)}) %collective-permute-start.21) | collective-permute-done | bytes 524320 | tf_op jit(solution)/shard_map/ppermute | solution.py:497
  101.8 0.7 copy-done.25
  104.9 1.2 gather_fusion
  106.4 0.6 slice.110
  107.0 0.7 pad.20.clone
  108.3 0.6 copy.23
  109.0 1.4 collective-permute-done.24.refs_23_
  110.3 0.7 copy-done.28
  111.2 38.4 %attend_forward.1 = (f32[16384,256]{1,0:T(8,128)}, f32[1024,256]{1,0:T(8,128)}, f32[1024,256]{1,0:T(8,128)}, f32[8,8,128]{2,1,0:T(8,128)}, f32[256,128]{1,0:T(8,128)}, /*index=5*/f32[128,256]{1,0:T(8,128)}) custom-call(s32[8,8]{1,0:T(8,128)} %get-tuple-element.126.ids, f32[1024,256]{1,0:T(8,128)} %own_ref.1, f32[1024,256]{1,0:T(8,128)} %collective-permute-done.2.refs_1_, ...), custom_call_target="tpu_custom_call" | custom-call | tf_op jit(solution)/shard_map/attend_forward/pallas_call | solution.py:188
  149.7 1.6 collective-permute-start.25
  151.3 2.1 constant_dynamic-slice_fusion
  153.3 2.0 collective-permute-done.25
  155.3 0.8 broadcast_select_fusion.12
  156.1 1.1 collective-permute-start.29
  157.2 0.9 fusion.37
  158.0 7.6 %collective-permute-done.29 = f32[16,8,128]{2,1,0:T(8,128)S(1)} collective-permute-done((f32[16,8,128]{2,1,0:T(8,128)S(1)}, f32[16,8,128]{2,1,0:T(8,128)S(1)}, u32[]{:S(2)}, u32[]{:S(2)}) %collective-permute-start.29) | collective-permute-done | bytes 65568 | tf_op jit(solution)/shard_map/ppermute | solution.py:452
  165.9 4.8 %collective-permute-done.30 = f32[32,8,128]{2,1,0:T(8,128)S(1)} collective-permute-done((f32[32,8,128]{2,1,0:T(8,128)S(1)}, f32[32,8,128]{2,1,0:T(8,128)S(1)}, u32[]{:S(2)}, u32[]{:S(2)}) %collective-permute-start.30) | collective-permute-done | bytes 131104 | tf_op jit(solution)/shard_map/ppermute | solution.py:452
  171.0 1.6 collective-permute-start.26
  172.6 4.3 %collective-permute-done.28 = f32[256,128]{1,0:T(8,128)S(1)} collective-permute-done((f32[256,128]{1,0:T(8,128)S(1)}, f32[256,128]{1,0:T(8,128)S(1)}, u32[]{:S(2)}, u32[]{:S(2)}) %collective-permute-start.28) | collective-permute-done | bytes 131104 | tf_op jit(solution)/shard_map/ppermute | solution.py:431
  176.9 1.0 broadcast_select_fusion.1
  178.0 41.6 %attend_backward.1 = (f32[1024,256]{1,0:T(8,128)S(1)}, f32[256,128]{1,0:T(8,128)S(1)}, f32[256,128]{1,0:T(8,128)S(1)}) custom-call(s32[3,40]{1,0:T(4,128)S(1)} %add_add_fusion.steps_ref, s32[5,80]{1,0:T(8,128)S(1)} %stack.8.readers_ref, f32[16384,256]{1,0:T(8,128)} %get-tuple-element.112.feats_ref, f32[16384,128]{1,0:T(8,128)} %all-gather.2.cloned.1.call-done.cots_ref, ...), custom_call_target="tpu_custom_call" | custom-call | tf_op jit(solution)/shard_map/attend_backward/pallas_call | solution.py:353
  219.9 1.3 collective-permute-done.36
  221.1 1.0 collective-permute-start.37
  222.1 3.6 %collective-permute-done.33 = f32[256,128]{1,0:T(8,128)S(1)} collective-permute-done((f32[256,128]{1,0:T(8,128)S(1)}, f32[256,128]{1,0:T(8,128)S(1)}, u32[]{:S(2)}, u32[]{:S(2)}) %collective-permute-start.33) | collective-permute-done | bytes 131104 | tf_op jit(solution)/shard_map/ppermute | solution.py:431
  225.7 2.2 collective-permute-start.34
  227.9 1.8 collective-permute-start.38
  229.7 4.9 %collective-permute-done.34 = f32[256,128]{1,0:T(8,128)S(1)} collective-permute-done((f32[256,128]{1,0:T(8,128)S(1)}, f32[256,128]{1,0:T(8,128)S(1)}, u32[]{:S(2)}, u32[]{:S(2)}) %collective-permute-start.34) | collective-permute-done | bytes 131104 | tf_op jit(solution)/shard_map/ppermute | solution.py:431
  234.8 1.9 add.524
  236.8 0.8 collective-permute-start.39
  237.6 0.7 broadcast_select_fusion.4
  238.3 0.7 pad_maximum_fusion.7
  238.9 7.5 %collective-permute-done.39 = f32[256,128]{1,0:T(8,128)S(1)} collective-permute-done((f32[256,128]{1,0:T(8,128)S(1)}, f32[256,128]{1,0:T(8,128)S(1)}, u32[]{:S(2)}, u32[]{:S(2)}) %collective-permute-start.39) | collective-permute-done | bytes 131104 | tf_op jit(solution)/shard_map/ppermute | solution.py:431
  246.6 4.5 %collective-permute-done.32 = f32[1024,128]{1,0:T(8,128)S(1)} collective-permute-done((f32[1024,128]{1,0:T(8,128)S(1)}, f32[1024,128]{1,0:T(8,128)S(1)}, u32[]{:S(2)}, u32[]{:S(2)}) %collective-permute-start.32) | collective-permute-done | bytes 524320 | tf_op jit(solution)/shard_map/ppermute | solution.py:426
  251.1 0.9 dynamic-slice_add_fusion
  251.9 0.7 broadcast_select_fusion.5
  (180 shorter events, 9.7 us)
Async XLA Ops:
  7.2 170.8 %all-gather.2.cloned.1.call-start = ((), (), s32[]{:S(2)}) async-start(), calls=%async_computation | async-start | bytes 8912896 | tf_op jit(solution)/shard_map/all_gather | solution.py:630
  7.2 27.0 %collective-permute-start.2 = (f32[1024,256]{1,0:T(8,128)}, f32[1024,256]{1,0:T(8,128)}, u32[]{:S(2)}, u32[]{:S(2)}) collective-permute-start(f32[1024,256]{1,0:T(8,128)} %own_ref.1), channel_id=1, source_target_pairs={{0,2},{2,0},{4,6},{6,4},{8,10},{10,8},{12,14},{14,12},{16,18},{18,... | collective-permute-start | bytes 3145736 | tf_op jit(solution)/shard_map/ppermute | solution.py:497
  11.2 21.5 %collective-permute-start = (f32[800,256]{1,0:T(8,128)S(1)}, f32[800,256]{1,0:T(8,128)S(1)}, u32[]{:S(2)}, u32[]{:S(2)}) collective-permute-start(f32[800,256]{1,0:T(8,128)S(1)} %maximum_maximum_fusion), channel_id=1, source_target_pairs={{0,8},{2,10},{8,16},{10,18},{16,24},{18,26},{24,28},{26,30},{28,20... | collective-permute-start | bytes 2457608 | tf_op jit(solution)/shard_map/ppermute | solution.py:517
  14.0 20.2 %collective-permute-start.1 = (f32[800,256]{1,0:T(8,128)S(1)}, f32[800,256]{1,0:T(8,128)S(1)}, u32[]{:S(2)}, u32[]{:S(2)}) collective-permute-start(f32[800,256]{1,0:T(8,128)S(1)} %maximum_maximum_fusion), channel_id=1, source_target_pairs={{8,0},{10,2},{16,8},{18,10},{24,16},{26,18},{28,24},{30,26},{20,28... | collective-permute-start | bytes 2457608 | tf_op jit(solution)/shard_map/ppermute | solution.py:517
  32.7 26.9 %copy-start.8 = (f32[800,256]{1,0:T(8,128)}, f32[800,256]{1,0:T(8,128)S(1)}, u32[]{:S(2)}) copy-start(f32[800,256]{1,0:T(8,128)S(1)} %collective-permute-done.refs_2_) | copy-start | bytes 2457604
  34.2 25.4 %copy-start.9 = (f32[800,256]{1,0:T(8,128)}, f32[800,256]{1,0:T(8,128)S(1)}, u32[]{:S(2)}) copy-start(f32[800,256]{1,0:T(8,128)S(1)} %collective-permute-done.1.refs_4_) | copy-start | bytes 2457604
  34.2 19.3 %collective-permute-start.3 = (f32[800,256]{1,0:T(8,128)S(1)}, f32[800,256]{1,0:T(8,128)S(1)}, u32[]{:S(2)}, u32[]{:S(2)}) collective-permute-start(f32[800,256]{1,0:T(8,128)S(1)} %collective-permute-done.refs_2_), channel_id=1, source_target_pairs={{0,8},{2,10},{8,16},{10,18},{16,24},{18,26},{24,28},{26,30},{28,20... | collective-permute-start | bytes 2457608 | tf_op jit(solution)/shard_map/ppermute | solution.py:540
  35.8 20.7 %collective-permute-start.6 = (f32[800,256]{1,0:T(8,128)S(1)}, f32[800,256]{1,0:T(8,128)S(1)}, u32[]{:S(2)}, u32[]{:S(2)}) collective-permute-start(f32[800,256]{1,0:T(8,128)S(1)} %collective-permute-done.refs_2_), channel_id=1, source_target_pairs={{0,2},{2,0},{4,6},{6,4},{8,10},{10,8},{12,14},{14,12},{16,18},{18,... | collective-permute-start | bytes 2457608 | tf_op jit(solution)/shard_map/ppermute | solution.py:497
  35.8 20.7 %collective-permute-start.4 = (f32[800,256]{1,0:T(8,128)S(1)}, f32[800,256]{1,0:T(8,128)S(1)}, u32[]{:S(2)}, u32[]{:S(2)}) collective-permute-start(f32[800,256]{1,0:T(8,128)S(1)} %collective-permute-done.1.refs_4_), channel_id=1, source_target_pairs={{8,0},{10,2},{16,8},{18,10},{24,16},{26,18},{28,24},{30,26},{20,28... | collective-permute-start | bytes 2457608 | tf_op jit(solution)/shard_map/ppermute | solution.py:540
  36.2 20.2 %collective-permute-start.7 = (f32[800,256]{1,0:T(8,128)S(1)}, f32[800,256]{1,0:T(8,128)S(1)}, u32[]{:S(2)}, u32[]{:S(2)}) collective-permute-start(f32[800,256]{1,0:T(8,128)S(1)} %collective-permute-done.1.refs_4_), channel_id=1, source_target_pairs={{0,2},{2,0},{4,6},{6,4},{8,10},{10,8},{12,14},{14,12},{16,18},{18,... | collective-permute-start | bytes 2457608 | tf_op jit(solution)/shard_map/ppermute | solution.py:497
  36.6 14.2 %collective-permute-start.5 = (f32[512,256]{1,0:T(8,128)S(1)}, f32[512,256]{1,0:T(8,128)S(1)}, u32[]{:S(2)}, u32[]{:S(2)}) collective-permute-start(f32[512,256]{1,0:T(8,128)S(1)} %pad_maximum_fusion), channel_id=1, source_target_pairs={{0,1},{1,0},{2,3},{3,2},{4,5},{5,4},{6,7},{7,6},{8,9},{9,8},{10,11... | collective-permute-start | bytes 1572872 | tf_op jit(solution)/shard_map/ppermute | solution.py:554
  50.7 44.8 %copy-start.20 = (f32[512,256]{1,0:T(8,128)}, f32[512,256]{1,0:T(8,128)S(1)}, u32[]{:S(2)}) copy-start(f32[512,256]{1,0:T(8,128)S(1)} %collective-permute-done.5.refs_10_) | copy-start | bytes 1572868
  53.6 41.1 %copy-start.10 = (f32[800,256]{1,0:T(8,128)}, f32[800,256]{1,0:T(8,128)S(1)}, u32[]{:S(2)}) copy-start(f32[800,256]{1,0:T(8,128)S(1)} %collective-permute-done.3.refs_6_) | copy-start | bytes 2457604
  56.4 38.2 %copy-start.11 = (f32[800,256]{1,0:T(8,128)}, f32[800,256]{1,0:T(8,128)S(1)}, u32[]{:S(2)}) copy-start(f32[800,256]{1,0:T(8,128)S(1)} %collective-permute-done.4.refs_8_) | copy-start | bytes 2457604
  56.5 38.2 %copy-start.12 = (f32[800,256]{1,0:T(8,128)}, f32[800,256]{1,0:T(8,128)S(1)}, u32[]{:S(2)}) copy-start(f32[800,256]{1,0:T(8,128)S(1)} %collective-permute-done.6.refs_3_) | copy-start | bytes 2457604
  56.5 38.2 %copy-start.13 = (f32[800,256]{1,0:T(8,128)}, f32[800,256]{1,0:T(8,128)S(1)}, u32[]{:S(2)}) copy-start(f32[800,256]{1,0:T(8,128)S(1)} %collective-permute-done.7.refs_5_) | copy-start | bytes 2457604
  56.6 13.6 %collective-permute-start.10 = (f32[512,256]{1,0:T(8,128)S(1)}, f32[512,256]{1,0:T(8,128)S(1)}, u32[]{:S(2)}, u32[]{:S(2)}) collective-permute-start(f32[512,256]{1,0:T(8,128)S(1)} %pad_maximum_fusion.1), channel_id=1, source_target_pairs={{0,1},{1,0},{2,3},{3,2},{4,5},{5,4},{6,7},{7,6},{8,9},{9,8},{10,11... | collective-permute-start | bytes 1572872 | tf_op jit(solution)/shard_map/ppermute | solution.py:554
  58.2 1.2 collective-permute-start.17
  59.4 12.7 %collective-permute-start.11 = (f32[800,256]{1,0:T(8,128)S(1)}, f32[800,256]{1,0:T(8,128)S(1)}, u32[]{:S(2)}, u32[]{:S(2)}) collective-permute-start(f32[800,256]{1,0:T(8,128)S(1)} %collective-permute-done.3.refs_6_), channel_id=1, source_target_pairs={{0,2},{2,0},{4,6},{6,4},{8,10},{10,8},{12,14},{14,12},{16,18},{18,... | collective-permute-start | bytes 2457608 | tf_op jit(solution)/shard_map/ppermute | solution.py:497
  59.6 12.6 %collective-permute-start.12 = (f32[800,256]{1,0:T(8,128)S(1)}, f32[800,256]{1,0:T(8,128)S(1)}, u32[]{:S(2)}, u32[]{:S(2)}) collective-permute-start(f32[800,256]{1,0:T(8,128)S(1)} %collective-permute-done.4.refs_8_), channel_id=1, source_target_pairs={{0,2},{2,0},{4,6},{6,4},{8,10},{10,8},{12,14},{14,12},{16,18},{18,... | collective-permute-start | bytes 2457608 | tf_op jit(solution)/shard_map/ppermute | solution.py:497
  59.9 20.3 %collective-permute-start.8 = (f32[800,256]{1,0:T(8,128)S(1)}, f32[800,256]{1,0:T(8,128)S(1)}, u32[]{:S(2)}, u32[]{:S(2)}) collective-permute-start(f32[800,256]{1,0:T(8,128)S(1)} %collective-permute-done.3.refs_6_), channel_id=1, source_target_pairs={{0,8},{2,10},{8,16},{10,18},{16,24},{18,26},{24,28},{26,30},{28,20... | collective-permute-start | bytes 2457608 | tf_op jit(solution)/shard_map/ppermute | solution.py:540
  61.5 20.0 %collective-permute-start.9 = (f32[800,256]{1,0:T(8,128)S(1)}, f32[800,256]{1,0:T(8,128)S(1)}, u32[]{:S(2)}, u32[]{:S(2)}) collective-permute-start(f32[800,256]{1,0:T(8,128)S(1)} %collective-permute-done.4.refs_8_), channel_id=1, source_target_pairs={{8,0},{10,2},{16,8},{18,10},{24,16},{26,18},{28,24},{30,26},{20,28... | collective-permute-start | bytes 2457608 | tf_op jit(solution)/shard_map/ppermute | solution.py:540
  70.2 33.0 %copy-start.21 = (f32[512,256]{1,0:T(8,128)}, f32[512,256]{1,0:T(8,128)S(1)}, u32[]{:S(2)}) copy-start(f32[512,256]{1,0:T(8,128)S(1)} %collective-permute-done.10.refs_16_) | copy-start | bytes 1572868
  70.2 1.9 collective-permute-start.13
  72.1 20.6 %copy-start.22 = (f32[512,256]{1,0:T(8,128)}, f32[512,256]{1,0:T(8,128)S(1)}, u32[]{:S(2)}) copy-start(f32[512,256]{1,0:T(8,128)S(1)} %collective-permute-done.13.refs_11_) | copy-start | bytes 1572868
  72.1 22.6 %copy-start.14 = (f32[800,256]{1,0:T(8,128)}, f32[800,256]{1,0:T(8,128)S(1)}, u32[]{:S(2)}) copy-start(f32[800,256]{1,0:T(8,128)S(1)} %collective-permute-done.11.refs_7_) | copy-start | bytes 2457604
  72.1 22.6 %copy-start.15 = (f32[800,256]{1,0:T(8,128)}, f32[800,256]{1,0:T(8,128)S(1)}, u32[]{:S(2)}) copy-start(f32[800,256]{1,0:T(8,128)S(1)} %collective-permute-done.12.refs_9_) | copy-start | bytes 2457604
  80.2 23.0 %copy-start.6 = (f32[800,256]{1,0:T(8,128)}, f32[800,256]{1,0:T(8,128)S(1)}, u32[]{:S(2)}) copy-start(f32[800,256]{1,0:T(8,128)S(1)} %collective-permute-done.8.refs_12_) | copy-start | bytes 2457604
  81.5 21.7 %copy-start.5 = (f32[800,256]{1,0:T(8,128)}, f32[800,256]{1,0:T(8,128)S(1)}, u32[]{:S(2)}) copy-start(f32[800,256]{1,0:T(8,128)S(1)} %collective-permute-done.9.refs_14_) | copy-start | bytes 2457604
  81.6 26.7 %copy-start.29 = (s32[8,7,128]{2,0,1:T(8,128)S(1)}, s32[8,7,128]{2,0,1:T(8,128)}, u32[]{:S(2)}) copy-start(s32[8,7,128]{2,0,1:T(8,128)} %param.16) | copy-start | bytes 86020
  81.7 12.9 %collective-permute-start.16 = (f32[512,256]{1,0:T(8,128)S(1)}, f32[512,256]{1,0:T(8,128)S(1)}, u32[]{:S(2)}, u32[]{:S(2)}) collective-permute-start(f32[512,256]{1,0:T(8,128)S(1)} %pad_maximum_fusion.2), channel_id=1, source_target_pairs={{0,1},{1,0},{2,3},{3,2},{4,5},{5,4},{6,7},{7,6},{8,9},{9,8},{10,11... | collective-permute-start | bytes 1572872 | tf_op jit(solution)/shard_map/ppermute | solution.py:554
  82.3 10.5 %collective-permute-start.15 = (f32[416,256]{1,0:T(8,128)S(1)}, f32[416,256]{1,0:T(8,128)S(1)}, u32[]{:S(2)}, u32[]{:S(2)}) collective-permute-start(f32[416,256]{1,0:T(8,128)S(1)} %slice.92), channel_id=1, source_target_pairs={{8,0},{10,2},{16,8},{18,10},{24,16},{26,18},{28,24},{30,26},{20,28... | collective-permute-start | bytes 1277960 | tf_op jit(solution)/shard_map/ppermute | solution.py:545
  82.7 9.5 %collective-permute-start.14 = (f32[384,256]{1,0:T(8,128)S(1)}, f32[384,256]{1,0:T(8,128)S(1)}, u32[]{:S(2)}, u32[]{:S(2)}) collective-permute-start(f32[384,256]{1,0:T(8,128)S(1)} %slice.91), channel_id=1, source_target_pairs={{0,8},{2,10},{8,16},{10,18},{16,24},{18,26},{24,28},{26,30},{28,20... | collective-permute-start | bytes 1179656 | tf_op jit(solution)/shard_map/ppermute | solution.py:544
  84.3 10.4 %copy-start.27 = (f32[320,256]{1,0:T(8,128)}, f32[320,256]{1,0:T(8,128)S(1)}, u32[]{:S(2)}) copy-start(f32[320,256]{1,0:T(8,128)S(1)} %constant_dynamic-update-slice_fusion) | copy-start | bytes 983044
  95.5 14.9 %copy-start.7 = (f32[800,256]{1,0:T(8,128)}, f32[800,256]{1,0:T(8,128)S(1)}, u32[]{:S(2)}) copy-start(f32[800,256]{1,0:T(8,128)S(1)} %constant_dynamic-update-slice_fusion.10.refs_18_) | copy-start | bytes 2457604
  96.3 11.5 %copy-start.24 = (f32[512,256]{1,0:T(8,128)S(1)}, f32[512,256]{1,0:T(8,128)}, u32[]{:S(2)}) copy-start(f32[512,256]{1,0:T(8,128)} %copy-done.23) | copy-start | bytes 1572868
  96.3 5.4 %collective-permute-start.18 = (f32[800,256]{1,0:T(8,128)S(1)}, f32[800,256]{1,0:T(8,128)S(1)}, u32[]{:S(2)}, u32[]{:S(2)}) collective-permute-start(f32[800,256]{1,0:T(8,128)S(1)} %constant_dynamic-update-slice_fusion.10.refs_18_), channel_id=1, source_target_pairs={{0,2},{2,0},{4,6},{6,4},{8,10},{10,8},{12,14},{14,12},{16,18},{18,... | collective-permute-start | bytes 2457608 | tf_op jit(solution)/shard_map/ppermute | solution.py:497
  96.3 5.4 %collective-permute-start.19 = (f32[800,256]{1,0:T(8,128)S(1)}, f32[800,256]{1,0:T(8,128)S(1)}, u32[]{:S(2)}, u32[]{:S(2)}) collective-permute-start(f32[800,256]{1,0:T(8,128)S(1)} %collective-permute-done.8.refs_12_), channel_id=1, source_target_pairs={{0,2},{2,0},{4,6},{6,4},{8,10},{10,8},{12,14},{14,12},{16,18},{18,... | collective-permute-start | bytes 2457608 | tf_op jit(solution)/shard_map/ppermute | solution.py:497
  96.8 4.9 %collective-permute-start.20 = (f32[800,256]{1,0:T(8,128)S(1)}, f32[800,256]{1,0:T(8,128)S(1)}, u32[]{:S(2)}, u32[]{:S(2)}) collective-permute-start(f32[800,256]{1,0:T(8,128)S(1)} %collective-permute-done.9.refs_14_), channel_id=1, source_target_pairs={{0,2},{2,0},{4,6},{6,4},{8,10},{10,8},{12,14},{14,12},{16,18},{18,... | collective-permute-start | bytes 2457608 | tf_op jit(solution)/shard_map/ppermute | solution.py:497
  96.8 4.9 %collective-permute-start.21 = (f32[512,256]{1,0:T(8,128)S(1)}, f32[512,256]{1,0:T(8,128)S(1)}, u32[]{:S(2)}, u32[]{:S(2)}) collective-permute-start(f32[512,256]{1,0:T(8,128)S(1)} %collective-permute-done.10.refs_16_), channel_id=1, source_target_pairs={{0,2},{2,0},{4,6},{6,4},{8,10},{10,8},{12,14},{14,12},{16,18},{18,... | collective-permute-start | bytes 1572872 | tf_op jit(solution)/shard_map/ppermute | solution.py:497
  97.3 10.5 %collective-permute-start.22 = (f32[256,256]{1,0:T(8,128)}, f32[256,256]{1,0:T(8,128)}, u32[]{:S(2)}, u32[]{:S(2)}) collective-permute-start(f32[256,256]{1,0:T(8,128)} %constant_dynamic-slice_fusion.3), channel_id=1, source_target_pairs={{0,1},{1,0},{2,3},{3,2},{4,5},{5,4},{6,7},{7,6},{8,9},{9,8},{10,11... | collective-permute-start | bytes 786440 | tf_op jit(solution)/shard_map/ppermute | solution.py:554
  107.8 2.5 collective-permute-start.23
  107.9 2.4 collective-permute-start.24
  149.6 21.3 %copy-start.19 = (f32[256,128]{1,0:T(8,128)S(1)}, f32[256,128]{1,0:T(8,128)}, u32[]{:S(2)}) copy-start(f32[256,128]{1,0:T(8,128)} %get-tuple-element.109) | copy-start | bytes 393220
  149.6 28.4 %copy-start = (f32[1024,256]{1,0:T(8,128)S(1)}, f32[1024,256]{1,0:T(8,128)}, u32[]{:S(2)}) copy-start(f32[1024,256]{1,0:T(8,128)} %own_ref.1) | copy-start | bytes 3145732
  149.6 28.4 %copy-start.1 = (f32[256,128]{1,0:T(8,128)S(1)}, f32[256,128]{1,0:T(8,128)}, u32[]{:S(2)}) copy-start(f32[256,128]{1,0:T(8,128)} %wq_ref.1) | copy-start | bytes 393220
  149.7 28.4 %copy-start.2 = (f32[256,128]{1,0:T(8,128)S(1)}, f32[256,128]{1,0:T(8,128)}, u32[]{:S(2)}) copy-start(f32[256,128]{1,0:T(8,128)} %wk_ref.1) | copy-start | bytes 393220
  149.7 28.4 %copy-start.3 = (f32[256,128]{1,0:T(8,128)S(1)}, f32[256,128]{1,0:T(8,128)}, u32[]{:S(2)}) copy-start(f32[256,128]{1,0:T(8,128)} %wv_ref.1) | copy-start | bytes 393220
  149.7 5.6 %collective-permute-start.25 = (f32[8,8,128]{2,1,0:T(8,128)}, f32[8,8,128]{2,1,0:T(8,128)S(1)}, u32[]{:S(2)}, u32[]{:S(2)}) collective-permute-start(f32[8,8,128]{2,1,0:T(8,128)} %get-tuple-element.104), channel_id=1, source_target_pairs={{0,16},{2,18},{4,20},{6,22},{8,24},{10,26},{12,28},{14,30},{16,0},... | collective-permute-start | bytes 98312 | tf_op jit(solution)/shard_map/ppermute | solution.py:452
  156.1 9.6 %collective-permute-start.29 = (f32[16,8,128]{2,1,0:T(8,128)S(1)}, f32[16,8,128]{2,1,0:T(8,128)S(1)}, u32[]{:S(2)}, u32[]{:S(2)}) collective-permute-start(f32[16,8,128]{2,1,0:T(8,128)S(1)} %pad_maximum_fusion.8), channel_id=1, source_target_pairs={{0,8},{2,10},{4,12},{6,14},{8,0},{10,2},{12,4},{14,6},{16,24},{18,... | collective-permute-start | bytes 196616 | tf_op jit(solution)/shard_map/ppermute | solution.py:452
  165.7 5.0 %collective-permute-start.30 = (f32[32,8,128]{2,1,0:T(8,128)S(1)}, f32[32,8,128]{2,1,0:T(8,128)S(1)}, u32[]{:S(2)}, u32[]{:S(2)}) collective-permute-start(f32[32,8,128]{2,1,0:T(8,128)S(1)} %pad_maximum_fusion.6), channel_id=1, source_target_pairs={{0,4},{2,6},{4,0},{6,2},{8,12},{10,14},{12,8},{14,10},{16,20},{18,... | collective-permute-start | bytes 393224 | tf_op jit(solution)/shard_map/ppermute | solution.py:452
  165.8 5.1 %collective-permute-start.27 = (f32[256,128]{1,0:T(8,128)S(1)}, f32[256,128]{1,0:T(8,128)S(1)}, u32[]{:S(2)}, u32[]{:S(2)}) collective-permute-start(f32[256,128]{1,0:T(8,128)S(1)} %fusion.1), channel_id=1, source_target_pairs={{0,2},{2,0},{4,6},{6,4},{8,10},{10,8},{12,14},{14,12},{16,18},{18,... | collective-permute-start | bytes 393224 | tf_op jit(solution)/shard_map/ppermute | solution.py:431
  170.8 6.1 %collective-permute-start.31 = (f32[64,8,128]{2,1,0:T(8,128)S(1)}, f32[64,8,128]{2,1,0:T(8,128)}, u32[]{:S(2)}, u32[]{:S(2)}) collective-permute-start(f32[64,8,128]{2,1,0:T(8,128)S(1)} %pad_maximum_fusion.4), channel_id=1, source_target_pairs={{0,2},{2,0},{4,6},{6,4},{8,10},{10,8},{12,14},{14,12},{16,18},{18,... | collective-permute-start | bytes 786440 | tf_op jit(solution)/shard_map/ppermute | solution.py:452
  170.9 5.9 %collective-permute-start.28 = (f32[256,128]{1,0:T(8,128)S(1)}, f32[256,128]{1,0:T(8,128)S(1)}, u32[]{:S(2)}, u32[]{:S(2)}) collective-permute-start(f32[256,128]{1,0:T(8,128)S(1)} %select_add_fusion.1), channel_id=1, source_target_pairs={{0,4},{2,6},{4,0},{6,2},{8,12},{10,14},{12,8},{14,10},{16,20},{18,... | collective-permute-start | bytes 393224 | tf_op jit(solution)/shard_map/ppermute | solution.py:431
  171.0 63.7 %collective-permute-start.26 = (f32[1024,128]{1,0:T(8,128)}, f32[1024,128]{1,0:T(8,128)}, u32[]{:S(2)}, u32[]{:S(2)}) collective-permute-start(f32[1024,128]{1,0:T(8,128)} %get-tuple-element.107), channel_id=1, source_target_pairs={{0,1},{1,0},{2,3},{3,2},{4,5},{5,4},{6,7},{7,6},{8,9},{9,8},{10,11... | collective-permute-start | bytes 1572872 | tf_op jit(solution)/shard_map/ppermute | solution.py:426
  219.7 1.4 collective-permute-start.36
  219.8 5.9 %collective-permute-start.33 = (f32[256,128]{1,0:T(8,128)S(1)}, f32[256,128]{1,0:T(8,128)S(1)}, u32[]{:S(2)}, u32[]{:S(2)}) collective-permute-start(f32[256,128]{1,0:T(8,128)S(1)} %add.526), channel_id=1, source_target_pairs={{0,8},{2,10},{4,12},{6,14},{8,0},{10,2},{12,4},{14,6},{16,24},{18,... | collective-permute-start | bytes 393224 | tf_op jit(solution)/shard_map/ppermute | solution.py:431
  221.1 6.8 %collective-permute-start.37 = (f32[256,128]{1,0:T(8,128)S(1)}, f32[256,128]{1,0:T(8,128)S(1)}, u32[]{:S(2)}, u32[]{:S(2)}) collective-permute-start(f32[256,128]{1,0:T(8,128)S(1)} %select_add_fusion), channel_id=1, source_target_pairs={{0,4},{2,6},{4,0},{6,2},{8,12},{10,14},{12,8},{14,10},{16,20},{18,... | collective-permute-start | bytes 393224 | tf_op jit(solution)/shard_map/ppermute | solution.py:431
  225.7 8.9 %collective-permute-start.34 = (f32[256,128]{1,0:T(8,128)S(1)}, f32[256,128]{1,0:T(8,128)S(1)}, u32[]{:S(2)}, u32[]{:S(2)}) collective-permute-start(f32[256,128]{1,0:T(8,128)S(1)} %add.528), channel_id=1, source_target_pairs={{0,16},{2,18},{4,20},{6,22},{8,24},{10,26},{12,28},{14,30},{16,0},... | collective-permute-start | bytes 393224 | tf_op jit(solution)/shard_map/ppermute | solution.py:431
  227.9 8.9 %collective-permute-start.38 = (f32[256,128]{1,0:T(8,128)S(1)}, f32[256,128]{1,0:T(8,128)S(1)}, u32[]{:S(2)}, u32[]{:S(2)}) collective-permute-start(f32[256,128]{1,0:T(8,128)S(1)} %add.531), channel_id=1, source_target_pairs={{0,8},{2,10},{4,12},{6,14},{8,0},{10,2},{12,4},{14,6},{16,24},{18,... | collective-permute-start | bytes 393224 | tf_op jit(solution)/shard_map/ppermute | solution.py:431
  234.7 2.9 %collective-permute-start.35 = (f32[256,128]{1,0:T(8,128)S(1)}, f32[256,128]{1,0:T(8,128)S(1)}, u32[]{:S(2)}, u32[]{:S(2)}) collective-permute-start(f32[256,128]{1,0:T(8,128)S(1)} %add.529), channel_id=1, source_target_pairs={{0,2},{2,0},{4,6},{6,4},{8,10},{10,8},{12,14},{14,12},{16,18},{18,... | collective-permute-start | bytes 393224 | tf_op jit(solution)/shard_map/ppermute | solution.py:431
  236.7 14.4 %collective-permute-start.32 = (f32[1024,128]{1,0:T(8,128)S(1)}, f32[1024,128]{1,0:T(8,128)S(1)}, u32[]{:S(2)}, u32[]{:S(2)}) collective-permute-start(f32[1024,128]{1,0:T(8,128)S(1)} %constant_dynamic-slice_fusion.2), channel_id=1, source_target_pairs={{0,1},{1,0},{2,3},{3,2},{4,5},{5,4},{6,7},{7,6},{8,9},{9,8},{10,11... | collective-permute-start | bytes 1572872 | tf_op jit(solution)/shard_map/ppermute | solution.py:426
  236.8 9.7 %collective-permute-start.39 = (f32[256,128]{1,0:T(8,128)S(1)}, f32[256,128]{1,0:T(8,128)S(1)}, u32[]{:S(2)}, u32[]{:S(2)}) collective-permute-start(f32[256,128]{1,0:T(8,128)S(1)} %add.532), channel_id=1, source_target_pairs={{0,16},{2,18},{4,20},{6,22},{8,24},{10,26},{12,28},{14,30},{16,0},... | collective-permute-start | bytes 393224 | tf_op jit(solution)/shard_map/ppermute | solution.py:431
  246.5 5.5 %collective-permute-start.40 = (f32[256,128]{1,0:T(8,128)S(1)}, f32[256,128]{1,0:T(8,128)S(1)}, u32[]{:S(2)}, u32[]{:S(2)}) collective-permute-start(f32[256,128]{1,0:T(8,128)S(1)} %add.533), channel_id=1, source_target_pairs={{0,2},{2,0},{4,6},{6,4},{8,10},{10,8},{12,14},{14,12},{16,18},{18,... | collective-permute-start | bytes 393224 | tf_op jit(solution)/shard_map/ppermute | solution.py:431
  (8 other events, 14.2 us)
Sparse Core Ops, SparseCore 0:
  95.6 73.3 all-gather.1

commit v11 on v10

--- a/solution.py
+++ b/solution.py
@@ -431,15 +431,10 @@
     return lax.ppermute(value, "dom", pairs)
 
 
-def dom_sum_start(first, second):
+def dom_sum(first, second):
     odd = lax.axis_index("dom") % 2 == 1
     mine = jnp.where(odd, second, first) + from_across(jnp.where(odd, first, second), 1)
-    return mine + from_across(mine, 2)
-
-
-def dom_sum_end(mine):
-    odd = lax.axis_index("dom") % 2 == 1
-    bit = 4
+    bit = 2
     while bit < lax.axis_size("dom"):
         mine = mine + from_across(mine, bit)
         bit *= 2
@@ -640,20 +635,15 @@
         bit //= 2
     layer_out = head_scatter(out_part, out_parts)
     pieces = [grad_out[:, at:at + cols] for at in range(0, width, cols)]
-    early_sum = dom_sum_start(grad_query, jnp.concatenate(pieces, axis=0))
+    grad_query, grad_out = dom_sum(grad_query, jnp.concatenate(pieces, axis=0))
+    pieces = [grad_out[at:at + cols] for at in range(0, width, cols)]
+    grad_out = jnp.concatenate(pieces, axis=1)
     feats_part, grad_key, grad_value = attend_backward(
         steps, spots, all_feats, all_grads, all_stats, lists, node_features, feat_part,
         w_query, w_key, w_value, rows,
     )
-    early_sum, feats_part, grad_key, grad_value = lax.optimization_barrier(
-        (early_sum, feats_part, grad_key, grad_value)
-    )
     grad_features = head_scatter(feats_part)
-    late_sum = dom_sum_start(grad_key, grad_value)
-    grad_query, grad_out = dom_sum_end(early_sum)
-    pieces = [grad_out[at:at + cols] for at in range(0, width, cols)]
-    grad_out = jnp.concatenate(pieces, axis=1)
-    grad_key, grad_value = dom_sum_end(late_sum)
+    grad_key, grad_value = dom_sum(grad_key, grad_value)
     return (layer_out, grad_features, grad_query, grad_key, grad_value, grad_out)
 
 

time: 261 us -> 258 us (0.989)
  waiting for transfers between devices: 110 us -> 107 us
    ppermute x2, waiting for transfers between devices: 4.51 us -> 0.01 us  [head_scatter(): return kept + lax.ppermute(sent, 'head', [(0, 1), (1, 0)])]
  transfers between devices with their start and end apart: 42 -> 42, of which waited for: 24 -> 23; matrix products, arithmetic and copies ran while one was open for 9% -> 10% of each run, Pallas kernels for 31% -> 32%
where the time goes in v11:
time: 258 us; the launch traced here: 257 us
  waiting for transfers between devices  107 us (41%)
  Pallas kernels  81 us (31%)
  starting transfers between devices  25.4 us (10%)
  between operations  14.8 us (6%)
  local copies, waits for them, and re-layouts  14.4 us (6%)
  other arithmetic  11.7 us (5%)
  matrix products  2.69 us (1%)
    pallas_call x1, Pallas kernels, attend_backward(): pl.pallas_call(backward_kernel, out_shape=(jax.ShapeDtypeStruct((node_row...  42.6 us
    pallas_call x1, Pallas kernels, attend_forward(): pl.pallas_call(functools.partial(forward_kernel, entries, layout, len(arr...  38.4 us
    ppermute x10, waiting for transfers between devices, from_across(): return lax.ppermute(value, 'dom', pairs)  22.8 us
    ppermute x4, waiting for transfers between devices, gather_feats(): more = (lax.ppermute(sent, 'head', other_head),)  22 us
    ppermute x1, waiting for transfers between devices, gather_feats(): lax.ppermute(start, 'dom', onward)  15.9 us
    ppermute x4, waiting for transfers between devices, double(): other = lax.ppermute(value, 'dom', [(at, at ^ bit) for at in range(size)])  14.5 us
    ppermute x2, waiting for transfers between devices, gather_feats(): lax.ppermute(held[0], 'dom', onward)  10.9 us
    ppermute x1, waiting for transfers between devices, gather_feats(): lax.ppermute(held[0][:RING // 2 * rows], 'dom', onward)  7.85 us
  transfers between devices with their start and end apart: 42, of which 23 were waited for; matrix products, arithmetic and copies ran while one was open for 10% of the time, Pallas kernels for 32%

profile of v11, /device:TPU:0, one launch (start us, length us, event | category | flops | bytes accessed | tf_op | source)
XLA Modules:
  0.0 256.8 jit_solution(1985185640129075004)
XLA Ops:
  7.7 0.7 multiply_add_fusion
  8.5 0.7 fusion.10
  9.2 0.8 convert_element_type.58
  9.9 1.2 constant_dynamic-slice_fusion.10
  11.2 2.8 %collective-permute-start = (f32[800,256]{1,0:T(8,128)S(1)}, f32[800,256]{1,0:T(8,128)S(1)}, u32[]{:S(2)}, u32[]{:S(2)}) collective-permute-start(f32[800,256]{1,0:T(8,128)S(1)} %maximum_maximum_fusion), channel_id=1, source_target_pairs={{0,8},{2,10},{8,16},{10,18},{16,24},{18,26},{24,28},{26,30},{28,20... | collective-permute-start | bytes 2457608 | tf_op jit(solution)/shard_map/ppermute | solution.py:512
  14.0 2.7 %fusion.38.refs_25_ = f32[1024,128]{1,0:T(8,128)} fusion(f32[1024,256]{1,0:T(8,128)S(1)} %copy-done.4, f32[128,256]{1,0:T(8,128)} %refs_30_.1), kind=kOutput, calls=%fused_computation.222 | convolution fusion | flops 402653184 | bytes 1703936 | tf_op jit(solution)/shard_map/dot_general | solution.py:618
  16.7 15.9 %collective-permute-done.refs_2_ = f32[800,256]{1,0:T(8,128)S(1)} collective-permute-done((f32[800,256]{1,0:T(8,128)S(1)}, f32[800,256]{1,0:T(8,128)S(1)}, u32[]{:S(2)}, u32[]{:S(2)}) %collective-permute-start) | collective-permute-done | bytes 819232 | tf_op jit(solution)/shard_map/ppermute | solution.py:512
  32.7 1.5 collective-permute-done.1.refs_4_
  34.2 1.6 collective-permute-start.3
  36.6 1.6 collective-permute-start.5
  38.2 12.6 %collective-permute-done.5.refs_10_ = f32[512,256]{1,0:T(8,128)S(1)} collective-permute-done((f32[512,256]{1,0:T(8,128)S(1)}, f32[512,256]{1,0:T(8,128)S(1)}, u32[]{:S(2)}, u32[]{:S(2)}) %collective-permute-start.5) | collective-permute-done | bytes 524320 | tf_op jit(solution)/shard_map/ppermute | solution.py:549
  50.7 2.8 %collective-permute-done.3.refs_6_ = f32[800,256]{1,0:T(8,128)S(1)} collective-permute-done((f32[800,256]{1,0:T(8,128)S(1)}, f32[800,256]{1,0:T(8,128)S(1)}, u32[]{:S(2)}, u32[]{:S(2)}) %collective-permute-start.3) | collective-permute-done | bytes 819232 | tf_op jit(solution)/shard_map/ppermute | solution.py:535
  53.6 2.9 %collective-permute-done.4.refs_8_ = f32[800,256]{1,0:T(8,128)S(1)} collective-permute-done((f32[800,256]{1,0:T(8,128)S(1)}, f32[800,256]{1,0:T(8,128)S(1)}, u32[]{:S(2)}, u32[]{:S(2)}) %collective-permute-start.4) | collective-permute-done | bytes 819232 | tf_op jit(solution)/shard_map/ppermute | solution.py:535
  56.6 1.6 collective-permute-start.10
  58.2 1.2 collective-permute-done.17
  59.9 1.6 collective-permute-start.8
  61.9 0.8 constant_dynamic-update-slice_fusion.7
  62.7 7.5 %collective-permute-done.10.refs_16_ = f32[512,256]{1,0:T(8,128)S(1)} collective-permute-done((f32[512,256]{1,0:T(8,128)S(1)}, f32[512,256]{1,0:T(8,128)S(1)}, u32[]{:S(2)}, u32[]{:S(2)}) %collective-permute-start.10) | collective-permute-done | bytes 524320 | tf_op jit(solution)/shard_map/ppermute | solution.py:549
  70.2 0.8 constant_dynamic-update-slice_fusion.5
  71.0 1.1 collective-permute-done.13.refs_11_
  72.1 8.1 %collective-permute-done.8.refs_12_ = f32[800,256]{1,0:T(8,128)S(1)} collective-permute-done((f32[800,256]{1,0:T(8,128)S(1)}, f32[800,256]{1,0:T(8,128)S(1)}, u32[]{:S(2)}, u32[]{:S(2)}) %collective-permute-start.8) | collective-permute-done | bytes 819232 | tf_op jit(solution)/shard_map/ppermute | solution.py:535
  80.2 1.3 collective-permute-done.9.refs_14_
  81.7 0.6 collective-permute-start.16
  82.7 1.6 collective-permute-start.14
  84.3 7.8 %collective-permute-done.14 = f32[384,256]{1,0:T(8,128)S(1)} collective-permute-done((f32[384,256]{1,0:T(8,128)S(1)}, f32[384,256]{1,0:T(8,128)S(1)}, u32[]{:S(2)}, u32[]{:S(2)}) %collective-permute-start.14) | collective-permute-done | bytes 393248 | tf_op jit(solution)/shard_map/ppermute | solution.py:539
  92.2 0.5 collective-permute-done.15
  92.7 1.9 collective-permute-done.16.refs_20_
  94.7 0.7 copy-done.23
  95.5 0.8 constant_dynamic-slice_fusion.3
  97.8 1.0 constant_dynamic-update-slice_fusion.18
  98.8 2.9 %collective-permute-done.21.refs_17_ = f32[512,256]{1,0:T(8,128)S(1)} collective-permute-done((f32[512,256]{1,0:T(8,128)S(1)}, f32[512,256]{1,0:T(8,128)S(1)}, u32[]{:S(2)}, u32[]{:S(2)}) %collective-permute-start.21) | collective-permute-done | bytes 524320 | tf_op jit(solution)/shard_map/ppermute | solution.py:492
  101.8 0.7 copy-done.25
  104.0 0.5 convert_reduce_fusion
  104.9 1.2 gather_fusion
  106.4 0.6 slice.110
  107.0 0.7 pad.20.clone
  108.3 0.6 copy.23
  109.0 1.4 collective-permute-done.24.refs_23_
  110.3 0.7 copy-done.28
  111.2 38.4 %attend_forward.1 = (f32[16384,256]{1,0:T(8,128)}, f32[1024,256]{1,0:T(8,128)}, f32[1024,256]{1,0:T(8,128)}, f32[8,8,128]{2,1,0:T(8,128)}, f32[256,128]{1,0:T(8,128)}, /*index=5*/f32[128,256]{1,0:T(8,128)}) custom-call(s32[8,8]{1,0:T(8,128)} %get-tuple-element.118.ids, f32[1024,256]{1,0:T(8,128)} %own_ref.1, f32[1024,256]{1,0:T(8,128)} %collective-permute-done.2.refs_1_, ...), custom_call_target="tpu_custom_call" | custom-call | tf_op jit(solution)/shard_map/attend_forward/pallas_call | solution.py:188
  149.7 1.6 collective-permute-start.25
  151.3 2.1 constant_dynamic-slice_fusion
  153.3 2.0 collective-permute-done.25
  155.3 0.8 broadcast_select_fusion.12
  156.1 1.1 collective-permute-start.27
  157.2 0.9 fusion.37
  158.0 7.6 %collective-permute-done.27 = f32[16,8,128]{2,1,0:T(8,128)S(1)} collective-permute-done((f32[16,8,128]{2,1,0:T(8,128)S(1)}, f32[16,8,128]{2,1,0:T(8,128)S(1)}, u32[]{:S(2)}, u32[]{:S(2)}) %collective-permute-start.27) | collective-permute-done | bytes 65568 | tf_op jit(solution)/shard_map/ppermute | solution.py:447
  165.9 4.8 %collective-permute-done.28 = f32[32,8,128]{2,1,0:T(8,128)S(1)} collective-permute-done((f32[32,8,128]{2,1,0:T(8,128)S(1)}, f32[32,8,128]{2,1,0:T(8,128)S(1)}, u32[]{:S(2)}, u32[]{:S(2)}) %collective-permute-start.28) | collective-permute-done | bytes 131104 | tf_op jit(solution)/shard_map/ppermute | solution.py:447
  171.0 1.6 collective-permute-start.26
  172.6 4.3 %collective-permute-done.32 = f32[256,128]{1,0:T(8,128)S(1)} collective-permute-done((f32[256,128]{1,0:T(8,128)S(1)}, f32[256,128]{1,0:T(8,128)S(1)}, u32[]{:S(2)}, u32[]{:S(2)}) %collective-permute-start.32) | collective-permute-done | bytes 131104 | tf_op jit(solution)/shard_map/ppermute | solution.py:431
  177.0 1.0 broadcast_select_fusion.1
  178.1 42.6 %attend_backward.1 = (f32[1024,256]{1,0:T(8,128)S(1)}, f32[256,128]{1,0:T(8,128)S(1)}, f32[256,128]{1,0:T(8,128)S(1)}) custom-call(s32[3,40]{1,0:T(4,128)S(1)} %add_add_fusion.steps_ref, s32[5,80]{1,0:T(8,128)S(1)} %stack.8.readers_ref, f32[16384,256]{1,0:T(8,128)} %get-tuple-element.106.feats_ref, f32[16384,128]{1,0:T(8,128)} %all-gather.2.cloned.1.call-done.cots_ref, ...), custom_call_target="tpu_custom_call" | custom-call | tf_op jit(solution)/shard_map/attend_backward/pallas_call | solution.py:353
  220.8 0.9 add.526
  221.8 2.1 collective-permute-start.34
  223.9 0.9 collective-permute-start.37
  224.7 6.2 %collective-permute-done.34 = f32[256,128]{1,0:T(8,128)S(1)} collective-permute-done((f32[256,128]{1,0:T(8,128)S(1)}, f32[256,128]{1,0:T(8,128)S(1)}, u32[]{:S(2)}, u32[]{:S(2)}) %collective-permute-start.34) | collective-permute-done | bytes 131104 | tf_op jit(solution)/shard_map/ppermute | solution.py:431
  231.1 1.9 add.522
  233.2 0.7 broadcast_select_fusion.2
  233.9 5.1 %collective-permute-done.38 = f32[256,128]{1,0:T(8,128)S(1)} collective-permute-done((f32[256,128]{1,0:T(8,128)S(1)}, f32[256,128]{1,0:T(8,128)S(1)}, u32[]{:S(2)}, u32[]{:S(2)}) %collective-permute-start.38) | collective-permute-done | bytes 131104 | tf_op jit(solution)/shard_map/ppermute | solution.py:431
  239.1 1.4 collective-permute-start.39
  240.4 0.7 pad_maximum_fusion.7
  241.1 6.7 %collective-permute-done.39 = f32[256,128]{1,0:T(8,128)S(1)} collective-permute-done((f32[256,128]{1,0:T(8,128)S(1)}, f32[256,128]{1,0:T(8,128)S(1)}, u32[]{:S(2)}, u32[]{:S(2)}) %collective-permute-start.39) | collective-permute-done | bytes 131104 | tf_op jit(solution)/shard_map/ppermute | solution.py:431
  247.9 0.9 dynamic-slice_add_fusion
  249.2 0.7 broadcast_select_fusion.3
  (180 shorter events, 9.3 us)
Async XLA Ops:
  7.2 170.9 %all-gather.2.cloned.1.call-start = ((), (), s32[]{:S(2)}) async-start(), calls=%async_computation | async-start | bytes 8912896 | tf_op jit(solution)/shard_map/all_gather | solution.py:625
  7.2 27.0 %collective-permute-start.2 = (f32[1024,256]{1,0:T(8,128)}, f32[1024,256]{1,0:T(8,128)}, u32[]{:S(2)}, u32[]{:S(2)}) collective-permute-start(f32[1024,256]{1,0:T(8,128)} %own_ref.1), channel_id=1, source_target_pairs={{0,2},{2,0},{4,6},{6,4},{8,10},{10,8},{12,14},{14,12},{16,18},{18,... | collective-permute-start | bytes 3145736 | tf_op jit(solution)/shard_map/ppermute | solution.py:492
  11.2 21.5 %collective-permute-start = (f32[800,256]{1,0:T(8,128)S(1)}, f32[800,256]{1,0:T(8,128)S(1)}, u32[]{:S(2)}, u32[]{:S(2)}) collective-permute-start(f32[800,256]{1,0:T(8,128)S(1)} %maximum_maximum_fusion), channel_id=1, source_target_pairs={{0,8},{2,10},{8,16},{10,18},{16,24},{18,26},{24,28},{26,30},{28,20... | collective-permute-start | bytes 2457608 | tf_op jit(solution)/shard_map/ppermute | solution.py:512
  14.0 20.2 %collective-permute-start.1 = (f32[800,256]{1,0:T(8,128)S(1)}, f32[800,256]{1,0:T(8,128)S(1)}, u32[]{:S(2)}, u32[]{:S(2)}) collective-permute-start(f32[800,256]{1,0:T(8,128)S(1)} %maximum_maximum_fusion), channel_id=1, source_target_pairs={{8,0},{10,2},{16,8},{18,10},{24,16},{26,18},{28,24},{30,26},{20,28... | collective-permute-start | bytes 2457608 | tf_op jit(solution)/shard_map/ppermute | solution.py:512
  32.7 26.9 %copy-start.8 = (f32[800,256]{1,0:T(8,128)}, f32[800,256]{1,0:T(8,128)S(1)}, u32[]{:S(2)}) copy-start(f32[800,256]{1,0:T(8,128)S(1)} %collective-permute-done.refs_2_) | copy-start | bytes 2457604
  34.2 25.4 %copy-start.9 = (f32[800,256]{1,0:T(8,128)}, f32[800,256]{1,0:T(8,128)S(1)}, u32[]{:S(2)}) copy-start(f32[800,256]{1,0:T(8,128)S(1)} %collective-permute-done.1.refs_4_) | copy-start | bytes 2457604
  34.2 19.3 %collective-permute-start.3 = (f32[800,256]{1,0:T(8,128)S(1)}, f32[800,256]{1,0:T(8,128)S(1)}, u32[]{:S(2)}, u32[]{:S(2)}) collective-permute-start(f32[800,256]{1,0:T(8,128)S(1)} %collective-permute-done.refs_2_), channel_id=1, source_target_pairs={{0,8},{2,10},{8,16},{10,18},{16,24},{18,26},{24,28},{26,30},{28,20... | collective-permute-start | bytes 2457608 | tf_op jit(solution)/shard_map/ppermute | solution.py:535
  35.8 20.7 %collective-permute-start.6 = (f32[800,256]{1,0:T(8,128)S(1)}, f32[800,256]{1,0:T(8,128)S(1)}, u32[]{:S(2)}, u32[]{:S(2)}) collective-permute-start(f32[800,256]{1,0:T(8,128)S(1)} %collective-permute-done.refs_2_), channel_id=1, source_target_pairs={{0,2},{2,0},{4,6},{6,4},{8,10},{10,8},{12,14},{14,12},{16,18},{18,... | collective-permute-start | bytes 2457608 | tf_op jit(solution)/shard_map/ppermute | solution.py:492
  35.8 20.7 %collective-permute-start.4 = (f32[800,256]{1,0:T(8,128)S(1)}, f32[800,256]{1,0:T(8,128)S(1)}, u32[]{:S(2)}, u32[]{:S(2)}) collective-permute-start(f32[800,256]{1,0:T(8,128)S(1)} %collective-permute-done.1.refs_4_), channel_id=1, source_target_pairs={{8,0},{10,2},{16,8},{18,10},{24,16},{26,18},{28,24},{30,26},{20,28... | collective-permute-start | bytes 2457608 | tf_op jit(solution)/shard_map/ppermute | solution.py:535
  36.2 20.2 %collective-permute-start.7 = (f32[800,256]{1,0:T(8,128)S(1)}, f32[800,256]{1,0:T(8,128)S(1)}, u32[]{:S(2)}, u32[]{:S(2)}) collective-permute-start(f32[800,256]{1,0:T(8,128)S(1)} %collective-permute-done.1.refs_4_), channel_id=1, source_target_pairs={{0,2},{2,0},{4,6},{6,4},{8,10},{10,8},{12,14},{14,12},{16,18},{18,... | collective-permute-start | bytes 2457608 | tf_op jit(solution)/shard_map/ppermute | solution.py:492
  36.6 14.2 %collective-permute-start.5 = (f32[512,256]{1,0:T(8,128)S(1)}, f32[512,256]{1,0:T(8,128)S(1)}, u32[]{:S(2)}, u32[]{:S(2)}) collective-permute-start(f32[512,256]{1,0:T(8,128)S(1)} %pad_maximum_fusion), channel_id=1, source_target_pairs={{0,1},{1,0},{2,3},{3,2},{4,5},{5,4},{6,7},{7,6},{8,9},{9,8},{10,11... | collective-permute-start | bytes 1572872 | tf_op jit(solution)/shard_map/ppermute | solution.py:549
  50.7 44.8 %copy-start.20 = (f32[512,256]{1,0:T(8,128)}, f32[512,256]{1,0:T(8,128)S(1)}, u32[]{:S(2)}) copy-start(f32[512,256]{1,0:T(8,128)S(1)} %collective-permute-done.5.refs_10_) | copy-start | bytes 1572868
  53.6 41.1 %copy-start.10 = (f32[800,256]{1,0:T(8,128)}, f32[800,256]{1,0:T(8,128)S(1)}, u32[]{:S(2)}) copy-start(f32[800,256]{1,0:T(8,128)S(1)} %collective-permute-done.3.refs_6_) | copy-start | bytes 2457604
  56.4 38.2 %copy-start.11 = (f32[800,256]{1,0:T(8,128)}, f32[800,256]{1,0:T(8,128)S(1)}, u32[]{:S(2)}) copy-start(f32[800,256]{1,0:T(8,128)S(1)} %collective-permute-done.4.refs_8_) | copy-start | bytes 2457604
  56.5 38.2 %copy-start.12 = (f32[800,256]{1,0:T(8,128)}, f32[800,256]{1,0:T(8,128)S(1)}, u32[]{:S(2)}) copy-start(f32[800,256]{1,0:T(8,128)S(1)} %collective-permute-done.6.refs_3_) | copy-start | bytes 2457604
  56.5 38.2 %copy-start.13 = (f32[800,256]{1,0:T(8,128)}, f32[800,256]{1,0:T(8,128)S(1)}, u32[]{:S(2)}) copy-start(f32[800,256]{1,0:T(8,128)S(1)} %collective-permute-done.7.refs_5_) | copy-start | bytes 2457604
  56.6 13.6 %collective-permute-start.10 = (f32[512,256]{1,0:T(8,128)S(1)}, f32[512,256]{1,0:T(8,128)S(1)}, u32[]{:S(2)}, u32[]{:S(2)}) collective-permute-start(f32[512,256]{1,0:T(8,128)S(1)} %pad_maximum_fusion.1), channel_id=1, source_target_pairs={{0,1},{1,0},{2,3},{3,2},{4,5},{5,4},{6,7},{7,6},{8,9},{9,8},{10,11... | collective-permute-start | bytes 1572872 | tf_op jit(solution)/shard_map/ppermute | solution.py:549
  58.2 1.2 collective-permute-start.17
  59.4 12.7 %collective-permute-start.11 = (f32[800,256]{1,0:T(8,128)S(1)}, f32[800,256]{1,0:T(8,128)S(1)}, u32[]{:S(2)}, u32[]{:S(2)}) collective-permute-start(f32[800,256]{1,0:T(8,128)S(1)} %collective-permute-done.3.refs_6_), channel_id=1, source_target_pairs={{0,2},{2,0},{4,6},{6,4},{8,10},{10,8},{12,14},{14,12},{16,18},{18,... | collective-permute-start | bytes 2457608 | tf_op jit(solution)/shard_map/ppermute | solution.py:492
  59.6 12.6 %collective-permute-start.12 = (f32[800,256]{1,0:T(8,128)S(1)}, f32[800,256]{1,0:T(8,128)S(1)}, u32[]{:S(2)}, u32[]{:S(2)}) collective-permute-start(f32[800,256]{1,0:T(8,128)S(1)} %collective-permute-done.4.refs_8_), channel_id=1, source_target_pairs={{0,2},{2,0},{4,6},{6,4},{8,10},{10,8},{12,14},{14,12},{16,18},{18,... | collective-permute-start | bytes 2457608 | tf_op jit(solution)/shard_map/ppermute | solution.py:492
  59.9 20.3 %collective-permute-start.8 = (f32[800,256]{1,0:T(8,128)S(1)}, f32[800,256]{1,0:T(8,128)S(1)}, u32[]{:S(2)}, u32[]{:S(2)}) collective-permute-start(f32[800,256]{1,0:T(8,128)S(1)} %collective-permute-done.3.refs_6_), channel_id=1, source_target_pairs={{0,8},{2,10},{8,16},{10,18},{16,24},{18,26},{24,28},{26,30},{28,20... | collective-permute-start | bytes 2457608 | tf_op jit(solution)/shard_map/ppermute | solution.py:535
  61.5 20.0 %collective-permute-start.9 = (f32[800,256]{1,0:T(8,128)S(1)}, f32[800,256]{1,0:T(8,128)S(1)}, u32[]{:S(2)}, u32[]{:S(2)}) collective-permute-start(f32[800,256]{1,0:T(8,128)S(1)} %collective-permute-done.4.refs_8_), channel_id=1, source_target_pairs={{8,0},{10,2},{16,8},{18,10},{24,16},{26,18},{28,24},{30,26},{20,28... | collective-permute-start | bytes 2457608 | tf_op jit(solution)/shard_map/ppermute | solution.py:535
  70.2 33.0 %copy-start.21 = (f32[512,256]{1,0:T(8,128)}, f32[512,256]{1,0:T(8,128)S(1)}, u32[]{:S(2)}) copy-start(f32[512,256]{1,0:T(8,128)S(1)} %collective-permute-done.10.refs_16_) | copy-start | bytes 1572868
  70.2 1.9 collective-permute-start.13
  72.1 20.6 %copy-start.22 = (f32[512,256]{1,0:T(8,128)}, f32[512,256]{1,0:T(8,128)S(1)}, u32[]{:S(2)}) copy-start(f32[512,256]{1,0:T(8,128)S(1)} %collective-permute-done.13.refs_11_) | copy-start | bytes 1572868
  72.1 22.6 %copy-start.14 = (f32[800,256]{1,0:T(8,128)}, f32[800,256]{1,0:T(8,128)S(1)}, u32[]{:S(2)}) copy-start(f32[800,256]{1,0:T(8,128)S(1)} %collective-permute-done.11.refs_7_) | copy-start | bytes 2457604
  72.1 22.6 %copy-start.15 = (f32[800,256]{1,0:T(8,128)}, f32[800,256]{1,0:T(8,128)S(1)}, u32[]{:S(2)}) copy-start(f32[800,256]{1,0:T(8,128)S(1)} %collective-permute-done.12.refs_9_) | copy-start | bytes 2457604
  80.2 23.0 %copy-start.6 = (f32[800,256]{1,0:T(8,128)}, f32[800,256]{1,0:T(8,128)S(1)}, u32[]{:S(2)}) copy-start(f32[800,256]{1,0:T(8,128)S(1)} %collective-permute-done.8.refs_12_) | copy-start | bytes 2457604
  81.5 21.7 %copy-start.5 = (f32[800,256]{1,0:T(8,128)}, f32[800,256]{1,0:T(8,128)S(1)}, u32[]{:S(2)}) copy-start(f32[800,256]{1,0:T(8,128)S(1)} %collective-permute-done.9.refs_14_) | copy-start | bytes 2457604
  81.6 26.7 %copy-start.29 = (s32[8,7,128]{2,0,1:T(8,128)S(1)}, s32[8,7,128]{2,0,1:T(8,128)}, u32[]{:S(2)}) copy-start(s32[8,7,128]{2,0,1:T(8,128)} %param.16) | copy-start | bytes 86020
  81.7 12.9 %collective-permute-start.16 = (f32[512,256]{1,0:T(8,128)S(1)}, f32[512,256]{1,0:T(8,128)S(1)}, u32[]{:S(2)}, u32[]{:S(2)}) collective-permute-start(f32[512,256]{1,0:T(8,128)S(1)} %pad_maximum_fusion.2), channel_id=1, source_target_pairs={{0,1},{1,0},{2,3},{3,2},{4,5},{5,4},{6,7},{7,6},{8,9},{9,8},{10,11... | collective-permute-start | bytes 1572872 | tf_op jit(solution)/shard_map/ppermute | solution.py:549
  82.3 10.5 %collective-permute-start.15 = (f32[416,256]{1,0:T(8,128)S(1)}, f32[416,256]{1,0:T(8,128)S(1)}, u32[]{:S(2)}, u32[]{:S(2)}) collective-permute-start(f32[416,256]{1,0:T(8,128)S(1)} %slice.92), channel_id=1, source_target_pairs={{8,0},{10,2},{16,8},{18,10},{24,16},{26,18},{28,24},{30,26},{20,28... | collective-permute-start | bytes 1277960 | tf_op jit(solution)/shard_map/ppermute | solution.py:540
  82.7 9.5 %collective-permute-start.14 = (f32[384,256]{1,0:T(8,128)S(1)}, f32[384,256]{1,0:T(8,128)S(1)}, u32[]{:S(2)}, u32[]{:S(2)}) collective-permute-start(f32[384,256]{1,0:T(8,128)S(1)} %slice.91), channel_id=1, source_target_pairs={{0,8},{2,10},{8,16},{10,18},{16,24},{18,26},{24,28},{26,30},{28,20... | collective-permute-start | bytes 1179656 | tf_op jit(solution)/shard_map/ppermute | solution.py:539
  84.3 10.4 %copy-start.27 = (f32[320,256]{1,0:T(8,128)}, f32[320,256]{1,0:T(8,128)S(1)}, u32[]{:S(2)}) copy-start(f32[320,256]{1,0:T(8,128)S(1)} %constant_dynamic-update-slice_fusion) | copy-start | bytes 983044
  95.5 14.9 %copy-start.7 = (f32[800,256]{1,0:T(8,128)}, f32[800,256]{1,0:T(8,128)S(1)}, u32[]{:S(2)}) copy-start(f32[800,256]{1,0:T(8,128)S(1)} %constant_dynamic-update-slice_fusion.10.refs_18_) | copy-start | bytes 2457604
  96.3 11.5 %copy-start.24 = (f32[512,256]{1,0:T(8,128)S(1)}, f32[512,256]{1,0:T(8,128)}, u32[]{:S(2)}) copy-start(f32[512,256]{1,0:T(8,128)} %copy-done.23) | copy-start | bytes 1572868
  96.3 5.4 %collective-permute-start.18 = (f32[800,256]{1,0:T(8,128)S(1)}, f32[800,256]{1,0:T(8,128)S(1)}, u32[]{:S(2)}, u32[]{:S(2)}) collective-permute-start(f32[800,256]{1,0:T(8,128)S(1)} %constant_dynamic-update-slice_fusion.10.refs_18_), channel_id=1, source_target_pairs={{0,2},{2,0},{4,6},{6,4},{8,10},{10,8},{12,14},{14,12},{16,18},{18,... | collective-permute-start | bytes 2457608 | tf_op jit(solution)/shard_map/ppermute | solution.py:492
  96.3 5.4 %collective-permute-start.19 = (f32[800,256]{1,0:T(8,128)S(1)}, f32[800,256]{1,0:T(8,128)S(1)}, u32[]{:S(2)}, u32[]{:S(2)}) collective-permute-start(f32[800,256]{1,0:T(8,128)S(1)} %collective-permute-done.8.refs_12_), channel_id=1, source_target_pairs={{0,2},{2,0},{4,6},{6,4},{8,10},{10,8},{12,14},{14,12},{16,18},{18,... | collective-permute-start | bytes 2457608 | tf_op jit(solution)/shard_map/ppermute | solution.py:492
  96.8 4.9 %collective-permute-start.20 = (f32[800,256]{1,0:T(8,128)S(1)}, f32[800,256]{1,0:T(8,128)S(1)}, u32[]{:S(2)}, u32[]{:S(2)}) collective-permute-start(f32[800,256]{1,0:T(8,128)S(1)} %collective-permute-done.9.refs_14_), channel_id=1, source_target_pairs={{0,2},{2,0},{4,6},{6,4},{8,10},{10,8},{12,14},{14,12},{16,18},{18,... | collective-permute-start | bytes 2457608 | tf_op jit(solution)/shard_map/ppermute | solution.py:492
  96.8 4.9 %collective-permute-start.21 = (f32[512,256]{1,0:T(8,128)S(1)}, f32[512,256]{1,0:T(8,128)S(1)}, u32[]{:S(2)}, u32[]{:S(2)}) collective-permute-start(f32[512,256]{1,0:T(8,128)S(1)} %collective-permute-done.10.refs_16_), channel_id=1, source_target_pairs={{0,2},{2,0},{4,6},{6,4},{8,10},{10,8},{12,14},{14,12},{16,18},{18,... | collective-permute-start | bytes 1572872 | tf_op jit(solution)/shard_map/ppermute | solution.py:492
  97.3 10.5 %collective-permute-start.22 = (f32[256,256]{1,0:T(8,128)}, f32[256,256]{1,0:T(8,128)}, u32[]{:S(2)}, u32[]{:S(2)}) collective-permute-start(f32[256,256]{1,0:T(8,128)} %constant_dynamic-slice_fusion.3), channel_id=1, source_target_pairs={{0,1},{1,0},{2,3},{3,2},{4,5},{5,4},{6,7},{7,6},{8,9},{9,8},{10,11... | collective-permute-start | bytes 786440 | tf_op jit(solution)/shard_map/ppermute | solution.py:549
  107.8 2.5 collective-permute-start.23
  107.9 2.4 collective-permute-start.24
  149.6 21.3 %copy-start.19 = (f32[256,128]{1,0:T(8,128)S(1)}, f32[256,128]{1,0:T(8,128)}, u32[]{:S(2)}) copy-start(f32[256,128]{1,0:T(8,128)} %get-tuple-element.113) | copy-start | bytes 393220
  149.6 28.4 %copy-start = (f32[1024,256]{1,0:T(8,128)S(1)}, f32[1024,256]{1,0:T(8,128)}, u32[]{:S(2)}) copy-start(f32[1024,256]{1,0:T(8,128)} %own_ref.1) | copy-start | bytes 3145732
  149.6 28.4 %copy-start.1 = (f32[256,128]{1,0:T(8,128)S(1)}, f32[256,128]{1,0:T(8,128)}, u32[]{:S(2)}) copy-start(f32[256,128]{1,0:T(8,128)} %wq_ref.1) | copy-start | bytes 393220
  149.7 28.4 %copy-start.2 = (f32[256,128]{1,0:T(8,128)S(1)}, f32[256,128]{1,0:T(8,128)}, u32[]{:S(2)}) copy-start(f32[256,128]{1,0:T(8,128)} %wk_ref.1) | copy-start | bytes 393220
  149.7 28.4 %copy-start.3 = (f32[256,128]{1,0:T(8,128)S(1)}, f32[256,128]{1,0:T(8,128)}, u32[]{:S(2)}) copy-start(f32[256,128]{1,0:T(8,128)} %wv_ref.1) | copy-start | bytes 393220
  149.7 5.6 %collective-permute-start.25 = (f32[8,8,128]{2,1,0:T(8,128)}, f32[8,8,128]{2,1,0:T(8,128)S(1)}, u32[]{:S(2)}, u32[]{:S(2)}) collective-permute-start(f32[8,8,128]{2,1,0:T(8,128)} %get-tuple-element.100), channel_id=1, source_target_pairs={{0,16},{2,18},{4,20},{6,22},{8,24},{10,26},{12,28},{14,30},{16,0},... | collective-permute-start | bytes 98312 | tf_op jit(solution)/shard_map/ppermute | solution.py:447
  156.1 9.6 %collective-permute-start.27 = (f32[16,8,128]{2,1,0:T(8,128)S(1)}, f32[16,8,128]{2,1,0:T(8,128)S(1)}, u32[]{:S(2)}, u32[]{:S(2)}) collective-permute-start(f32[16,8,128]{2,1,0:T(8,128)S(1)} %pad_maximum_fusion.8), channel_id=1, source_target_pairs={{0,8},{2,10},{4,12},{6,14},{8,0},{10,2},{12,4},{14,6},{16,24},{18,... | collective-permute-start | bytes 196616 | tf_op jit(solution)/shard_map/ppermute | solution.py:447
  165.7 5.0 %collective-permute-start.28 = (f32[32,8,128]{2,1,0:T(8,128)S(1)}, f32[32,8,128]{2,1,0:T(8,128)S(1)}, u32[]{:S(2)}, u32[]{:S(2)}) collective-permute-start(f32[32,8,128]{2,1,0:T(8,128)S(1)} %pad_maximum_fusion.5), channel_id=1, source_target_pairs={{0,4},{2,6},{4,0},{6,2},{8,12},{10,14},{12,8},{14,10},{16,20},{18,... | collective-permute-start | bytes 393224 | tf_op jit(solution)/shard_map/ppermute | solution.py:447
  165.8 5.1 %collective-permute-start.31 = (f32[256,128]{1,0:T(8,128)S(1)}, f32[256,128]{1,0:T(8,128)S(1)}, u32[]{:S(2)}, u32[]{:S(2)}) collective-permute-start(f32[256,128]{1,0:T(8,128)S(1)} %fusion.1), channel_id=1, source_target_pairs={{0,2},{2,0},{4,6},{6,4},{8,10},{10,8},{12,14},{14,12},{16,18},{18,... | collective-permute-start | bytes 393224 | tf_op jit(solution)/shard_map/ppermute | solution.py:431
  170.8 6.2 %collective-permute-start.29 = (f32[64,8,128]{2,1,0:T(8,128)S(1)}, f32[64,8,128]{2,1,0:T(8,128)}, u32[]{:S(2)}, u32[]{:S(2)}) collective-permute-start(f32[64,8,128]{2,1,0:T(8,128)S(1)} %pad_maximum_fusion.4), channel_id=1, source_target_pairs={{0,2},{2,0},{4,6},{6,4},{8,10},{10,8},{12,14},{14,12},{16,18},{18,... | collective-permute-start | bytes 786440 | tf_op jit(solution)/shard_map/ppermute | solution.py:447
  170.9 5.9 %collective-permute-start.32 = (f32[256,128]{1,0:T(8,128)S(1)}, f32[256,128]{1,0:T(8,128)S(1)}, u32[]{:S(2)}, u32[]{:S(2)}) collective-permute-start(f32[256,128]{1,0:T(8,128)S(1)} %select_add_fusion.1), channel_id=1, source_target_pairs={{0,4},{2,6},{4,0},{6,2},{8,12},{10,14},{12,8},{14,10},{16,20},{18,... | collective-permute-start | bytes 393224 | tf_op jit(solution)/shard_map/ppermute | solution.py:431
  171.0 60.0 %collective-permute-start.26 = (f32[1024,128]{1,0:T(8,128)}, f32[1024,128]{1,0:T(8,128)}, u32[]{:S(2)}, u32[]{:S(2)}) collective-permute-start(f32[1024,128]{1,0:T(8,128)} %get-tuple-element.103), channel_id=1, source_target_pairs={{0,1},{1,0},{2,3},{3,2},{4,5},{5,4},{6,7},{7,6},{8,9},{9,8},{10,11... | collective-permute-start | bytes 1572872 | tf_op jit(solution)/shard_map/ppermute | solution.py:426
  176.9 43.9 %collective-permute-start.33 = (f32[256,128]{1,0:T(8,128)S(1)}, f32[256,128]{1,0:T(8,128)}, u32[]{:S(2)}, u32[]{:S(2)}) collective-permute-start(f32[256,128]{1,0:T(8,128)S(1)} %add.525), channel_id=1, source_target_pairs={{0,8},{2,10},{4,12},{6,14},{8,0},{10,2},{12,4},{14,6},{16,24},{18,... | collective-permute-start | bytes 393224 | tf_op jit(solution)/shard_map/ppermute | solution.py:431
  220.8 3.1 %collective-permute-start.36 = (f32[256,128]{1,0:T(8,128)S(1)}, f32[256,128]{1,0:T(8,128)S(1)}, u32[]{:S(2)}, u32[]{:S(2)}) collective-permute-start(f32[256,128]{1,0:T(8,128)S(1)} %broadcast_select_fusion.5), channel_id=1, source_target_pairs={{0,2},{2,0},{4,6},{6,4},{8,10},{10,8},{12,14},{14,12},{16,18},{18,... | collective-permute-start | bytes 393224 | tf_op jit(solution)/shard_map/ppermute | solution.py:431
  221.8 9.1 %collective-permute-start.34 = (f32[256,128]{1,0:T(8,128)S(1)}, f32[256,128]{1,0:T(8,128)S(1)}, u32[]{:S(2)}, u32[]{:S(2)}) collective-permute-start(f32[256,128]{1,0:T(8,128)S(1)} %add.526), channel_id=1, source_target_pairs={{0,16},{2,18},{4,20},{6,22},{8,24},{10,26},{12,28},{14,30},{16,0},... | collective-permute-start | bytes 393224 | tf_op jit(solution)/shard_map/ppermute | solution.py:431
  223.9 9.2 %collective-permute-start.37 = (f32[256,128]{1,0:T(8,128)S(1)}, f32[256,128]{1,0:T(8,128)S(1)}, u32[]{:S(2)}, u32[]{:S(2)}) collective-permute-start(f32[256,128]{1,0:T(8,128)S(1)} %select_add_fusion), channel_id=1, source_target_pairs={{0,4},{2,6},{4,0},{6,2},{8,12},{10,14},{12,8},{14,10},{16,20},{18,... | collective-permute-start | bytes 393224 | tf_op jit(solution)/shard_map/ppermute | solution.py:431
  230.9 2.3 collective-permute-start.35
  233.0 14.9 %collective-permute-start.30 = (f32[1024,128]{1,0:T(8,128)S(1)}, f32[1024,128]{1,0:T(8,128)S(1)}, u32[]{:S(2)}, u32[]{:S(2)}) collective-permute-start(f32[1024,128]{1,0:T(8,128)S(1)} %constant_dynamic-slice_fusion.2), channel_id=1, source_target_pairs={{0,1},{1,0},{2,3},{3,2},{4,5},{5,4},{6,7},{7,6},{8,9},{9,8},{10,11... | collective-permute-start | bytes 1572872 | tf_op jit(solution)/shard_map/ppermute | solution.py:426
  233.1 5.9 %collective-permute-start.38 = (f32[256,128]{1,0:T(8,128)S(1)}, f32[256,128]{1,0:T(8,128)S(1)}, u32[]{:S(2)}, u32[]{:S(2)}) collective-permute-start(f32[256,128]{1,0:T(8,128)S(1)} %add.529), channel_id=1, source_target_pairs={{0,8},{2,10},{4,12},{6,14},{8,0},{10,2},{12,4},{14,6},{16,24},{18,... | collective-permute-start | bytes 393224 | tf_op jit(solution)/shard_map/ppermute | solution.py:431
  239.1 8.7 %collective-permute-start.39 = (f32[256,128]{1,0:T(8,128)S(1)}, f32[256,128]{1,0:T(8,128)S(1)}, u32[]{:S(2)}, u32[]{:S(2)}) collective-permute-start(f32[256,128]{1,0:T(8,128)S(1)} %add.530), channel_id=1, source_target_pairs={{0,16},{2,18},{4,20},{6,22},{8,24},{10,26},{12,28},{14,30},{16,0},... | collective-permute-start | bytes 393224 | tf_op jit(solution)/shard_map/ppermute | solution.py:431
  247.8 1.4 collective-permute-start.40
  (8 other events, 14.2 us)
Sparse Core Ops, SparseCore 0:
  95.6 73.3 all-gather.1
